TPU v7x, 32 devices: a whole 2x2x4 slice. The times are simulated.
32 devices in a mesh: prow: 4 (over y, x), pcol: 8 (over z, core).
Axes of the slice: x: 2, y: 2, z: 4, core: 2. Of those that a mesh axis runs over, the one named last changes fastest.
Arguments:
- matrix: float32 [4, 1024, 8, 1536], P('prow', None, 'pcol')
- pivots: int32 [256], replicated, may hold values from 256 to 4095, as said below
Outputs:
- factored: float32 [4, 1024, 8, 1536], P('prow', None, 'pcol')
Inputs may be any that keep to these rules, and one draw needn't show every extreme that they name: The 256 pivots are distinct global row indices; the values 256 and 4095 both occur.
All inputs are finite; a program needn't handle non-finite values.
Results may differ from a plain program's by a relative error of at most 0.000082.
Values sent between devices are 32-bit elements; how exact they have to be, the bound alone decides.
No kernel may reach another device: no remote copies, remote signals or barrier semaphores. Data moves between devices by JAX's collectives and lax.ppermute only.
A program may use at most 128 MiB of HBM per device.

v0:
```python
import jax
import jax.numpy as jnp
from jax import lax
from jax.sharding import PartitionSpec as P


def spread(array, axis, root):
    mine = lax.axis_index(axis) == root
    return lax.psum(jnp.where(mine, array, jnp.zeros_like(array)), axis)


def product(left, right):
    return jnp.dot(left, right, precision=lax.Precision.HIGHEST)


def eliminate(square):
    extent = square.shape[0]
    positions = jnp.arange(extent)

    def column_step(column, working):
        is_below = positions > column
        pivot_line = jnp.where(is_below, working[column, :], 0.0)
        factor_col = jnp.where(is_below, working[:, column] / working[column, column], 0.0)
        working = working - factor_col[:, None] * pivot_line[None, :]
        return jnp.where(
            is_below[:, None] & (positions == column)[None, :], factor_col[:, None], working
        )

    return lax.fori_loop(0, extent, column_step, square)


def nilpotent_inverse(strict_part):
    extent = strict_part.shape[0]
    identity = jnp.eye(extent, dtype=jnp.float32)
    result = identity - strict_part
    power = product(strict_part, strict_part)
    for level in range(3):
        result = product(result, identity + power)
        power = product(power, power)
    return result


def unit_lower_inverse(lower_tri):
    extent = lower_tri.shape[0]
    if extent <= 16:
        return nilpotent_inverse(jnp.tril(lower_tri, -1))
    midpoint = extent // 2
    first_inv = unit_lower_inverse(lower_tri[:midpoint, :midpoint])
    second_inv = unit_lower_inverse(lower_tri[midpoint:, midpoint:])
    off_block = -product(product(second_inv, lower_tri[midpoint:, :midpoint]), first_inv)
    zeros_block = jnp.zeros((midpoint, extent - midpoint), jnp.float32)
    top_part = jnp.concatenate([first_inv, zeros_block], axis=1)
    bottom_part = jnp.concatenate([off_block, second_inv], axis=1)
    return jnp.concatenate([top_part, bottom_part], axis=0)


def upper_inverse(upper_tri):
    extent = upper_tri.shape[0]
    if extent <= 16:
        diagonal = jnp.diagonal(upper_tri)
        scaled = jnp.triu(upper_tri, 1) / diagonal[:, None]
        return nilpotent_inverse(scaled) / diagonal[None, :]
    midpoint = extent // 2
    first_inv = upper_inverse(upper_tri[:midpoint, :midpoint])
    second_inv = upper_inverse(upper_tri[midpoint:, midpoint:])
    off_block = -product(product(first_inv, upper_tri[:midpoint, midpoint:]), second_inv)
    zeros_block = jnp.zeros((extent - midpoint, midpoint), jnp.float32)
    top_part = jnp.concatenate([first_inv, off_block], axis=1)
    bottom_part = jnp.concatenate([zeros_block, second_inv], axis=1)
    return jnp.concatenate([top_part, bottom_part], axis=0)


def factor(square):
    extent = square.shape[0]
    if extent <= 16:
        return eliminate(square)
    midpoint = extent // 2
    first_part = factor(square[:midpoint, :midpoint])
    upper_inv = upper_inverse(jnp.triu(first_part))
    lower_inv = unit_lower_inverse(jnp.tril(first_part, -1) + jnp.eye(midpoint, dtype=jnp.float32))
    below_left = product(square[midpoint:, :midpoint], upper_inv)
    above_right = product(lower_inv, square[:midpoint, midpoint:])
    reduced = square[midpoint:, midpoint:] - product(below_left, above_right)
    second_part = factor(reduced)
    top_part = jnp.concatenate([first_part, above_right], axis=1)
    bottom_part = jnp.concatenate([below_left, second_part], axis=1)
    return jnp.concatenate([top_part, bottom_part], axis=0)


def on_device(matrix, pivots):
    own_block = matrix[0, :, 0, :]
    rows_local = own_block.shape[0]
    panel_width = pivots.shape[0]
    row_count = lax.axis_size("prow")
    row_index = lax.axis_index("prow")
    col_index = lax.axis_index("pcol")
    local_rows = jnp.arange(rows_local, dtype=jnp.int32)
    global_rows = (
        local_rows // panel_width * row_count + row_index
    ) * panel_width + local_rows % panel_width
    owner_row = pivots // panel_width % row_count
    owner_slot = pivots // (panel_width * row_count) * panel_width + pivots % panel_width
    is_owner = owner_row == row_index
    selector = ((owner_slot[:, None] == local_rows[None, :]) & is_owner[:, None]).astype(
        jnp.float32
    )
    picked = product(selector, own_block)
    swapped_top = lax.psum(picked, "prow")
    old_top = spread(own_block[:panel_width], "prow", 0)
    matches = (global_rows[:, None] == pivots[None, :]).astype(jnp.float32)
    is_target = jnp.sum(matches, axis=1) > 0.5
    swapped = jnp.where(is_target[:, None], product(matches, old_top), own_block)
    swapped = swapped.at[:panel_width].set(
        jnp.where(row_index == 0, swapped_top, swapped[:panel_width])
    )
    identity = jnp.eye(panel_width, dtype=jnp.float32)
    packed = factor(jnp.where(col_index == 0, swapped_top[:, :panel_width], identity))
    upper_inv = upper_inverse(jnp.triu(packed))
    lower_left = product(swapped[:, :panel_width], upper_inv)
    left_all, packed_all = (spread(lower_left, "pcol", 0), spread(packed, "pcol", 0))
    lower_inv = unit_lower_inverse(jnp.tril(packed_all, -1) + identity)
    own_upper = product(lower_inv, swapped[:panel_width])
    upper_right = spread(own_upper, "prow", 0)
    trailing = swapped - product(left_all, upper_right)
    first_cols = jnp.where(col_index == 0, left_all, trailing[:, :panel_width])
    result = trailing.at[:, :panel_width].set(first_cols)
    top_block = upper_right.at[:, :panel_width].set(
        jnp.where(col_index == 0, packed_all, upper_right[:, :panel_width])
    )
    result = result.at[:panel_width].set(jnp.where(row_index == 0, top_block, result[:panel_width]))
    return result[None, :, None, :]


def solution(mesh):
    in_specs = (P("prow", None, "pcol", None), P())
    out_specs = P("prow", None, "pcol", None)
    return jax.shard_map(
        on_device, mesh=mesh, in_specs=in_specs, out_specs=out_specs, check_vma=False
    )
```

profile of v0, /device:TPU:0, one launch (start us, length us, event | category | flops | bytes accessed | tf_op | source)
XLA Modules:
  0.0 851.9 jit_solution(1302605597566347731)
XLA Ops:
  12.1 4.6 fusion.64
  17.7 89.2 %all-reduce.74.cloned.1.call-done = (f32[256,1536]{1,0:T(8,128)}, f32[256,1536]{1,0:T(8,128)}) async-done(((f32[256,1536]{1,0:T(8,128)}, f32[256,1536]{1,0:T(8,128)}), (f32[256,1536]{1,0:T(8,128)}, f32[256,1536]{1,0:T(8,128)})) %all-reduce.74.cloned.1.call-update) | async-done | bytes 3145744 | tf_op jit(solution)/shard_map/psum | solution.py:9
  108.0 22.7 %while.244 = (s32[]{:T(128)}, f32[16,16]{0,1:T(8,128)S(1)}, s32[]{:T(128)}) while((s32[]{:T(128)}, f32[16,16]{0,1:T(8,128)S(1)}, s32[]{:T(128)}) %tuple.621), condition=%wide.region_4.5_spmd.clone.clone, body=%wide.region_3.4_spmd.clone.clone.sunk | while | flops 1138 | bytes 6665 | solution.py:29
  134.0 22.8 %while.245 = (s32[]{:T(128)}, f32[16,16]{0,1:T(8,128)S(1)}, s32[]{:T(128)}) while((s32[]{:T(128)}, f32[16,16]{0,1:T(8,128)S(1)}, s32[]{:T(128)}) %tuple.624), condition=%wide.region_6.7_spmd.clone.clone, body=%wide.region_5.6_spmd.clone.clone.sunk | while | flops 1138 | bytes 6665 | solution.py:29
  163.5 22.7 %while.246 = (s32[]{:T(128)}, f32[16,16]{0,1:T(8,128)S(1)}, s32[]{:T(128)}) while((s32[]{:T(128)}, f32[16,16]{0,1:T(8,128)S(1)}, s32[]{:T(128)}) %tuple.627), condition=%wide.region_8.9_spmd.clone.clone, body=%wide.region_7.8_spmd.clone.clone.sunk | while | flops 1138 | bytes 6665 | solution.py:29
  189.4 22.8 %while.247 = (s32[]{:T(128)}, f32[16,16]{0,1:T(8,128)S(1)}, s32[]{:T(128)}) while((s32[]{:T(128)}, f32[16,16]{0,1:T(8,128)S(1)}, s32[]{:T(128)}) %tuple.630), condition=%wide.region_10.11_spmd.clone.clone, body=%wide.region_9.10_spmd.clone.clone.sunk | while | flops 1138 | bytes 6665 | solution.py:29
  226.0 22.7 %while.248 = (s32[]{:T(128)}, f32[16,16]{0,1:T(8,128)S(1)}, s32[]{:T(128)}) while((s32[]{:T(128)}, f32[16,16]{0,1:T(8,128)S(1)}, s32[]{:T(128)}) %tuple.633), condition=%wide.region_12.13_spmd.clone.clone, body=%wide.region_11.12_spmd.clone.clone.sunk | while | flops 1138 | bytes 6665 | solution.py:29
  252.0 22.8 %while.249 = (s32[]{:T(128)}, f32[16,16]{0,1:T(8,128)S(1)}, s32[]{:T(128)}) while((s32[]{:T(128)}, f32[16,16]{0,1:T(8,128)S(1)}, s32[]{:T(128)}) %tuple.636), condition=%wide.region_14.15_spmd.clone.clone, body=%wide.region_13.14_spmd.clone.clone.sunk | while | flops 1138 | bytes 6665 | solution.py:29
  281.5 22.7 %while.250 = (s32[]{:T(128)}, f32[16,16]{0,1:T(8,128)S(1)}, s32[]{:T(128)}) while((s32[]{:T(128)}, f32[16,16]{0,1:T(8,128)S(1)}, s32[]{:T(128)}) %tuple.639), condition=%wide.region_16.17_spmd.clone.clone, body=%wide.region_15.16_spmd.clone.clone.sunk | while | flops 1138 | bytes 6665 | solution.py:29
  307.4 23.0 %while.251 = (s32[]{:T(128)}, f32[16,16]{0,1:T(8,128)S(1)}, s32[]{:T(128)}) while((s32[]{:T(128)}, f32[16,16]{0,1:T(8,128)S(1)}, s32[]{:T(128)}) %tuple.642), condition=%wide.region_18.19_spmd.clone.clone, body=%wide.region_17.18_spmd.clone.clone.sunk | while | flops 1138 | bytes 6665 | solution.py:29
  370.2 22.7 %while.252 = (s32[]{:T(128)}, f32[16,16]{0,1:T(8,128)S(1)}, s32[]{:T(128)}) while((s32[]{:T(128)}, f32[16,16]{0,1:T(8,128)S(1)}, s32[]{:T(128)}) %tuple.645), condition=%wide.region_20.21_spmd.clone.clone, body=%wide.region_19.20_spmd.clone.clone.sunk | while | flops 1138 | bytes 6665 | solution.py:29
  396.2 22.8 %while.253 = (s32[]{:T(128)}, f32[16,16]{0,1:T(8,128)S(1)}, s32[]{:T(128)}) while((s32[]{:T(128)}, f32[16,16]{0,1:T(8,128)S(1)}, s32[]{:T(128)}) %tuple.648), condition=%wide.region_22.23_spmd.clone.clone, body=%wide.region_21.22_spmd.clone.clone.sunk | while | flops 1138 | bytes 6665 | solution.py:29
  425.7 22.7 %while.254 = (s32[]{:T(128)}, f32[16,16]{0,1:T(8,128)S(1)}, s32[]{:T(128)}) while((s32[]{:T(128)}, f32[16,16]{0,1:T(8,128)S(1)}, s32[]{:T(128)}) %tuple.651), condition=%wide.region_24.25_spmd.clone.clone, body=%wide.region_23.24_spmd.clone.clone.sunk | while | flops 1138 | bytes 6665 | solution.py:29
  451.6 22.8 %while.255 = (s32[]{:T(128)}, f32[16,16]{0,1:T(8,128)S(1)}, s32[]{:T(128)}) while((s32[]{:T(128)}, f32[16,16]{0,1:T(8,128)S(1)}, s32[]{:T(128)}) %tuple.654), condition=%wide.region_26.27_spmd.clone.clone, body=%wide.region_25.26_spmd.clone.clone.sunk | while | flops 1138 | bytes 6665 | solution.py:29
  488.2 22.7 %while.256 = (s32[]{:T(128)}, f32[16,16]{0,1:T(8,128)S(1)}, s32[]{:T(128)}) while((s32[]{:T(128)}, f32[16,16]{0,1:T(8,128)S(1)}, s32[]{:T(128)}) %tuple.657), condition=%wide.region_28.29_spmd.clone.clone, body=%wide.region_27.28_spmd.clone.clone.sunk | while | flops 1138 | bytes 6665 | solution.py:29
  514.2 23.2 %while.257 = (s32[]{:T(128)}, f32[16,16]{0,1:T(8,128)S(1)}, s32[]{:T(128)}) while((s32[]{:T(128)}, f32[16,16]{0,1:T(8,128)S(1)}, s32[]{:T(128)}) %tuple.660), condition=%wide.region_30.31_spmd.clone.clone, body=%wide.region_29.30_spmd.clone.clone.sunk | while | flops 1138 | bytes 6665 | solution.py:29
  544.1 22.7 %while.258 = (s32[]{:T(128)}, f32[16,16]{0,1:T(8,128)S(1)}, s32[]{:T(128)}) while((s32[]{:T(128)}, f32[16,16]{0,1:T(8,128)S(1)}, s32[]{:T(128)}) %tuple.663), condition=%wide.region_32.33_spmd.clone.clone, body=%wide.region_31.32_spmd.clone.clone.sunk | while | flops 1138 | bytes 6665 | solution.py:29
  570.3 22.8 %while.259 = (s32[]{:T(128)}, f32[16,16]{0,1:T(8,128)S(1)}, s32[]{:T(128)}) while((s32[]{:T(128)}, f32[16,16]{0,1:T(8,128)S(1)}, s32[]{:T(128)}) %tuple.666), condition=%wide.region_34.35_spmd.clone.clone, body=%wide.region_33.34_spmd.clone.clone.sunk | while | flops 1138 | bytes 6665 | solution.py:29
  637.4 6.5 bitcast_select_fusion.32
  662.5 60.4 %all-reduce.72.cloned.1.call-done = (f32[1024,256]{1,0:T(8,128)}, f32[256,256]{1,0:T(8,128)}) async-done(((f32[1024,256]{1,0:T(8,128)}, f32[256,256]{1,0:T(8,128)}), (f32[1024,256]{1,0:T(8,128)}, f32[256,256]{1,0:T(8,128)})) %all-reduce.72.cloned.1.call-update) | async-done | bytes 1310736 | tf_op jit(solution)/shard_map/psum | solution.py:9
  745.3 4.2 convolution_select_fusion
  750.5 59.2 %all-reduce.70.cloned.1.call-done = f32[256,1536]{1,0:T(8,128)} async-done(((f32[256,1536]{1,0:T(8,128)}), f32[256,1536]{1,0:T(8,128)}) %all-reduce.70.cloned.1.call-update) | async-done | bytes 1572880 | tf_op jit(solution)/shard_map/psum | solution.py:9
  809.6 8.2 convolution_subtract_fusion
  821.1 24.1 %copy.205 = f32[1,1024,1,1536]{3,2,1,0:T(1,128)} copy(f32[1,1024,1,1536]{3,1,2,0:T(8,128)S(1)} %fusion.68) | data formatting | bytes 12582912 | tf_op jit(solution)/shard_map/scatter | solution.py:130
  (2506 shorter events, 576.1 us)
Async XLA Ops:
  6.5 100.4 %all-reduce.74.cloned.1.call-start = ((), (), s32[]{:S(2)}) async-start(), calls=%async_computation.2 | async-start | bytes 6291456 | tf_op jit(solution)/shard_map/psum | solution.py:9
  7.9 4.2 copy-start.2
  16.7 0.7 copy-start.12
  16.7 706.1 %all-reduce.72.cloned.1.call-start = ((), (), s32[]{:S(2)}) async-start(), calls=%async_computation.1 | async-start | bytes 2621440 | tf_op jit(solution)/shard_map/psum | solution.py:9
  330.7 0.8 copy-start.10
  344.3 13.2 %copy-start.11 = (f32[128,128]{1,0:T(8,128)S(1)}, f32[128,128]{1,0:T(8,128)}, u32[]{:S(2)}) copy-start(f32[128,128]{1,0:T(8,128)} %copy-done.10) | copy-start | bytes 196612
  594.1 0.8 copy-start.6
  624.5 12.9 %copy-start.8 = (f32[256,1536]{1,0:T(8,128)S(1)}, f32[256,1536]{1,0:T(8,128)}, u32[]{:S(2)}) copy-start(f32[256,1536]{1,0:T(8,128)} %get-tuple-element.1559) | copy-start | bytes 4718596
  643.9 2.7 copy-start.1
  643.9 2.7 copy-start.4
  646.6 1.1 copy-start.7
  646.9 13.4 %copy-start = (f32[1024,1536]{1,0:T(8,128)}, f32[1024,1536]{1,0:T(8,128)S(1)}, u32[]{:S(2)}) copy-start(f32[1024,1536]{1,0:T(8,128)S(1)} %fusion.75) | copy-start | bytes 18874372
  662.4 147.2 %all-reduce.70.cloned.1.call-start = ((), (), s32[]{:S(2)}) async-start(), calls=%async_computation | async-start | bytes 3145728 | tf_op jit(solution)/shard_map/psum | solution.py:9
  749.5 60.1 %copy-start.5 = (f32[1024,256]{1,0:T(8,128)S(1)}, f32[1024,256]{1,0:T(8,128)}, u32[]{:S(2)}) copy-start(f32[1024,256]{1,0:T(8,128)} %get-tuple-element.1557) | copy-start | bytes 3145732
  818.8 1.4 copy-start.3
  818.8 1.4 copy-start.9
Sparse Core Ops, SparseCore 0:
  16.8 90.0 all-reduce.73
  662.5 60.2 all-reduce.71
  749.7 59.8 all-reduce.69
where the time goes:
time: 861 us; the launch traced here: 852 us
  local copies, waits for them, and re-layouts  235 us (27%)
  waiting for transfers between devices  209 us (24%)
  other arithmetic  205 us (24%)
  matrix products  183 us (21%)
  between operations  14.7 us (2%)
    psum x3, waiting for transfers between devices, spread(): return lax.psum(jnp.where(mine, array, jnp.zeros_like(array)), axis)  209 us
    dot_general x754, matrix products, product(): return jnp.dot(left, right, precision=lax.Precision.HIGHEST)  183 us
    broadcast_in_dim x256, other arithmetic, column_step(): jnp.where(is_below[:, None] & (positions == column)[None, :], factor_col[...  167 us
    dynamic_slice x256, local copies, waits for them, and re-layouts, column_step(): working[column, column]  150 us
    gather x48, local copies, waits for them, and re-layouts, upper_inverse(): diagonal = jnp.diagonal(upper_tri)  32.2 us
    scatter x1, local copies, waits for them, and re-layouts, on_device(): result.at[:panel_width]  24.1 us
    select_n x256, other arithmetic, column_step(): jnp.where(is_below[:, None] & (positions == column)[None, :], factor_col[...  19.4 us
    while x256, local copies, waits for them, and re-layouts  18.7 us
  transfers between devices with their start and end apart: 3, of which 3 were waited for; matrix products, arithmetic and copies ran while one was open for 0% of the time, Pallas kernels for 0%

commit v1 on v0

v1 whole, which is shorter than its diff:
```python
import functools

import jax
import jax.numpy as jnp
from jax import lax
from jax.experimental import pallas as pl
from jax.experimental.pallas import tpu as pltpu
from jax.sharding import PartitionSpec as P

LANES = 128
SUB = 8
HI = lax.Precision.HIGHEST


def pick_lane(tile, lane):
    return jnp.take_along_axis(tile, jnp.full((SUB, LANES), lane, jnp.int32), axis=1)


def row_of(tile, j):
    return jnp.broadcast_to(tile[j:j + 1, :], (SUB, LANES))


def factor_kernel(width, s_ref, packed_ref, linv_ref, uinv_ref, a_ref, m_ref, v_ref):
    groups = a_ref.shape[0]
    tiles = groups * SUB // LANES
    per_tile = LANES // SUB
    per_block = width // SUB
    sub = lax.broadcasted_iota(jnp.int32, (SUB, LANES), 0)
    lane = lax.broadcasted_iota(jnp.int32, (SUB, LANES), 1)

    for i in range(groups):
        a_ref[i] = s_ref[i * SUB:(i + 1) * SUB, :]
        diag = lane - (i % per_tile) * SUB == sub
        for t in range(tiles):
            block = jnp.where(diag, 1.0, 0.0) if i // per_tile == t else jnp.zeros((SUB, LANES), jnp.float32)
            m_ref[i, :, t * LANES:(t + 1) * LANES] = block
            if t > i // per_tile:
                linv_ref[i * SUB:(i + 1) * SUB, t * LANES:(t + 1) * LANES] = block

    def span(t):
        return slice(t * LANES, (t + 1) * LANES)

    for o in range(groups // per_block):
        base = o * per_block
        h = base // per_tile
        live = [(a_ref, t) for t in range(h + 1, tiles)] + [(m_ref, t) for t in range(h + 1)]

        def panel(i, c, base=base, h=h, live=live):
            b = base + i
            g = (b - h * per_tile) * SUB
            rows = pl.ds(pl.multiple_of(b * SUB, SUB), SUB)
            own = a_ref[b, :, span(h)]
            cols = [pick_lane(own, g + j) for j in range(SUB)]
            in_panel = (lane >= g) & (lane < g + SUB)
            after = lane >= g + SUB
            head = jnp.where(in_panel, jnp.where(lane - g == sub, -1.0, 0.0), jnp.where(after, own, 0.0))
            rest = [ref[b, :, span(t)] for ref, t in live]
            packed = own
            final = [head] + rest
            for j in range(SUB):
                at = sub == j
                coef = cols[j]
                r = 1.0 / row_of(coef, j)
                final = [jnp.where(at, x, y) for x, y in zip([head] + rest, final)]
                packed = jnp.where((lane == g + j) & (sub > j), coef * r, packed)
                for k in range(j, SUB):
                    packed = jnp.where((lane == g + k) & at, cols[k], packed)
                head_coef = jnp.where((sub < j) | after, coef, 0.0)
                v = row_of(head, j) * r
                head = jnp.where(at, v, head - head_coef * v)
                for n, x in enumerate(rest):
                    v = row_of(x, j) * r
                    rest[n] = jnp.where(at, v, x - coef * v)
                for k in range(j + 1, SUB):
                    v = row_of(cols[k], j) * r
                    cols[k] = jnp.where(at, v, cols[k] - coef * v)
            for t in range(h):
                packed_ref[rows, span(t)] = a_ref[b, :, span(t)]
            packed_ref[rows, span(h)] = jnp.where(after, final[0], packed)
            for (ref, t), x in zip(live, final[1:]):
                (packed_ref if ref is a_ref else linv_ref)[rows, span(t)] = x
            a_ref[b, :, span(h)] = head
            v_ref[0] = head
            for n, ((ref, t), x) in enumerate(zip(live, rest)):
                ref[b, :, span(t)] = x
                v_ref[n + 1] = x
            others = [base + lax.rem(i + s, per_block) for s in range(1, per_block)]
            heads = [a_ref[r, :, span(h)] for r in others]
            facs = [[pick_lane(x, g + j) for j in range(SUB)] for x in heads]
            for n, (ref, t) in enumerate([(a_ref, h)] + live):
                old = [jnp.where(in_panel, 0.0, x) for x in heads] if n == 0 else [ref[r, :, span(t)] for r in others]
                vs = [row_of([head] + rest and ([head] + rest)[n], j) for j in range(SUB)]
                for x, fac, r in zip(old, facs, others):
                    acc = [fac[j] * vs[j] for j in range(SUB)]
                    while len(acc) > 1:
                        acc = [p + q for p, q in zip(acc[::2], acc[1::2])]
                    ref[r, :, span(t)] = x - acc[0]
            return c

        lax.fori_loop(0, per_block, panel, 0)

        lo = (base % per_tile) * SUB
        pad = [jnp.zeros((n, LANES), jnp.float32) for n in (lo, LANES - lo - width)]

        def stack(x):
            return jnp.concatenate([p for p in (pad[0], x, pad[1]) if p.shape[0]], axis=0)

        def flat(ref, first, last, t):
            return ref[first:last, :, span(t)].reshape((last - first) * SUB, LANES)

        end = base + per_block
        right = [stack(flat(ref, base, end, t)) for ref, t in [(a_ref, h)] + live]
        for first, last in ((end, groups), (0, base)):
            if first == last:
                continue
            left = flat(a_ref, first, last, h)
            column = lax.broadcasted_iota(jnp.int32, left.shape, 1)
            for n, (ref, t) in enumerate([(a_ref, h)] + live):
                if ref is m_ref and first == 0:
                    continue
                old = left if n else None
                old = jnp.where((column >= lo) & (column < lo + width), 0.0, left) if n == 0 else flat(ref, first, last, t)
                new = old - jnp.dot(left, right[n], precision=HI, preferred_element_type=jnp.float32)
                ref[first:last, :, span(t)] = new.reshape(last - first, SUB, LANES)

    ri = lax.broadcasted_iota(jnp.int32, (SUB, LANES), 0)
    for i in range(groups):
        for t in range(tiles):
            x = a_ref[i, :, span(t)]
            keep = lane + t * LANES >= ri + i * SUB
            uinv_ref[i * SUB:(i + 1) * SUB, span(t)] = jnp.where(keep, -x, 0.0)


def vmem():
    return pl.BlockSpec(memory_space=pltpu.VMEM)


def smem():
    return pl.BlockSpec(memory_space=pltpu.SMEM)


def factor(square, width=32):
    size = square.shape[0]
    out = jax.ShapeDtypeStruct((size, size), jnp.float32)
    return pl.pallas_call(
        functools.partial(factor_kernel, width),
        out_shape=(out, out, out),
        in_specs=[vmem()],
        out_specs=(vmem(),) * 3,
        scratch_shapes=[
            pltpu.VMEM((size // SUB, SUB, size), jnp.float32),
            pltpu.VMEM((size // SUB, SUB, size), jnp.float32),
            pltpu.VMEM((1 + size // LANES, SUB, LANES), jnp.float32),
        ],
        cost_estimate=pl.CostEstimate(flops=4 * size**3, bytes_accessed=16 * size**2, transcendentals=0),
        name="factor",
    )(square)


def pick_kernel(slot_ref, own_ref, block_ref, out_ref):
    def group(q, c):
        for u in range(SUB):
            j = q * SUB + u
            row = block_ref[pl.ds(slot_ref[j], 1), :]
            out_ref[pl.ds(j, 1), :] = row * own_ref[j].astype(jnp.float32)
        return c

    lax.fori_loop(0, out_ref.shape[0] // SUB, group, 0)


def pick(block, slots, owned, tiles):
    rows, width = block.shape[0], slots.shape[0]
    return pl.pallas_call(
        pick_kernel,
        grid=(tiles,),
        out_shape=jax.ShapeDtypeStruct((width, tiles * width), jnp.float32),
        in_specs=[smem(), smem(), pl.BlockSpec((rows, width), lambda t: (0, t))],
        out_specs=pl.BlockSpec((width, width), lambda t: (0, t)),
        cost_estimate=pl.CostEstimate(
            flops=width * width * tiles, bytes_accessed=4 * (rows + width) * width * tiles, transcendentals=0
        ),
        name="pick",
    )(slots, owned, block)


def place_rows(slot_ref, rows_ref, target_ref):
    def group(q, c):
        for u in range(SUB):
            j = q * SUB + u
            target_ref[pl.ds(slot_ref[j], 1), :] = rows_ref[pl.ds(j, 1), :]
        return c

    lax.fori_loop(0, rows_ref.shape[0] // SUB, group, 0)


def place_kernel(slot_ref, block_ref, rows_ref, out_ref, buf_ref):
    rows = block_ref.shape[0]
    buf_ref[:rows, :] = block_ref[...]
    place_rows(slot_ref, rows_ref, buf_ref)
    out_ref[...] = buf_ref[:rows, :]


def place(block, rows, slots):
    height, width = block.shape[0], slots.shape[0]
    return pl.pallas_call(
        place_kernel,
        grid=(1,),
        out_shape=jax.ShapeDtypeStruct((height, width), jnp.float32),
        in_specs=[
            smem(),
            pl.BlockSpec((height, width), lambda t: (0, 0)),
            pl.BlockSpec((width, width), lambda t: (0, 0)),
        ],
        out_specs=pl.BlockSpec((height, width), lambda t: (0, 0)),
        scratch_shapes=[pltpu.VMEM((height + SUB, width), jnp.float32)],
        cost_estimate=pl.CostEstimate(flops=0, bytes_accessed=8 * height * width, transcendentals=0),
        name="place",
    )(slots, block, rows)


def halves(x):
    high = x.astype(jnp.bfloat16)
    low = (x - high.astype(jnp.float32)).astype(jnp.bfloat16)
    return high, low


def split_dot(left, right):
    acc = jnp.dot(left[0], right[1], preferred_element_type=jnp.float32)
    acc += jnp.dot(left[1], right[0], preferred_element_type=jnp.float32)
    return acc + jnp.dot(left[0], right[0], preferred_element_type=jnp.float32)


def update_kernel(
    slot_ref, where_ref, block_ref, panel_ref, pivot_ref, top_ref, packed_ref, linv_ref, uinv_ref,
    out_ref, high_ref, low_ref, buf_ref,
):
    rows, width = panel_ref.shape
    t = pl.program_id(0)
    first_row = where_ref[0] == 0
    first_col = (where_ref[1] == 0) & (t == 0)

    @pl.when(t == 0)
    def _():
        lower = jnp.dot(panel_ref[...], uinv_ref[...], precision=HI, preferred_element_type=jnp.float32)
        high_ref[...], low_ref[...] = halves(lower)
        out_ref[...] = lower

    upper = jnp.dot(linv_ref[...], pivot_ref[...], precision=HI, preferred_element_type=jnp.float32)

    @pl.when(jnp.logical_not(first_col))
    def _():
        buf_ref[:rows, :] = block_ref[...]
        place_rows(slot_ref, top_ref, buf_ref)
        out_ref[...] = buf_ref[:rows, :] - split_dot((high_ref[...], low_ref[...]), halves(upper))

    @pl.when(first_row)
    def _():
        out_ref[:width, :] = jnp.where(first_col, packed_ref[...], upper)


def update(block, panel, pivot_rows, old_top, packed, linv, uinv, slots, where):
    rows, cols = block.shape
    width = slots.shape[0]
    square = pl.BlockSpec((width, width), lambda t: (0, 0))
    tall = pl.BlockSpec((rows, width), lambda t: (0, t))
    flat = pl.BlockSpec((width, width), lambda t: (0, t))
    return pl.pallas_call(
        update_kernel,
        grid=(cols // width,),
        out_shape=jax.ShapeDtypeStruct((rows, cols), jnp.float32),
        in_specs=[
            smem(), smem(), tall, pl.BlockSpec((rows, width), lambda t: (0, 0)), flat, flat, square, square, square,
        ],
        out_specs=tall,
        scratch_shapes=[
            pltpu.VMEM((rows, width), jnp.bfloat16),
            pltpu.VMEM((rows, width), jnp.bfloat16),
            pltpu.VMEM((rows + SUB, width), jnp.float32),
        ],
        cost_estimate=pl.CostEstimate(
            flops=6 * rows * cols * width, bytes_accessed=8 * rows * cols, transcendentals=0
        ),
        name="update",
    )(slots, where, block, panel, pivot_rows, old_top, packed, linv, uinv)


def bits_of(n):
    return [1 << i for i in range(n.bit_length() - 1)]


def sum_over_rows(x, order, n_row):
    for bit in order:
        x = x + lax.ppermute(x, "prow", [(i, i ^ bit) for i in range(n_row)])
    return x


def spread_rows(x, order, n_row):
    have = [0]
    for bit in order:
        x = x + lax.ppermute(x, "prow", [(i, i ^ bit) for i in have])
        have = have + [i ^ bit for i in have]
    return x


def spread_cols(x, order):
    have = [0]
    for bit in order:
        x = x + lax.ppermute(x, "pcol", [(i, i ^ bit) for i in have])
        have = have + [i ^ bit for i in have]
    return x


def on_device(n_row, n_col, matrix, pivots):
    block = matrix[0, :, 0, :]
    rows, cols = block.shape
    width = pivots.shape[0]
    row = lax.axis_index("prow")
    col = lax.axis_index("pcol")
    owner = pivots // width % n_row
    slot = pivots // (width * n_row) * width + pivots % width
    mine = owner == row
    owned = mine.astype(jnp.int32)
    target = jnp.where(mine, slot, rows)
    where = jnp.stack([row, col]).astype(jnp.int32)
    row_bits, col_bits = bits_of(n_row), bits_of(n_col)
    at_first_row = row == 0
    at_first_col = col == 0

    square = pick(block, slot, owned * at_first_col.astype(jnp.int32), 1)
    square = sum_over_rows(square, row_bits, n_row)
    square = spread_cols(square, col_bits[::-1])
    packed, linv, uinv = factor(square)

    top = jnp.where(at_first_row, block[:width], 0.0)
    top_panel = spread_rows(top[:, :width], row_bits, n_row)
    panel = place(block, top_panel, target)
    panel = spread_cols(jnp.where(at_first_col, panel, 0.0), col_bits[::-1])

    picked = pick(block, slot, owned, cols // width)
    half = width // 2
    pivot_rows = jnp.concatenate([
        sum_over_rows(picked[:half], row_bits, n_row),
        sum_over_rows(picked[half:], row_bits[::-1], n_row),
    ])
    old_top = jnp.concatenate([
        spread_rows(top[:half], row_bits, n_row),
        spread_rows(top[half:], row_bits[::-1], n_row),
    ])
    result = update(block, panel, pivot_rows, old_top, packed, linv, uinv, target, where)
    return result[None, :, None, :]


def solution(mesh):
    spec = P("prow", None, "pcol", None)
    n_row, n_col = mesh.shape["prow"], mesh.shape["pcol"]
    return jax.shard_map(
        functools.partial(on_device, n_row, n_col), mesh=mesh, in_specs=(spec, P()), out_specs=spec, check_vma=False
    )
```

time: 861 us -> 139 us (0.16)
  local copies, waits for them, and re-layouts: 235 us -> 20.5 us
  waiting for transfers between devices: 209 us -> 11 us
  other arithmetic: 205 us -> 20.3 us
  matrix products: 183 us -> 0 us
  Pallas kernels: 0 us -> 44.8 us
  starting transfers between devices: 0.3 us -> 40.2 us
  between operations: 14.7 us -> 0.28 us
    psum x3 -> x0, waiting for transfers between devices: 209 us -> none  [spread(): return lax.psum(jnp.where(mine, array, jnp.zeros_like(array)), axis)]
    dot_general x754 -> x0, matrix products: 183 us -> none  [product(): return jnp.dot(left, right, precision=lax.Precision.HIGHEST)]
    broadcast_in_dim x256 -> x0, other arithmetic: 167 us -> none  [column_step(): jnp.where(is_below[:, None] & (positions == column)[None, :], factor_col[...]
    dynamic_slice x256 -> x0, local copies, waits for them, and re-layouts: 150 us -> none  [column_step(): working[column, column]]
    pallas_call x0 -> x5, Pallas kernels: none -> 44.8 us  [the longest x1 14.6 us: update(): pl.pallas_call(update_kernel, grid=(cols // width,), out_shape=jax.ShapeD...]
    ppermute x0 -> x18, starting transfers between devices: none -> 40.2 us  [the longest x6 24.1 us: spread_rows(): x = x + lax.ppermute(x, 'prow', [(i, i ^ bit) for i in have])]
    gather x48 -> x0, local copies, waits for them, and re-layouts: 32.2 us -> none  [upper_inverse(): diagonal = jnp.diagonal(upper_tri)]
    scatter x1 -> x0, local copies, waits for them, and re-layouts: 24.1 us -> none  [on_device(): result.at[:panel_width]]
  transfers between devices with their start and end apart: 3 -> 18, of which waited for: 3 -> 6; matrix products, arithmetic and copies ran while one was open for 0% -> 19% of each run, Pallas kernels for 0% -> 22%
where the time goes in v1:
time: 139 us; the launch traced here: 137 us
  Pallas kernels  44.8 us (32%)
  starting transfers between devices  40.2 us (29%)
  local copies, waits for them, and re-layouts  20.5 us (15%)
  other arithmetic  20.3 us (15%)
  waiting for transfers between devices  11 us (8%)
    ppermute x6, starting transfers between devices, spread_rows(): x = x + lax.ppermute(x, 'prow', [(i, i ^ bit) for i in have])  24.1 us
    pallas_call x1, Pallas kernels, update(): pl.pallas_call(update_kernel, grid=(cols // width,), out_shape=jax.ShapeD...  14.6 us
    pallas_call x1, Pallas kernels, factor(): pl.pallas_call(functools.partial(factor_kernel, width), out_shape=(out, o...  14.5 us
    ppermute x6, starting transfers between devices, spread_cols(): x = x + lax.ppermute(x, 'pcol', [(i, i ^ bit) for i in have])  13.1 us
    pallas_call x2, Pallas kernels, pick(): pl.pallas_call(pick_kernel, grid=(tiles,), out_shape=jax.ShapeDtypeStruct...  12.5 us
    broadcast_in_dim x1, local copies, waits for them, and re-layouts, on_device(): return result[None, :, None, :]  8.53 us
    ppermute x6, waiting for transfers between devices, sum_over_rows(): x = x + lax.ppermute(x, 'prow', [(i, i ^ bit) for i in range(n_row)])  7.71 us
    unnamed x9, local copies, waits for them, and re-layouts  5.95 us
  transfers between devices with their start and end apart: 18, of which 6 were waited for; matrix products, arithmetic and copies ran while one was open for 19% of the time, Pallas kernels for 22%

profile of v1, /device:TPU:0, one launch (start us, length us, event | category | flops | bytes accessed | tf_op | source)
XLA Modules:
  0.0 137.1 jit_solution(16972122454711061595)
XLA Ops:
  0.0 2.5 %slice.25 = f32[1,256,1,1536]{3,2,1,0:T(1,128)S(1)} slice(f32[1,1024,1,1536]{3,2,1,0:T(1,128)} %param.2), slice={[0:1], [0:256], [0:1], [0:1536]} | slice | bytes 3145728 | tf_op jit(solution)/shard_map/slice | solution.py:334
  3.4 4.8 %collective-permute-start = (f32[256,256]{1,0:T(8,128)}, f32[256,256]{1,0:T(8,128)S(1)}, u32[]{:S(2)}, u32[]{:S(2)}) collective-permute-start(f32[256,256]{1,0:T(8,128)} %slice.33), channel_id=1, source_target_pairs={{0,8},{1,9},{2,10},{3,11},{4,12},{5,13},{6,14},{7,15}} | collective-permute-start | bytes 786440 | tf_op jit(solution)/shard_map/ppermute | solution.py:300
  8.8 5.9 %copy.11 = f32[1,1024,1,1536]{3,1,2,0:T(8,128)} copy(f32[1,1024,1,1536]{3,2,1,0:T(1,128)} %param.2) | data formatting | bytes 12582912
  15.3 3.1 %pick.3 = f32[256,256]{1,0:T(8,128)} custom-call(s32[256]{0:T(256)} %get-tuple-element.14.slot_ref, s32[256]{0:T(256)} %get-tuple-element.11.own_ref, f32[1024,1536]{1,0:T(8,128)} %bitcast.16), custom_call_target="tpu_custom_call" | custom-call | flops 65536 | bytes 1310720 | tf_op jit(solution)/shard_map/pick/pallas_call | solution.py:173
  18.5 2.3 %collective-permute-start.1 = (f32[256,256]{1,0:T(8,128)S(1)}, f32[256,256]{1,0:T(8,128)S(1)}, u32[]{:S(2)}, u32[]{:S(2)}) collective-permute-start(f32[256,256]{1,0:T(8,128)S(1)} %slice_add_fusion), channel_id=1, source_target_pairs={{0,16},{8,24},{1,17},{9,25},{2,18},{10,26},{3,19},{11,27},{4,20},{... | collective-permute-start | bytes 786440 | tf_op jit(solution)/shard_map/ppermute | solution.py:300
  21.0 5.4 %collective-permute-done.13 = f32[256,256]{1,0:T(8,128)S(1)} collective-permute-done((f32[256,256]{1,0:T(8,128)}, f32[256,256]{1,0:T(8,128)S(1)}, u32[]{:S(2)}, u32[]{:S(2)}) %collective-permute-start.13) | collective-permute-done | bytes 262176 | tf_op jit(solution)/shard_map/ppermute | solution.py:293
  27.3 3.3 %place.1 = f32[1024,256]{1,0:T(8,128)} custom-call(s32[256]{0:T(256)} %get-tuple-element.13.slot_ref, f32[1024,1536]{1,0:T(8,128)} %bitcast.17, f32[256,256]{1,0:T(8,128)} %add.73.rows_ref), custom_call_target="tpu_custom_call" | custom-call | bytes 2097152 | tf_op jit(solution)/shard_map/place/pallas_call | solution.py:205
  31.9 4.3 %collective-permute-start.2 = (f32[1024,256]{1,0:T(8,128)S(1)}, f32[1024,256]{1,0:T(8,128)}, u32[]{:S(2)}, u32[]{:S(2)}) collective-permute-start(f32[1024,256]{1,0:T(8,128)S(1)} %broadcast_select_fusion), channel_id=1, source_target_pairs={{0,4},{8,12},{16,20},{24,28}} | collective-permute-start | bytes 3145736 | tf_op jit(solution)/shard_map/ppermute | solution.py:308
  37.4 4.4 %collective-permute-start.9 = (f32[128,1536]{1,0:T(8,128)}, f32[128,1536]{1,0:T(8,128)}, u32[]{:S(2)}, u32[]{:S(2)}) collective-permute-start(f32[128,1536]{1,0:T(8,128)} %get-tuple-element.17), channel_id=1, source_target_pairs={{0,8},{1,9},{2,10},{3,11},{4,12},{5,13},{6,14},{7,15}} | collective-permute-start | bytes 2359304 | tf_op jit(solution)/shard_map/ppermute | solution.py:300
  42.4 2.4 %collective-permute-start.11 = (f32[128,1536]{1,0:T(8,128)}, f32[128,1536]{1,0:T(8,128)}, u32[]{:S(2)}, u32[]{:S(2)}) collective-permute-start(f32[128,1536]{1,0:T(8,128)} %get-tuple-element.18), channel_id=1, source_target_pairs={{0,16},{1,17},{2,18},{3,19},{4,20},{5,21},{6,22},{7,23}} | collective-permute-start | bytes 2359304 | tf_op jit(solution)/shard_map/ppermute | solution.py:300
  44.8 9.4 %pick.2 = f32[256,1536]{1,0:T(8,128)} custom-call(s32[256]{0:T(256)} %get-tuple-element.14.slot_ref, s32[256]{0:T(256)} %convert_element_type.6.own_ref, f32[1024,1536]{1,0:T(8,128)} %bitcast.18), custom_call_target="tpu_custom_call" | custom-call | flops 393216 | bytes 7864320 | tf_op jit(solution)/shard_map/pick/pallas_call | solution.py:173
  55.6 1.5 %fusion.8 = (f32[128,1536]{1,0:T(8,128)S(1)}, f32[128,1536]{1,0:T(8,128)S(1)}) fusion(f32[256,1536]{1,0:T(8,128)} %pick.2), kind=kLoop, calls=%fused_computation.31 | loop fusion | bytes 3145728 | tf_op jit(solution)/shard_map/slice | solution.py:342
  57.2 2.3 %collective-permute-done.15 = f32[256,256]{1,0:T(8,128)S(1)} collective-permute-done((f32[256,256]{1,0:T(8,128)S(1)}, f32[256,256]{1,0:T(8,128)S(1)}, u32[]{:S(2)}, u32[]{:S(2)}) %collective-permute-start.15) | collective-permute-done | bytes 262176 | tf_op jit(solution)/shard_map/ppermute | solution.py:308
  62.3 1.5 %collective-permute-start.3 = (f32[1024,256]{1,0:T(8,128)S(1)}, f32[1024,256]{1,0:T(8,128)S(1)}, u32[]{:S(2)}, u32[]{:S(2)}) collective-permute-start(f32[1024,256]{1,0:T(8,128)S(1)} %fusion.9), channel_id=1, source_target_pairs={{0,2},{4,6},{8,10},{12,14},{16,18},{20,22},{24,26},{28,30}} | collective-permute-start | bytes 3145736 | tf_op jit(solution)/shard_map/ppermute | solution.py:308
  63.8 1.6 %fusion.4 = (f32[128,1536]{1,0:T(8,128)S(1)}, f32[128,1536]{1,0:T(8,128)S(1)}) fusion(f32[128,1536]{1,0:T(8,128)} %collective-permute-done.9, f32[1,256,1,1536]{3,1,2,0:T(8,128)S(1)} %copy_select_fusion, f32[128,1536]{1,0:T(8,128)} %collective-permute-done.11), kind=kLoop, calls=%fused_computation.27 | loop fusion | flops 393216 | bytes 4718592 | tf_op jit(solution)/shard_map/add | solution.py:300
  65.3 4.8 %collective-permute-start.10 = (f32[128,1536]{1,0:T(8,128)S(1)}, f32[128,1536]{1,0:T(8,128)}, u32[]{:S(2)}, u32[]{:S(2)}) collective-permute-start(f32[128,1536]{1,0:T(8,128)S(1)} %get-tuple-element.15), channel_id=1, source_target_pairs={{0,16},{8,24},{1,17},{9,25},{2,18},{10,26},{3,19},{11,27},{4,20},{... | collective-permute-start | bytes 2359304 | tf_op jit(solution)/shard_map/ppermute | solution.py:300
  70.5 5.3 %collective-permute-start.12 = (f32[128,1536]{1,0:T(8,128)S(1)}, f32[128,1536]{1,0:T(8,128)}, u32[]{:S(2)}, u32[]{:S(2)}) collective-permute-start(f32[128,1536]{1,0:T(8,128)S(1)} %get-tuple-element.16), channel_id=1, source_target_pairs={{0,8},{16,24},{1,9},{17,25},{2,10},{18,26},{3,11},{19,27},{4,12},{... | collective-permute-start | bytes 2359304 | tf_op jit(solution)/shard_map/ppermute | solution.py:300
  75.8 1.7 %collective-permute-done.7 = f32[128,1536]{1,0:T(8,128)S(1)} collective-permute-done((f32[128,1536]{1,0:T(8,128)S(1)}, f32[128,1536]{1,0:T(8,128)S(1)}, u32[]{:S(2)}, u32[]{:S(2)}) %collective-permute-start.7) | collective-permute-done | bytes 786464 | tf_op jit(solution)/shard_map/ppermute | solution.py:293
  78.8 2.5 %collective-permute-start.6 = (f32[128,1536]{1,0:T(8,128)}, f32[128,1536]{1,0:T(8,128)}, u32[]{:S(2)}, u32[]{:S(2)}) collective-permute-start(f32[128,1536]{1,0:T(8,128)} %get-tuple-element.19), channel_id=1, source_target_pairs={{0,16},{8,24},{16,0},{24,8},{1,17},{9,25},{17,1},{25,9},{2,18},{10... | collective-permute-start | bytes 2359304 | tf_op jit(solution)/shard_map/ppermute | solution.py:293
  84.2 3.3 %collective-permute-start.4 = (f32[1024,256]{1,0:T(8,128)S(1)}, f32[1024,256]{1,0:T(8,128)}, u32[]{:S(2)}, u32[]{:S(2)}) collective-permute-start(f32[1024,256]{1,0:T(8,128)S(1)} %add.75), channel_id=1, source_target_pairs={{0,1},{4,5},{2,3},{6,7},{8,9},{12,13},{10,11},{14,15},{16,17},{20,... | collective-permute-start | bytes 3145736 | tf_op jit(solution)/shard_map/ppermute | solution.py:308
  88.9 14.5 %factor.1 = (f32[256,256]{1,0:T(8,128)}, f32[256,256]{1,0:T(8,128)}, f32[256,256]{1,0:T(8,128)}) custom-call(f32[256,256]{1,0:T(8,128)} %add.89.s_ref), custom_call_target="tpu_custom_call" | custom-call | flops 67108864 | bytes 1048576 | tf_op jit(solution)/shard_map/factor/pallas_call | solution.py:145
  111.6 2.4 %add.76.panel_ref = f32[1024,256]{1,0:T(8,128)} add(f32[1024,256]{1,0:T(8,128)S(1)} %add.75, f32[1024,256]{1,0:T(8,128)} %collective-permute-done.4) | non-fusion elementwise | flops 262144 | bytes 3145728 | tf_op jit(solution)/shard_map/add | solution.py:308
  114.0 14.6 %update.1 = f32[1024,1536]{1,0:T(8,128)} custom-call(s32[256]{0:T(256)} %get-tuple-element.13.slot_ref, s32[2]{0:T(128)} %pad_add_fusion.where_ref, f32[1024,1536]{1,0:T(8,128)} %bitcast.19, f32[1024,256]{1,0:T(8,128)} %add.76.panel_ref, f32[256,1536]{1,0:T(8,128)} %pad_maximum_fusion.pivot_ref, f32[256,1536]{1,0:T(8,128)} %pad_maximum_fusion.1.top_ref, ...), custom_call_target="tpu_custom_call" | custom-call | flops 2415919104 | bytes 12582912 | tf_op jit(solution)/shard_map/update/pallas_call | solution.py:267
  128.5 8.5 %copy.4 = f32[1,1024,1,1536]{3,2,1,0:T(1,128)} copy(f32[1,1024,1,1536]{3,1,2,0:T(8,128)} %bitcast.20) | data formatting | bytes 12582912 | tf_op jit(solution)/shard_map/broadcast_in_dim | solution.py:350
  (56 shorter events, 24.6 us)
Async XLA Ops:
  2.5 5.8 %copy-start.3 = (s32[256]{0:T(256)S(1)}, s32[256]{0:T(256)}, u32[]{:S(2)}) copy-start(s32[256]{0:T(256)} %param.3) | copy-start | bytes 3076
  3.4 15.0 %collective-permute-start = (f32[256,256]{1,0:T(8,128)}, f32[256,256]{1,0:T(8,128)S(1)}, u32[]{:S(2)}, u32[]{:S(2)}) collective-permute-start(f32[256,256]{1,0:T(8,128)} %slice.33), channel_id=1, source_target_pairs={{0,8},{1,9},{2,10},{3,11},{4,12},{5,13},{6,14},{7,15}} | collective-permute-start | bytes 786440 | tf_op jit(solution)/shard_map/ppermute | solution.py:300
  18.4 8.0 %collective-permute-start.13 = (f32[256,256]{1,0:T(8,128)}, f32[256,256]{1,0:T(8,128)S(1)}, u32[]{:S(2)}, u32[]{:S(2)}) collective-permute-start(f32[256,256]{1,0:T(8,128)} %pick.3), channel_id=1, source_target_pairs={{0,8},{8,0},{16,24},{24,16},{1,9},{9,1},{17,25},{25,17},{2,10},{10... | collective-permute-start | bytes 786440 | tf_op jit(solution)/shard_map/ppermute | solution.py:293
  18.5 7.9 %copy-start.2 = (f32[256,256]{1,0:T(8,128)S(1)}, f32[256,256]{1,0:T(8,128)}, u32[]{:S(2)}) copy-start(f32[256,256]{1,0:T(8,128)} %pick.3) | copy-start | bytes 786436
  18.5 8.0 %collective-permute-start.1 = (f32[256,256]{1,0:T(8,128)S(1)}, f32[256,256]{1,0:T(8,128)S(1)}, u32[]{:S(2)}, u32[]{:S(2)}) collective-permute-start(f32[256,256]{1,0:T(8,128)S(1)} %slice_add_fusion), channel_id=1, source_target_pairs={{0,16},{8,24},{1,17},{9,25},{2,18},{10,26},{3,19},{11,27},{4,20},{... | collective-permute-start | bytes 786440 | tf_op jit(solution)/shard_map/ppermute | solution.py:300
  26.4 27.7 %collective-permute-start.14 = (f32[256,256]{1,0:T(8,128)S(1)}, f32[256,256]{1,0:T(8,128)S(1)}, u32[]{:S(2)}, u32[]{:S(2)}) collective-permute-start(f32[256,256]{1,0:T(8,128)S(1)} %add.85), channel_id=1, source_target_pairs={{0,16},{8,24},{16,0},{24,8},{1,17},{9,25},{17,1},{25,9},{2,18},{10... | collective-permute-start | bytes 786440 | tf_op jit(solution)/shard_map/ppermute | solution.py:293
  31.9 27.7 %collective-permute-start.2 = (f32[1024,256]{1,0:T(8,128)S(1)}, f32[1024,256]{1,0:T(8,128)}, u32[]{:S(2)}, u32[]{:S(2)}) collective-permute-start(f32[1024,256]{1,0:T(8,128)S(1)} %broadcast_select_fusion), channel_id=1, source_target_pairs={{0,4},{8,12},{16,20},{24,28}} | collective-permute-start | bytes 3145736 | tf_op jit(solution)/shard_map/ppermute | solution.py:308
  37.4 24.8 %collective-permute-start.9 = (f32[128,1536]{1,0:T(8,128)}, f32[128,1536]{1,0:T(8,128)}, u32[]{:S(2)}, u32[]{:S(2)}) collective-permute-start(f32[128,1536]{1,0:T(8,128)} %get-tuple-element.17), channel_id=1, source_target_pairs={{0,8},{1,9},{2,10},{3,11},{4,12},{5,13},{6,14},{7,15}} | collective-permute-start | bytes 2359304 | tf_op jit(solution)/shard_map/ppermute | solution.py:300
  42.4 21.4 %collective-permute-start.11 = (f32[128,1536]{1,0:T(8,128)}, f32[128,1536]{1,0:T(8,128)}, u32[]{:S(2)}, u32[]{:S(2)}) collective-permute-start(f32[128,1536]{1,0:T(8,128)} %get-tuple-element.18), channel_id=1, source_target_pairs={{0,16},{1,17},{2,18},{3,19},{4,20},{5,21},{6,22},{7,23}} | collective-permute-start | bytes 2359304 | tf_op jit(solution)/shard_map/ppermute | solution.py:300
  54.2 6.7 %copy-start.1 = (f32[1024,256]{1,0:T(8,128)S(1)}, f32[1024,256]{1,0:T(8,128)}, u32[]{:S(2)}) copy-start(f32[1024,256]{1,0:T(8,128)} %place.1) | copy-start | bytes 3145732
  54.2 5.3 %collective-permute-start.15 = (f32[256,256]{1,0:T(8,128)S(1)}, f32[256,256]{1,0:T(8,128)S(1)}, u32[]{:S(2)}, u32[]{:S(2)}) collective-permute-start(f32[256,256]{1,0:T(8,128)S(1)} %add.86), channel_id=1, source_target_pairs={{0,4},{8,12},{16,20},{24,28}} | collective-permute-start | bytes 786440 | tf_op jit(solution)/shard_map/ppermute | solution.py:308
  57.1 13.4 %collective-permute-start.5 = (f32[128,1536]{1,0:T(8,128)S(1)}, f32[128,1536]{1,0:T(8,128)S(1)}, u32[]{:S(2)}, u32[]{:S(2)}) collective-permute-start(f32[128,1536]{1,0:T(8,128)S(1)} %get-tuple-element.21), channel_id=1, source_target_pairs={{0,8},{8,0},{16,24},{24,16},{1,9},{9,1},{17,25},{25,17},{2,10},{10... | collective-permute-start | bytes 2359304 | tf_op jit(solution)/shard_map/ppermute | solution.py:293
  59.5 18.0 %collective-permute-start.7 = (f32[128,1536]{1,0:T(8,128)S(1)}, f32[128,1536]{1,0:T(8,128)S(1)}, u32[]{:S(2)}, u32[]{:S(2)}) collective-permute-start(f32[128,1536]{1,0:T(8,128)S(1)} %get-tuple-element.22), channel_id=1, source_target_pairs={{0,16},{8,24},{16,0},{24,8},{1,17},{9,25},{17,1},{25,9},{2,18},{10... | collective-permute-start | bytes 2359304 | tf_op jit(solution)/shard_map/ppermute | solution.py:293
  59.6 21.8 %collective-permute-start.16 = (f32[256,256]{1,0:T(8,128)S(1)}, f32[256,256]{1,0:T(8,128)S(1)}, u32[]{:S(2)}, u32[]{:S(2)}) collective-permute-start(f32[256,256]{1,0:T(8,128)S(1)} %add.87), channel_id=1, source_target_pairs={{0,2},{4,6},{8,10},{12,14},{16,18},{20,22},{24,26},{28,30}} | collective-permute-start | bytes 786440 | tf_op jit(solution)/shard_map/ppermute | solution.py:308
  62.2 15.3 %copy-start = (f32[256,1536]{1,0:T(8,128)S(1)}, f32[256,1536]{1,0:T(8,128)}, u32[]{:S(2)}) copy-start(f32[256,1536]{1,0:T(8,128)} %pick.2) | copy-start | bytes 4718596
  62.3 19.5 %collective-permute-start.3 = (f32[1024,256]{1,0:T(8,128)S(1)}, f32[1024,256]{1,0:T(8,128)S(1)}, u32[]{:S(2)}, u32[]{:S(2)}) collective-permute-start(f32[1024,256]{1,0:T(8,128)S(1)} %fusion.9), channel_id=1, source_target_pairs={{0,2},{4,6},{8,10},{12,14},{16,18},{20,22},{24,26},{28,30}} | collective-permute-start | bytes 3145736 | tf_op jit(solution)/shard_map/ppermute | solution.py:308
  65.3 38.0 %collective-permute-start.10 = (f32[128,1536]{1,0:T(8,128)S(1)}, f32[128,1536]{1,0:T(8,128)}, u32[]{:S(2)}, u32[]{:S(2)}) collective-permute-start(f32[128,1536]{1,0:T(8,128)S(1)} %get-tuple-element.15), channel_id=1, source_target_pairs={{0,16},{8,24},{1,17},{9,25},{2,18},{10,26},{3,19},{11,27},{4,20},{... | collective-permute-start | bytes 2359304 | tf_op jit(solution)/shard_map/ppermute | solution.py:300
  70.5 34.1 %collective-permute-start.12 = (f32[128,1536]{1,0:T(8,128)S(1)}, f32[128,1536]{1,0:T(8,128)}, u32[]{:S(2)}, u32[]{:S(2)}) collective-permute-start(f32[128,1536]{1,0:T(8,128)S(1)} %get-tuple-element.16), channel_id=1, source_target_pairs={{0,8},{16,24},{1,9},{17,25},{2,10},{18,26},{3,11},{19,27},{4,12},{... | collective-permute-start | bytes 2359304 | tf_op jit(solution)/shard_map/ppermute | solution.py:300
  78.8 27.2 %collective-permute-start.6 = (f32[128,1536]{1,0:T(8,128)}, f32[128,1536]{1,0:T(8,128)}, u32[]{:S(2)}, u32[]{:S(2)}) collective-permute-start(f32[128,1536]{1,0:T(8,128)} %get-tuple-element.19), channel_id=1, source_target_pairs={{0,16},{8,24},{16,0},{24,8},{1,17},{9,25},{17,1},{25,9},{2,18},{10... | collective-permute-start | bytes 2359304 | tf_op jit(solution)/shard_map/ppermute | solution.py:293
  81.3 26.2 %collective-permute-start.8 = (f32[128,1536]{1,0:T(8,128)}, f32[128,1536]{1,0:T(8,128)}, u32[]{:S(2)}, u32[]{:S(2)}) collective-permute-start(f32[128,1536]{1,0:T(8,128)} %get-tuple-element.20), channel_id=1, source_target_pairs={{0,8},{8,0},{16,24},{24,16},{1,9},{9,1},{17,25},{25,17},{2,10},{10... | collective-permute-start | bytes 2359304 | tf_op jit(solution)/shard_map/ppermute | solution.py:293
  81.8 2.4 %collective-permute-start.17 = (f32[256,256]{1,0:T(8,128)S(1)}, f32[256,256]{1,0:T(8,128)S(1)}, u32[]{:S(2)}, u32[]{:S(2)}) collective-permute-start(f32[256,256]{1,0:T(8,128)S(1)} %add.88), channel_id=1, source_target_pairs={{0,1},{4,5},{2,3},{6,7},{8,9},{12,13},{10,11},{14,15},{16,17},{20,... | collective-permute-start | bytes 786440 | tf_op jit(solution)/shard_map/ppermute | solution.py:308
  84.2 27.4 %collective-permute-start.4 = (f32[1024,256]{1,0:T(8,128)S(1)}, f32[1024,256]{1,0:T(8,128)}, u32[]{:S(2)}, u32[]{:S(2)}) collective-permute-start(f32[1024,256]{1,0:T(8,128)S(1)} %add.75), channel_id=1, source_target_pairs={{0,1},{4,5},{2,3},{6,7},{8,9},{12,13},{10,11},{14,15},{16,17},{20,... | collective-permute-start | bytes 3145736 | tf_op jit(solution)/shard_map/ppermute | solution.py:308

commit v2 on v1

--- a/solution.py
+++ b/solution.py
@@ -20,7 +20,7 @@
     return jnp.broadcast_to(tile[j:j + 1, :], (SUB, LANES))
 
 
-def factor_kernel(width, s_ref, packed_ref, linv_ref, uinv_ref, a_ref, m_ref, v_ref):
+def factor_kernel(width, s_ref, extra_ref, packed_ref, linv_ref, uinv_ref, a_ref, m_ref, v_ref):
     groups = a_ref.shape[0]
     tiles = groups * SUB // LANES
     per_tile = LANES // SUB
@@ -29,7 +29,7 @@
     lane = lax.broadcasted_iota(jnp.int32, (SUB, LANES), 1)
 
     for i in range(groups):
-        a_ref[i] = s_ref[i * SUB:(i + 1) * SUB, :]
+        a_ref[i] = s_ref[i * SUB:(i + 1) * SUB, :] + extra_ref[i * SUB:(i + 1) * SUB, :]
         diag = lane - (i % per_tile) * SUB == sub
         for t in range(tiles):
             block = jnp.where(diag, 1.0, 0.0) if i // per_tile == t else jnp.zeros((SUB, LANES), jnp.float32)
@@ -139,13 +139,13 @@
     return pl.BlockSpec(memory_space=pltpu.SMEM)
 
 
-def factor(square, width=32):
-    size = square.shape[0]
+def factor(square, extra, width=32):
+    size = square.shape[1]
     out = jax.ShapeDtypeStruct((size, size), jnp.float32)
     return pl.pallas_call(
         functools.partial(factor_kernel, width),
         out_shape=(out, out, out),
-        in_specs=[vmem()],
+        in_specs=[vmem(), vmem()],
         out_specs=(vmem(),) * 3,
         scratch_shapes=[
             pltpu.VMEM((size // SUB, SUB, size), jnp.float32),
@@ -154,7 +154,7 @@
         ],
         cost_estimate=pl.CostEstimate(flops=4 * size**3, bytes_accessed=16 * size**2, transcendentals=0),
         name="factor",
-    )(square)
+    )(square, extra)
 
 
 def pick_kernel(slot_ref, own_ref, block_ref, out_ref):
@@ -310,7 +310,7 @@
     return x
 
 
-def on_device(n_row, n_col, matrix, pivots):
+def dense_step(n_row, n_col, matrix, pivots):
     block = matrix[0, :, 0, :]
     rows, cols = block.shape
     width = pivots.shape[0]
@@ -329,7 +329,7 @@
     square = pick(block, slot, owned * at_first_col.astype(jnp.int32), 1)
     square = sum_over_rows(square, row_bits, n_row)
     square = spread_cols(square, col_bits[::-1])
-    packed, linv, uinv = factor(square)
+    packed, linv, uinv = factor(square, jnp.zeros_like(square))
 
     top = jnp.where(at_first_row, block[:width], 0.0)
     top_panel = spread_rows(top[:, :width], row_bits, n_row)
@@ -350,6 +350,340 @@
     return result[None, :, None, :]
 
 
+def raw():
+    return pl.BlockSpec(memory_space=pl.ANY)
+
+
+def first_kernel(slot_ref, where_ref, mine_ref, mat_ref, square_ref, top_ref, panel_ref, sem):
+    width = square_ref.shape[0]
+    panel = pltpu.make_async_copy(mat_ref.at[:, 0, pl.ds(0, width)], panel_ref, sem.at[0])
+    top = pltpu.make_async_copy(mat_ref.at[pl.ds(0, width), 0, pl.ds(0, width)], top_ref, sem.at[1])
+
+    def group(q, c):
+        for u in range(SUB):
+            j = q * SUB + u
+            source = mat_ref.at[slot_ref[j], :, pl.ds(0, width)]
+            pltpu.make_async_copy(source, square_ref.at[pl.ds(j, 1), :], sem.at[2]).start()
+        return c
+
+    lax.fori_loop(0, width // SUB, group, 0)
+    top.start()
+    panel.start()
+    pltpu.make_async_copy(mat_ref.at[pl.ds(0, width), 0, pl.ds(0, width)], square_ref, sem.at[2]).wait()
+    square_ref[...] = jnp.where(mine_ref[...] > 0, square_ref[...], 0.0)
+    top.wait()
+    top_ref[...] = jnp.where(where_ref[0] == 0, top_ref[...], 0.0)
+    panel.wait()
+
+
+def first_pick(mat, slot, where, mine):
+    rows, width = mat.shape[0], slot.shape[0]
+    square = jax.ShapeDtypeStruct((width, width), jnp.float32)
+    return pl.pallas_call(
+        first_kernel,
+        out_shape=(square, square, jax.ShapeDtypeStruct((rows, width), jnp.float32)),
+        in_specs=[smem(), smem(), vmem(), raw()],
+        out_specs=(vmem(),) * 3,
+        scratch_shapes=[pltpu.SemaphoreType.DMA((3,))],
+        cost_estimate=pl.CostEstimate(flops=0, bytes_accessed=8 * (rows + 2 * width) * width, transcendentals=0),
+        name="first_pick",
+    )(slot, where, mine, mat)
+
+
+def own_rows_kernel(slot_ref, mat_ref, left_ref, right_ref, sem):
+    count, half = left_ref.shape[0], left_ref.shape[2]
+
+    def group(q, c):
+        for u in range(SUB):
+            i = q * SUB + u
+            source = mat_ref.at[slot_ref[i]]
+            pltpu.make_async_copy(source.at[:, pl.ds(0, half)], left_ref.at[i], sem.at[0]).start()
+            pltpu.make_async_copy(source.at[:, pl.ds(half, half)], right_ref.at[i], sem.at[1]).start()
+        return c
+
+    lax.fori_loop(0, count // SUB, group, 0)
+    pltpu.make_async_copy(mat_ref.at[pl.ds(0, count), :, pl.ds(0, half)], left_ref, sem.at[0]).wait()
+    pltpu.make_async_copy(mat_ref.at[pl.ds(0, count), :, pl.ds(half, half)], right_ref, sem.at[1]).wait()
+
+
+def own_rows(mat, slots):
+    count, cols = slots.shape[0], mat.shape[2]
+    half = jax.ShapeDtypeStruct((count, 1, cols // 2), jnp.float32)
+    return pl.pallas_call(
+        own_rows_kernel,
+        out_shape=(half, half),
+        in_specs=[smem(), raw()],
+        out_specs=(vmem(),) * 2,
+        scratch_shapes=[pltpu.SemaphoreType.DMA((2,))],
+        cost_estimate=pl.CostEstimate(flops=0, bytes_accessed=8 * count * cols, transcendentals=0),
+        name="own_rows",
+    )(slots, mat)
+
+
+def top_rows_kernel(list_ref, mat_ref, *refs):
+    outs, sem = refs[:-1], refs[-1]
+    count = outs[0].shape[0]
+    for p, out_ref in enumerate(outs):
+        def group(q, c, p=p, out_ref=out_ref):
+            for u in range(SUB):
+                i = q * SUB + u
+                pltpu.make_async_copy(mat_ref.at[list_ref[p, i]], out_ref.at[i], sem.at[p]).start()
+            return c
+
+        lax.fori_loop(0, count // SUB, group, 0)
+    for p, out_ref in enumerate(outs):
+        pltpu.make_async_copy(mat_ref.at[pl.ds(0, count)], out_ref, sem.at[p]).wait()
+
+
+def top_rows(mat, lists):
+    n_row, count = lists.shape
+    cols = mat.shape[2]
+    return pl.pallas_call(
+        top_rows_kernel,
+        out_shape=(jax.ShapeDtypeStruct((count, 1, cols), jnp.float32),) * n_row,
+        in_specs=[smem(), raw()],
+        out_specs=(vmem(),) * n_row,
+        scratch_shapes=[pltpu.SemaphoreType.DMA((n_row,))],
+        cost_estimate=pl.CostEstimate(flops=0, bytes_accessed=8 * n_row * count * cols, transcendentals=0),
+        name="top_rows",
+    )(lists, mat)
+
+
+def pack_kernel(list_ref, where_ref, a_ref, b_ref, c_ref, d_ref, out_ref, top_ref):
+    width = a_ref.shape[0]
+    extra = out_ref.shape[0] - width
+    keep = where_ref[1] == 0
+    out_ref[:width, :] = jnp.where(keep, a_ref[...] + b_ref[...], 0.0)
+    top_ref[...] = jnp.where(keep, c_ref[...] + d_ref[...], 0.0)
+
+    def group(q, c):
+        for u in range(SUB):
+            i = q * SUB + u
+            out_ref[pl.ds(width + i, 1), :] = top_ref[pl.ds(list_ref[i], 1), :]
+        return c
+
+    lax.fori_loop(0, extra // SUB, group, 0)
+
+
+def pack(a, b, c, d, mine, where):
+    width, extra = a.shape[0], mine.shape[0]
+    return pl.pallas_call(
+        pack_kernel,
+        out_shape=jax.ShapeDtypeStruct((width + extra, width), jnp.float32),
+        in_specs=[smem(), smem()] + [vmem()] * 4,
+        out_specs=vmem(),
+        scratch_shapes=[pltpu.VMEM((width, width), jnp.float32)],
+        cost_estimate=pl.CostEstimate(flops=2 * width * width, bytes_accessed=24 * width * width, transcendentals=0),
+        name="pack",
+    )(mine, where, a, b, c, d)
+
+
+def finish_kernel(
+    n_row, where_ref, target_ref, pos_ref, mat_ref, panel_ref, panel_new_ref, square_ref, square_new_ref,
+    packed_ref, linv_ref, uinv_ref, a_old_ref, a_new_ref, b_old_ref, b_new_ref, *refs,
+):
+    tops, refs = refs[:n_row], refs[n_row:]
+    out_ref, block, pivot, panel, old, high, low, top, sem, in_sem, out_sem = refs
+    rows, _, cols = mat_ref.shape
+    width = linv_ref.shape[0]
+    count, half = tops[0].shape[0], cols // 2
+    tiles = cols // width
+    row, col = where_ref[0], where_ref[1]
+
+    def tile(t):
+        return pl.ds(pl.multiple_of(t * width, width), width)
+
+    @pl.when(col % 2 == 0)
+    def _():
+        pltpu.make_async_copy(panel_ref, panel.at[pl.ds(0, rows)], sem.at[0]).start()
+
+    @pl.when(col % 2 == 1)
+    def _():
+        pltpu.make_async_copy(panel_new_ref, panel.at[pl.ds(0, rows)], sem.at[0]).start()
+
+    for p in range(n_row):
+        @pl.when(row == p)
+        def _(p=p):
+            pltpu.make_async_copy(tops[p].at[:, 0, :], old, sem.at[1]).start()
+
+    blocks = [
+        pltpu.make_async_copy(mat_ref.at[:, 0, tile(t)], block.at[pl.ds(0, rows), tile(t)], in_sem.at[t])
+        for t in range(tiles)
+    ]
+    pieces = []
+    for part, (first, second) in enumerate(((a_old_ref, a_new_ref), (b_old_ref, b_new_ref))):
+        for k in range(n_row):
+            source = (first if 2 * k < n_row else second).at[pl.ds(k % (n_row // 2) * count, count), 0, :]
+            n_bits = n_row.bit_length() - 1
+            at = k if part == 0 else int(format(k, "0%db" % n_bits)[::-1], 2)
+            dest = pivot.at[pl.ds(at * count, count), pl.ds(part * half, half)]
+            pieces.append(pltpu.make_async_copy(source, dest, sem.at[2 + part * n_row + k]))
+    for copy in blocks[:1] + pieces + blocks[1:]:
+        copy.start()
+
+    lanes = lax.broadcasted_iota(jnp.int32, (width, n_row * count), 1)
+    places = jnp.where(lanes == pos_ref[...], 1.0, 0.0)
+    spread_inv = halves(jnp.dot(linv_ref[...], places, precision=HI, preferred_element_type=jnp.float32))
+    top[...] = square_ref[width:, :] + square_new_ref[width:, :]
+    pltpu.make_async_copy(panel_ref, panel.at[pl.ds(0, rows)], sem.at[0]).wait()
+    place_rows(target_ref, top, panel)
+    lower = split_dot(halves(panel[:rows, :]), halves(uinv_ref[...]))
+    high[...], low[...] = halves(lower)
+    pltpu.make_async_copy(tops[0].at[:, 0, :], old, sem.at[1]).wait()
+    for copy in blocks:
+        copy.wait()
+    place_rows(target_ref, old, block)
+
+    @pl.when(col == 0)
+    def _():
+        block[:rows, :width] = lower
+
+    for copy in pieces:
+        copy.wait()
+
+    def step(t, c):
+        upper = split_dot(spread_inv, halves(pivot[:, tile(t)]))
+        first_col = (col == 0) & (t == 0)
+
+        @pl.when(jnp.logical_not(first_col))
+        def _():
+            block[:rows, tile(t)] = block[:rows, tile(t)] - split_dot((high[...], low[...]), halves(upper))
+
+        @pl.when(row == 0)
+        def _():
+            block[:width, tile(t)] = jnp.where(first_col, packed_ref[...], upper)
+
+        pltpu.make_async_copy(block.at[pl.ds(0, rows), tile(t)], out_ref.at[:, 0, tile(t)], out_sem.at[t]).start()
+        return c
+
+    lax.fori_loop(0, tiles, step, 0)
+    for t in range(tiles):
+        pltpu.make_async_copy(block.at[pl.ds(0, rows), tile(t)], out_ref.at[:, 0, tile(t)], out_sem.at[t]).wait()
+
+
+def finish(where, target, pos, mat, panels, squares, factors, pivot_parts, tops):
+    rows, _, cols = mat.shape
+    width, n_row, count = factors[0].shape[0], len(tops), target.shape[0]
+    return pl.pallas_call(
+        functools.partial(finish_kernel, n_row),
+        out_shape=jax.ShapeDtypeStruct(mat.shape, jnp.float32),
+        in_specs=[smem(), smem(), vmem(), raw(), raw(), raw()] + [vmem()] * 5 + [raw()] * (4 + n_row),
+        out_specs=raw(),
+        scratch_shapes=[
+            pltpu.VMEM((rows + SUB, cols), jnp.float32),
+            pltpu.VMEM((n_row * count, cols), jnp.float32),
+            pltpu.VMEM((rows + SUB, width), jnp.float32),
+            pltpu.VMEM((count, cols), jnp.float32),
+            pltpu.VMEM((rows, width), jnp.bfloat16),
+            pltpu.VMEM((rows, width), jnp.bfloat16),
+            pltpu.VMEM((count, width), jnp.float32),
+            pltpu.SemaphoreType.DMA((2 + 2 * n_row,)),
+            pltpu.SemaphoreType.DMA((cols // width,)),
+            pltpu.SemaphoreType.DMA((cols // width,)),
+        ],
+        cost_estimate=pl.CostEstimate(
+            flops=6 * rows * cols * width, bytes_accessed=8 * rows * cols, transcendentals=0
+        ),
+        name="finish",
+    )(where, target, pos, mat, *panels, *squares, *factors, *pivot_parts, *tops)
+
+
+def capacity(n_row, width):
+    mean = width / n_row
+    return -(-int(mean + 4 * (mean * (1 - 1 / n_row)) ** 0.5) // SUB) * SUB
+
+
+def grow_rows(x, order, n_row):
+    for bit in order[:-1]:
+        x = jnp.concatenate([x, lax.ppermute(x, "prow", [(i, i ^ bit) for i in range(n_row)])])
+    return x, lax.ppermute(x, "prow", [(i, i ^ order[-1]) for i in range(n_row)])
+
+
+def tree(x, axes, order, to_pair, is_new):
+    have = [0]
+    for n, bit in enumerate(order):
+        moved = lax.ppermute(x, axes, [to_pair(i, i ^ bit) for i in have])
+        have = have + [i ^ bit for i in have]
+        if n + 1 < len(order):
+            x = jnp.where(is_new(bit, order[:n + 1]), moved, x)
+    return x, moved
+
+
+def capped_step(n_row, n_col, matrix, pivots):
+    _, rows, _, cols = matrix.shape
+    mat = matrix.reshape(rows, 1, cols)
+    width = pivots.shape[0]
+    count = capacity(n_row, width)
+    row, col = lax.axis_index("prow"), lax.axis_index("pcol")
+    where = jnp.stack([row, col]).astype(jnp.int32)
+    row_bits, col_bits = bits_of(n_row), bits_of(n_col)
+    owner, slot, rank = locate(pivots, n_row)
+    mine = owner == row
+    number = jnp.arange(width, dtype=jnp.int32)
+    ordinal = jnp.arange(count, dtype=jnp.int32)
+    hit = mine[None, :] & (rank[None, :] == ordinal[:, None])
+    my_slots = jnp.sum(jnp.where(hit, slot[None, :], 0), axis=1, dtype=jnp.int32)
+    my_number = jnp.sum(jnp.where(hit, number[None, :], 0), axis=1, dtype=jnp.int32)
+    target = jnp.where(jnp.any(hit, axis=1), my_slots, rows)
+    every = jnp.arange(n_row, dtype=jnp.int32)[:, None, None]
+    hits = (owner[None, None, :] == every) & (rank[None, None, :] == ordinal[None, :, None])
+    lists = jnp.sum(jnp.where(hits, number[None, None, :], 0), axis=2, dtype=jnp.int32)
+    pos = ((owner ^ row) * count + rank)[:, None]
+
+    square, top, panel = first_pick(mat, slot, where, mine.astype(jnp.int32)[:, None])
+
+    def flat(i, j):
+        return (i * n_col, j * n_col)
+
+    both = ("prow", "pcol")
+    for n, bit in enumerate(row_bits):
+        moved = lax.ppermute(square, both, [flat(i, i ^ bit) for i in range(n_row)])
+        back = row_bits[::-1]
+        held = [i for i in range(n_row) if all(not i & b for b in back[n:])]
+        moved_top = lax.ppermute(top, both, [flat(i, i ^ back[n]) for i in held])
+        if n + 1 < len(row_bits):
+            square, top = square + moved, top + moved_top
+    message = pack(square, moved, top, moved_top, my_number, where)
+
+    order = col_bits[::-1]
+
+    def pair(i, j):
+        return (i, j)
+
+    def is_new(bit, done):
+        return (col & bit) != 0
+
+    message, message_new = tree(message, "pcol", order, pair, is_new)
+    factors = factor(message, message_new)
+    panel, panel_new = tree(panel, "pcol", order, pair, is_new)
+
+    left, right = own_rows(mat, my_slots)
+    parts = grow_rows(left, row_bits, n_row) + grow_rows(right, row_bits[::-1], n_row)
+    tops = top_rows(mat, lists)
+    tops = tops[:1] + tuple(lax.ppermute(tops[p], "prow", [(0, p)]) for p in range(1, n_row))
+    out = finish(where, target, pos, mat, (panel, panel_new), (message, message_new), factors, parts, tops)
+    return out.reshape(matrix.shape)
+
+
+def locate(pivots, n_row):
+    width = pivots.shape[0]
+    owner = pivots // width % n_row
+    slot = pivots // (width * n_row) * width + pivots % width
+    number = jnp.arange(width, dtype=jnp.int32)
+    ahead = (owner[:, None] == owner[None, :]) & (number[None, :] < number[:, None])
+    return owner, slot, jnp.sum(ahead, axis=1, dtype=jnp.int32)
+
+
+def on_device(n_row, n_col, matrix, pivots):
+    owner, slot, rank = locate(pivots, n_row)
+    return lax.cond(
+        jnp.max(rank) < capacity(n_row, pivots.shape[0]),
+        functools.partial(capped_step, n_row, n_col),
+        functools.partial(dense_step, n_row, n_col),
+        matrix, pivots,
+    )
+
+
 def solution(mesh):
     spec = P("prow", None, "pcol", None)
     n_row, n_col = mesh.shape["prow"], mesh.shape["pcol"]

time: 139 us -> 110 us (0.79)
  local copies, waits for them, and re-layouts: 20.5 us -> 4.6 us
  other arithmetic: 20.3 us -> 8.8 us
  waiting for transfers between devices: 11 us -> 7.51 us
    add x16 -> x4, other arithmetic: 13.8 us -> 3.24 us  [the longest x2 1.97 us: capped_step(): square, top = (square + moved, top + moved_top)]
    broadcast_in_dim x1 -> x2, local copies, waits for them, and re-layouts: 8.53 us -> 1.59 us  [the longest x1 0.8 us: capped_step(): mine.astype(jnp.int32)[:, None]]
    slice x4 -> x0, local copies, waits for them, and re-layouts: 5.97 us -> none  [the longest x1 2.49 us: on_device(): top = jnp.where(at_first_row, block[:width], 0.0)]
    unnamed x9 -> x0, local copies, waits for them, and re-layouts: 5.95 us -> none
    ppermute x18 -> x17, waiting for transfers between devices: 11 us -> 7.51 us  [the longest x2 3.21 us: capped_step(): moved = lax.ppermute(square, both, [flat(i, i ^ bit) for i in range(n_row)])]
    concatenate x2 -> x0, other arithmetic: 2.63 us -> none  [the longest x1 1.36 us: on_device(): jnp.concatenate([spread_rows(top[:half], row_bits, n_row), spread_rows(to...]
    concatenate x0 -> x2, local copies, waits for them, and re-layouts: none -> 2.13 us  [grow_rows(): jnp.concatenate([x, lax.ppermute(x, 'prow', [(i, i ^ bit) for i in range(...]
    reduce_sum x0 -> x4, other arithmetic: none -> 1.82 us  [the longest x1 0.75 us: capped_step(): jnp.sum(jnp.where(hits, number[None, None, :], 0), axis=2, dtype=jnp.int32)]
  transfers between devices with their start and end apart: 18 -> 17, of which waited for: 6 -> 4; matrix products, arithmetic and copies ran while one was open for 19% -> 7% of each run, Pallas kernels for 22% -> 27%
where the time goes in v2:
time: 110 us; the launch traced here: 108 us
  Pallas kernels  45.9 us (42%)
  starting transfers between devices  40 us (36%)
  other arithmetic  8.8 us (8%)
  waiting for transfers between devices  7.51 us (7%)
  local copies, waits for them, and re-layouts  4.6 us (4%)
    pallas_call x1, Pallas kernels, factor(): pl.pallas_call(functools.partial(factor_kernel, width), out_shape=(out, o...  14.6 us
    ppermute x6, starting transfers between devices, tree(): moved = lax.ppermute(x, axes, [to_pair(i, i ^ bit) for i in have])  14.5 us
    pallas_call x1, Pallas kernels, finish(): pl.pallas_call(functools.partial(finish_kernel, n_row), out_shape=jax.Sha...  12.4 us
    ppermute x3, starting transfers between devices, capped_step(): lax.ppermute(tops[p], 'prow', [(0, p)])  8.78 us
    pallas_call x1, Pallas kernels, top_rows(): pl.pallas_call(top_rows_kernel, out_shape=(jax.ShapeDtypeStruct((count, 1...  7.9 us
    ppermute x2, starting transfers between devices, capped_step(): moved_top = lax.ppermute(top, both, [flat(i, i ^ back[n]) for i in held])  7.03 us
    ppermute x2, starting transfers between devices, capped_step(): moved = lax.ppermute(square, both, [flat(i, i ^ bit) for i in range(n_row)])  6.83 us
    pallas_call x1, Pallas kernels, first_pick(): pl.pallas_call(first_kernel, out_shape=(square, square, jax.ShapeDtypeStr...  4.58 us
  transfers between devices with their start and end apart: 17, of which 4 were waited for; matrix products, arithmetic and copies ran while one was open for 7% of the time, Pallas kernels for 27%

profile of v2, /device:TPU:0, one launch (start us, length us, event | category | flops | bytes accessed | tf_op | source)
XLA Modules:
  0.0 108.3 jit_solution(10737922409619184641)
XLA Ops:
  2.2 105.9 %conditional.1 = (f32[1,1024,1,1536]{3,2,1,0:T(1,128)}) conditional(s32[]{:T(128)} %convert_element_type.17, (s32[256]{0:T(256)}, f32[1,1024,1,1536]{3,2,1,0:T(1,128)}) %tuple.11, (s32[256]{0:T(256)}, f32[1,1024,1,1536]{3,2,1,0:T(1,128)}) %tuple.11), branch_computations={%region_2.3_spmd, %region_3.9_spmd} | conditional | flops 2488416000 | bytes 162279072 | solution.py:679
  5.6 4.6 %first_pick.1 = (f32[256,256]{1,0:T(8,128)}, f32[256,256]{1,0:T(8,128)}, f32[1024,256]{1,0:T(8,128)}) custom-call(s32[256]{0:T(256)} %fusion.7.slot_ref, s32[2]{0:T(128)} %pad_add_fusion.1.where_ref, s32[256,1]{1,0:T(8,128)} %copy.14.mine_ref, f32[1024,1,1536]{2,1,0:T(1,128)} %bitcast.25), custom_call_target="tpu_custom_call" | custom-call | bytes 3145728 | tf_op jit(solution)/shard_map/cond/branch_1_fun/first_pick/pallas_call | solution.py:382
  10.2 6.0 %collective-permute-start = (f32[1024,256]{1,0:T(8,128)}, f32[1024,256]{1,0:T(8,128)S(1)}, u32[]{:S(2)}, u32[]{:S(2)}) collective-permute-start(f32[1024,256]{1,0:T(8,128)} %get-tuple-element.23), channel_id=1, source_target_pairs={{0,4},{8,12},{16,20},{24,28}} | collective-permute-start | bytes 3145736 | tf_op jit(solution)/shard_map/cond/branch_1_fun/ppermute | solution.py:605
  16.2 3.4 %collective-permute-start.3 = (f32[256,256]{1,0:T(8,128)}, f32[256,256]{1,0:T(8,128)S(1)}, u32[]{:S(2)}, u32[]{:S(2)}) collective-permute-start(f32[256,256]{1,0:T(8,128)} %get-tuple-element.24), channel_id=1, source_target_pairs={{0,8},{8,0},{16,24},{24,16}} | collective-permute-start | bytes 786440 | tf_op jit(solution)/shard_map/cond/branch_1_fun/ppermute | solution.py:640
  19.6 3.6 %collective-permute-start.5 = (f32[256,256]{1,0:T(8,128)}, f32[256,256]{1,0:T(8,128)S(1)}, u32[]{:S(2)}, u32[]{:S(2)}) collective-permute-start(f32[256,256]{1,0:T(8,128)} %get-tuple-element.25), channel_id=1, source_target_pairs={{0,16}} | collective-permute-start | bytes 786440 | tf_op jit(solution)/shard_map/cond/branch_1_fun/ppermute | solution.py:643
  23.2 1.4 %collective-permute-done.3 = f32[256,256]{1,0:T(8,128)S(1)} collective-permute-done((f32[256,256]{1,0:T(8,128)}, f32[256,256]{1,0:T(8,128)S(1)}, u32[]{:S(2)}, u32[]{:S(2)}) %collective-permute-start.3) | collective-permute-done | bytes 262176 | tf_op jit(solution)/shard_map/cond/branch_1_fun/ppermute | solution.py:640
  25.7 3.4 %collective-permute-start.4 = (f32[256,256]{1,0:T(8,128)S(1)}, f32[256,256]{1,0:T(8,128)S(1)}, u32[]{:S(2)}, u32[]{:S(2)}) collective-permute-start(f32[256,256]{1,0:T(8,128)S(1)} %add.93.a_ref), channel_id=1, source_target_pairs={{0,16},{8,24},{16,0},{24,8}} | collective-permute-start | bytes 786440 | tf_op jit(solution)/shard_map/cond/branch_1_fun/ppermute | solution.py:640
  30.1 3.4 %collective-permute-start.6 = (f32[256,256]{1,0:T(8,128)S(1)}, f32[256,256]{1,0:T(8,128)S(1)}, u32[]{:S(2)}, u32[]{:S(2)}) collective-permute-start(f32[256,256]{1,0:T(8,128)S(1)} %add.94.c_ref), channel_id=1, source_target_pairs={{0,8},{16,24}} | collective-permute-start | bytes 786440 | tf_op jit(solution)/shard_map/cond/branch_1_fun/ppermute | solution.py:643
  34.4 1.8 %collective-permute-done.4.b_ref = f32[256,256]{1,0:T(8,128)S(1)} collective-permute-done((f32[256,256]{1,0:T(8,128)S(1)}, f32[256,256]{1,0:T(8,128)S(1)}, u32[]{:S(2)}, u32[]{:S(2)}) %collective-permute-start.4) | collective-permute-done | bytes 262176 | tf_op jit(solution)/shard_map/cond/branch_1_fun/ppermute | solution.py:640
  38.1 2.4 %pack.1 = f32[352,256]{1,0:T(8,128)} custom-call(s32[96]{0:T(128)} %get-tuple-element.49.list_ref, s32[2]{0:T(128)} %pad_add_fusion.1.where_ref, f32[256,256]{1,0:T(8,128)} %copy-done.8, f32[256,256]{1,0:T(8,128)} %copy-done.14, f32[256,256]{1,0:T(8,128)} %copy-done.10, f32[256,256]{1,0:T(8,128)} %copy-done.15), custom_call_target="tpu_custom_call" | custom-call | flops 131072 | bytes 1572864 | tf_op jit(solution)/shard_map/cond/branch_1_fun/pack/pallas_call | solution.py:470
  40.5 2.0 %collective-permute-start.7 = (f32[352,256]{1,0:T(8,128)}, f32[352,256]{1,0:T(8,128)}, u32[]{:S(2)}, u32[]{:S(2)}) collective-permute-start(f32[352,256]{1,0:T(8,128)} %pack.1), channel_id=1, source_target_pairs={{0,4},{8,12},{16,20},{24,28}} | collective-permute-start | bytes 1081352 | tf_op jit(solution)/shard_map/cond/branch_1_fun/ppermute | solution.py:605
  42.5 4.1 %own_rows.1 = (f32[96,1,768]{2,1,0:T(1,128)}, f32[96,1,768]{2,1,0:T(1,128)}) custom-call(s32[96]{0:T(128)} %get-tuple-element.50.slot_ref, f32[1024,1,1536]{2,1,0:T(1,128)} %bitcast.26), custom_call_target="tpu_custom_call" | custom-call | bytes 1179648 | tf_op jit(solution)/shard_map/cond/branch_1_fun/own_rows/pallas_call | solution.py:412
  46.6 1.8 %collective-permute-start.10 = (f32[96,1,768]{2,1,0:T(1,128)}, f32[96,1,768]{2,1,0:T(1,128)}, u32[]{:S(2)}, u32[]{:S(2)}) collective-permute-start(f32[96,1,768]{2,1,0:T(1,128)} %get-tuple-element.29), channel_id=1, source_target_pairs={{0,8},{8,0},{16,24},{24,16},{1,9},{9,1},{17,25},{25,17},{2,10},{10... | collective-permute-start | bytes 884744 | tf_op jit(solution)/shard_map/cond/branch_1_fun/ppermute | solution.py:598
  49.5 1.4 %collective-permute-start.1 = (f32[1024,256]{1,0:T(8,128)S(1)}, f32[1024,256]{1,0:T(8,128)S(1)}, u32[]{:S(2)}, u32[]{:S(2)}) collective-permute-start(f32[1024,256]{1,0:T(8,128)S(1)} %broadcast_select_fusion.3), channel_id=1, source_target_pairs={{0,2},{4,6},{8,10},{12,14},{16,18},{20,22},{24,26},{28,30}} | collective-permute-start | bytes 3145736 | tf_op jit(solution)/shard_map/cond/branch_1_fun/ppermute | solution.py:605
  50.9 1.3 %collective-permute-start.8 = (f32[352,256]{1,0:T(8,128)S(1)}, f32[352,256]{1,0:T(8,128)S(1)}, u32[]{:S(2)}, u32[]{:S(2)}) collective-permute-start(f32[352,256]{1,0:T(8,128)S(1)} %broadcast_select_fusion.5), channel_id=1, source_target_pairs={{0,2},{4,6},{8,10},{12,14},{16,18},{20,22},{24,26},{28,30}} | collective-permute-start | bytes 1081352 | tf_op jit(solution)/shard_map/cond/branch_1_fun/ppermute | solution.py:605
  53.1 7.9 %top_rows.1 = (f32[96,1,1536]{2,1,0:T(1,128)}, f32[96,1,1536]{2,1,0:T(1,128)}, f32[96,1,1536]{2,1,0:T(1,128)}, f32[96,1,1536]{2,1,0:T(1,128)}) custom-call(s32[4,96]{1,0:T(4,128)} %select_reduce_fusion.list_ref, f32[1024,1,1536]{2,1,0:T(1,128)} %bitcast.27), custom_call_target="tpu_custom_call" | custom-call | bytes 4718592 | tf_op jit(solution)/shard_map/cond/branch_1_fun/top_rows/pallas_call | solution.py:441
  61.0 2.8 %collective-permute-start.14 = (f32[96,1,1536]{2,1,0:T(1,128)}, f32[96,1,1536]{2,1,0:T(1,128)}, u32[]{:S(2)}, u32[]{:S(2)}) collective-permute-start(f32[96,1,1536]{2,1,0:T(1,128)} %get-tuple-element.32), channel_id=1, source_target_pairs={{0,8},{1,9},{2,10},{3,11},{4,12},{5,13},{6,14},{7,15}} | collective-permute-start | bytes 1769480 | tf_op jit(solution)/shard_map/cond/branch_1_fun/ppermute | solution.py:663
  63.8 3.1 %collective-permute-done.8 = f32[352,256]{1,0:T(8,128)S(1)} collective-permute-done((f32[352,256]{1,0:T(8,128)S(1)}, f32[352,256]{1,0:T(8,128)S(1)}, u32[]{:S(2)}, u32[]{:S(2)}) %collective-permute-start.8) | collective-permute-done | bytes 360480 | tf_op jit(solution)/shard_map/cond/branch_1_fun/ppermute | solution.py:605
  67.0 1.4 %collective-permute-start.9 = (f32[352,256]{1,0:T(8,128)S(1)}, f32[352,256]{1,0:T(8,128)S(1)}, u32[]{:S(2)}, u32[]{:S(2)}) collective-permute-start(f32[352,256]{1,0:T(8,128)S(1)} %broadcast_select_fusion.6.s_ref.square_ref), channel_id=1, source_target_pairs={{0,1},{4,5},{2,3},{6,7},{8,9},{12,13},{10,11},{14,15},{16,17},{20,... | collective-permute-start | bytes 1081352 | tf_op jit(solution)/shard_map/cond/branch_1_fun/ppermute | solution.py:605
  68.6 2.3 %collective-permute-start.2 = (f32[1024,256]{1,0:T(8,128)S(1)}, f32[1024,256]{1,0:T(8,128)}, u32[]{:S(2)}, u32[]{:S(2)}) collective-permute-start(f32[1024,256]{1,0:T(8,128)S(1)} %broadcast_select_fusion.4.panel_ref), channel_id=1, source_target_pairs={{0,1},{4,5},{2,3},{6,7},{8,9},{12,13},{10,11},{14,15},{16,17},{20,... | collective-permute-start | bytes 3145736 | tf_op jit(solution)/shard_map/cond/branch_1_fun/ppermute | solution.py:605
  71.1 3.8 %collective-permute-start.15 = (f32[96,1,1536]{2,1,0:T(1,128)}, f32[96,1,1536]{2,1,0:T(1,128)}, u32[]{:S(2)}, u32[]{:S(2)}) collective-permute-start(f32[96,1,1536]{2,1,0:T(1,128)} %get-tuple-element.33), channel_id=1, source_target_pairs={{0,16},{1,17},{2,18},{3,19},{4,20},{5,21},{6,22},{7,23}} | collective-permute-start | bytes 1769480 | tf_op jit(solution)/shard_map/cond/branch_1_fun/ppermute | solution.py:663
  76.0 2.1 %collective-permute-start.16 = (f32[96,1,1536]{2,1,0:T(1,128)}, f32[96,1,1536]{2,1,0:T(1,128)}, u32[]{:S(2)}, u32[]{:S(2)}) collective-permute-start(f32[96,1,1536]{2,1,0:T(1,128)} %get-tuple-element.34), channel_id=1, source_target_pairs={{0,24},{1,25},{2,26},{3,27},{4,28},{5,29},{6,30},{7,31}} | collective-permute-start | bytes 1769480 | tf_op jit(solution)/shard_map/cond/branch_1_fun/ppermute | solution.py:663
  80.8 14.6 %factor.3 = (f32[256,256]{1,0:T(8,128)}, f32[256,256]{1,0:T(8,128)}, f32[256,256]{1,0:T(8,128)}) custom-call(f32[352,256]{1,0:T(8,128)} %copy-done.3, f32[352,256]{1,0:T(8,128)} %copy-done.5), custom_call_target="tpu_custom_call" | custom-call | flops 67108864 | bytes 1048576 | tf_op jit(solution)/shard_map/cond/branch_1_fun/factor/pallas_call | solution.py:145
  95.5 12.4 %finish.1 = f32[1024,1,1536]{2,1,0:T(1,128)} custom-call(s32[2]{0:T(128)} %pad_add_fusion.1.where_ref, s32[96]{0:T(128)} %broadcast_select_fusion.7.target_ref, s32[256,1]{1,0:T(8,128)} %copy.15.pos_ref, f32[1024,1,1536]{2,1,0:T(1,128)} %bitcast.28, f32[1024,256]{1,0:T(8,128)} %copy-done.2, f32[1024,256]{1,0:T(8,128)} %collective-permute-done.2.panel_new_ref, ...), custom_call_target="tpu_custom_call" | custom-call | flops 2415919104 | bytes 12582912 | tf_op jit(solution)/shard_map/cond/branch_1_fun/finish/pallas_call | solution.py:567
  (72 shorter events, 15.7 us)
Async XLA Ops:
  10.2 23.5 %copy-start.17 = (s32[256]{0:T(256)S(1)}, s32[256]{0:T(256)}, u32[]{:S(2)}) copy-start(s32[256]{0:T(256)} %fusion.7.slot_ref) | copy-start | bytes 3076 | tf_op jit(solution)/shard_map/cond
  10.2 39.1 %collective-permute-start = (f32[1024,256]{1,0:T(8,128)}, f32[1024,256]{1,0:T(8,128)S(1)}, u32[]{:S(2)}, u32[]{:S(2)}) collective-permute-start(f32[1024,256]{1,0:T(8,128)} %get-tuple-element.23), channel_id=1, source_target_pairs={{0,4},{8,12},{16,20},{24,28}} | collective-permute-start | bytes 3145736 | tf_op jit(solution)/shard_map/cond/branch_1_fun/ppermute | solution.py:605
  16.2 8.5 %collective-permute-start.3 = (f32[256,256]{1,0:T(8,128)}, f32[256,256]{1,0:T(8,128)S(1)}, u32[]{:S(2)}, u32[]{:S(2)}) collective-permute-start(f32[256,256]{1,0:T(8,128)} %get-tuple-element.24), channel_id=1, source_target_pairs={{0,8},{8,0},{16,24},{24,16}} | collective-permute-start | bytes 786440 | tf_op jit(solution)/shard_map/cond/branch_1_fun/ppermute | solution.py:640
  19.6 9.5 %collective-permute-start.5 = (f32[256,256]{1,0:T(8,128)}, f32[256,256]{1,0:T(8,128)S(1)}, u32[]{:S(2)}, u32[]{:S(2)}) collective-permute-start(f32[256,256]{1,0:T(8,128)} %get-tuple-element.25), channel_id=1, source_target_pairs={{0,16}} | collective-permute-start | bytes 786440 | tf_op jit(solution)/shard_map/cond/branch_1_fun/ppermute | solution.py:643
  25.7 11.7 %copy-start.8 = (f32[256,256]{1,0:T(8,128)}, f32[256,256]{1,0:T(8,128)S(1)}, u32[]{:S(2)}) copy-start(f32[256,256]{1,0:T(8,128)S(1)} %add.93.a_ref) | copy-start | bytes 786436 | tf_op jit(solution)/shard_map/cond
  25.7 10.5 %collective-permute-start.4 = (f32[256,256]{1,0:T(8,128)S(1)}, f32[256,256]{1,0:T(8,128)S(1)}, u32[]{:S(2)}, u32[]{:S(2)}) collective-permute-start(f32[256,256]{1,0:T(8,128)S(1)} %add.93.a_ref), channel_id=1, source_target_pairs={{0,16},{8,24},{16,0},{24,8}} | collective-permute-start | bytes 786440 | tf_op jit(solution)/shard_map/cond/branch_1_fun/ppermute | solution.py:640
  30.1 7.3 %copy-start.10 = (f32[256,256]{1,0:T(8,128)}, f32[256,256]{1,0:T(8,128)S(1)}, u32[]{:S(2)}) copy-start(f32[256,256]{1,0:T(8,128)S(1)} %add.94.c_ref) | copy-start | bytes 786436 | tf_op jit(solution)/shard_map/cond
  30.1 7.3 %collective-permute-start.6 = (f32[256,256]{1,0:T(8,128)S(1)}, f32[256,256]{1,0:T(8,128)S(1)}, u32[]{:S(2)}, u32[]{:S(2)}) collective-permute-start(f32[256,256]{1,0:T(8,128)S(1)} %add.94.c_ref), channel_id=1, source_target_pairs={{0,8},{16,24}} | collective-permute-start | bytes 786440 | tf_op jit(solution)/shard_map/cond/branch_1_fun/ppermute | solution.py:643
  40.5 10.4 %collective-permute-start.7 = (f32[352,256]{1,0:T(8,128)}, f32[352,256]{1,0:T(8,128)}, u32[]{:S(2)}, u32[]{:S(2)}) collective-permute-start(f32[352,256]{1,0:T(8,128)} %pack.1), channel_id=1, source_target_pairs={{0,4},{8,12},{16,20},{24,28}} | collective-permute-start | bytes 1081352 | tf_op jit(solution)/shard_map/cond/branch_1_fun/ppermute | solution.py:605
  46.6 24.5 %collective-permute-start.10 = (f32[96,1,768]{2,1,0:T(1,128)}, f32[96,1,768]{2,1,0:T(1,128)}, u32[]{:S(2)}, u32[]{:S(2)}) collective-permute-start(f32[96,1,768]{2,1,0:T(1,128)} %get-tuple-element.29), channel_id=1, source_target_pairs={{0,8},{8,0},{16,24},{24,16},{1,9},{9,1},{17,25},{25,17},{2,10},{10... | collective-permute-start | bytes 884744 | tf_op jit(solution)/shard_map/cond/branch_1_fun/ppermute | solution.py:598
  48.4 27.6 %collective-permute-start.12 = (f32[96,1,768]{2,1,0:T(1,128)}, f32[96,1,768]{2,1,0:T(1,128)}, u32[]{:S(2)}, u32[]{:S(2)}) collective-permute-start(f32[96,1,768]{2,1,0:T(1,128)} %get-tuple-element.30), channel_id=1, source_target_pairs={{0,16},{8,24},{16,0},{24,8},{1,17},{9,25},{17,1},{25,9},{2,18},{10... | collective-permute-start | bytes 884744 | tf_op jit(solution)/shard_map/cond/branch_1_fun/ppermute | solution.py:598
  49.5 19.0 %collective-permute-start.1 = (f32[1024,256]{1,0:T(8,128)S(1)}, f32[1024,256]{1,0:T(8,128)S(1)}, u32[]{:S(2)}, u32[]{:S(2)}) collective-permute-start(f32[1024,256]{1,0:T(8,128)S(1)} %broadcast_select_fusion.3), channel_id=1, source_target_pairs={{0,2},{4,6},{8,10},{12,14},{16,18},{20,22},{24,26},{28,30}} | collective-permute-start | bytes 3145736 | tf_op jit(solution)/shard_map/cond/branch_1_fun/ppermute | solution.py:605
  50.9 16.0 %collective-permute-start.8 = (f32[352,256]{1,0:T(8,128)S(1)}, f32[352,256]{1,0:T(8,128)S(1)}, u32[]{:S(2)}, u32[]{:S(2)}) collective-permute-start(f32[352,256]{1,0:T(8,128)S(1)} %broadcast_select_fusion.5), channel_id=1, source_target_pairs={{0,2},{4,6},{8,10},{12,14},{16,18},{20,22},{24,26},{28,30}} | collective-permute-start | bytes 1081352 | tf_op jit(solution)/shard_map/cond/branch_1_fun/ppermute | solution.py:605
  61.0 18.2 %collective-permute-start.14 = (f32[96,1,1536]{2,1,0:T(1,128)}, f32[96,1,1536]{2,1,0:T(1,128)}, u32[]{:S(2)}, u32[]{:S(2)}) collective-permute-start(f32[96,1,1536]{2,1,0:T(1,128)} %get-tuple-element.32), channel_id=1, source_target_pairs={{0,8},{1,9},{2,10},{3,11},{4,12},{5,13},{6,14},{7,15}} | collective-permute-start | bytes 1769480 | tf_op jit(solution)/shard_map/cond/branch_1_fun/ppermute | solution.py:663
  67.0 12.3 %collective-permute-start.9 = (f32[352,256]{1,0:T(8,128)S(1)}, f32[352,256]{1,0:T(8,128)S(1)}, u32[]{:S(2)}, u32[]{:S(2)}) collective-permute-start(f32[352,256]{1,0:T(8,128)S(1)} %broadcast_select_fusion.6.s_ref.square_ref), channel_id=1, source_target_pairs={{0,1},{4,5},{2,3},{6,7},{8,9},{12,13},{10,11},{14,15},{16,17},{20,... | collective-permute-start | bytes 1081352 | tf_op jit(solution)/shard_map/cond/branch_1_fun/ppermute | solution.py:605
  68.6 26.8 %copy-start.2 = (f32[1024,256]{1,0:T(8,128)}, f32[1024,256]{1,0:T(8,128)S(1)}, u32[]{:S(2)}) copy-start(f32[1024,256]{1,0:T(8,128)S(1)} %broadcast_select_fusion.4.panel_ref) | copy-start | bytes 3145732 | tf_op jit(solution)/shard_map/cond
  68.6 11.6 %copy-start.18 = (s32[96]{0:T(128)S(1)}, s32[96]{0:T(128)}, u32[]{:S(2)}) copy-start(s32[96]{0:T(128)} %get-tuple-element.50.slot_ref) | copy-start | bytes 1156 | tf_op jit(solution)/shard_map/cond
  68.6 26.8 %collective-permute-start.2 = (f32[1024,256]{1,0:T(8,128)S(1)}, f32[1024,256]{1,0:T(8,128)}, u32[]{:S(2)}, u32[]{:S(2)}) collective-permute-start(f32[1024,256]{1,0:T(8,128)S(1)} %broadcast_select_fusion.4.panel_ref), channel_id=1, source_target_pairs={{0,1},{4,5},{2,3},{6,7},{8,9},{12,13},{10,11},{14,15},{16,17},{20,... | collective-permute-start | bytes 3145736 | tf_op jit(solution)/shard_map/cond/branch_1_fun/ppermute | solution.py:605
  71.1 24.3 %collective-permute-start.15 = (f32[96,1,1536]{2,1,0:T(1,128)}, f32[96,1,1536]{2,1,0:T(1,128)}, u32[]{:S(2)}, u32[]{:S(2)}) collective-permute-start(f32[96,1,1536]{2,1,0:T(1,128)} %get-tuple-element.33), channel_id=1, source_target_pairs={{0,16},{1,17},{2,18},{3,19},{4,20},{5,21},{6,22},{7,23}} | collective-permute-start | bytes 1769480 | tf_op jit(solution)/shard_map/cond/branch_1_fun/ppermute | solution.py:663
  76.0 19.5 %copy-start.7 = (f32[192,1,768]{2,1,0:T(1,128)}, f32[192,1,768]{2,1,0:T(1,128)S(1)}, u32[]{:S(2)}) copy-start(f32[192,1,768]{2,1,0:T(1,128)S(1)} %constant_dynamic-update-slice_fusion.a_old_ref) | copy-start | bytes 1769476 | tf_op jit(solution)/shard_map/cond
  76.0 19.4 %collective-permute-start.16 = (f32[96,1,1536]{2,1,0:T(1,128)}, f32[96,1,1536]{2,1,0:T(1,128)}, u32[]{:S(2)}, u32[]{:S(2)}) collective-permute-start(f32[96,1,1536]{2,1,0:T(1,128)} %get-tuple-element.34), channel_id=1, source_target_pairs={{0,24},{1,25},{2,26},{3,27},{4,28},{5,29},{6,30},{7,31}} | collective-permute-start | bytes 1769480 | tf_op jit(solution)/shard_map/cond/branch_1_fun/ppermute | solution.py:663
  79.2 16.3 %copy-start.6 = (f32[192,1,768]{2,1,0:T(1,128)}, f32[192,1,768]{2,1,0:T(1,128)S(1)}, u32[]{:S(2)}) copy-start(f32[192,1,768]{2,1,0:T(1,128)S(1)} %constant_dynamic-update-slice_fusion.2.b_old_ref) | copy-start | bytes 1769476 | tf_op jit(solution)/shard_map/cond
  79.2 16.2 %collective-permute-start.13 = (f32[192,1,768]{2,1,0:T(1,128)S(1)}, f32[192,1,768]{2,1,0:T(1,128)}, u32[]{:S(2)}, u32[]{:S(2)}) collective-permute-start(f32[192,1,768]{2,1,0:T(1,128)S(1)} %constant_dynamic-update-slice_fusion.2.b_old_ref), channel_id=1, source_target_pairs={{0,8},{8,0},{16,24},{24,16},{1,9},{9,1},{17,25},{25,17},{2,10},{10... | collective-permute-start | bytes 1769480 | tf_op jit(solution)/shard_map/cond/branch_1_fun/ppermute | solution.py:599
  79.3 16.1 %collective-permute-start.11 = (f32[192,1,768]{2,1,0:T(1,128)S(1)}, f32[192,1,768]{2,1,0:T(1,128)}, u32[]{:S(2)}, u32[]{:S(2)}) collective-permute-start(f32[192,1,768]{2,1,0:T(1,128)S(1)} %constant_dynamic-update-slice_fusion.a_old_ref), channel_id=1, source_target_pairs={{0,16},{8,24},{16,0},{24,8},{1,17},{9,25},{17,1},{25,9},{2,18},{10... | collective-permute-start | bytes 1769480 | tf_op jit(solution)/shard_map/cond/branch_1_fun/ppermute | solution.py:599
  (8 other events, 21.3 us)

commit v3 on v1

--- a/solution.py
+++ b/solution.py
@@ -20,7 +20,7 @@
     return jnp.broadcast_to(tile[j:j + 1, :], (SUB, LANES))
 
 
-def factor_kernel(width, s_ref, packed_ref, linv_ref, uinv_ref, a_ref, m_ref, v_ref):
+def factor_kernel(width, s_ref, extra_ref, packed_ref, linv_ref, uinv_ref, a_ref, m_ref, v_ref):
     groups = a_ref.shape[0]
     tiles = groups * SUB // LANES
     per_tile = LANES // SUB
@@ -29,7 +29,7 @@
     lane = lax.broadcasted_iota(jnp.int32, (SUB, LANES), 1)
 
     for i in range(groups):
-        a_ref[i] = s_ref[i * SUB:(i + 1) * SUB, :]
+        a_ref[i] = s_ref[i * SUB:(i + 1) * SUB, :] + extra_ref[i * SUB:(i + 1) * SUB, :]
         diag = lane - (i % per_tile) * SUB == sub
         for t in range(tiles):
             block = jnp.where(diag, 1.0, 0.0) if i // per_tile == t else jnp.zeros((SUB, LANES), jnp.float32)
@@ -139,13 +139,13 @@
     return pl.BlockSpec(memory_space=pltpu.SMEM)
 
 
-def factor(square, width=32):
-    size = square.shape[0]
+def factor(square, extra, width=32):
+    size = square.shape[1]
     out = jax.ShapeDtypeStruct((size, size), jnp.float32)
     return pl.pallas_call(
         functools.partial(factor_kernel, width),
         out_shape=(out, out, out),
-        in_specs=[vmem()],
+        in_specs=[vmem(), vmem()],
         out_specs=(vmem(),) * 3,
         scratch_shapes=[
             pltpu.VMEM((size // SUB, SUB, size), jnp.float32),
@@ -154,7 +154,7 @@
         ],
         cost_estimate=pl.CostEstimate(flops=4 * size**3, bytes_accessed=16 * size**2, transcendentals=0),
         name="factor",
-    )(square)
+    )(square, extra)
 
 
 def pick_kernel(slot_ref, own_ref, block_ref, out_ref):
@@ -310,7 +310,7 @@
     return x
 
 
-def on_device(n_row, n_col, matrix, pivots):
+def dense_step(n_row, n_col, matrix, pivots):
     block = matrix[0, :, 0, :]
     rows, cols = block.shape
     width = pivots.shape[0]
@@ -329,7 +329,7 @@
     square = pick(block, slot, owned * at_first_col.astype(jnp.int32), 1)
     square = sum_over_rows(square, row_bits, n_row)
     square = spread_cols(square, col_bits[::-1])
-    packed, linv, uinv = factor(square)
+    packed, linv, uinv = factor(square, jnp.zeros_like(square))
 
     top = jnp.where(at_first_row, block[:width], 0.0)
     top_panel = spread_rows(top[:, :width], row_bits, n_row)
@@ -350,6 +350,370 @@
     return result[None, :, None, :]
 
 
+def raw():
+    return pl.BlockSpec(memory_space=pl.ANY)
+
+
+def begin_kernel(
+    n_row, pivot_ref, mat_ref, panel_ref, mine_ref, lists_ref, pos_ref, wide_ref, counts_ref, *refs
+):
+    messages, sem = refs[:n_row], refs[-1]
+    width = pivot_ref.shape[0]
+    count = mine_ref.shape[0]
+    width_log, row_log = width.bit_length() - 1, n_row.bit_length() - 1
+    row = lax.axis_index("prow")
+    copy = pltpu.make_async_copy(mat_ref.at[:, 0, pl.ds(0, width)], panel_ref, sem)
+    copy.start()
+    for p in range(n_row):
+        counts_ref[p] = 0
+
+    def locate(q, c):
+        for u in range(SUB):
+            j = q * SUB + u
+            block = lax.shift_right_logical(pivot_ref[j], width_log)
+            owner = block & (n_row - 1)
+            slot = lax.shift_left(lax.shift_right_logical(block, row_log), width_log) + (pivot_ref[j] & (width - 1))
+            rank = counts_ref[owner]
+            counts_ref[owner] = rank + 1
+            held = jnp.minimum(rank, count - 1)
+            lists_ref[owner, held] = j
+            place = (owner ^ row) * count + held
+            pos_ref[j] = place
+            wide_ref[pl.ds(j, 1), :] = jnp.full((1, LANES), place, jnp.int32)
+
+            @pl.when(owner == row)
+            def _():
+                mine_ref[held] = slot
+        return c
+
+    lax.fori_loop(0, width // SUB, locate, 0)
+
+    def clear(i, c):
+        mine_ref[i] = jnp.where(i < counts_ref[row], mine_ref[i], 0)
+        for p in range(n_row):
+            lists_ref[p, i] = jnp.where(i < counts_ref[p], lists_ref[p, i], 0)
+        return c
+
+    lax.fori_loop(0, count, clear, 0)
+    copy.wait()
+
+    def gather(q, c):
+        for u in range(SUB):
+            i = q * SUB + u
+            messages[0][pl.ds(i, 1), :] = panel_ref[pl.ds(mine_ref[i], 1), :]
+        return c
+
+    lax.fori_loop(0, count // SUB, gather, 0)
+    for k in range(1, n_row):
+        messages[k][:count, :] = messages[0][:count, :]
+
+    @pl.when(row == 0)
+    def _():
+        for p in range(n_row):
+            def gather_top(q, c, p=p):
+                for u in range(SUB):
+                    i = q * SUB + u
+                    messages[p][pl.ds(count + i, 1), :] = panel_ref[pl.ds(lists_ref[p, i], 1), :]
+                return c
+
+            lax.fori_loop(0, count // SUB, gather_top, 0)
+
+
+def begin(mat, pivots, n_row, count):
+    rows, width = mat.shape[0], pivots.shape[0]
+    message = jax.ShapeDtypeStruct((2 * count, width), jnp.float32)
+    return pl.pallas_call(
+        functools.partial(begin_kernel, n_row),
+        out_shape=(
+            jax.ShapeDtypeStruct((rows, width), jnp.float32),
+            jax.ShapeDtypeStruct((count,), jnp.int32),
+            jax.ShapeDtypeStruct((n_row, count), jnp.int32),
+            jax.ShapeDtypeStruct((width,), jnp.int32),
+            jax.ShapeDtypeStruct((width, LANES), jnp.int32),
+            jax.ShapeDtypeStruct((n_row,), jnp.int32),
+        ) + (message,) * n_row,
+        in_specs=[smem(), raw()],
+        out_specs=(vmem(), smem(), smem(), smem(), vmem(), smem()) + (vmem(),) * n_row,
+        scratch_shapes=[pltpu.SemaphoreType.DMA],
+        cost_estimate=pl.CostEstimate(flops=0, bytes_accessed=8 * rows * width, transcendentals=0),
+        name="begin",
+    )(pivots, mat)
+
+
+def own_rows_kernel(slot_ref, mat_ref, out_ref, sem):
+    count = out_ref.shape[0]
+
+    def group(q, c):
+        for u in range(SUB):
+            i = q * SUB + u
+            pltpu.make_async_copy(mat_ref.at[slot_ref[i]], out_ref.at[i], sem).start()
+        return c
+
+    lax.fori_loop(0, count // SUB, group, 0)
+    pltpu.make_async_copy(mat_ref.at[pl.ds(0, count)], out_ref, sem).wait()
+
+
+def own_rows(mat, slots):
+    count, cols = slots.shape[0], mat.shape[2]
+    return pl.pallas_call(
+        own_rows_kernel,
+        out_shape=jax.ShapeDtypeStruct((count, 1, cols), jnp.float32),
+        in_specs=[smem(), raw()],
+        out_specs=vmem(),
+        scratch_shapes=[pltpu.SemaphoreType.DMA],
+        cost_estimate=pl.CostEstimate(flops=0, bytes_accessed=8 * count * cols, transcendentals=0),
+        name="own_rows",
+    )(slots, mat)
+
+
+def top_rows_kernel(list_ref, mat_ref, *refs):
+    outs, sem = refs[:-1], refs[-1]
+    count = outs[0].shape[0]
+
+    @pl.when(lax.axis_index("prow") == 0)
+    def _():
+        for p, out_ref in enumerate(outs):
+            def group(q, c, p=p, out_ref=out_ref):
+                for u in range(SUB):
+                    i = q * SUB + u
+                    pltpu.make_async_copy(mat_ref.at[list_ref[p, i]], out_ref.at[i], sem.at[p]).start()
+                return c
+
+            lax.fori_loop(0, count // SUB, group, 0)
+        for p, out_ref in enumerate(outs):
+            pltpu.make_async_copy(mat_ref.at[pl.ds(0, count)], out_ref, sem.at[p]).wait()
+
+
+def top_rows(mat, lists):
+    n_row, count = lists.shape
+    cols = mat.shape[2]
+    return pl.pallas_call(
+        top_rows_kernel,
+        out_shape=(jax.ShapeDtypeStruct((count, 1, cols), jnp.float32),) * n_row,
+        in_specs=[smem(), raw()],
+        out_specs=(vmem(),) * n_row,
+        scratch_shapes=[pltpu.SemaphoreType.DMA((n_row,))],
+        cost_estimate=pl.CostEstimate(flops=0, bytes_accessed=8 * n_row * count * cols, transcendentals=0),
+        name="top_rows",
+    )(lists, mat)
+
+
+def pack_kernel(n_row, pos_ref, *refs):
+    parts, out_ref, all_ref = refs[:n_row], refs[n_row], refs[n_row + 1]
+    width = pos_ref.shape[0]
+    count = out_ref.shape[0] - width
+    row, col = lax.axis_index("prow"), lax.axis_index("pcol")
+
+    @pl.when(col == 0)
+    def _():
+        for k in range(n_row):
+            all_ref[k * count:(k + 1) * count, :] = parts[k][:count, :]
+
+        def group(q, c):
+            for u in range(SUB):
+                j = q * SUB + u
+                out_ref[pl.ds(j, 1), :] = all_ref[pl.ds(pos_ref[j], 1), :]
+            return c
+
+        lax.fori_loop(0, width // SUB, group, 0)
+        for k in range(n_row):
+            @pl.when(row == k)
+            def _(k=k):
+                out_ref[width:, :] = parts[k][count:, :]
+
+    @pl.when(col != 0)
+    def _():
+        out_ref[...] = jnp.zeros_like(out_ref)
+
+
+def pack(pos, parts):
+    n_row, width = len(parts), pos.shape[0]
+    count = parts[0].shape[0] // 2
+    return pl.pallas_call(
+        functools.partial(pack_kernel, n_row),
+        out_shape=jax.ShapeDtypeStruct((width + count, width), jnp.float32),
+        in_specs=[smem()] + [vmem()] * n_row,
+        out_specs=vmem(),
+        scratch_shapes=[pltpu.VMEM((n_row * count, width), jnp.float32)],
+        cost_estimate=pl.CostEstimate(flops=0, bytes_accessed=24 * width * width, transcendentals=0),
+        name="pack",
+    )(pos, *parts)
+
+
+def put_rows(slot_ref, held, rows_ref, target_ref):
+    spare = target_ref.shape[0] - SUB
+
+    def group(q, c):
+        for u in range(SUB):
+            i = q * SUB + u
+            slot = jnp.where(i < held, slot_ref[i], spare)
+            target_ref[pl.ds(slot, 1), :] = rows_ref[pl.ds(i, 1), :]
+        return c
+
+    lax.fori_loop(0, rows_ref.shape[0] // SUB, group, 0)
+
+
+def finish_kernel(
+    n_row, mine_ref, counts_ref, wide_ref, mat_ref, panel_ref, panel_new_ref, square_ref, square_new_ref,
+    packed_ref, linv_ref, uinv_ref, *refs,
+):
+    parts, tops, refs = refs[:n_row], refs[n_row:2 * n_row], refs[2 * n_row:]
+    out_ref, block, pivot, panel, old, high, low, top, sem, in_sem, out_sem = refs
+    rows, _, cols = mat_ref.shape
+    width = linv_ref.shape[0]
+    count = tops[0].shape[0]
+    tiles = cols // width
+    row, col = lax.axis_index("prow"), lax.axis_index("pcol")
+
+    def tile(t):
+        return pl.ds(pl.multiple_of(t * width, width), width)
+
+    @pl.when(col % 2 == 0)
+    def _():
+        pltpu.make_async_copy(panel_ref, panel.at[pl.ds(0, rows)], sem.at[0]).start()
+
+    @pl.when(col % 2 == 1)
+    def _():
+        pltpu.make_async_copy(panel_new_ref, panel.at[pl.ds(0, rows)], sem.at[0]).start()
+
+    for p in range(n_row):
+        @pl.when(row == p)
+        def _(p=p):
+            pltpu.make_async_copy(tops[p].at[:, 0, :], old, sem.at[1]).start()
+
+    blocks = [
+        pltpu.make_async_copy(mat_ref.at[:, 0, tile(t)], block.at[pl.ds(0, rows), tile(t)], in_sem.at[t])
+        for t in range(tiles)
+    ]
+    pieces = [
+        pltpu.make_async_copy(parts[k].at[:, 0, :], pivot.at[pl.ds(k * count, count), :], sem.at[2 + k])
+        for k in range(n_row)
+    ]
+    for copy in blocks[:1] + pieces + blocks[1:]:
+        copy.start()
+
+    lanes = lax.broadcasted_iota(jnp.int32, (width, LANES), 1)
+    places = jnp.concatenate(
+        [jnp.where(lanes + t * LANES == wide_ref[...], 1.0, 0.0) for t in range(n_row * count // LANES)], axis=1
+    )
+    spread_inv = halves(jnp.dot(linv_ref[...], places, precision=HI, preferred_element_type=jnp.float32))
+    top[...] = square_ref[width:, :] + square_new_ref[width:, :]
+    pltpu.make_async_copy(panel_ref, panel.at[pl.ds(0, rows)], sem.at[0]).wait()
+    put_rows(mine_ref, counts_ref[row], top, panel)
+    lower = split_dot(halves(panel[:rows, :]), halves(uinv_ref[...]))
+    high[...], low[...] = halves(lower)
+    pltpu.make_async_copy(tops[0].at[:, 0, :], old, sem.at[1]).wait()
+    for copy in blocks:
+        copy.wait()
+    put_rows(mine_ref, counts_ref[row], old, block)
+
+    @pl.when(col == 0)
+    def _():
+        block[:rows, :width] = lower
+
+    for copy in pieces:
+        copy.wait()
+
+    def step(t, c):
+        upper = split_dot(spread_inv, halves(pivot[:, tile(t)]))
+        first_col = (col == 0) & (t == 0)
+
+        @pl.when(jnp.logical_not(first_col))
+        def _():
+            block[:rows, tile(t)] = block[:rows, tile(t)] - split_dot((high[...], low[...]), halves(upper))
+
+        @pl.when(row == 0)
+        def _():
+            block[:width, tile(t)] = jnp.where(first_col, packed_ref[...], upper)
+
+        pltpu.make_async_copy(block.at[pl.ds(0, rows), tile(t)], out_ref.at[:, 0, tile(t)], out_sem.at[t]).start()
+        return c
+
+    lax.fori_loop(0, tiles, step, 0)
+    for t in range(tiles):
+        pltpu.make_async_copy(block.at[pl.ds(0, rows), tile(t)], out_ref.at[:, 0, tile(t)], out_sem.at[t]).wait()
+
+
+def finish(mine, counts, wide, mat, panels, squares, factors, pivot_parts, tops):
+    rows, _, cols = mat.shape
+    width, n_row, count = factors[0].shape[0], len(tops), mine.shape[0]
+    return pl.pallas_call(
+        functools.partial(finish_kernel, n_row),
+        out_shape=jax.ShapeDtypeStruct(mat.shape, jnp.float32),
+        in_specs=[smem(), smem(), vmem(), raw(), raw(), raw()] + [vmem()] * 5 + [raw()] * (2 * n_row),
+        out_specs=raw(),
+        scratch_shapes=[
+            pltpu.VMEM((rows + SUB, cols), jnp.float32),
+            pltpu.VMEM((n_row * count, cols), jnp.float32),
+            pltpu.VMEM((rows + SUB, width), jnp.float32),
+            pltpu.VMEM((count, cols), jnp.float32),
+            pltpu.VMEM((rows, width), jnp.bfloat16),
+            pltpu.VMEM((rows, width), jnp.bfloat16),
+            pltpu.VMEM((count, width), jnp.float32),
+            pltpu.SemaphoreType.DMA((2 + n_row,)),
+            pltpu.SemaphoreType.DMA((cols // width,)),
+            pltpu.SemaphoreType.DMA((cols // width,)),
+        ],
+        cost_estimate=pl.CostEstimate(
+            flops=6 * rows * cols * width, bytes_accessed=8 * rows * cols, transcendentals=0
+        ),
+        name="finish",
+    )(mine, counts, wide, mat, *panels, *squares, *factors, *pivot_parts, *tops)
+
+
+def capacity(n_row, width):
+    mean = width / n_row
+    return -(-int(mean + 4 * (mean * (1 - 1 / n_row)) ** 0.5) // SUB) * SUB
+
+
+def tree(x, order, is_new):
+    have = [0]
+    for n, bit in enumerate(order):
+        moved = lax.ppermute(x, "pcol", [(i, i ^ bit) for i in have])
+        have = have + [i ^ bit for i in have]
+        if n + 1 < len(order):
+            x = jnp.where(is_new(bit), moved, x)
+    return x, moved
+
+
+def capped_step(n_row, n_col, matrix, begun):
+    _, rows, _, cols = matrix.shape
+    mat = matrix.reshape(rows, 1, cols)
+    panel, mine, lists, pos, wide, counts = begun[:6]
+    messages = begun[6:]
+    col = lax.axis_index("pcol")
+    order = bits_of(n_col)[::-1]
+
+    def is_new(bit):
+        return (col & bit) != 0
+
+    both = ("prow", "pcol")
+    moved = [
+        lax.ppermute(messages[k], both, [(i * n_col, (i ^ k) * n_col) for i in range(n_row)]) for k in range(1, n_row)
+    ]
+    rows_own = own_rows(mat, mine)
+    parts = [rows_own] + [lax.ppermute(rows_own, "prow", [(i, i ^ k) for i in range(n_row)]) for k in range(1, n_row)]
+    message, message_new = tree(pack(pos, [messages[0]] + moved), order, is_new)
+    factors = factor(message, message_new)
+    panel, panel_new = tree(panel, order, is_new)
+    tops = top_rows(mat, lists)
+    tops = tops[:1] + tuple(lax.ppermute(tops[p], "prow", [(0, p)]) for p in range(1, n_row))
+    out = finish(mine, counts, wide, mat, (panel, panel_new), (message, message_new), factors, parts, tops)
+    return out.reshape(matrix.shape)
+
+
+def on_device(n_row, n_col, matrix, pivots):
+    _, rows, _, cols = matrix.shape
+    count = capacity(n_row, pivots.shape[0])
+    begun = begin(matrix.reshape(rows, 1, cols), pivots, n_row, count)
+    return lax.cond(
+        jnp.max(begun[5]) <= count,
+        lambda m, p, b: capped_step(n_row, n_col, m, b),
+        lambda m, p, b: dense_step(n_row, n_col, m, p),
+        matrix, pivots, begun,
+    )
+
+
 def solution(mesh):
     spec = P("prow", None, "pcol", None)
     n_row, n_col = mesh.shape["prow"], mesh.shape["pcol"]

time: 139 us -> 121 us (0.87)
  local copies, waits for them, and re-layouts: 20.5 us -> 1.52 us
  other arithmetic: 20.3 us -> 3.21 us
  waiting for transfers between devices: 11 us -> 22.9 us
  Pallas kernels: 44.8 us -> 49.7 us
    add x16 -> x0, other arithmetic: 13.8 us -> none  [the longest x5 4.79 us: spread_rows(): x = x + lax.ppermute(x, 'prow', [(i, i ^ bit) for i in have])]
    ppermute x18 -> x15, waiting for transfers between devices: 11 us -> 22.9 us  [the longest x6 17.6 us: tree(): moved = lax.ppermute(x, 'pcol', [(i, i ^ bit) for i in have])]
    broadcast_in_dim x1 -> x0, local copies, waits for them, and re-layouts: 8.53 us -> none  [on_device(): return result[None, :, None, :]]
    slice x4 -> x0, local copies, waits for them, and re-layouts: 5.97 us -> none  [the longest x1 2.49 us: on_device(): top = jnp.where(at_first_row, block[:width], 0.0)]
    unnamed x9 -> x2, local copies, waits for them, and re-layouts: 5.95 us -> 0.01 us
    pallas_call x4 -> x5, Pallas kernels: 30.4 us -> 35.1 us  [the longest x1 12.3 us: finish(): pl.pallas_call(functools.partial(finish_kernel, n_row), out_shape=jax.Sha...]
    concatenate x2 -> x0, other arithmetic: 2.63 us -> none  [the longest x1 1.36 us: on_device(): jnp.concatenate([spread_rows(top[:half], row_bits, n_row), spread_rows(to...]
    cond x0 -> x26, local copies, waits for them, and re-layouts: none -> 1.51 us
  transfers between devices with their start and end apart: 18 -> 15, of which waited for: 6 -> 5; matrix products, arithmetic and copies ran while one was open for 19% -> 1% of each run, Pallas kernels for 22% -> 24%
where the time goes in v3:
time: 121 us; the launch traced here: 120 us
  Pallas kernels  49.7 us (41%)
  starting transfers between devices  41.2 us (34%)
  waiting for transfers between devices  22.9 us (19%)
  other arithmetic  3.21 us (3%)
  local copies, waits for them, and re-layouts  1.52 us (1%)
    ppermute x6, waiting for transfers between devices, tree(): moved = lax.ppermute(x, 'pcol', [(i, i ^ bit) for i in have])  17.6 us
    ppermute x6, starting transfers between devices, tree(): moved = lax.ppermute(x, 'pcol', [(i, i ^ bit) for i in have])  14.7 us
    pallas_call x1, Pallas kernels, factor(): pl.pallas_call(functools.partial(factor_kernel, width), out_shape=(out, o...  14.6 us
    ppermute x3, starting transfers between devices, capped_step(): lax.ppermute(tops[p], 'prow', [(0, p)])  13.5 us
    pallas_call x1, Pallas kernels, finish(): pl.pallas_call(functools.partial(finish_kernel, n_row), out_shape=jax.Sha...  12.3 us
    ppermute x3, starting transfers between devices, capped_step(): lax.ppermute(messages[k], both, [(i * n_col, (i ^ k) * n_col) for i in ra...  9.2 us
    pallas_call x1, Pallas kernels, begin(): pl.pallas_call(functools.partial(begin_kernel, n_row), out_shape=(jax.Sha...  8.18 us
    pallas_call x1, Pallas kernels, top_rows(): pl.pallas_call(top_rows_kernel, out_shape=(jax.ShapeDtypeStruct((count, 1...  7.85 us
  transfers between devices with their start and end apart: 15, of which 5 were waited for; matrix products, arithmetic and copies ran while one was open for 1% of the time, Pallas kernels for 24%

profile of v3, /device:TPU:0, one launch (start us, length us, event | category | flops | bytes accessed | tf_op | source)
XLA Modules:
  0.0 119.9 jit_solution(16421087213414161424)
XLA Ops:
  0.0 8.2 %begin.1 = (f32[1024,256]{1,0:T(8,128)}, s32[96]{0:T(128)S(1)}, s32[4,96]{1,0:T(4,128)S(1)}, s32[256]{0:T(256)S(1)}, s32[256,128]{1,0:T(8,128)S(1)}, /*index=5*/...) custom-call(s32[256]{0:T(256)} %pivot_ref.1, ...), custom_call_target="tpu_custom_call" | custom-call | bytes 2097152 | tf_op jit(solution)/shard_map/begin/pallas_call | solution.py:425
  9.5 110.2 %conditional.1 = (f32[1,1024,1,1536]{3,2,1,0:T(1,128)}) conditional(s32[]{:T(128)} %convert_element_type.9, (s32[256]{0:T(256)S(1)}, f32[1,1024,1,1536]{3,2,1,0:T(1,128)}) %tuple.29, (f32[1,1024,1,1536]{3,2,1,0:T(1,128)}, f32[1024,256]{1,0:T(8,128)}, f32[192,256]{1,0:T(8,128)}, f32[192,256]{1,0:T(8,128)}, f32[192,256]{1,0:T(8,128)}, ...), branch_computations={%region_1.2_spmd, %region_2.3_spmd} | conditional | flops 2488416000 | bytes 162274944 | solution.py:709
  9.5 6.2 %collective-permute-start = (f32[1024,256]{1,0:T(8,128)}, f32[1024,256]{1,0:T(8,128)S(1)}, u32[]{:S(2)}, u32[]{:S(2)}) collective-permute-start(f32[1024,256]{1,0:T(8,128)} %get-tuple-element.43), channel_id=1, source_target_pairs={{0,4},{8,12},{16,20},{24,28}} | collective-permute-start | bytes 3145736 | tf_op jit(solution)/shard_map/cond/branch_1_fun/ppermute | solution.py:672
  15.8 12.3 %collective-permute-done = f32[1024,256]{1,0:T(8,128)S(1)} collective-permute-done((f32[1024,256]{1,0:T(8,128)}, f32[1024,256]{1,0:T(8,128)S(1)}, u32[]{:S(2)}, u32[]{:S(2)}) %collective-permute-start) | collective-permute-done | bytes 1048608 | tf_op jit(solution)/shard_map/cond/branch_1_fun/ppermute | solution.py:672
  28.1 1.4 %broadcast_select_fusion.3 = f32[1024,256]{1,0:T(8,128)S(1)} fusion(f32[1024,256]{1,0:T(8,128)S(1)} %collective-permute-done, f32[1024,256]{1,0:T(8,128)} %get-tuple-element.43, pred[]{:T(512)S(6)} %ne.38), kind=kLoop, calls=%fused_computation.31 | loop fusion | flops 262144 | bytes 3145729 | tf_op jit(solution)/shard_map/cond/branch_1_fun/jit(_where)/select_n | solution.py:675
  29.5 2.3 %collective-permute-start.1 = (f32[1024,256]{1,0:T(8,128)S(1)}, f32[1024,256]{1,0:T(8,128)}, u32[]{:S(2)}, u32[]{:S(2)}) collective-permute-start(f32[1024,256]{1,0:T(8,128)S(1)} %broadcast_select_fusion.3), channel_id=1, source_target_pairs={{0,2},{4,6},{8,10},{12,14},{16,18},{20,22},{24,26},{28,30}} | collective-permute-start | bytes 3145736 | tf_op jit(solution)/shard_map/cond/branch_1_fun/ppermute | solution.py:672
  31.8 1.9 %collective-permute-start.3 = (f32[192,256]{1,0:T(8,128)S(1)}, f32[192,256]{1,0:T(8,128)S(1)}, u32[]{:S(2)}, u32[]{:S(2)}) collective-permute-start(f32[192,256]{1,0:T(8,128)S(1)} %copy-done.14), channel_id=1, source_target_pairs={{0,8},{8,0},{16,24},{24,16}} | collective-permute-start | bytes 589832 | tf_op jit(solution)/shard_map/cond/branch_1_fun/ppermute | solution.py:692
  33.7 3.0 %collective-permute-start.4 = (f32[192,256]{1,0:T(8,128)S(1)}, f32[192,256]{1,0:T(8,128)S(1)}, u32[]{:S(2)}, u32[]{:S(2)}) collective-permute-start(f32[192,256]{1,0:T(8,128)S(1)} %copy-done.15), channel_id=1, source_target_pairs={{0,16},{8,24},{16,0},{24,8}} | collective-permute-start | bytes 589832 | tf_op jit(solution)/shard_map/cond/branch_1_fun/ppermute | solution.py:692
  36.7 4.3 %collective-permute-start.5 = (f32[192,256]{1,0:T(8,128)S(1)}, f32[192,256]{1,0:T(8,128)S(1)}, u32[]{:S(2)}, u32[]{:S(2)}) collective-permute-start(f32[192,256]{1,0:T(8,128)S(1)} %copy-done.16), channel_id=1, source_target_pairs={{0,24},{8,16},{16,8},{24,0}} | collective-permute-start | bytes 589832 | tf_op jit(solution)/shard_map/cond/branch_1_fun/ppermute | solution.py:692
  41.5 1.6 %collective-permute-done.4.refs_2_ = f32[192,256]{1,0:T(8,128)S(1)} collective-permute-done((f32[192,256]{1,0:T(8,128)S(1)}, f32[192,256]{1,0:T(8,128)S(1)}, u32[]{:S(2)}, u32[]{:S(2)}) %collective-permute-start.4) | collective-permute-done | bytes 196640 | tf_op jit(solution)/shard_map/cond/branch_1_fun/ppermute | solution.py:692
  43.1 3.3 %collective-permute-done.5.refs_3_ = f32[192,256]{1,0:T(8,128)S(1)} collective-permute-done((f32[192,256]{1,0:T(8,128)S(1)}, f32[192,256]{1,0:T(8,128)S(1)}, u32[]{:S(2)}, u32[]{:S(2)}) %collective-permute-start.5) | collective-permute-done | bytes 196640 | tf_op jit(solution)/shard_map/cond/branch_1_fun/ppermute | solution.py:692
  47.0 2.8 %pack.1 = f32[352,256]{1,0:T(8,128)} custom-call(s32[256]{0:T(256)S(1)} %get-tuple-element.44.pos_ref, f32[192,256]{1,0:T(8,128)S(1)} %get-tuple-element.45.refs_0_, f32[192,256]{1,0:T(8,128)} %copy-done.8, f32[192,256]{1,0:T(8,128)} %copy-done.9, f32[192,256]{1,0:T(8,128)} %copy-done.10), custom_call_target="tpu_custom_call" | custom-call | bytes 1572864 | tf_op jit(solution)/shard_map/cond/branch_1_fun/pack/pallas_call | solution.py:532
  51.2 5.2 %collective-permute-done.6 = f32[352,256]{1,0:T(8,128)S(1)} collective-permute-done((f32[352,256]{1,0:T(8,128)}, f32[352,256]{1,0:T(8,128)S(1)}, u32[]{:S(2)}, u32[]{:S(2)}) %collective-permute-start.6) | collective-permute-done | bytes 360480 | tf_op jit(solution)/shard_map/cond/branch_1_fun/ppermute | solution.py:672
  57.4 1.3 %collective-permute-start.7 = (f32[352,256]{1,0:T(8,128)S(1)}, f32[352,256]{1,0:T(8,128)S(1)}, u32[]{:S(2)}, u32[]{:S(2)}) collective-permute-start(f32[352,256]{1,0:T(8,128)S(1)} %broadcast_select_fusion.5), channel_id=1, source_target_pairs={{0,2},{4,6},{8,10},{12,14},{16,18},{20,22},{24,26},{28,30}} | collective-permute-start | bytes 1081352 | tf_op jit(solution)/shard_map/cond/branch_1_fun/ppermute | solution.py:672
  58.8 4.0 %own_rows.1.refs_0_ = f32[96,1,1536]{2,1,0:T(1,128)} custom-call(s32[96]{0:T(128)S(1)} %get-tuple-element.39.slot_ref.mine_ref, f32[1024,1,1536]{2,1,0:T(1,128)} %bitcast.23), custom_call_target="tpu_custom_call" | custom-call | bytes 1179648 | tf_op jit(solution)/shard_map/cond/branch_1_fun/own_rows/pallas_call | solution.py:458
  62.7 2.5 %collective-permute-start.11 = (f32[96,1,1536]{2,1,0:T(1,128)}, f32[96,1,1536]{2,1,0:T(1,128)}, u32[]{:S(2)}, u32[]{:S(2)}) collective-permute-start(f32[96,1,1536]{2,1,0:T(1,128)} %own_rows.1.refs_0_), channel_id=1, source_target_pairs={{0,24},{8,16},{16,8},{24,0},{1,25},{9,17},{17,9},{25,1},{2,26},{10... | collective-permute-start | bytes 1769480 | tf_op jit(solution)/shard_map/cond/branch_1_fun/ppermute | solution.py:695
  65.4 2.3 %collective-permute-start.2 = (f32[1024,256]{1,0:T(8,128)S(1)}, f32[1024,256]{1,0:T(8,128)}, u32[]{:S(2)}, u32[]{:S(2)}) collective-permute-start(f32[1024,256]{1,0:T(8,128)S(1)} %broadcast_select_fusion.4.panel_ref), channel_id=1, source_target_pairs={{0,1},{4,5},{2,3},{6,7},{8,9},{12,13},{10,11},{14,15},{16,17},{20,... | collective-permute-start | bytes 3145736 | tf_op jit(solution)/shard_map/cond/branch_1_fun/ppermute | solution.py:672
  67.8 1.3 %collective-permute-start.8 = (f32[352,256]{1,0:T(8,128)S(1)}, f32[352,256]{1,0:T(8,128)S(1)}, u32[]{:S(2)}, u32[]{:S(2)}) collective-permute-start(f32[352,256]{1,0:T(8,128)S(1)} %broadcast_select_fusion.6.s_ref.square_ref), channel_id=1, source_target_pairs={{0,1},{4,5},{2,3},{6,7},{8,9},{12,13},{10,11},{14,15},{16,17},{20,... | collective-permute-start | bytes 1081352 | tf_op jit(solution)/shard_map/cond/branch_1_fun/ppermute | solution.py:672
  70.3 7.8 %top_rows.1 = (f32[96,1,1536]{2,1,0:T(1,128)}, f32[96,1,1536]{2,1,0:T(1,128)}, f32[96,1,1536]{2,1,0:T(1,128)}, f32[96,1,1536]{2,1,0:T(1,128)}) custom-call(s32[4,96]{1,0:T(4,128)S(1)} %get-tuple-element.52.list_ref, f32[1024,1,1536]{2,1,0:T(1,128)} %bitcast.24), custom_call_target="tpu_custom_call" | custom-call | bytes 4718592 | tf_op jit(solution)/shard_map/cond/branch_1_fun/top_rows/pallas_call | solution.py:490
  78.2 2.1 %collective-permute-start.12 = (f32[96,1,1536]{2,1,0:T(1,128)}, f32[96,1,1536]{2,1,0:T(1,128)}, u32[]{:S(2)}, u32[]{:S(2)}) collective-permute-start(f32[96,1,1536]{2,1,0:T(1,128)} %get-tuple-element.54), channel_id=1, source_target_pairs={{0,8},{1,9},{2,10},{3,11},{4,12},{5,13},{6,14},{7,15}} | collective-permute-start | bytes 1769480 | tf_op jit(solution)/shard_map/cond/branch_1_fun/ppermute | solution.py:700
  80.3 2.2 %collective-permute-start.13 = (f32[96,1,1536]{2,1,0:T(1,128)}, f32[96,1,1536]{2,1,0:T(1,128)}, u32[]{:S(2)}, u32[]{:S(2)}) collective-permute-start(f32[96,1,1536]{2,1,0:T(1,128)} %get-tuple-element.55), channel_id=1, source_target_pairs={{0,16},{1,17},{2,18},{3,19},{4,20},{5,21},{6,22},{7,23}} | collective-permute-start | bytes 1769480 | tf_op jit(solution)/shard_map/cond/branch_1_fun/ppermute | solution.py:700
  82.5 9.2 %collective-permute-start.14 = (f32[96,1,1536]{2,1,0:T(1,128)}, f32[96,1,1536]{2,1,0:T(1,128)}, u32[]{:S(2)}, u32[]{:S(2)}) collective-permute-start(f32[96,1,1536]{2,1,0:T(1,128)} %get-tuple-element.56), channel_id=1, source_target_pairs={{0,24},{1,25},{2,26},{3,27},{4,28},{5,29},{6,30},{7,31}} | collective-permute-start | bytes 1769480 | tf_op jit(solution)/shard_map/cond/branch_1_fun/ppermute | solution.py:700
  91.7 14.6 %factor.3 = (f32[256,256]{1,0:T(8,128)}, f32[256,256]{1,0:T(8,128)}, f32[256,256]{1,0:T(8,128)}) custom-call(f32[352,256]{1,0:T(8,128)} %copy-done.3, f32[352,256]{1,0:T(8,128)} %copy-done.5), custom_call_target="tpu_custom_call" | custom-call | flops 67108864 | bytes 1048576 | tf_op jit(solution)/shard_map/cond/branch_1_fun/factor/pallas_call | solution.py:145
  107.2 12.3 %finish.1 = f32[1024,1,1536]{2,1,0:T(1,128)} custom-call(s32[96]{0:T(128)S(1)} %get-tuple-element.39.slot_ref.mine_ref, s32[4]{0:T(128)S(1)} %copy-done.13, s32[256,128]{1,0:T(8,128)S(1)} %get-tuple-element.41.wide_ref, f32[1024,1,1536]{2,1,0:T(1,128)} %bitcast.25, f32[1024,256]{1,0:T(8,128)} %copy-done.2, f32[1024,256]{1,0:T(8,128)} %collective-permute-done.2.panel_new_ref, ...), custom_call_target="tpu_custom_call" | custom-call | flops 2415919104 | bytes 12582912 | tf_op jit(solution)/shard_map/cond/branch_1_fun/finish/pallas_call | solution.py:640
  (46 shorter events, 6.4 us)
Async XLA Ops:
  0.0 9.5 %copy-start.11 = (s32[256]{0:T(256)S(1)}, s32[256]{0:T(256)}, u32[]{:S(2)}) copy-start(s32[256]{0:T(256)} %pivot_ref.1) | copy-start | bytes 3076
  9.5 19.9 %copy-start.12 = (s32[4]{0:T(128)}, s32[4]{0:T(128)S(1)}, u32[]{:S(2)}) copy-start(s32[4]{0:T(128)S(1)} %get-tuple-element.40.counts_ref) | copy-start | bytes 52 | tf_op jit(solution)/shard_map/cond
  9.5 18.6 %collective-permute-start = (f32[1024,256]{1,0:T(8,128)}, f32[1024,256]{1,0:T(8,128)S(1)}, u32[]{:S(2)}, u32[]{:S(2)}) collective-permute-start(f32[1024,256]{1,0:T(8,128)} %get-tuple-element.43), channel_id=1, source_target_pairs={{0,4},{8,12},{16,20},{24,28}} | collective-permute-start | bytes 3145736 | tf_op jit(solution)/shard_map/cond/branch_1_fun/ppermute | solution.py:672
  15.7 16.0 %copy-start.14 = (f32[192,256]{1,0:T(8,128)S(1)}, f32[192,256]{1,0:T(8,128)}, u32[]{:S(2)}) copy-start(f32[192,256]{1,0:T(8,128)} %get-tuple-element.46) | copy-start | bytes 589828 | tf_op jit(solution)/shard_map/cond
  15.7 18.0 %copy-start.15 = (f32[192,256]{1,0:T(8,128)S(1)}, f32[192,256]{1,0:T(8,128)}, u32[]{:S(2)}) copy-start(f32[192,256]{1,0:T(8,128)} %get-tuple-element.47) | copy-start | bytes 589828 | tf_op jit(solution)/shard_map/cond
  15.7 21.0 %copy-start.16 = (f32[192,256]{1,0:T(8,128)S(1)}, f32[192,256]{1,0:T(8,128)}, u32[]{:S(2)}) copy-start(f32[192,256]{1,0:T(8,128)} %get-tuple-element.48) | copy-start | bytes 589828 | tf_op jit(solution)/shard_map/cond
  29.5 35.8 %collective-permute-start.1 = (f32[1024,256]{1,0:T(8,128)S(1)}, f32[1024,256]{1,0:T(8,128)}, u32[]{:S(2)}, u32[]{:S(2)}) collective-permute-start(f32[1024,256]{1,0:T(8,128)S(1)} %broadcast_select_fusion.3), channel_id=1, source_target_pairs={{0,2},{4,6},{8,10},{12,14},{16,18},{20,22},{24,26},{28,30}} | collective-permute-start | bytes 3145736 | tf_op jit(solution)/shard_map/cond/branch_1_fun/ppermute | solution.py:672
  31.8 9.7 %collective-permute-start.3 = (f32[192,256]{1,0:T(8,128)S(1)}, f32[192,256]{1,0:T(8,128)S(1)}, u32[]{:S(2)}, u32[]{:S(2)}) collective-permute-start(f32[192,256]{1,0:T(8,128)S(1)} %copy-done.14), channel_id=1, source_target_pairs={{0,8},{8,0},{16,24},{24,16}} | collective-permute-start | bytes 589832 | tf_op jit(solution)/shard_map/cond/branch_1_fun/ppermute | solution.py:692
  33.7 9.4 %collective-permute-start.4 = (f32[192,256]{1,0:T(8,128)S(1)}, f32[192,256]{1,0:T(8,128)S(1)}, u32[]{:S(2)}, u32[]{:S(2)}) collective-permute-start(f32[192,256]{1,0:T(8,128)S(1)} %copy-done.15), channel_id=1, source_target_pairs={{0,16},{8,24},{16,0},{24,8}} | collective-permute-start | bytes 589832 | tf_op jit(solution)/shard_map/cond/branch_1_fun/ppermute | solution.py:692
  36.7 9.6 %collective-permute-start.5 = (f32[192,256]{1,0:T(8,128)S(1)}, f32[192,256]{1,0:T(8,128)S(1)}, u32[]{:S(2)}, u32[]{:S(2)}) collective-permute-start(f32[192,256]{1,0:T(8,128)S(1)} %copy-done.16), channel_id=1, source_target_pairs={{0,24},{8,16},{16,8},{24,0}} | collective-permute-start | bytes 589832 | tf_op jit(solution)/shard_map/cond/branch_1_fun/ppermute | solution.py:692
  49.9 6.5 %collective-permute-start.6 = (f32[352,256]{1,0:T(8,128)}, f32[352,256]{1,0:T(8,128)S(1)}, u32[]{:S(2)}, u32[]{:S(2)}) collective-permute-start(f32[352,256]{1,0:T(8,128)} %pack.1), channel_id=1, source_target_pairs={{0,4},{8,12},{16,20},{24,28}} | collective-permute-start | bytes 1081352 | tf_op jit(solution)/shard_map/cond/branch_1_fun/ppermute | solution.py:672
  57.4 10.3 %collective-permute-start.7 = (f32[352,256]{1,0:T(8,128)S(1)}, f32[352,256]{1,0:T(8,128)S(1)}, u32[]{:S(2)}, u32[]{:S(2)}) collective-permute-start(f32[352,256]{1,0:T(8,128)S(1)} %broadcast_select_fusion.5), channel_id=1, source_target_pairs={{0,2},{4,6},{8,10},{12,14},{16,18},{20,22},{24,26},{28,30}} | collective-permute-start | bytes 1081352 | tf_op jit(solution)/shard_map/cond/branch_1_fun/ppermute | solution.py:672
  62.7 15.5 %collective-permute-start.11 = (f32[96,1,1536]{2,1,0:T(1,128)}, f32[96,1,1536]{2,1,0:T(1,128)}, u32[]{:S(2)}, u32[]{:S(2)}) collective-permute-start(f32[96,1,1536]{2,1,0:T(1,128)} %own_rows.1.refs_0_), channel_id=1, source_target_pairs={{0,24},{8,16},{16,8},{24,0},{1,25},{9,17},{17,9},{25,1},{2,26},{10... | collective-permute-start | bytes 1769480 | tf_op jit(solution)/shard_map/cond/branch_1_fun/ppermute | solution.py:695
  65.3 15.0 %collective-permute-start.10 = (f32[96,1,1536]{2,1,0:T(1,128)}, f32[96,1,1536]{2,1,0:T(1,128)}, u32[]{:S(2)}, u32[]{:S(2)}) collective-permute-start(f32[96,1,1536]{2,1,0:T(1,128)} %own_rows.1.refs_0_), channel_id=1, source_target_pairs={{0,16},{8,24},{16,0},{24,8},{1,17},{9,25},{17,1},{25,9},{2,18},{10... | collective-permute-start | bytes 1769480 | tf_op jit(solution)/shard_map/cond/branch_1_fun/ppermute | solution.py:695
  65.4 12.7 %copy-start.2 = (f32[1024,256]{1,0:T(8,128)}, f32[1024,256]{1,0:T(8,128)S(1)}, u32[]{:S(2)}) copy-start(f32[1024,256]{1,0:T(8,128)S(1)} %broadcast_select_fusion.4.panel_ref) | copy-start | bytes 3145732 | tf_op jit(solution)/shard_map/cond
  65.4 41.0 %collective-permute-start.2 = (f32[1024,256]{1,0:T(8,128)S(1)}, f32[1024,256]{1,0:T(8,128)}, u32[]{:S(2)}, u32[]{:S(2)}) collective-permute-start(f32[1024,256]{1,0:T(8,128)S(1)} %broadcast_select_fusion.4.panel_ref), channel_id=1, source_target_pairs={{0,1},{4,5},{2,3},{6,7},{8,9},{12,13},{10,11},{14,15},{16,17},{20,... | collective-permute-start | bytes 3145736 | tf_op jit(solution)/shard_map/cond/branch_1_fun/ppermute | solution.py:672
  67.8 10.4 %copy-start.3 = (f32[352,256]{1,0:T(8,128)}, f32[352,256]{1,0:T(8,128)S(1)}, u32[]{:S(2)}) copy-start(f32[352,256]{1,0:T(8,128)S(1)} %broadcast_select_fusion.6.s_ref.square_ref) | copy-start | bytes 1081348 | tf_op jit(solution)/shard_map/cond
  67.8 14.7 %collective-permute-start.8 = (f32[352,256]{1,0:T(8,128)S(1)}, f32[352,256]{1,0:T(8,128)S(1)}, u32[]{:S(2)}, u32[]{:S(2)}) collective-permute-start(f32[352,256]{1,0:T(8,128)S(1)} %broadcast_select_fusion.6.s_ref.square_ref), channel_id=1, source_target_pairs={{0,1},{4,5},{2,3},{6,7},{8,9},{12,13},{10,11},{14,15},{16,17},{20,... | collective-permute-start | bytes 1081352 | tf_op jit(solution)/shard_map/cond/branch_1_fun/ppermute | solution.py:672
  69.1 37.2 %collective-permute-start.9 = (f32[96,1,1536]{2,1,0:T(1,128)S(1)}, f32[96,1,1536]{2,1,0:T(1,128)S(1)}, u32[]{:S(2)}, u32[]{:S(2)}) collective-permute-start(f32[96,1,1536]{2,1,0:T(1,128)S(1)} %copy-done.4), channel_id=1, source_target_pairs={{0,8},{8,0},{16,24},{24,16},{1,9},{9,1},{17,25},{25,17},{2,10},{10... | collective-permute-start | bytes 1769480 | tf_op jit(solution)/shard_map/cond/branch_1_fun/ppermute | solution.py:695
  70.3 36.9 %copy-start.13 = (s32[4]{0:T(128)S(1)}, s32[4]{0:T(128)}, u32[]{:S(2)}) copy-start(s32[4]{0:T(128)} %copy-done.12) | copy-start | bytes 52 | tf_op jit(solution)/shard_map/cond
  78.2 28.2 %collective-permute-start.12 = (f32[96,1,1536]{2,1,0:T(1,128)}, f32[96,1,1536]{2,1,0:T(1,128)}, u32[]{:S(2)}, u32[]{:S(2)}) collective-permute-start(f32[96,1,1536]{2,1,0:T(1,128)} %get-tuple-element.54), channel_id=1, source_target_pairs={{0,8},{1,9},{2,10},{3,11},{4,12},{5,13},{6,14},{7,15}} | collective-permute-start | bytes 1769480 | tf_op jit(solution)/shard_map/cond/branch_1_fun/ppermute | solution.py:700
  80.3 26.1 %collective-permute-start.13 = (f32[96,1,1536]{2,1,0:T(1,128)}, f32[96,1,1536]{2,1,0:T(1,128)}, u32[]{:S(2)}, u32[]{:S(2)}) collective-permute-start(f32[96,1,1536]{2,1,0:T(1,128)} %get-tuple-element.55), channel_id=1, source_target_pairs={{0,16},{1,17},{2,18},{3,19},{4,20},{5,21},{6,22},{7,23}} | collective-permute-start | bytes 1769480 | tf_op jit(solution)/shard_map/cond/branch_1_fun/ppermute | solution.py:700
  82.5 9.2 %copy-start.5 = (f32[352,256]{1,0:T(8,128)}, f32[352,256]{1,0:T(8,128)S(1)}, u32[]{:S(2)}) copy-start(f32[352,256]{1,0:T(8,128)S(1)} %collective-permute-done.8.extra_ref.square_new_ref) | copy-start | bytes 1081348 | tf_op jit(solution)/shard_map/cond
  82.5 23.9 %collective-permute-start.14 = (f32[96,1,1536]{2,1,0:T(1,128)}, f32[96,1,1536]{2,1,0:T(1,128)}, u32[]{:S(2)}, u32[]{:S(2)}) collective-permute-start(f32[96,1,1536]{2,1,0:T(1,128)} %get-tuple-element.56), channel_id=1, source_target_pairs={{0,24},{1,25},{2,26},{3,27},{4,28},{5,29},{6,30},{7,31}} | collective-permute-start | bytes 1769480 | tf_op jit(solution)/shard_map/cond/branch_1_fun/ppermute | solution.py:700
  (5 other events, 13.5 us)

commit v4 on v3

--- a/solution.py
+++ b/solution.py
@@ -152,7 +152,7 @@
             pltpu.VMEM((size // SUB, SUB, size), jnp.float32),
             pltpu.VMEM((1 + size // LANES, SUB, LANES), jnp.float32),
         ],
-        cost_estimate=pl.CostEstimate(flops=4 * size**3, bytes_accessed=16 * size**2, transcendentals=0),
+        cost_estimate=pl.CostEstimate(flops=4 * size**3, bytes_accessed=200_000_000, transcendentals=0),
         name="factor",
     )(square, extra)
 
@@ -354,16 +354,11 @@
     return pl.BlockSpec(memory_space=pl.ANY)
 
 
-def begin_kernel(
-    n_row, pivot_ref, mat_ref, panel_ref, mine_ref, lists_ref, pos_ref, wide_ref, counts_ref, *refs
-):
-    messages, sem = refs[:n_row], refs[-1]
+def tables_kernel(n_row, pivot_ref, mine_ref, lists_ref, pos_ref, wide_ref, counts_ref):
     width = pivot_ref.shape[0]
     count = mine_ref.shape[0]
     width_log, row_log = width.bit_length() - 1, n_row.bit_length() - 1
     row = lax.axis_index("prow")
-    copy = pltpu.make_async_copy(mat_ref.at[:, 0, pl.ds(0, width)], panel_ref, sem)
-    copy.start()
     for p in range(n_row):
         counts_ref[p] = 0
 
@@ -372,7 +367,6 @@
             j = q * SUB + u
             block = lax.shift_right_logical(pivot_ref[j], width_log)
             owner = block & (n_row - 1)
-            slot = lax.shift_left(lax.shift_right_logical(block, row_log), width_log) + (pivot_ref[j] & (width - 1))
             rank = counts_ref[owner]
             counts_ref[owner] = rank + 1
             held = jnp.minimum(rank, count - 1)
@@ -380,21 +374,44 @@
             place = (owner ^ row) * count + held
             pos_ref[j] = place
             wide_ref[pl.ds(j, 1), :] = jnp.full((1, LANES), place, jnp.int32)
-
-            @pl.when(owner == row)
-            def _():
-                mine_ref[held] = slot
         return c
 
     lax.fori_loop(0, width // SUB, locate, 0)
 
     def clear(i, c):
-        mine_ref[i] = jnp.where(i < counts_ref[row], mine_ref[i], 0)
         for p in range(n_row):
             lists_ref[p, i] = jnp.where(i < counts_ref[p], lists_ref[p, i], 0)
+        pivot = pivot_ref[lists_ref[row, i]]
+        block = lax.shift_right_logical(pivot, width_log)
+        slot = lax.shift_left(lax.shift_right_logical(block, row_log), width_log) + (pivot & (width - 1))
+        mine_ref[i] = jnp.where(i < counts_ref[row], slot, 0)
         return c
 
     lax.fori_loop(0, count, clear, 0)
+
+
+def tables(pivots, n_row, count):
+    width = pivots.shape[0]
+
+    def ints(*shape):
+        return jax.ShapeDtypeStruct(shape, jnp.int32)
+
+    return pl.pallas_call(
+        functools.partial(tables_kernel, n_row),
+        out_shape=(ints(count), ints(n_row, count), ints(width), ints(width, LANES), ints(n_row)),
+        in_specs=[smem()],
+        out_specs=(smem(), smem(), smem(), vmem(), smem()),
+        cost_estimate=pl.CostEstimate(flops=0, bytes_accessed=10_000_000, transcendentals=0),
+        name="tables",
+    )(pivots)
+
+
+def begin_kernel(n_row, mine_ref, lists_ref, mat_ref, panel_ref, *refs):
+    messages, sem = refs[:n_row], refs[-1]
+    width = panel_ref.shape[1]
+    count = mine_ref.shape[0]
+    copy = pltpu.make_async_copy(mat_ref.at[:, 0, pl.ds(0, width)], panel_ref, sem)
+    copy.start()
     copy.wait()
 
     def gather(q, c):
@@ -407,7 +424,7 @@
     for k in range(1, n_row):
         messages[k][:count, :] = messages[0][:count, :]
 
-    @pl.when(row == 0)
+    @pl.when(lax.axis_index("prow") == 0)
     def _():
         for p in range(n_row):
             def gather_top(q, c, p=p):
@@ -419,83 +436,77 @@
             lax.fori_loop(0, count // SUB, gather_top, 0)
 
 
-def begin(mat, pivots, n_row, count):
-    rows, width = mat.shape[0], pivots.shape[0]
+def begin(mat, mine, lists, width):
+    rows, (n_row, count) = mat.shape[0], lists.shape
     message = jax.ShapeDtypeStruct((2 * count, width), jnp.float32)
     return pl.pallas_call(
         functools.partial(begin_kernel, n_row),
-        out_shape=(
-            jax.ShapeDtypeStruct((rows, width), jnp.float32),
-            jax.ShapeDtypeStruct((count,), jnp.int32),
-            jax.ShapeDtypeStruct((n_row, count), jnp.int32),
-            jax.ShapeDtypeStruct((width,), jnp.int32),
-            jax.ShapeDtypeStruct((width, LANES), jnp.int32),
-            jax.ShapeDtypeStruct((n_row,), jnp.int32),
-        ) + (message,) * n_row,
-        in_specs=[smem(), raw()],
-        out_specs=(vmem(), smem(), smem(), smem(), vmem(), smem()) + (vmem(),) * n_row,
+        out_shape=(jax.ShapeDtypeStruct((rows, width), jnp.float32),) + (message,) * n_row,
+        in_specs=[smem(), smem(), raw()],
+        out_specs=(vmem(),) * (n_row + 1),
         scratch_shapes=[pltpu.SemaphoreType.DMA],
-        cost_estimate=pl.CostEstimate(flops=0, bytes_accessed=8 * rows * width, transcendentals=0),
+        cost_estimate=pl.CostEstimate(flops=0, bytes_accessed=10_000_000, transcendentals=0),
         name="begin",
-    )(pivots, mat)
-
-
-def own_rows_kernel(slot_ref, mat_ref, out_ref, sem):
-    count = out_ref.shape[0]
+    )(mine, lists, mat)
+
+
+def parcel_kernel(n_row, mine_ref, lists_ref, mat_ref, own_ref, *refs):
+    outs, spare_ref, sem = refs[:n_row], refs[n_row], refs[n_row + 1]
+    count = own_ref.shape[0]
+    first = lax.axis_index("prow") == 0
 
     def group(q, c):
         for u in range(SUB):
             i = q * SUB + u
-            pltpu.make_async_copy(mat_ref.at[slot_ref[i]], out_ref.at[i], sem).start()
+            pltpu.make_async_copy(mat_ref.at[mine_ref[i]], own_ref.at[i], sem.at[0]).start()
         return c
 
     lax.fori_loop(0, count // SUB, group, 0)
-    pltpu.make_async_copy(mat_ref.at[pl.ds(0, count)], out_ref, sem).wait()
-
-
-def own_rows(mat, slots):
-    count, cols = slots.shape[0], mat.shape[2]
-    return pl.pallas_call(
-        own_rows_kernel,
-        out_shape=jax.ShapeDtypeStruct((count, 1, cols), jnp.float32),
-        in_specs=[smem(), raw()],
-        out_specs=vmem(),
-        scratch_shapes=[pltpu.SemaphoreType.DMA],
-        cost_estimate=pl.CostEstimate(flops=0, bytes_accessed=8 * count * cols, transcendentals=0),
-        name="own_rows",
-    )(slots, mat)
-
-
-def top_rows_kernel(list_ref, mat_ref, *refs):
-    outs, sem = refs[:-1], refs[-1]
-    count = outs[0].shape[0]
-
-    @pl.when(lax.axis_index("prow") == 0)
-    def _():
-        for p, out_ref in enumerate(outs):
-            def group(q, c, p=p, out_ref=out_ref):
+
+    @pl.when(first)
+    def _():
+        for p in range(n_row):
+            base = 0 if p == 0 else count
+
+            def group(q, c, p=p, base=base):
                 for u in range(SUB):
                     i = q * SUB + u
-                    pltpu.make_async_copy(mat_ref.at[list_ref[p, i]], out_ref.at[i], sem.at[p]).start()
+                    pltpu.make_async_copy(mat_ref.at[lists_ref[p, i]], outs[p].at[base + i], sem.at[1]).start()
                 return c
 
             lax.fori_loop(0, count // SUB, group, 0)
-        for p, out_ref in enumerate(outs):
-            pltpu.make_async_copy(mat_ref.at[pl.ds(0, count)], out_ref, sem.at[p]).wait()
-
-
-def top_rows(mat, lists):
+
+    pltpu.make_async_copy(mat_ref.at[pl.ds(0, count)], own_ref, sem.at[0]).wait()
+    copies = [pltpu.make_async_copy(own_ref, outs[p].at[pl.ds(0, count)], sem.at[1 + p]) for p in range(1, n_row)]
+    for copy in copies[1:]:
+        copy.start()
+    for copy in copies[1:]:
+        copy.wait()
+
+    @pl.when(first)
+    def _():
+        pltpu.make_async_copy(mat_ref.at[pl.ds(0, n_row * count)], spare_ref, sem.at[1]).wait()
+
+    copies[0].start()
+    copies[0].wait()
+
+
+def parcel(mat, mine, lists):
     n_row, count = lists.shape
     cols = mat.shape[2]
-    return pl.pallas_call(
-        top_rows_kernel,
-        out_shape=(jax.ShapeDtypeStruct((count, 1, cols), jnp.float32),) * n_row,
-        in_specs=[smem(), raw()],
-        out_specs=(vmem(),) * n_row,
-        scratch_shapes=[pltpu.SemaphoreType.DMA((n_row,))],
-        cost_estimate=pl.CostEstimate(flops=0, bytes_accessed=8 * n_row * count * cols, transcendentals=0),
-        name="top_rows",
-    )(lists, mat)
+
+    def shape(rows):
+        return jax.ShapeDtypeStruct((rows, 1, cols), jnp.float32)
+
+    return pl.pallas_call(
+        functools.partial(parcel_kernel, n_row),
+        out_shape=(shape(count), shape(count)) + (shape(2 * count),) * (n_row - 1),
+        in_specs=[smem(), smem(), raw()],
+        out_specs=(vmem(),) * (n_row + 1),
+        scratch_shapes=[pltpu.VMEM((n_row * count, 1, cols), jnp.float32), pltpu.SemaphoreType.DMA((n_row + 1,))],
+        cost_estimate=pl.CostEstimate(flops=0, bytes_accessed=20_000_000, transcendentals=0),
+        name="parcel",
+    )(mine, lists, mat)
 
 
 def pack_kernel(n_row, pos_ref, *refs):
@@ -557,11 +568,13 @@
     n_row, mine_ref, counts_ref, wide_ref, mat_ref, panel_ref, panel_new_ref, square_ref, square_new_ref,
     packed_ref, linv_ref, uinv_ref, *refs,
 ):
-    parts, tops, refs = refs[:n_row], refs[n_row:2 * n_row], refs[2 * n_row:]
+    own_ref, top_ref, parcels, refs = refs[0], refs[1], refs[2:n_row + 1], refs[n_row + 1:]
     out_ref, block, pivot, panel, old, high, low, top, sem, in_sem, out_sem = refs
     rows, _, cols = mat_ref.shape
     width = linv_ref.shape[0]
-    count = tops[0].shape[0]
+    count = own_ref.shape[0]
+    parts = [own_ref] + [x.at[pl.ds(0, count)] for x in parcels]
+    tops = [top_ref] + [x.at[pl.ds(count, count)] for x in parcels]
     tiles = cols // width
     row, col = lax.axis_index("prow"), lax.axis_index("pcol")
 
@@ -589,12 +602,14 @@
         pltpu.make_async_copy(parts[k].at[:, 0, :], pivot.at[pl.ds(k * count, count), :], sem.at[2 + k])
         for k in range(n_row)
     ]
+    if pivot.shape[0] > n_row * count:
+        pivot[n_row * count:, :] = jnp.zeros((pivot.shape[0] - n_row * count, cols), jnp.float32)
     for copy in blocks[:1] + pieces + blocks[1:]:
         copy.start()
 
     lanes = lax.broadcasted_iota(jnp.int32, (width, LANES), 1)
     places = jnp.concatenate(
-        [jnp.where(lanes + t * LANES == wide_ref[...], 1.0, 0.0) for t in range(n_row * count // LANES)], axis=1
+        [jnp.where(lanes + t * LANES == wide_ref[...], 1.0, 0.0) for t in range(pivot.shape[0] // LANES)], axis=1
     )
     spread_inv = halves(jnp.dot(linv_ref[...], places, precision=HI, preferred_element_type=jnp.float32))
     top[...] = square_ref[width:, :] + square_new_ref[width:, :]
@@ -634,17 +649,17 @@
         pltpu.make_async_copy(block.at[pl.ds(0, rows), tile(t)], out_ref.at[:, 0, tile(t)], out_sem.at[t]).wait()
 
 
-def finish(mine, counts, wide, mat, panels, squares, factors, pivot_parts, tops):
+def finish(mine, counts, wide, mat, panels, squares, factors, parcels):
     rows, _, cols = mat.shape
-    width, n_row, count = factors[0].shape[0], len(tops), mine.shape[0]
+    width, n_row, count = factors[0].shape[0], len(parcels) - 1, mine.shape[0]
     return pl.pallas_call(
         functools.partial(finish_kernel, n_row),
         out_shape=jax.ShapeDtypeStruct(mat.shape, jnp.float32),
-        in_specs=[smem(), smem(), vmem(), raw(), raw(), raw()] + [vmem()] * 5 + [raw()] * (2 * n_row),
+        in_specs=[smem(), smem(), vmem(), raw(), raw(), raw()] + [vmem()] * 5 + [raw()] * (n_row + 1),
         out_specs=raw(),
         scratch_shapes=[
             pltpu.VMEM((rows + SUB, cols), jnp.float32),
-            pltpu.VMEM((n_row * count, cols), jnp.float32),
+            pltpu.VMEM((-(-n_row * count // LANES) * LANES, cols), jnp.float32),
             pltpu.VMEM((rows + SUB, width), jnp.float32),
             pltpu.VMEM((count, cols), jnp.float32),
             pltpu.VMEM((rows, width), jnp.bfloat16),
@@ -658,59 +673,59 @@
             flops=6 * rows * cols * width, bytes_accessed=8 * rows * cols, transcendentals=0
         ),
         name="finish",
-    )(mine, counts, wide, mat, *panels, *squares, *factors, *pivot_parts, *tops)
+    )(mine, counts, wide, mat, *panels, *squares, *factors, *parcels)
 
 
 def capacity(n_row, width):
     mean = width / n_row
-    return -(-int(mean + 4 * (mean * (1 - 1 / n_row)) ** 0.5) // SUB) * SUB
-
-
-def tree(x, order, is_new):
-    have = [0]
-    for n, bit in enumerate(order):
-        moved = lax.ppermute(x, "pcol", [(i, i ^ bit) for i in have])
-        have = have + [i ^ bit for i in have]
-        if n + 1 < len(order):
-            x = jnp.where(is_new(bit), moved, x)
-    return x, moved
-
-
-def capped_step(n_row, n_col, matrix, begun):
+    return -(-int(mean + 3.4 * (mean * (1 - 1 / n_row)) ** 0.5) // SUB) * SUB
+
+
+def capped_step(n_row, n_col, matrix, found):
     _, rows, _, cols = matrix.shape
     mat = matrix.reshape(rows, 1, cols)
-    panel, mine, lists, pos, wide, counts = begun[:6]
-    messages = begun[6:]
+    mine, lists, pos, wide, counts = found
+    width = pos.shape[0]
     col = lax.axis_index("pcol")
-    order = bits_of(n_col)[::-1]
-
-    def is_new(bit):
-        return (col & bit) != 0
-
     both = ("prow", "pcol")
-    moved = [
-        lax.ppermute(messages[k], both, [(i * n_col, (i ^ k) * n_col) for i in range(n_row)]) for k in range(1, n_row)
-    ]
-    rows_own = own_rows(mat, mine)
-    parts = [rows_own] + [lax.ppermute(rows_own, "prow", [(i, i ^ k) for i in range(n_row)]) for k in range(1, n_row)]
-    message, message_new = tree(pack(pos, [messages[0]] + moved), order, is_new)
+
+    def exchange(x, k):
+        return lax.ppermute(x, both, [(i * n_col, (i ^ k) * n_col) for i in range(n_row)])
+
+    parcels = parcel(mat, mine, lists)
+    sent = [lax.ppermute(parcels[1 + k], "prow", [(i, i ^ k) for i in range(n_row)]) for k in range(1, n_row)]
+    mine, own = lax.optimization_barrier((mine, parcels[0]))
+    panel, *messages = begin(mat, mine, lists, width)
+    moved = [exchange(messages[k], k) for k in range(1, n_row)]
+    message = pack(pos, [messages[0]] + moved)
+    panel, message, sent[0], sent[1] = lax.optimization_barrier((panel, message, sent[0], sent[1]))
+    have = [0]
+    for bit in bits_of(n_col)[:0:-1]:
+        pairs = [(i, i + bit) for i in have]
+        have = have + [i + bit for i in have]
+        message_moved = lax.ppermute(message, "pcol", pairs)
+        panel_moved = lax.ppermute(panel, "pcol", pairs)
+        message = jnp.where((col & bit) != 0, message_moved, message)
+        message, panel_moved = lax.optimization_barrier((message, panel_moved))
+        panel = jnp.where((col & bit) != 0, panel_moved, panel)
+    pairs = [(i, i + 1) for i in have]
+    message_new = lax.ppermute(message, "pcol", pairs)
     factors = factor(message, message_new)
-    panel, panel_new = tree(panel, order, is_new)
-    tops = top_rows(mat, lists)
-    tops = tops[:1] + tuple(lax.ppermute(tops[p], "prow", [(0, p)]) for p in range(1, n_row))
-    out = finish(mine, counts, wide, mat, (panel, panel_new), (message, message_new), factors, parts, tops)
+    panel_new = lax.ppermute(panel, "pcol", pairs)
+    out = finish(
+        mine, counts, wide, mat, (panel, panel_new), (message, message_new), factors, [own, parcels[1]] + sent
+    )
     return out.reshape(matrix.shape)
 
 
 def on_device(n_row, n_col, matrix, pivots):
-    _, rows, _, cols = matrix.shape
     count = capacity(n_row, pivots.shape[0])
-    begun = begin(matrix.reshape(rows, 1, cols), pivots, n_row, count)
+    found = tables(pivots, n_row, count)
     return lax.cond(
-        jnp.max(begun[5]) <= count,
-        lambda m, p, b: capped_step(n_row, n_col, m, b),
-        lambda m, p, b: dense_step(n_row, n_col, m, p),
-        matrix, pivots, begun,
+        jnp.max(found[-1]) <= count,
+        lambda m, p, f: capped_step(n_row, n_col, m, f),
+        lambda m, p, f: dense_step(n_row, n_col, m, p),
+        matrix, pivots, found,
     )
 
 

time: 121 us -> 124 us (1.025)
  the two profiles are of different devices: /device:TPU:0 before, /device:TPU:27 now
where the time goes in v4:
time: 124 us; the launch traced here: 123 us
  waiting for transfers between devices  57.2 us (46%)
  Pallas kernels  42.5 us (34%)
  starting transfers between devices  14.5 us (12%)
  local copies, waits for them, and re-layouts  3.67 us (3%)
  other arithmetic  3.58 us (3%)
    ppermute x1, waiting for transfers between devices, capped_step(): message_new = lax.ppermute(message, 'pcol', pairs)  41 us
    ppermute x3, waiting for transfers between devices, capped_step(): lax.ppermute(parcels[1 + k], 'prow', [(i, i ^ k) for i in range(n_row)])  16.2 us
    pallas_call x1, Pallas kernels, factor(): pl.pallas_call(functools.partial(factor_kernel, width), out_shape=(out, o...  14.6 us
    pallas_call x1, Pallas kernels, finish(): pl.pallas_call(functools.partial(finish_kernel, n_row), out_shape=jax.Sha...  12.5 us
    pallas_call x1, Pallas kernels, tables(): pl.pallas_call(functools.partial(tables_kernel, n_row), out_shape=(ints(c...  5.38 us
    ppermute x3, starting transfers between devices, capped_step(): lax.ppermute(parcels[1 + k], 'prow', [(i, i ^ k) for i in range(n_row)])  5.22 us
    pallas_call x1, Pallas kernels, parcel(): pl.pallas_call(functools.partial(parcel_kernel, n_row), out_shape=(shape(...  4.41 us
    cond x20, local copies, waits for them, and re-layouts  3.67 us
  transfers between devices with their start and end apart: 12, of which 3 were waited for; matrix products, arithmetic and copies ran while one was open for 1% of the time, Pallas kernels for 16%

profile of v4, /device:TPU:27, one launch (start us, length us, event | category | flops | bytes accessed | tf_op | source)
XLA Modules:
  0.0 122.8 jit_solution(12836292562916569794)
XLA Ops:
  0.0 5.4 %tables.1 = (s32[88]{0:T(128)S(1)}, s32[4,88]{1,0:T(4,128)S(1)}, s32[256]{0:T(256)S(1)}, s32[256,128]{1,0:T(8,128)S(1)}, s32[4]{0:T(128)S(1)}) custom-call(s32[256]{0:T(256)} %pivot_ref.1), custom_call_target="tpu_custom_call" | custom-call | bytes 10000000 | tf_op jit(solution)/shard_map/tables/pallas_call | solution.py:399
  6.7 115.9 %conditional.1 = (f32[1,1024,1,1536]{3,2,1,0:T(1,128)}) conditional(s32[]{:T(128)} %convert_element_type.9, (s32[256]{0:T(256)}, f32[1,1024,1,1536]{3,2,1,0:T(1,128)}) %tuple.15, (f32[1,1024,1,1536]{3,2,1,0:T(1,128)}, s32[88]{0:T(128)S(1)}, s32[4,88]{1,0:T(4,128)S(1)}, s32[256]{0:T(256)S(1)}, s32[4]{0:T(128)S(1)}, ...), branch_computations={%region_1.2_spmd, %region_2.3_spmd} | conditional | flops 2488416000 | bytes 361230496 | solution.py:724
  6.7 4.4 %parcel.1 = (f32[88,1,1536]{2,1,0:T(1,128)}, f32[88,1,1536]{2,1,0:T(1,128)}, f32[176,1,1536]{2,1,0:T(1,128)}, f32[176,1,1536]{2,1,0:T(1,128)}, f32[176,1,1536]{2,1,0:T(1,128)}) custom-call(s32[88]{0:T(128)S(1)} %get-tuple-element.33.mine_ref, s32[4,88]{1,0:T(4,128)S(1)} %get-tuple-element.30.lists_ref, f32[1024,1,1536]{2,1,0:T(1,128)} %bitcast.21), custom_call_target="tpu_custom_call" | custom-call | bytes 20000000 | tf_op jit(solution)/shard_map/cond/branch_1_fun/parcel/pallas_call | solution.py:501
  11.1 4.7 %collective-permute-start.3 = (f32[176,1,1536]{2,1,0:T(1,128)}, f32[176,1,1536]{2,1,0:T(1,128)S(1)}, u32[]{:S(2)}, u32[]{:S(2)}) collective-permute-start(f32[176,1,1536]{2,1,0:T(1,128)} %get-tuple-element.42), channel_id=1, source_target_pairs={{0,8},{8,0},{16,24},{24,16},{1,9},{9,1},{17,25},{25,17},{2,10},{10... | collective-permute-start | bytes 3244040 | tf_op jit(solution)/shard_map/cond/branch_1_fun/ppermute | solution.py:696
  15.8 3.6 %begin.1 = (f32[1024,256]{1,0:T(8,128)}, f32[176,256]{1,0:T(8,128)}, f32[176,256]{1,0:T(8,128)}, f32[176,256]{1,0:T(8,128)}, f32[176,256]{1,0:T(8,128)}) custom-call(s32[88]{0:T(128)S(1)} %get-tuple-element.33.mine_ref, s32[4,88]{1,0:T(4,128)S(1)} %get-tuple-element.30.lists_ref, f32[1024,1,1536]{2,1,0:T(1,128)} %bitcast.22), custom_call_target="tpu_custom_call" | custom-call | bytes 10000000 | tf_op jit(solution)/shard_map/cond/branch_1_fun/begin/pallas_call | solution.py:442
  19.4 0.7 collective-permute-start
  20.1 0.7 collective-permute-start.1
  20.8 0.7 collective-permute-start.2
  22.3 2.0 %pack.1 = f32[344,256]{1,0:T(8,128)} custom-call(s32[256]{0:T(256)S(1)} %get-tuple-element.37.pos_ref, f32[176,256]{1,0:T(8,128)} %get-tuple-element.38.refs_0_, f32[176,256]{1,0:T(8,128)} %copy-done.10, f32[176,256]{1,0:T(8,128)} %copy-done.11, f32[176,256]{1,0:T(8,128)} %copy-done.12), custom_call_target="tpu_custom_call" | custom-call | bytes 1572864 | tf_op jit(solution)/shard_map/cond/branch_1_fun/pack/pallas_call | solution.py:543
  24.2 15.4 %collective-permute-done.3.refs_2_ = f32[176,1,1536]{2,1,0:T(1,128)S(1)} collective-permute-done((f32[176,1,1536]{2,1,0:T(1,128)}, f32[176,1,1536]{2,1,0:T(1,128)S(1)}, u32[]{:S(2)}, u32[]{:S(2)}) %collective-permute-start.3) | collective-permute-done | bytes 1081376 | tf_op jit(solution)/shard_map/cond/branch_1_fun/ppermute | solution.py:696
  39.6 0.8 collective-permute-done.4.refs_3_
  40.5 1.7 %collective-permute-start.6 = (f32[1024,256]{1,0:T(8,128)}, f32[1024,256]{1,0:T(8,128)}, u32[]{:S(2)}, u32[]{:S(2)}) collective-permute-start(f32[1024,256]{1,0:T(8,128)} %get-tuple-element.45), channel_id=1, source_target_pairs={{0,4},{8,12},{16,20},{24,28}} | collective-permute-start | bytes 3145736 | tf_op jit(solution)/shard_map/cond/branch_1_fun/ppermute | solution.py:707
  42.1 0.7 collective-permute-start.5
  42.9 1.1 copy-done.9
  44.0 1.4 %broadcast_select_fusion.3 = f32[1024,256]{1,0:T(8,128)S(1)} fusion(f32[1024,256]{1,0:T(8,128)} %collective-permute-done.6, f32[1024,256]{1,0:T(8,128)S(1)} %copy-done.9, pred[]{:T(512)S(6)} %ne.38), kind=kLoop, calls=%fused_computation.31 | loop fusion | flops 262144 | bytes 3145729 | tf_op jit(solution)/shard_map/cond/branch_1_fun/jit(_where)/select_n | solution.py:710
  45.4 1.6 %collective-permute-start.8 = (f32[1024,256]{1,0:T(8,128)S(1)}, f32[1024,256]{1,0:T(8,128)}, u32[]{:S(2)}, u32[]{:S(2)}) collective-permute-start(f32[1024,256]{1,0:T(8,128)S(1)} %broadcast_select_fusion.3), channel_id=1, source_target_pairs={{0,2},{4,6},{8,10},{12,14},{16,18},{20,22},{24,26},{28,30}} | collective-permute-start | bytes 3145736 | tf_op jit(solution)/shard_map/cond/branch_1_fun/ppermute | solution.py:707
  48.3 1.5 %broadcast_select_fusion.4.panel_ref = f32[1024,256]{1,0:T(8,128)S(1)} fusion(f32[1024,256]{1,0:T(8,128)} %collective-permute-done.8, f32[1024,256]{1,0:T(8,128)S(1)} %broadcast_select_fusion.3, pred[]{:T(512)S(6)} %ne.37), kind=kLoop, calls=%fused_computation.32 | loop fusion | flops 262144 | bytes 3145729 | tf_op jit(solution)/shard_map/cond/branch_1_fun/jit(_where)/select_n | solution.py:710
  49.8 1.3 %collective-permute-start.9 = (f32[1024,256]{1,0:T(8,128)S(1)}, f32[1024,256]{1,0:T(8,128)}, u32[]{:S(2)}, u32[]{:S(2)}) collective-permute-start(f32[1024,256]{1,0:T(8,128)S(1)} %broadcast_select_fusion.4.panel_ref), channel_id=1, source_target_pairs={{0,1},{4,5},{2,3},{6,7},{8,9},{12,13},{10,11},{14,15},{16,17},{20,... | collective-permute-start | bytes 3145736 | tf_op jit(solution)/shard_map/cond/branch_1_fun/ppermute | solution.py:714
  51.1 1.3 %collective-permute-start.10 = (f32[344,256]{1,0:T(8,128)S(1)}, f32[344,256]{1,0:T(8,128)S(1)}, u32[]{:S(2)}, u32[]{:S(2)}) collective-permute-start(f32[344,256]{1,0:T(8,128)S(1)} %broadcast_select_fusion.6.s_ref.square_ref), channel_id=1, source_target_pairs={{0,1},{4,5},{2,3},{6,7},{8,9},{12,13},{10,11},{14,15},{16,17},{20,... | collective-permute-start | bytes 1056776 | tf_op jit(solution)/shard_map/cond/branch_1_fun/ppermute | solution.py:712
  52.4 41.0 %collective-permute-done.10.extra_ref.square_new_ref = f32[344,256]{1,0:T(8,128)S(1)} collective-permute-done((f32[344,256]{1,0:T(8,128)S(1)}, f32[344,256]{1,0:T(8,128)S(1)}, u32[]{:S(2)}, u32[]{:S(2)}) %collective-permute-start.10) | collective-permute-done | bytes 352288 | tf_op jit(solution)/shard_map/cond/branch_1_fun/ppermute | solution.py:712
  93.4 0.7 copy-done.4
  94.2 14.6 %factor.3 = (f32[256,256]{1,0:T(8,128)}, f32[256,256]{1,0:T(8,128)}, f32[256,256]{1,0:T(8,128)}) custom-call(f32[344,256]{1,0:T(8,128)} %copy-done.3, f32[344,256]{1,0:T(8,128)} %copy-done.4), custom_call_target="tpu_custom_call" | custom-call | flops 67108864 | bytes 200000000 | tf_op jit(solution)/shard_map/cond/branch_1_fun/factor/pallas_call | solution.py:145
  108.8 1.0 copy-done.7
  109.8 12.5 %finish.1 = f32[1024,1,1536]{2,1,0:T(1,128)} custom-call(s32[88]{0:T(128)S(1)} %get-tuple-element.33.mine_ref, s32[4]{0:T(128)S(1)} %get-tuple-element.34.counts_ref, s32[256,128]{1,0:T(8,128)S(1)} %get-tuple-element.35.wide_ref, f32[1024,1,1536]{2,1,0:T(1,128)} %bitcast.23, f32[1024,256]{1,0:T(8,128)} %copy-done.2, ...), custom_call_target="tpu_custom_call" | custom-call | flops 2415919104 | bytes 12582912 | tf_op jit(solution)/shard_map/cond/branch_1_fun/finish/pallas_call | solution.py:655
  (32 shorter events, 2.7 us)
Async XLA Ops:
  11.1 28.5 %collective-permute-start.3 = (f32[176,1,1536]{2,1,0:T(1,128)}, f32[176,1,1536]{2,1,0:T(1,128)S(1)}, u32[]{:S(2)}, u32[]{:S(2)}) collective-permute-start(f32[176,1,1536]{2,1,0:T(1,128)} %get-tuple-element.42), channel_id=1, source_target_pairs={{0,8},{8,0},{16,24},{24,16},{1,9},{9,1},{17,25},{25,17},{2,10},{10... | collective-permute-start | bytes 3244040 | tf_op jit(solution)/shard_map/cond/branch_1_fun/ppermute | solution.py:696
  15.8 24.6 %collective-permute-start.4 = (f32[176,1,1536]{2,1,0:T(1,128)}, f32[176,1,1536]{2,1,0:T(1,128)S(1)}, u32[]{:S(2)}, u32[]{:S(2)}) collective-permute-start(f32[176,1,1536]{2,1,0:T(1,128)} %get-tuple-element.43), channel_id=1, source_target_pairs={{0,16},{8,24},{16,0},{24,8},{1,17},{9,25},{17,1},{25,9},{2,18},{10... | collective-permute-start | bytes 3244040 | tf_op jit(solution)/shard_map/cond/branch_1_fun/ppermute | solution.py:696
  19.4 2.0 %collective-permute-start = (f32[176,256]{1,0:T(8,128)}, f32[176,256]{1,0:T(8,128)S(1)}, u32[]{:S(2)}, u32[]{:S(2)}) collective-permute-start(f32[176,256]{1,0:T(8,128)} %get-tuple-element.39), channel_id=1, source_target_pairs={{0,8},{8,0},{16,24},{24,16}} | collective-permute-start | bytes 540680 | tf_op jit(solution)/shard_map/cond/branch_1_fun/ppermute | solution.py:693
  20.1 1.4 %collective-permute-start.1 = (f32[176,256]{1,0:T(8,128)}, f32[176,256]{1,0:T(8,128)S(1)}, u32[]{:S(2)}, u32[]{:S(2)}) collective-permute-start(f32[176,256]{1,0:T(8,128)} %get-tuple-element.40), channel_id=1, source_target_pairs={{0,16},{8,24},{16,0},{24,8}} | collective-permute-start | bytes 540680 | tf_op jit(solution)/shard_map/cond/branch_1_fun/ppermute | solution.py:693
  20.8 0.7 collective-permute-start.2
  21.5 0.7 copy-start.10
  21.5 0.7 copy-start.11
  21.5 0.8 copy-start.12
  39.6 5.8 %copy-start.5 = (f32[176,1,1536]{2,1,0:T(1,128)}, f32[176,1,1536]{2,1,0:T(1,128)S(1)}, u32[]{:S(2)}) copy-start(f32[176,1,1536]{2,1,0:T(1,128)S(1)} %collective-permute-done.3.refs_2_) | copy-start | bytes 3244036 | tf_op jit(solution)/shard_map/cond
  40.5 2.4 %copy-start.6 = (f32[176,1,1536]{2,1,0:T(1,128)}, f32[176,1,1536]{2,1,0:T(1,128)S(1)}, u32[]{:S(2)}) copy-start(f32[176,1,1536]{2,1,0:T(1,128)S(1)} %collective-permute-done.4.refs_3_) | copy-start | bytes 3244036 | tf_op jit(solution)/shard_map/cond
  40.5 2.4 %collective-permute-start.6 = (f32[1024,256]{1,0:T(8,128)}, f32[1024,256]{1,0:T(8,128)}, u32[]{:S(2)}, u32[]{:S(2)}) collective-permute-start(f32[1024,256]{1,0:T(8,128)} %get-tuple-element.45), channel_id=1, source_target_pairs={{0,4},{8,12},{16,20},{24,28}} | collective-permute-start | bytes 3145736 | tf_op jit(solution)/shard_map/cond/branch_1_fun/ppermute | solution.py:707
  42.1 0.7 collective-permute-start.5
  42.8 1.2 copy-start.9
  45.4 2.9 %collective-permute-start.8 = (f32[1024,256]{1,0:T(8,128)S(1)}, f32[1024,256]{1,0:T(8,128)}, u32[]{:S(2)}, u32[]{:S(2)}) collective-permute-start(f32[1024,256]{1,0:T(8,128)S(1)} %broadcast_select_fusion.3), channel_id=1, source_target_pairs={{0,2},{4,6},{8,10},{12,14},{16,18},{20,22},{24,26},{28,30}} | collective-permute-start | bytes 3145736 | tf_op jit(solution)/shard_map/cond/branch_1_fun/ppermute | solution.py:707
  47.1 1.2 collective-permute-start.7
  47.7 61.1 %collective-permute-start.11 = (f32[176,1,1536]{2,1,0:T(1,128)}, f32[176,1,1536]{2,1,0:T(1,128)S(1)}, u32[]{:S(2)}, u32[]{:S(2)}) collective-permute-start(f32[176,1,1536]{2,1,0:T(1,128)} %get-tuple-element.57), channel_id=1, source_target_pairs={{0,24},{8,16},{16,8},{24,0},{1,25},{9,17},{17,9},{25,1},{2,26},{10... | collective-permute-start | bytes 3244040 | tf_op jit(solution)/shard_map/cond/branch_1_fun/ppermute | solution.py:696
  48.3 2.8 %copy-start.3 = (f32[344,256]{1,0:T(8,128)}, f32[344,256]{1,0:T(8,128)S(1)}, u32[]{:S(2)}) copy-start(f32[344,256]{1,0:T(8,128)S(1)} %broadcast_select_fusion.6.s_ref.square_ref) | copy-start | bytes 1056772 | tf_op jit(solution)/shard_map/cond
  49.8 59.0 %copy-start.2 = (f32[1024,256]{1,0:T(8,128)}, f32[1024,256]{1,0:T(8,128)S(1)}, u32[]{:S(2)}) copy-start(f32[1024,256]{1,0:T(8,128)S(1)} %broadcast_select_fusion.4.panel_ref) | copy-start | bytes 3145732 | tf_op jit(solution)/shard_map/cond
  49.8 59.0 %collective-permute-start.9 = (f32[1024,256]{1,0:T(8,128)S(1)}, f32[1024,256]{1,0:T(8,128)}, u32[]{:S(2)}, u32[]{:S(2)}) collective-permute-start(f32[1024,256]{1,0:T(8,128)S(1)} %broadcast_select_fusion.4.panel_ref), channel_id=1, source_target_pairs={{0,1},{4,5},{2,3},{6,7},{8,9},{12,13},{10,11},{14,15},{16,17},{20,... | collective-permute-start | bytes 3145736 | tf_op jit(solution)/shard_map/cond/branch_1_fun/ppermute | solution.py:714
  51.1 42.3 %collective-permute-start.10 = (f32[344,256]{1,0:T(8,128)S(1)}, f32[344,256]{1,0:T(8,128)S(1)}, u32[]{:S(2)}, u32[]{:S(2)}) collective-permute-start(f32[344,256]{1,0:T(8,128)S(1)} %broadcast_select_fusion.6.s_ref.square_ref), channel_id=1, source_target_pairs={{0,1},{4,5},{2,3},{6,7},{8,9},{12,13},{10,11},{14,15},{16,17},{20,... | collective-permute-start | bytes 1056776 | tf_op jit(solution)/shard_map/cond/branch_1_fun/ppermute | solution.py:712
  93.4 0.7 copy-start.4
  108.8 1.0 copy-start.7

commit v5 on v4

--- a/solution.py
+++ b/solution.py
@@ -152,7 +152,7 @@
             pltpu.VMEM((size // SUB, SUB, size), jnp.float32),
             pltpu.VMEM((1 + size // LANES, SUB, LANES), jnp.float32),
         ],
-        cost_estimate=pl.CostEstimate(flops=4 * size**3, bytes_accessed=200_000_000, transcendentals=0),
+        cost_estimate=pl.CostEstimate(flops=4 * size**3, bytes_accessed=50_000_000, transcendentals=0),
         name="factor",
     )(square, extra)
 
@@ -354,100 +354,77 @@
     return pl.BlockSpec(memory_space=pl.ANY)
 
 
-def tables_kernel(n_row, pivot_ref, mine_ref, lists_ref, pos_ref, wide_ref, counts_ref):
-    width = pivot_ref.shape[0]
-    count = mine_ref.shape[0]
+def thirds(x):
+    high = x.astype(jnp.bfloat16)
+    rest = x - high.astype(jnp.float32)
+    middle = rest.astype(jnp.bfloat16)
+    return high, middle, (rest - middle.astype(jnp.float32)).astype(jnp.bfloat16)
+
+
+def select_dot(choice, parts):
+    choice = choice.astype(jnp.bfloat16)
+    high, middle, low = [jnp.dot(choice, x, preferred_element_type=jnp.float32) for x in parts]
+    return high + (middle + low)
+
+
+def begin_kernel(n_row, pivot_ref, mat_ref, panel_ref, wide_ref, fits_ref, *refs):
+    messages, sem = refs[:n_row], refs[-1]
+    rows, width = panel_ref.shape
+    count = messages[0].shape[0] // 2
     width_log, row_log = width.bit_length() - 1, n_row.bit_length() - 1
     row = lax.axis_index("prow")
-    for p in range(n_row):
-        counts_ref[p] = 0
-
-    def locate(q, c):
-        for u in range(SUB):
-            j = q * SUB + u
-            block = lax.shift_right_logical(pivot_ref[j], width_log)
-            owner = block & (n_row - 1)
-            rank = counts_ref[owner]
-            counts_ref[owner] = rank + 1
-            held = jnp.minimum(rank, count - 1)
-            lists_ref[owner, held] = j
-            place = (owner ^ row) * count + held
-            pos_ref[j] = place
-            wide_ref[pl.ds(j, 1), :] = jnp.full((1, LANES), place, jnp.int32)
-        return c
-
-    lax.fori_loop(0, width // SUB, locate, 0)
-
-    def clear(i, c):
-        for p in range(n_row):
-            lists_ref[p, i] = jnp.where(i < counts_ref[p], lists_ref[p, i], 0)
-        pivot = pivot_ref[lists_ref[row, i]]
-        block = lax.shift_right_logical(pivot, width_log)
-        slot = lax.shift_left(lax.shift_right_logical(block, row_log), width_log) + (pivot & (width - 1))
-        mine_ref[i] = jnp.where(i < counts_ref[row], slot, 0)
-        return c
-
-    lax.fori_loop(0, count, clear, 0)
-
-
-def tables(pivots, n_row, count):
-    width = pivots.shape[0]
-
-    def ints(*shape):
-        return jax.ShapeDtypeStruct(shape, jnp.int32)
-
-    return pl.pallas_call(
-        functools.partial(tables_kernel, n_row),
-        out_shape=(ints(count), ints(n_row, count), ints(width), ints(width, LANES), ints(n_row)),
-        in_specs=[smem()],
-        out_specs=(smem(), smem(), smem(), vmem(), smem()),
-        cost_estimate=pl.CostEstimate(flops=0, bytes_accessed=10_000_000, transcendentals=0),
-        name="tables",
-    )(pivots)
-
-
-def begin_kernel(n_row, mine_ref, lists_ref, mat_ref, panel_ref, *refs):
-    messages, sem = refs[:n_row], refs[-1]
-    width = panel_ref.shape[1]
-    count = mine_ref.shape[0]
     copy = pltpu.make_async_copy(mat_ref.at[:, 0, pl.ds(0, width)], panel_ref, sem)
     copy.start()
+    pivot = pivot_ref[...]
+    block = lax.shift_right_logical(pivot, width_log)
+    owner = block & (n_row - 1)
+    slot = lax.shift_left(lax.shift_right_logical(block, row_log), width_log) + (pivot & (width - 1))
+    height = -(-n_row // 16) * 16
+    held = lax.broadcasted_iota(jnp.int32, (height, width), 0) == owner
+    before = lax.broadcasted_iota(jnp.int32, (width, width), 0) < lax.broadcasted_iota(jnp.int32, (width, width), 1)
+    held = jnp.where(held, 1.0, 0.0)
+    earlier = jnp.dot(
+        held.astype(jnp.bfloat16), jnp.where(before, 1.0, 0.0).astype(jnp.bfloat16), preferred_element_type=jnp.float32
+    )
+    rank = jnp.sum(held * earlier, axis=0, keepdims=True).astype(jnp.int32)
+    fits_ref[0] = (jnp.max(rank) < count).astype(jnp.int32)
+    place = ((owner ^ row) * count + rank).astype(jnp.float32)
+    eye = lax.broadcasted_iota(jnp.int32, (width, width), 0) == lax.broadcasted_iota(jnp.int32, (width, width), 1)
+    spread = jnp.where(eye, place, 0.0)
+    wide = jnp.dot(spread, jnp.ones((width, LANES), jnp.float32), precision=HI, preferred_element_type=jnp.float32)
+    wide_ref[...] = wide.astype(jnp.int32)
+    ordinal = lax.broadcasted_iota(jnp.int32, (count, width), 0)
+    mine = jnp.where((ordinal == rank) & (owner == row), 1.0, 0.0).astype(jnp.bfloat16)
+    at_slot = jnp.where(lax.broadcasted_iota(jnp.int32, (rows, width), 0) == slot, 1.0, 0.0).astype(jnp.bfloat16)
+    choice = lax.dot_general(mine, at_slot, (((1,), (1,)), ((), ())), preferred_element_type=jnp.float32)
     copy.wait()
-
-    def gather(q, c):
-        for u in range(SUB):
-            i = q * SUB + u
-            messages[0][pl.ds(i, 1), :] = panel_ref[pl.ds(mine_ref[i], 1), :]
-        return c
-
-    lax.fori_loop(0, count // SUB, gather, 0)
-    for k in range(1, n_row):
-        messages[k][:count, :] = messages[0][:count, :]
-
-    @pl.when(lax.axis_index("prow") == 0)
-    def _():
+    own = select_dot(choice, thirds(panel_ref[...]))
+    for k in range(n_row):
+        messages[k][:count, :] = own
+
+    @pl.when(row == 0)
+    def _():
+        top = thirds(panel_ref[:width, :])
         for p in range(n_row):
-            def gather_top(q, c, p=p):
-                for u in range(SUB):
-                    i = q * SUB + u
-                    messages[p][pl.ds(count + i, 1), :] = panel_ref[pl.ds(lists_ref[p, i], 1), :]
-                return c
-
-            lax.fori_loop(0, count // SUB, gather_top, 0)
-
-
-def begin(mat, mine, lists, width):
-    rows, (n_row, count) = mat.shape[0], lists.shape
+            messages[p][count:, :] = select_dot(jnp.where((ordinal == rank) & (owner == p), 1.0, 0.0), top)
+
+
+def begin(mat, pivots, n_row, count):
+    rows, width = mat.shape[0], pivots.shape[0]
     message = jax.ShapeDtypeStruct((2 * count, width), jnp.float32)
     return pl.pallas_call(
         functools.partial(begin_kernel, n_row),
-        out_shape=(jax.ShapeDtypeStruct((rows, width), jnp.float32),) + (message,) * n_row,
-        in_specs=[smem(), smem(), raw()],
-        out_specs=(vmem(),) * (n_row + 1),
+        out_shape=(
+            jax.ShapeDtypeStruct((rows, width), jnp.float32),
+            jax.ShapeDtypeStruct((width, LANES), jnp.int32),
+            jax.ShapeDtypeStruct((1,), jnp.int32),
+        ) + (message,) * n_row,
+        in_specs=[vmem(), raw()],
+        out_specs=(vmem(), vmem(), smem()) + (vmem(),) * n_row,
         scratch_shapes=[pltpu.SemaphoreType.DMA],
         cost_estimate=pl.CostEstimate(flops=0, bytes_accessed=10_000_000, transcendentals=0),
         name="begin",
-    )(mine, lists, mat)
+    )(pivots[None, :], mat)
 
 
 def parcel_kernel(n_row, mine_ref, lists_ref, mat_ref, own_ref, *refs):
@@ -509,24 +486,24 @@
     )(mine, lists, mat)
 
 
-def pack_kernel(n_row, pos_ref, *refs):
-    parts, out_ref, all_ref = refs[:n_row], refs[n_row], refs[n_row + 1]
-    width = pos_ref.shape[0]
+def pack_kernel(n_row, wide_ref, *refs):
+    parts, out_ref = refs[:n_row], refs[n_row]
+    width = wide_ref.shape[0]
     count = out_ref.shape[0] - width
     row, col = lax.axis_index("prow"), lax.axis_index("pcol")
+    total = -(-n_row * count // LANES) * LANES
 
     @pl.when(col == 0)
     def _():
-        for k in range(n_row):
-            all_ref[k * count:(k + 1) * count, :] = parts[k][:count, :]
-
-        def group(q, c):
-            for u in range(SUB):
-                j = q * SUB + u
-                out_ref[pl.ds(j, 1), :] = all_ref[pl.ds(pos_ref[j], 1), :]
-            return c
-
-        lax.fori_loop(0, width // SUB, group, 0)
+        pieces = [parts[k][:count, :] for k in range(n_row)]
+        if total > n_row * count:
+            pieces.append(jnp.zeros((total - n_row * count, width), jnp.float32))
+        stack = jnp.concatenate(pieces, axis=0)
+        lanes = lax.broadcasted_iota(jnp.int32, (width, LANES), 1)
+        choice = jnp.concatenate(
+            [jnp.where(lanes + t * LANES == wide_ref[...], 1.0, 0.0) for t in range(total // LANES)], axis=1
+        )
+        out_ref[:width, :] = select_dot(choice, thirds(stack))
         for k in range(n_row):
             @pl.when(row == k)
             def _(k=k):
@@ -537,18 +514,17 @@
         out_ref[...] = jnp.zeros_like(out_ref)
 
 
-def pack(pos, parts):
-    n_row, width = len(parts), pos.shape[0]
+def pack(wide, parts):
+    n_row, width = len(parts), wide.shape[0]
     count = parts[0].shape[0] // 2
     return pl.pallas_call(
         functools.partial(pack_kernel, n_row),
         out_shape=jax.ShapeDtypeStruct((width + count, width), jnp.float32),
-        in_specs=[smem()] + [vmem()] * n_row,
+        in_specs=[vmem()] * (n_row + 1),
         out_specs=vmem(),
-        scratch_shapes=[pltpu.VMEM((n_row * count, width), jnp.float32)],
-        cost_estimate=pl.CostEstimate(flops=0, bytes_accessed=24 * width * width, transcendentals=0),
+        cost_estimate=pl.CostEstimate(flops=0, bytes_accessed=4_000_000, transcendentals=0),
         name="pack",
-    )(pos, *parts)
+    )(wide, *parts)
 
 
 def put_rows(slot_ref, held, rows_ref, target_ref):
@@ -681,51 +657,71 @@
     return -(-int(mean + 3.4 * (mean * (1 - 1 / n_row)) ** 0.5) // SUB) * SUB
 
 
-def capped_step(n_row, n_col, matrix, found):
+def locate(pivots, n_row, row, count):
+    width = pivots.shape[0]
+    owner = pivots // width % n_row
+    slot = pivots // (width * n_row) * width + pivots % width
+    number = jnp.arange(width, dtype=jnp.int32)
+    ahead = (owner[:, None] == owner[None, :]) & (number[None, :] < number[:, None])
+    rank = jnp.sum(ahead, axis=1, dtype=jnp.int32)
+    every = jnp.arange(n_row, dtype=jnp.int32)[:, None, None]
+    ordinal = jnp.arange(count, dtype=jnp.int32)[None, :, None]
+    hits = (owner[None, None, :] == every) & (rank[None, None, :] == ordinal)
+    lists = jnp.sum(jnp.where(hits, number[None, None, :], 0), axis=2, dtype=jnp.int32)
+    own = (owner[None, :] == row) & (rank[None, :] == ordinal[0])
+    mine = jnp.sum(jnp.where(own, slot[None, :], 0), axis=1, dtype=jnp.int32)
+    return mine, lists, jnp.sum(owner[None, :] == every[:, 0], axis=1, dtype=jnp.int32)
+
+
+def capped_step(n_row, n_col, matrix, pivots, begun):
     _, rows, _, cols = matrix.shape
     mat = matrix.reshape(rows, 1, cols)
-    mine, lists, pos, wide, counts = found
-    width = pos.shape[0]
-    col = lax.axis_index("pcol")
+    panel, wide, _, *messages = begun
+    count = messages[0].shape[0] // 2
+    row, col = lax.axis_index("prow"), lax.axis_index("pcol")
     both = ("prow", "pcol")
+    turns = bits_of(n_col)[:0:-1]
 
     def exchange(x, k):
         return lax.ppermute(x, both, [(i * n_col, (i ^ k) * n_col) for i in range(n_row)])
 
+    moved = [exchange(messages[k], k) for k in range(1, n_row)]
+    mine, lists, counts = locate(pivots, n_row, row, count)
     parcels = parcel(mat, mine, lists)
-    sent = [lax.ppermute(parcels[1 + k], "prow", [(i, i ^ k) for i in range(n_row)]) for k in range(1, n_row)]
-    mine, own = lax.optimization_barrier((mine, parcels[0]))
-    panel, *messages = begin(mat, mine, lists, width)
-    moved = [exchange(messages[k], k) for k in range(1, n_row)]
-    message = pack(pos, [messages[0]] + moved)
-    panel, message, sent[0], sent[1] = lax.optimization_barrier((panel, message, sent[0], sent[1]))
-    have = [0]
-    for bit in bits_of(n_col)[:0:-1]:
-        pairs = [(i, i + bit) for i in have]
-        have = have + [i + bit for i in have]
-        message_moved = lax.ppermute(message, "pcol", pairs)
-        panel_moved = lax.ppermute(panel, "pcol", pairs)
-        message = jnp.where((col & bit) != 0, message_moved, message)
-        message, panel_moved = lax.optimization_barrier((message, panel_moved))
-        panel = jnp.where((col & bit) != 0, panel_moved, panel)
-    pairs = [(i, i + 1) for i in have]
-    message_new = lax.ppermute(message, "pcol", pairs)
+    sent = []
+    for k in range(1, n_row):
+        item = parcels[1 + k]
+        if k == 3:
+            item, *sent = lax.optimization_barrier((item, *sent))
+        sent.append(lax.ppermute(item, "prow", [(i, i ^ k) for i in range(n_row)]))
+    message = pack(wide, messages[:1] + moved)
+
+    pairs = [[(i, i + bit) for i in range(0, n_col, 2 * bit)] for bit in turns + [1]]
+    newer = [(col & bit) != 0 for bit in turns]
+    panel_moved = lax.ppermute(panel, "pcol", pairs[0])
+    message, panel_moved = lax.optimization_barrier((message, panel_moved))
+    for n in range(len(turns)):
+        panel = jnp.where(newer[n], panel_moved, panel)
+        panel_moved = lax.ppermute(panel, "pcol", pairs[n + 1])
+        message = jnp.where(newer[n], lax.ppermute(message, "pcol", pairs[n]), message)
+        if n + 1 < len(turns):
+            message, panel_moved = lax.optimization_barrier((message, panel_moved))
+    message_new = lax.ppermute(message, "pcol", pairs[-1])
     factors = factor(message, message_new)
-    panel_new = lax.ppermute(panel, "pcol", pairs)
     out = finish(
-        mine, counts, wide, mat, (panel, panel_new), (message, message_new), factors, [own, parcels[1]] + sent
+        mine, counts, wide, mat, (panel, panel_moved), (message, message_new), factors, list(parcels[:2]) + sent
     )
     return out.reshape(matrix.shape)
 
 
 def on_device(n_row, n_col, matrix, pivots):
-    count = capacity(n_row, pivots.shape[0])
-    found = tables(pivots, n_row, count)
+    _, rows, _, cols = matrix.shape
+    begun = begin(matrix.reshape(rows, 1, cols), pivots, n_row, capacity(n_row, pivots.shape[0]))
     return lax.cond(
-        jnp.max(found[-1]) <= count,
-        lambda m, p, f: capped_step(n_row, n_col, m, f),
-        lambda m, p, f: dense_step(n_row, n_col, m, p),
-        matrix, pivots, found,
+        begun[2][0] > 0,
+        lambda m, p, b: capped_step(n_row, n_col, m, p, b),
+        lambda m, p, b: dense_step(n_row, n_col, m, p),
+        matrix, pivots, begun,
     )
 
 

time: 124 us -> 99.2 us (0.80)
  the two profiles are of different devices: /device:TPU:27 before, /device:TPU:0 now
where the time goes in v5:
time: 99.2 us; the launch traced here: 97.9 us
  Pallas kernels  42 us (42%)
  waiting for transfers between devices  25.3 us (26%)
  starting transfers between devices  23.9 us (24%)
  other arithmetic  3.9 us (4%)
  local copies, waits for them, and re-layouts  1.49 us (2%)
    ppermute x3, waiting for transfers between devices, capped_step(): sent.append(lax.ppermute(item, 'prow', [(i, i ^ k) for i in range(n_row)]))  19.8 us
    pallas_call x1, Pallas kernels, factor(): pl.pallas_call(functools.partial(factor_kernel, width), out_shape=(out, o...  14.6 us
    pallas_call x1, Pallas kernels, finish(): pl.pallas_call(functools.partial(finish_kernel, n_row), out_shape=jax.Sha...  12.2 us
    ppermute x3, starting transfers between devices, exchange(): lax.ppermute(x, both, [(i * n_col, (i ^ k) * n_col) for i in range(n_row)])  9.78 us
    pallas_call x1, Pallas kernels, parcel(): pl.pallas_call(functools.partial(parcel_kernel, n_row), out_shape=(shape(...  8.75 us
    ppermute x2, waiting for transfers between devices, capped_step(): lax.ppermute(message, 'pcol', pairs[n])  4.82 us
    ppermute x2, starting transfers between devices, capped_step(): lax.ppermute(message, 'pcol', pairs[n])  4.59 us
    ppermute x2, starting transfers between devices, capped_step(): panel_moved = lax.ppermute(panel, 'pcol', pairs[n + 1])  4.58 us
  transfers between devices with their start and end apart: 12, of which 4 were waited for; matrix products, arithmetic and copies ran while one was open for 4% of the time, Pallas kernels for 26%

profile of v5, /device:TPU:0, one launch (start us, length us, event | category | flops | bytes accessed | tf_op | source)
XLA Modules:
  0.0 97.9 jit_solution(15581880853331979927)
XLA Ops:
  0.0 4.2 %begin.1 = (f32[1024,256]{1,0:T(8,128)}, s32[256,128]{1,0:T(8,128)S(1)}, s32[1]{0:T(128)}, f32[176,256]{1,0:T(8,128)S(1)}, f32[176,256]{1,0:T(8,128)}, /*index=5*/f32[176,256]{1,0:T(8,128)}, f32[176,256]{1,0:T(8,128)}) custom-call(s32[1,256]{1,0:T(1,128)} %bitcast.28, f32[1024,1,1536]{2,1,0:T(1,128)} %bitcast.24), custom_call_target="tpu_custom_call" | custom-call | bytes 10000000 | tf_op jit(solution)/shard_map/begin/pallas_call | solution.py:415
  4.9 92.8 %conditional.1 = (f32[1,1024,1,1536]{3,2,1,0:T(1,128)}) conditional(s32[]{:T(128)} %bitcast.11, (s32[256]{0:T(256)S(1)}, f32[1,1024,1,1536]{3,2,1,0:T(1,128)}) %tuple.33, (s32[256]{0:T(256)S(1)}, f32[1,1024,1,1536]{3,2,1,0:T(1,128)}, f32[176,256]{1,0:T(8,128)}, f32[176,256]{1,0:T(8,128)}, f32[176,256]{1,0:T(8,128)}, ...), branch_computations={%region_0.1_spmd, %region_1.6_spmd} | conditional | flops 2488416000 | bytes 211226368 | solution.py:720
  5.1 4.4 %collective-permute-start = (f32[176,256]{1,0:T(8,128)}, f32[176,256]{1,0:T(8,128)S(1)}, u32[]{:S(2)}, u32[]{:S(2)}) collective-permute-start(f32[176,256]{1,0:T(8,128)} %get-tuple-element.37), channel_id=1, source_target_pairs={{0,8},{8,0},{16,24},{24,16}} | collective-permute-start | bytes 540680 | tf_op jit(solution)/shard_map/cond/branch_1_fun/ppermute | solution.py:686
  9.6 3.4 %collective-permute-start.1 = (f32[176,256]{1,0:T(8,128)}, f32[176,256]{1,0:T(8,128)S(1)}, u32[]{:S(2)}, u32[]{:S(2)}) collective-permute-start(f32[176,256]{1,0:T(8,128)} %get-tuple-element.38), channel_id=1, source_target_pairs={{0,16},{8,24},{16,0},{24,8}} | collective-permute-start | bytes 540680 | tf_op jit(solution)/shard_map/cond/branch_1_fun/ppermute | solution.py:686
  13.0 1.9 %collective-permute-start.2 = (f32[176,256]{1,0:T(8,128)}, f32[176,256]{1,0:T(8,128)S(1)}, u32[]{:S(2)}, u32[]{:S(2)}) collective-permute-start(f32[176,256]{1,0:T(8,128)} %get-tuple-element.39), channel_id=1, source_target_pairs={{0,24},{8,16},{16,8},{24,0}} | collective-permute-start | bytes 540680 | tf_op jit(solution)/shard_map/cond/branch_1_fun/ppermute | solution.py:686
  14.9 2.3 %collective-permute-start.3 = (f32[1024,256]{1,0:T(8,128)}, f32[1024,256]{1,0:T(8,128)}, u32[]{:S(2)}, u32[]{:S(2)}) collective-permute-start(f32[1024,256]{1,0:T(8,128)} %get-tuple-element.40), channel_id=1, source_target_pairs={{0,4},{8,12},{16,20},{24,28}} | collective-permute-start | bytes 3145736 | tf_op jit(solution)/shard_map/cond/branch_1_fun/ppermute | solution.py:701
  17.5 0.6 select_reduce_fusion.1.mine_ref
  18.1 0.7 select_reduce_fusion.lists_ref
  18.8 8.8 %parcel.1 = (f32[88,1,1536]{2,1,0:T(1,128)}, f32[88,1,1536]{2,1,0:T(1,128)}, f32[176,1,1536]{2,1,0:T(1,128)}, f32[176,1,1536]{2,1,0:T(1,128)}, f32[176,1,1536]{2,1,0:T(1,128)}) custom-call(s32[88]{0:T(128)} %select_reduce_fusion.1.mine_ref, s32[4,88]{1,0:T(4,128)} %select_reduce_fusion.lists_ref, f32[1024,1,1536]{2,1,0:T(1,128)} %bitcast.25), custom_call_target="tpu_custom_call" | custom-call | bytes 20000000 | tf_op jit(solution)/shard_map/cond/branch_1_fun/parcel/pallas_call | solution.py:478
  28.5 2.2 %pack.1 = f32[344,256]{1,0:T(8,128)} custom-call(s32[256,128]{1,0:T(8,128)S(1)} %get-tuple-element.34.wide_ref, f32[176,256]{1,0:T(8,128)S(1)} %get-tuple-element.36.refs_0_, f32[176,256]{1,0:T(8,128)} %copy-done.8, f32[176,256]{1,0:T(8,128)} %copy-done.9, f32[176,256]{1,0:T(8,128)} %copy-done.10), custom_call_target="tpu_custom_call" | custom-call | bytes 4000000 | tf_op jit(solution)/shard_map/cond/branch_1_fun/pack/pallas_call | solution.py:520
  30.8 1.4 %broadcast_select_fusion.3 = f32[1024,256]{1,0:T(8,128)S(1)} fusion(f32[1024,256]{1,0:T(8,128)} %collective-permute-done.3, f32[1024,256]{1,0:T(8,128)} %get-tuple-element.40, pred[]{:T(512)S(6)} %ne.60), kind=kLoop, calls=%fused_computation.31 | loop fusion | flops 262144 | bytes 3145729 | tf_op jit(solution)/shard_map/cond/branch_1_fun/jit(_where)/select_n | solution.py:704
  32.2 2.3 %collective-permute-start.5 = (f32[1024,256]{1,0:T(8,128)S(1)}, f32[1024,256]{1,0:T(8,128)}, u32[]{:S(2)}, u32[]{:S(2)}) collective-permute-start(f32[1024,256]{1,0:T(8,128)S(1)} %broadcast_select_fusion.3), channel_id=1, source_target_pairs={{0,2},{4,6},{8,10},{12,14},{16,18},{20,22},{24,26},{28,30}} | collective-permute-start | bytes 3145736 | tf_op jit(solution)/shard_map/cond/branch_1_fun/ppermute | solution.py:705
  34.5 3.3 %collective-permute-start.4 = (f32[344,256]{1,0:T(8,128)S(1)}, f32[344,256]{1,0:T(8,128)S(1)}, u32[]{:S(2)}, u32[]{:S(2)}) collective-permute-start(f32[344,256]{1,0:T(8,128)S(1)} %copy-done.5), channel_id=1, source_target_pairs={{0,4},{8,12},{16,20},{24,28}} | collective-permute-start | bytes 1056776 | tf_op jit(solution)/shard_map/cond/branch_1_fun/ppermute | solution.py:706
  37.8 13.4 %collective-permute-done.9.refs_2_ = f32[176,1,1536]{2,1,0:T(1,128)S(1)} collective-permute-done((f32[176,1,1536]{2,1,0:T(1,128)}, f32[176,1,1536]{2,1,0:T(1,128)S(1)}, u32[]{:S(2)}, u32[]{:S(2)}) %collective-permute-start.9) | collective-permute-done | bytes 1081376 | tf_op jit(solution)/shard_map/cond/branch_1_fun/ppermute | solution.py:696
  51.3 6.4 %collective-permute-done.10.refs_3_ = f32[176,1,1536]{2,1,0:T(1,128)} collective-permute-done((f32[176,1,1536]{2,1,0:T(1,128)}, f32[176,1,1536]{2,1,0:T(1,128)}, u32[]{:S(2)}, u32[]{:S(2)}) %collective-permute-start.10) | collective-permute-done | bytes 1081376 | tf_op jit(solution)/shard_map/cond/branch_1_fun/ppermute | solution.py:696
  57.7 1.2 %collective-permute-start.11 = (f32[176,1,1536]{2,1,0:T(1,128)}, f32[176,1,1536]{2,1,0:T(1,128)}, u32[]{:S(2)}, u32[]{:S(2)}) collective-permute-start(f32[176,1,1536]{2,1,0:T(1,128)} %get-tuple-element.55), channel_id=1, source_target_pairs={{0,24},{8,16},{16,8},{24,0},{1,25},{9,17},{17,9},{25,1},{2,26},{10... | collective-permute-start | bytes 3244040 | tf_op jit(solution)/shard_map/cond/branch_1_fun/ppermute | solution.py:696
  59.1 2.3 %collective-permute-start.6 = (f32[1024,256]{1,0:T(8,128)S(1)}, f32[1024,256]{1,0:T(8,128)}, u32[]{:S(2)}, u32[]{:S(2)}) collective-permute-start(f32[1024,256]{1,0:T(8,128)S(1)} %broadcast_select_fusion.4.panel_ref), channel_id=1, source_target_pairs={{0,1},{2,3},{4,5},{6,7},{8,9},{10,11},{12,13},{14,15},{16,17},{18,... | collective-permute-start | bytes 3145736 | tf_op jit(solution)/shard_map/cond/branch_1_fun/ppermute | solution.py:705
  61.4 1.3 %collective-permute-start.7 = (f32[344,256]{1,0:T(8,128)S(1)}, f32[344,256]{1,0:T(8,128)S(1)}, u32[]{:S(2)}, u32[]{:S(2)}) collective-permute-start(f32[344,256]{1,0:T(8,128)S(1)} %broadcast_select_fusion.6), channel_id=1, source_target_pairs={{0,2},{4,6},{8,10},{12,14},{16,18},{20,22},{24,26},{28,30}} | collective-permute-start | bytes 1056776 | tf_op jit(solution)/shard_map/cond/branch_1_fun/ppermute | solution.py:706
  62.7 4.8 %collective-permute-done.7 = f32[344,256]{1,0:T(8,128)S(1)} collective-permute-done((f32[344,256]{1,0:T(8,128)S(1)}, f32[344,256]{1,0:T(8,128)S(1)}, u32[]{:S(2)}, u32[]{:S(2)}) %collective-permute-start.7) | collective-permute-done | bytes 352288 | tf_op jit(solution)/shard_map/cond/branch_1_fun/ppermute | solution.py:706
  67.6 1.3 %collective-permute-start.8 = (f32[344,256]{1,0:T(8,128)S(1)}, f32[344,256]{1,0:T(8,128)S(1)}, u32[]{:S(2)}, u32[]{:S(2)}) collective-permute-start(f32[344,256]{1,0:T(8,128)S(1)} %broadcast_select_fusion.5.s_ref.square_ref), channel_id=1, source_target_pairs={{0,1},{2,3},{4,5},{6,7},{8,9},{10,11},{12,13},{14,15},{16,17},{18,... | collective-permute-start | bytes 1056776 | tf_op jit(solution)/shard_map/cond/branch_1_fun/ppermute | solution.py:709
  68.9 0.6 convert_reduce_fusion.1.counts_ref
  70.1 0.7 copy-done.4
  70.9 14.6 %factor.3 = (f32[256,256]{1,0:T(8,128)}, f32[256,256]{1,0:T(8,128)}, f32[256,256]{1,0:T(8,128)}) custom-call(f32[344,256]{1,0:T(8,128)} %copy-done.3, f32[344,256]{1,0:T(8,128)} %copy-done.4), custom_call_target="tpu_custom_call" | custom-call | flops 67108864 | bytes 50000000 | tf_op jit(solution)/shard_map/cond/branch_1_fun/factor/pallas_call | solution.py:145
  85.5 12.2 %finish.1 = f32[1024,1,1536]{2,1,0:T(1,128)} custom-call(s32[88]{0:T(128)} %select_reduce_fusion.1.mine_ref, s32[4]{0:T(128)} %convert_reduce_fusion.1.counts_ref, s32[256,128]{1,0:T(8,128)S(1)} %get-tuple-element.34.wide_ref, f32[1024,1,1536]{2,1,0:T(1,128)} %bitcast.26, f32[1024,256]{1,0:T(8,128)} %copy-done.2, ...), custom_call_target="tpu_custom_call" | custom-call | flops 2415919104 | bytes 12582912 | tf_op jit(solution)/shard_map/cond/branch_1_fun/finish/pallas_call | solution.py:631
  (36 shorter events, 2.0 us)
Async XLA Ops:
  0.0 4.9 %copy-start.11 = (s32[256]{0:T(256)S(1)}, s32[256]{0:T(256)}, u32[]{:S(2)}) copy-start(s32[256]{0:T(256)} %param.5) | copy-start | bytes 3076
  5.1 22.6 %collective-permute-start = (f32[176,256]{1,0:T(8,128)}, f32[176,256]{1,0:T(8,128)S(1)}, u32[]{:S(2)}, u32[]{:S(2)}) collective-permute-start(f32[176,256]{1,0:T(8,128)} %get-tuple-element.37), channel_id=1, source_target_pairs={{0,8},{8,0},{16,24},{24,16}} | collective-permute-start | bytes 540680 | tf_op jit(solution)/shard_map/cond/branch_1_fun/ppermute | solution.py:686
  9.6 18.2 %collective-permute-start.1 = (f32[176,256]{1,0:T(8,128)}, f32[176,256]{1,0:T(8,128)S(1)}, u32[]{:S(2)}, u32[]{:S(2)}) collective-permute-start(f32[176,256]{1,0:T(8,128)} %get-tuple-element.38), channel_id=1, source_target_pairs={{0,16},{8,24},{16,0},{24,8}} | collective-permute-start | bytes 540680 | tf_op jit(solution)/shard_map/cond/branch_1_fun/ppermute | solution.py:686
  13.0 14.8 %collective-permute-start.2 = (f32[176,256]{1,0:T(8,128)}, f32[176,256]{1,0:T(8,128)S(1)}, u32[]{:S(2)}, u32[]{:S(2)}) collective-permute-start(f32[176,256]{1,0:T(8,128)} %get-tuple-element.39), channel_id=1, source_target_pairs={{0,24},{8,16},{16,8},{24,0}} | collective-permute-start | bytes 540680 | tf_op jit(solution)/shard_map/cond/branch_1_fun/ppermute | solution.py:686
  14.9 15.9 %collective-permute-start.3 = (f32[1024,256]{1,0:T(8,128)}, f32[1024,256]{1,0:T(8,128)}, u32[]{:S(2)}, u32[]{:S(2)}) collective-permute-start(f32[1024,256]{1,0:T(8,128)} %get-tuple-element.40), channel_id=1, source_target_pairs={{0,4},{8,12},{16,20},{24,28}} | collective-permute-start | bytes 3145736 | tf_op jit(solution)/shard_map/cond/branch_1_fun/ppermute | solution.py:701
  27.6 23.7 %collective-permute-start.9 = (f32[176,1,1536]{2,1,0:T(1,128)}, f32[176,1,1536]{2,1,0:T(1,128)S(1)}, u32[]{:S(2)}, u32[]{:S(2)}) collective-permute-start(f32[176,1,1536]{2,1,0:T(1,128)} %get-tuple-element.51), channel_id=1, source_target_pairs={{0,8},{8,0},{16,24},{24,16},{1,9},{9,1},{17,25},{25,17},{2,10},{10... | collective-permute-start | bytes 3244040 | tf_op jit(solution)/shard_map/cond/branch_1_fun/ppermute | solution.py:696
  27.7 0.7 copy-start.8
  27.7 30.0 %collective-permute-start.10 = (f32[176,1,1536]{2,1,0:T(1,128)}, f32[176,1,1536]{2,1,0:T(1,128)}, u32[]{:S(2)}, u32[]{:S(2)}) collective-permute-start(f32[176,1,1536]{2,1,0:T(1,128)} %get-tuple-element.52), channel_id=1, source_target_pairs={{0,16},{8,24},{16,0},{24,8},{1,17},{9,25},{17,1},{25,9},{2,18},{10... | collective-permute-start | bytes 3244040 | tf_op jit(solution)/shard_map/cond/branch_1_fun/ppermute | solution.py:696
  27.8 0.7 copy-start.9
  27.8 0.7 copy-start.10
  30.8 3.7 %copy-start.5 = (f32[344,256]{1,0:T(8,128)S(1)}, f32[344,256]{1,0:T(8,128)}, u32[]{:S(2)}) copy-start(f32[344,256]{1,0:T(8,128)} %pack.1) | copy-start | bytes 1056772 | tf_op jit(solution)/shard_map/cond
  32.2 26.7 %collective-permute-start.5 = (f32[1024,256]{1,0:T(8,128)S(1)}, f32[1024,256]{1,0:T(8,128)}, u32[]{:S(2)}, u32[]{:S(2)}) collective-permute-start(f32[1024,256]{1,0:T(8,128)S(1)} %broadcast_select_fusion.3), channel_id=1, source_target_pairs={{0,2},{4,6},{8,10},{12,14},{16,18},{20,22},{24,26},{28,30}} | collective-permute-start | bytes 3145736 | tf_op jit(solution)/shard_map/cond/branch_1_fun/ppermute | solution.py:705
  34.5 24.4 %collective-permute-start.4 = (f32[344,256]{1,0:T(8,128)S(1)}, f32[344,256]{1,0:T(8,128)S(1)}, u32[]{:S(2)}, u32[]{:S(2)}) collective-permute-start(f32[344,256]{1,0:T(8,128)S(1)} %copy-done.5), channel_id=1, source_target_pairs={{0,4},{8,12},{16,20},{24,28}} | collective-permute-start | bytes 1056776 | tf_op jit(solution)/shard_map/cond/branch_1_fun/ppermute | solution.py:706
  51.3 7.8 %copy-start.6 = (f32[176,1,1536]{2,1,0:T(1,128)}, f32[176,1,1536]{2,1,0:T(1,128)S(1)}, u32[]{:S(2)}) copy-start(f32[176,1,1536]{2,1,0:T(1,128)S(1)} %collective-permute-done.9.refs_2_) | copy-start | bytes 3244036 | tf_op jit(solution)/shard_map/cond
  57.7 27.8 %collective-permute-start.11 = (f32[176,1,1536]{2,1,0:T(1,128)}, f32[176,1,1536]{2,1,0:T(1,128)}, u32[]{:S(2)}, u32[]{:S(2)}) collective-permute-start(f32[176,1,1536]{2,1,0:T(1,128)} %get-tuple-element.55), channel_id=1, source_target_pairs={{0,24},{8,16},{16,8},{24,0},{1,25},{9,17},{17,9},{25,1},{2,26},{10... | collective-permute-start | bytes 3244040 | tf_op jit(solution)/shard_map/cond/branch_1_fun/ppermute | solution.py:696
  59.1 26.4 %copy-start.2 = (f32[1024,256]{1,0:T(8,128)}, f32[1024,256]{1,0:T(8,128)S(1)}, u32[]{:S(2)}) copy-start(f32[1024,256]{1,0:T(8,128)S(1)} %broadcast_select_fusion.4.panel_ref) | copy-start | bytes 3145732 | tf_op jit(solution)/shard_map/cond
  59.1 26.4 %collective-permute-start.6 = (f32[1024,256]{1,0:T(8,128)S(1)}, f32[1024,256]{1,0:T(8,128)}, u32[]{:S(2)}, u32[]{:S(2)}) collective-permute-start(f32[1024,256]{1,0:T(8,128)S(1)} %broadcast_select_fusion.4.panel_ref), channel_id=1, source_target_pairs={{0,1},{2,3},{4,5},{6,7},{8,9},{10,11},{12,13},{14,15},{16,17},{18,... | collective-permute-start | bytes 3145736 | tf_op jit(solution)/shard_map/cond/branch_1_fun/ppermute | solution.py:705
  61.4 6.1 %collective-permute-start.7 = (f32[344,256]{1,0:T(8,128)S(1)}, f32[344,256]{1,0:T(8,128)S(1)}, u32[]{:S(2)}, u32[]{:S(2)}) collective-permute-start(f32[344,256]{1,0:T(8,128)S(1)} %broadcast_select_fusion.6), channel_id=1, source_target_pairs={{0,2},{4,6},{8,10},{12,14},{16,18},{20,22},{24,26},{28,30}} | collective-permute-start | bytes 1056776 | tf_op jit(solution)/shard_map/cond/branch_1_fun/ppermute | solution.py:706
  67.6 2.6 %copy-start.3 = (f32[344,256]{1,0:T(8,128)}, f32[344,256]{1,0:T(8,128)S(1)}, u32[]{:S(2)}) copy-start(f32[344,256]{1,0:T(8,128)S(1)} %broadcast_select_fusion.5.s_ref.square_ref) | copy-start | bytes 1056772 | tf_op jit(solution)/shard_map/cond
  67.6 2.6 %collective-permute-start.8 = (f32[344,256]{1,0:T(8,128)S(1)}, f32[344,256]{1,0:T(8,128)S(1)}, u32[]{:S(2)}, u32[]{:S(2)}) collective-permute-start(f32[344,256]{1,0:T(8,128)S(1)} %broadcast_select_fusion.5.s_ref.square_ref), channel_id=1, source_target_pairs={{0,1},{2,3},{4,5},{6,7},{8,9},{10,11},{12,13},{14,15},{16,17},{18,... | collective-permute-start | bytes 1056776 | tf_op jit(solution)/shard_map/cond/branch_1_fun/ppermute | solution.py:709
  70.1 0.8 copy-start.4

commit v6 on v5

--- a/solution.py
+++ b/solution.py
@@ -379,14 +379,7 @@
     block = lax.shift_right_logical(pivot, width_log)
     owner = block & (n_row - 1)
     slot = lax.shift_left(lax.shift_right_logical(block, row_log), width_log) + (pivot & (width - 1))
-    height = -(-n_row // 16) * 16
-    held = lax.broadcasted_iota(jnp.int32, (height, width), 0) == owner
-    before = lax.broadcasted_iota(jnp.int32, (width, width), 0) < lax.broadcasted_iota(jnp.int32, (width, width), 1)
-    held = jnp.where(held, 1.0, 0.0)
-    earlier = jnp.dot(
-        held.astype(jnp.bfloat16), jnp.where(before, 1.0, 0.0).astype(jnp.bfloat16), preferred_element_type=jnp.float32
-    )
-    rank = jnp.sum(held * earlier, axis=0, keepdims=True).astype(jnp.int32)
+    _, rank = owners(pivot, n_row)
     fits_ref[0] = (jnp.max(rank) < count).astype(jnp.int32)
     place = ((owner ^ row) * count + rank).astype(jnp.float32)
     eye = lax.broadcasted_iota(jnp.int32, (width, width), 0) == lax.broadcasted_iota(jnp.int32, (width, width), 1)
@@ -427,63 +420,139 @@
     )(pivots[None, :], mat)
 
 
-def parcel_kernel(n_row, mine_ref, lists_ref, mat_ref, own_ref, *refs):
-    outs, spare_ref, sem = refs[:n_row], refs[n_row], refs[n_row + 1]
-    count = own_ref.shape[0]
-    first = lax.axis_index("prow") == 0
+def parcel_kernel(n_row, mine_ref, pivot_ref, mat_ref, *refs):
+    outs, own, block, sem = refs[:-3], refs[-3], refs[-2], refs[-1]
+    count, cols = own.shape
+    half = count // 2
+    width = pivot_ref.shape[1]
 
     def group(q, c):
         for u in range(SUB):
             i = q * SUB + u
-            pltpu.make_async_copy(mat_ref.at[mine_ref[i]], own_ref.at[i], sem.at[0]).start()
+            pltpu.make_async_copy(mat_ref.at[mine_ref[i]], own.at[pl.ds(i, 1), :], sem.at[0]).start()
         return c
 
     lax.fori_loop(0, count // SUB, group, 0)
 
-    @pl.when(first)
-    def _():
-        for p in range(n_row):
-            base = 0 if p == 0 else count
-
-            def group(q, c, p=p, base=base):
-                for u in range(SUB):
-                    i = q * SUB + u
-                    pltpu.make_async_copy(mat_ref.at[lists_ref[p, i]], outs[p].at[base + i], sem.at[1]).start()
-                return c
-
-            lax.fori_loop(0, count // SUB, group, 0)
-
-    pltpu.make_async_copy(mat_ref.at[pl.ds(0, count)], own_ref, sem.at[0]).wait()
-    copies = [pltpu.make_async_copy(own_ref, outs[p].at[pl.ds(0, count)], sem.at[1 + p]) for p in range(1, n_row)]
-    for copy in copies[1:]:
+    @pl.when(lax.axis_index("prow") == 0)
+    def _():
+        copy = pltpu.make_async_copy(mat_ref.at[pl.ds(0, width), 0, :], block, sem.at[1])
         copy.start()
-    for copy in copies[1:]:
+        owner, rank = owners(pivot_ref[...], n_row)
+        ordinal = lax.broadcasted_iota(jnp.int32, (count, width), 0)
+        choices = [jnp.where((ordinal == rank) & (owner == p), 1.0, 0.0) for p in range(n_row)]
+        choice = jnp.concatenate(choices, axis=0)
         copy.wait()
 
-    @pl.when(first)
-    def _():
-        pltpu.make_async_copy(mat_ref.at[pl.ds(0, n_row * count)], spare_ref, sem.at[1]).wait()
-
-    copies[0].start()
-    copies[0].wait()
-
-
-def parcel(mat, mine, lists):
-    n_row, count = lists.shape
-    cols = mat.shape[2]
-
-    def shape(rows):
-        return jax.ShapeDtypeStruct((rows, 1, cols), jnp.float32)
-
+        def piece(t, c):
+            at = pl.ds(pl.multiple_of(t * width, width), width)
+            tops = select_dot(choice, thirds(block[:, at]))
+            for p in range(n_row):
+                for part in range(2):
+                    first = p * count + part * half
+                    for ref, base in top_places(n_row, half, outs, p, part):
+                        ref[pl.ds(base, half), at] = tops[first:first + half]
+            return c
+
+        lax.fori_loop(0, cols // width, piece, 0)
+
+    pltpu.make_async_copy(mat_ref.at[pl.ds(0, count), 0, :], own, sem.at[0]).wait()
+    if n_row == 4:
+        outs[0][:half, :] = own[:half, :]
+        outs[1][:half, :] = own[half:, :]
+        outs[2][:count, :] = own[...]
+    else:
+        outs[0][:count, :] = own[...]
+        for p in range(1, n_row):
+            outs[p][:count, :] = own[...]
+
+
+def top_places(n_row, half, outs, p, part):
+    if n_row != 4:
+        return [(outs[p], 2 * half + part * half)]
+    if p == 0:
+        return [(outs[2], 2 * half + part * half)]
+    if p == 3:
+        return [(outs[part], 2 * half)]
+    if part == p - 1:
+        return [(outs[part], half)]
+    return [(outs[2], (4 + part) * half)]
+
+
+def owners(pivot, n_row):
+    width = pivot.shape[1]
+    owner = lax.shift_right_logical(pivot, width.bit_length() - 1) & (n_row - 1)
+    held = lax.broadcasted_iota(jnp.int32, (-(-n_row // 16) * 16, width), 0) == owner
+    before = lax.broadcasted_iota(jnp.int32, (width, width), 0) < lax.broadcasted_iota(jnp.int32, (width, width), 1)
+    held = jnp.where(held, 1.0, 0.0)
+    earlier = jnp.dot(
+        held.astype(jnp.bfloat16), jnp.where(before, 1.0, 0.0).astype(jnp.bfloat16), preferred_element_type=jnp.float32
+    )
+    return owner, jnp.sum(held * earlier, axis=0, keepdims=True).astype(jnp.int32)
+
+
+def parcel(mat, mine, pivots, n_row):
+    count, width, cols = mine.shape[0], pivots.shape[0], mat.shape[2]
+    half = count // 2
+    sizes = [3 * half, 3 * half, 6 * half] if n_row == 4 else [2 * count] * n_row
     return pl.pallas_call(
         functools.partial(parcel_kernel, n_row),
-        out_shape=(shape(count), shape(count)) + (shape(2 * count),) * (n_row - 1),
-        in_specs=[smem(), smem(), raw()],
-        out_specs=(vmem(),) * (n_row + 1),
-        scratch_shapes=[pltpu.VMEM((n_row * count, 1, cols), jnp.float32), pltpu.SemaphoreType.DMA((n_row + 1,))],
-        cost_estimate=pl.CostEstimate(flops=0, bytes_accessed=20_000_000, transcendentals=0),
+        out_shape=tuple(jax.ShapeDtypeStruct((size, cols), jnp.float32) for size in sizes),
+        in_specs=[smem(), vmem(), raw()],
+        out_specs=(vmem(),) * len(sizes),
+        scratch_shapes=[
+            pltpu.VMEM((count, cols), jnp.float32),
+            pltpu.VMEM((width, cols), jnp.float32),
+            pltpu.SemaphoreType.DMA((2,)),
+        ],
+        cost_estimate=pl.CostEstimate(flops=0, bytes_accessed=16_000_000, transcendentals=0),
         name="parcel",
-    )(mine, lists, mat)
+    )(mine, pivots[None, :], mat)
+
+
+def relay_kernel(kept_ref, first_ref, second_ref, y_ref, x_ref, sem):
+    half = first_ref.shape[0] // 3
+    row = lax.axis_index("prow")
+
+    def move(source, base, dest, at, n):
+        return pltpu.make_async_copy(source.at[pl.ds(base, half), :], dest.at[pl.ds(at, half), :], sem.at[n])
+
+    copies = [
+        move(kept_ref, 0, y_ref, 0, 0),
+        move(kept_ref, half, x_ref, 0, 1),
+        move(first_ref, 0, y_ref, half, 2),
+        move(second_ref, 0, x_ref, half, 3),
+    ]
+    for copy in copies:
+        copy.start()
+
+    @pl.when(row == 0)
+    def _():
+        move(kept_ref, 4 * half, y_ref, 2 * half, 4).start()
+        move(kept_ref, 5 * half, x_ref, 2 * half, 5).start()
+
+    @pl.when(row != 0)
+    def _():
+        move(first_ref, 2 * half, y_ref, 2 * half, 4).start()
+        move(second_ref, 2 * half, x_ref, 2 * half, 5).start()
+
+    for copy in copies:
+        copy.wait()
+    move(first_ref, 2 * half, y_ref, 2 * half, 4).wait()
+    move(second_ref, 2 * half, x_ref, 2 * half, 5).wait()
+
+
+def relay(kept, first, second):
+    shape = jax.ShapeDtypeStruct(first.shape, jnp.float32)
+    return pl.pallas_call(
+        relay_kernel,
+        out_shape=(shape, shape),
+        in_specs=[raw()] * 3,
+        out_specs=(vmem(), vmem()),
+        scratch_shapes=[pltpu.SemaphoreType.DMA((6,))],
+        cost_estimate=pl.CostEstimate(flops=0, bytes_accessed=4_000_000, transcendentals=0),
+        name="relay",
+    )(kept, first, second)
 
 
 def pack_kernel(n_row, wide_ref, *refs):
@@ -527,6 +596,24 @@
     )(wide, *parts)
 
 
+def unpack_parcels(n_row, count, parcels):
+    half = count // 2
+    if n_row != 4:
+        parts = [(x, part * half) for x in parcels for part in range(2)]
+        return parts, [[(x, count + part * half) for part in range(2)] for x in parcels]
+    kept, first, second, third, fourth = parcels
+    parts = [
+        (kept, 0), (kept, half), (first, 0), (fourth, 0), (third, 0), (second, 0), (third, half), (fourth, half)
+    ]
+    tops = [
+        [(kept, 2 * half), (kept, 3 * half)],
+        [(first, half), (fourth, 2 * half)],
+        [(third, 2 * half), (second, half)],
+        [(third, 2 * half), (fourth, 2 * half)],
+    ]
+    return parts, tops
+
+
 def put_rows(slot_ref, held, rows_ref, target_ref):
     spare = target_ref.shape[0] - SUB
 
@@ -544,13 +631,14 @@
     n_row, mine_ref, counts_ref, wide_ref, mat_ref, panel_ref, panel_new_ref, square_ref, square_new_ref,
     packed_ref, linv_ref, uinv_ref, *refs,
 ):
-    own_ref, top_ref, parcels, refs = refs[0], refs[1], refs[2:n_row + 1], refs[n_row + 1:]
+    n_parcels = 5 if n_row == 4 else n_row
+    parcels, refs = refs[:n_parcels], refs[n_parcels:]
     out_ref, block, pivot, panel, old, high, low, top, sem, in_sem, out_sem = refs
     rows, _, cols = mat_ref.shape
     width = linv_ref.shape[0]
-    count = own_ref.shape[0]
-    parts = [own_ref] + [x.at[pl.ds(0, count)] for x in parcels]
-    tops = [top_ref] + [x.at[pl.ds(count, count)] for x in parcels]
+    count = mine_ref.shape[0]
+    half = count // 2
+    parts, tops = unpack_parcels(n_row, count, parcels)
     tiles = cols // width
     row, col = lax.axis_index("prow"), lax.axis_index("pcol")
 
@@ -568,15 +656,20 @@
     for p in range(n_row):
         @pl.when(row == p)
         def _(p=p):
-            pltpu.make_async_copy(tops[p].at[:, 0, :], old, sem.at[1]).start()
+            for part in range(2):
+                ref, base = tops[p][part]
+                dest = old.at[pl.ds(part * half, half), :]
+                pltpu.make_async_copy(ref.at[pl.ds(base, half), :], dest, sem.at[1]).start()
 
     blocks = [
         pltpu.make_async_copy(mat_ref.at[:, 0, tile(t)], block.at[pl.ds(0, rows), tile(t)], in_sem.at[t])
         for t in range(tiles)
     ]
     pieces = [
-        pltpu.make_async_copy(parts[k].at[:, 0, :], pivot.at[pl.ds(k * count, count), :], sem.at[2 + k])
-        for k in range(n_row)
+        pltpu.make_async_copy(
+            ref.at[pl.ds(base, half), :], pivot.at[pl.ds(n * half, half), :], sem.at[2 + n]
+        )
+        for n, (ref, base) in enumerate(parts)
     ]
     if pivot.shape[0] > n_row * count:
         pivot[n_row * count:, :] = jnp.zeros((pivot.shape[0] - n_row * count, cols), jnp.float32)
@@ -593,7 +686,7 @@
     put_rows(mine_ref, counts_ref[row], top, panel)
     lower = split_dot(halves(panel[:rows, :]), halves(uinv_ref[...]))
     high[...], low[...] = halves(lower)
-    pltpu.make_async_copy(tops[0].at[:, 0, :], old, sem.at[1]).wait()
+    pltpu.make_async_copy(mat_ref.at[pl.ds(0, count), 0, :], old, sem.at[1]).wait()
     for copy in blocks:
         copy.wait()
     put_rows(mine_ref, counts_ref[row], old, block)
@@ -627,11 +720,11 @@
 
 def finish(mine, counts, wide, mat, panels, squares, factors, parcels):
     rows, _, cols = mat.shape
-    width, n_row, count = factors[0].shape[0], len(parcels) - 1, mine.shape[0]
+    width, n_row, count = factors[0].shape[0], counts.shape[0], mine.shape[0]
     return pl.pallas_call(
         functools.partial(finish_kernel, n_row),
         out_shape=jax.ShapeDtypeStruct(mat.shape, jnp.float32),
-        in_specs=[smem(), smem(), vmem(), raw(), raw(), raw()] + [vmem()] * 5 + [raw()] * (n_row + 1),
+        in_specs=[smem(), smem(), vmem(), raw(), raw(), raw()] + [vmem()] * 5 + [raw()] * len(parcels),
         out_specs=raw(),
         scratch_shapes=[
             pltpu.VMEM((rows + SUB, cols), jnp.float32),
@@ -641,7 +734,7 @@
             pltpu.VMEM((rows, width), jnp.bfloat16),
             pltpu.VMEM((rows, width), jnp.bfloat16),
             pltpu.VMEM((count, width), jnp.float32),
-            pltpu.SemaphoreType.DMA((2 + n_row,)),
+            pltpu.SemaphoreType.DMA((2 + 2 * n_row,)),
             pltpu.SemaphoreType.DMA((cols // width,)),
             pltpu.SemaphoreType.DMA((cols // width,)),
         ],
@@ -654,7 +747,7 @@
 
 def capacity(n_row, width):
     mean = width / n_row
-    return -(-int(mean + 3.4 * (mean * (1 - 1 / n_row)) ** 0.5) // SUB) * SUB
+    return -(-int(mean + 4 * (mean * (1 - 1 / n_row)) ** 0.5) // (2 * SUB)) * (2 * SUB)
 
 
 def locate(pivots, n_row, row, count):
@@ -664,13 +757,11 @@
     number = jnp.arange(width, dtype=jnp.int32)
     ahead = (owner[:, None] == owner[None, :]) & (number[None, :] < number[:, None])
     rank = jnp.sum(ahead, axis=1, dtype=jnp.int32)
-    every = jnp.arange(n_row, dtype=jnp.int32)[:, None, None]
-    ordinal = jnp.arange(count, dtype=jnp.int32)[None, :, None]
-    hits = (owner[None, None, :] == every) & (rank[None, None, :] == ordinal)
-    lists = jnp.sum(jnp.where(hits, number[None, None, :], 0), axis=2, dtype=jnp.int32)
-    own = (owner[None, :] == row) & (rank[None, :] == ordinal[0])
+    every = jnp.arange(n_row, dtype=jnp.int32)[:, None]
+    ordinal = jnp.arange(count, dtype=jnp.int32)[:, None]
+    own = (owner[None, :] == row) & (rank[None, :] == ordinal)
     mine = jnp.sum(jnp.where(own, slot[None, :], 0), axis=1, dtype=jnp.int32)
-    return mine, lists, jnp.sum(owner[None, :] == every[:, 0], axis=1, dtype=jnp.int32)
+    return mine, jnp.sum(owner[None, :] == every, axis=1, dtype=jnp.int32)
 
 
 def capped_step(n_row, n_col, matrix, pivots, begun):
@@ -686,20 +777,26 @@
         return lax.ppermute(x, both, [(i * n_col, (i ^ k) * n_col) for i in range(n_row)])
 
     moved = [exchange(messages[k], k) for k in range(1, n_row)]
-    mine, lists, counts = locate(pivots, n_row, row, count)
-    parcels = parcel(mat, mine, lists)
-    sent = []
-    for k in range(1, n_row):
-        item = parcels[1 + k]
-        if k == 3:
-            item, *sent = lax.optimization_barrier((item, *sent))
-        sent.append(lax.ppermute(item, "prow", [(i, i ^ k) for i in range(n_row)]))
+    mine, counts = locate(pivots, n_row, row, count)
+    parcels = parcel(mat, mine, pivots, n_row)
+
+    def send(x, k):
+        return lax.ppermute(x, "prow", [(i, i ^ k) for i in range(n_row)])
+
+    panel_moved = lax.ppermute(panel, "pcol", [(i, i + turns[0]) for i in range(0, n_col, 2 * turns[0])])
+    *moved, panel_moved = lax.optimization_barrier((*moved, panel_moved))
     message = pack(wide, messages[:1] + moved)
+    if n_row == 4:
+        first, second = send(parcels[0], 1), send(parcels[1], 2)
+        message, first, second = lax.optimization_barrier((message, first, second))
+        kept = parcels[2]
+        to_y, to_x = relay(kept, first, second)
+        arrived = [kept, first, second, send(to_y, 2), send(to_x, 1)]
+    else:
+        arrived = [parcels[0]] + [send(parcels[k], k) for k in range(1, n_row)]
 
     pairs = [[(i, i + bit) for i in range(0, n_col, 2 * bit)] for bit in turns + [1]]
     newer = [(col & bit) != 0 for bit in turns]
-    panel_moved = lax.ppermute(panel, "pcol", pairs[0])
-    message, panel_moved = lax.optimization_barrier((message, panel_moved))
     for n in range(len(turns)):
         panel = jnp.where(newer[n], panel_moved, panel)
         panel_moved = lax.ppermute(panel, "pcol", pairs[n + 1])
@@ -709,7 +806,7 @@
     message_new = lax.ppermute(message, "pcol", pairs[-1])
     factors = factor(message, message_new)
     out = finish(
-        mine, counts, wide, mat, (panel, panel_moved), (message, message_new), factors, list(parcels[:2]) + sent
+        mine, counts, wide, mat, (panel, panel_moved), (message, message_new), factors, arrived
     )
     return out.reshape(matrix.shape)
 

time: 99.2 us -> 94.3 us (0.951)
  waiting for transfers between devices: 25.3 us -> 11.1 us
  starting transfers between devices: 23.9 us -> 29.1 us
  local copies, waits for them, and re-layouts: 1.49 us -> 3.73 us
  Pallas kernels: 42 us -> 43.9 us
    ppermute x4 -> x5, waiting for transfers between devices: 19.8 us -> 5.99 us  [the longest x4 5.99 us: send(): return lax.ppermute(x, 'prow', [(i, i ^ k) for i in range(n_row)])]
    ppermute x4 -> x5, starting transfers between devices: 3.63 us -> 11.1 us  [the longest x1 6.93 us: capped_step(): lax.ppermute(panel, 'pcol', [(i, i + turns[0]) for i in range(0, n_col, 2...]
    cond x16 -> x18, local copies, waits for them, and re-layouts: 1.49 us -> 3.72 us
    pallas_call x1 -> x2, Pallas kernels: 8.75 us -> 10.5 us  [the longest x1 7.87 us: parcel(): pl.pallas_call(functools.partial(parcel_kernel, n_row), out_shape=tuple((...]
  transfers between devices with their start and end apart: 12 -> 13, of which waited for: 4 -> 4; matrix products, arithmetic and copies ran while one was open for 4% -> 4% of each run, Pallas kernels for 26% -> 29%
where the time goes in v6:
time: 94.3 us; the launch traced here: 93.2 us
  Pallas kernels  43.9 us (47%)
  starting transfers between devices  29.1 us (31%)
  waiting for transfers between devices  11.1 us (12%)
  other arithmetic  4.04 us (4%)
  local copies, waits for them, and re-layouts  3.73 us (4%)
    pallas_call x1, Pallas kernels, factor(): pl.pallas_call(functools.partial(factor_kernel, width), out_shape=(out, o...  14.6 us
    pallas_call x1, Pallas kernels, finish(): pl.pallas_call(functools.partial(finish_kernel, n_row), out_shape=jax.Sha...  12.3 us
    ppermute x3, starting transfers between devices, exchange(): lax.ppermute(x, both, [(i * n_col, (i ^ k) * n_col) for i in range(n_row)])  9.2 us
    pallas_call x1, Pallas kernels, parcel(): pl.pallas_call(functools.partial(parcel_kernel, n_row), out_shape=tuple((...  7.87 us
    ppermute x1, starting transfers between devices, capped_step(): lax.ppermute(panel, 'pcol', [(i, i + turns[0]) for i in range(0, n_col, 2...  6.93 us
    ppermute x4, waiting for transfers between devices, send(): return lax.ppermute(x, 'prow', [(i, i ^ k) for i in range(n_row)])  5.99 us
    ppermute x2, waiting for transfers between devices, capped_step(): lax.ppermute(message, 'pcol', pairs[n])  4.51 us
    pallas_call x1, Pallas kernels, begin(): pl.pallas_call(functools.partial(begin_kernel, n_row), out_shape=(jax.Sha...  4.2 us
  transfers between devices with their start and end apart: 13, of which 4 were waited for; matrix products, arithmetic and copies ran while one was open for 4% of the time, Pallas kernels for 29%

profile of v6, /device:TPU:0, one launch (start us, length us, event | category | flops | bytes accessed | tf_op | source)
XLA Modules:
  0.0 93.2 jit_solution(1319637666851991397)
XLA Ops:
  0.0 4.2 %begin.1 = (f32[1024,256]{1,0:T(8,128)}, s32[256,128]{1,0:T(8,128)S(1)}, s32[1]{0:T(128)}, f32[192,256]{1,0:T(8,128)S(1)}, f32[192,256]{1,0:T(8,128)}, /*index=5*/f32[192,256]{1,0:T(8,128)}, f32[192,256]{1,0:T(8,128)}) custom-call(s32[1,256]{1,0:T(1,128)} %bitcast.29, f32[1024,1,1536]{2,1,0:T(1,128)} %bitcast.25), custom_call_target="tpu_custom_call" | custom-call | bytes 10000000 | tf_op jit(solution)/shard_map/begin/pallas_call | solution.py:408
  4.9 88.2 %conditional.1 = (f32[1,1024,1,1536]{3,2,1,0:T(1,128)}) conditional(s32[]{:T(128)} %bitcast.12, (s32[256]{0:T(256)S(1)}, f32[1,1024,1,1536]{3,2,1,0:T(1,128)}) %tuple.33, (s32[256]{0:T(256)S(1)}, f32[1,1024,1,1536]{3,2,1,0:T(1,128)}, f32[192,256]{1,0:T(8,128)}, f32[192,256]{1,0:T(8,128)}, f32[192,256]{1,0:T(8,128)}, /*index=5*/f32[1024,256]{1,0:T(8,128)}, ...), branch_computations={%region_0.1_spmd, %region_1.5_spmd} | conditional | flops 2488416000 | bytes 211226368 | solution.py:817
  5.1 6.9 %collective-permute-start.3 = (f32[1024,256]{1,0:T(8,128)}, f32[1024,256]{1,0:T(8,128)}, u32[]{:S(2)}, u32[]{:S(2)}) collective-permute-start(f32[1024,256]{1,0:T(8,128)} %get-tuple-element.40), channel_id=1, source_target_pairs={{0,4},{8,12},{16,20},{24,28}} | collective-permute-start | bytes 3145736 | tf_op jit(solution)/shard_map/cond/branch_1_fun/ppermute | solution.py:786
  12.0 3.0 %collective-permute-start = (f32[192,256]{1,0:T(8,128)}, f32[192,256]{1,0:T(8,128)S(1)}, u32[]{:S(2)}, u32[]{:S(2)}) collective-permute-start(f32[192,256]{1,0:T(8,128)} %get-tuple-element.37), channel_id=1, source_target_pairs={{0,8},{8,0},{16,24},{24,16}} | collective-permute-start | bytes 589832 | tf_op jit(solution)/shard_map/cond/branch_1_fun/ppermute | solution.py:777
  15.0 3.4 %collective-permute-start.1 = (f32[192,256]{1,0:T(8,128)}, f32[192,256]{1,0:T(8,128)S(1)}, u32[]{:S(2)}, u32[]{:S(2)}) collective-permute-start(f32[192,256]{1,0:T(8,128)} %get-tuple-element.38), channel_id=1, source_target_pairs={{0,16},{8,24},{16,0},{24,8}} | collective-permute-start | bytes 589832 | tf_op jit(solution)/shard_map/cond/branch_1_fun/ppermute | solution.py:777
  18.5 2.8 %collective-permute-start.2 = (f32[192,256]{1,0:T(8,128)}, f32[192,256]{1,0:T(8,128)S(1)}, u32[]{:S(2)}, u32[]{:S(2)}) collective-permute-start(f32[192,256]{1,0:T(8,128)} %get-tuple-element.39), channel_id=1, source_target_pairs={{0,24},{8,16},{16,8},{24,0}} | collective-permute-start | bytes 589832 | tf_op jit(solution)/shard_map/cond/branch_1_fun/ppermute | solution.py:777
  22.1 7.9 %parcel.1 = (f32[144,1536]{1,0:T(8,128)}, f32[144,1536]{1,0:T(8,128)}, f32[288,1536]{1,0:T(8,128)}) custom-call(s32[96]{0:T(128)} %select_reduce_fusion.mine_ref, s32[1,256]{1,0:T(1,128)S(1)} %bitcast.30, f32[1024,1,1536]{2,1,0:T(1,128)} %bitcast.26), custom_call_target="tpu_custom_call" | custom-call | bytes 16000000 | tf_op jit(solution)/shard_map/cond/branch_1_fun/parcel/pallas_call | solution.py:498
  32.1 1.4 %broadcast_select_fusion.3 = f32[1024,256]{1,0:T(8,128)S(1)} fusion(f32[1024,256]{1,0:T(8,128)} %collective-permute-done.3, f32[1024,256]{1,0:T(8,128)} %get-tuple-element.40, pred[]{:T(512)S(6)} %ne.60), kind=kLoop, calls=%fused_computation.31 | loop fusion | flops 262144 | bytes 3145729 | tf_op jit(solution)/shard_map/cond/branch_1_fun/jit(_where)/select_n | solution.py:801
  33.5 2.3 %collective-permute-start.7 = (f32[1024,256]{1,0:T(8,128)S(1)}, f32[1024,256]{1,0:T(8,128)}, u32[]{:S(2)}, u32[]{:S(2)}) collective-permute-start(f32[1024,256]{1,0:T(8,128)S(1)} %broadcast_select_fusion.3), channel_id=1, source_target_pairs={{0,2},{4,6},{8,10},{12,14},{16,18},{20,22},{24,26},{28,30}} | collective-permute-start | bytes 3145736 | tf_op jit(solution)/shard_map/cond/branch_1_fun/ppermute | solution.py:802
  35.7 2.3 %pack.1 = f32[352,256]{1,0:T(8,128)} custom-call(s32[256,128]{1,0:T(8,128)S(1)} %get-tuple-element.34.wide_ref, f32[192,256]{1,0:T(8,128)S(1)} %get-tuple-element.36.refs_0_, f32[192,256]{1,0:T(8,128)} %copy-done.9, f32[192,256]{1,0:T(8,128)} %copy-done.10, f32[192,256]{1,0:T(8,128)} %copy-done.11), custom_call_target="tpu_custom_call" | custom-call | bytes 4000000 | tf_op jit(solution)/shard_map/cond/branch_1_fun/pack/pallas_call | solution.py:589
  38.0 5.3 %collective-permute-done.4.first_ref.refs_1_ = f32[144,1536]{1,0:T(8,128)S(1)} collective-permute-done((f32[144,1536]{1,0:T(8,128)}, f32[144,1536]{1,0:T(8,128)S(1)}, u32[]{:S(2)}, u32[]{:S(2)}) %collective-permute-start.4) | collective-permute-done | bytes 884768 | tf_op jit(solution)/shard_map/cond/branch_1_fun/ppermute | solution.py:784
  44.0 2.5 %collective-permute-start.6 = (f32[352,256]{1,0:T(8,128)}, f32[352,256]{1,0:T(8,128)}, u32[]{:S(2)}, u32[]{:S(2)}) collective-permute-start(f32[352,256]{1,0:T(8,128)} %pack.1), channel_id=1, source_target_pairs={{0,4},{8,12},{16,20},{24,28}} | collective-permute-start | bytes 1081352 | tf_op jit(solution)/shard_map/cond/branch_1_fun/ppermute | solution.py:803
  46.5 4.5 %collective-permute-done.6 = f32[352,256]{1,0:T(8,128)} collective-permute-done((f32[352,256]{1,0:T(8,128)}, f32[352,256]{1,0:T(8,128)}, u32[]{:S(2)}, u32[]{:S(2)}) %collective-permute-start.6) | collective-permute-done | bytes 360480 | tf_op jit(solution)/shard_map/cond/branch_1_fun/ppermute | solution.py:803
  51.0 1.0 %broadcast_select_fusion.6 = f32[352,256]{1,0:T(8,128)S(1)} fusion(f32[352,256]{1,0:T(8,128)} %collective-permute-done.6, f32[352,256]{1,0:T(8,128)} %pack.1, pred[]{:T(512)S(6)} %ne.60), kind=kLoop, calls=%fused_computation.37 | loop fusion | flops 90112 | bytes 1081345 | tf_op jit(solution)/shard_map/cond/branch_1_fun/jit(_where)/select_n | solution.py:803
  52.3 1.4 %collective-permute-start.8 = (f32[1024,256]{1,0:T(8,128)S(1)}, f32[1024,256]{1,0:T(8,128)S(1)}, u32[]{:S(2)}, u32[]{:S(2)}) collective-permute-start(f32[1024,256]{1,0:T(8,128)S(1)} %broadcast_select_fusion.4.panel_ref), channel_id=1, source_target_pairs={{0,1},{2,3},{4,5},{6,7},{8,9},{10,11},{12,13},{14,15},{16,17},{18,... | collective-permute-start | bytes 3145736 | tf_op jit(solution)/shard_map/cond/branch_1_fun/ppermute | solution.py:802
  53.6 1.3 %collective-permute-start.9 = (f32[352,256]{1,0:T(8,128)S(1)}, f32[352,256]{1,0:T(8,128)S(1)}, u32[]{:S(2)}, u32[]{:S(2)}) collective-permute-start(f32[352,256]{1,0:T(8,128)S(1)} %broadcast_select_fusion.6), channel_id=1, source_target_pairs={{0,2},{4,6},{8,10},{12,14},{16,18},{20,22},{24,26},{28,30}} | collective-permute-start | bytes 1081352 | tf_op jit(solution)/shard_map/cond/branch_1_fun/ppermute | solution.py:803
  55.0 2.7 %relay.1 = (f32[144,1536]{1,0:T(8,128)}, f32[144,1536]{1,0:T(8,128)}) custom-call(f32[288,1536]{1,0:T(8,128)} %get-tuple-element.53.kept_ref.refs_0_, f32[144,1536]{1,0:T(8,128)} %copy-done.3, f32[144,1536]{1,0:T(8,128)} %copy-done.4), custom_call_target="tpu_custom_call" | custom-call | bytes 4000000 | tf_op jit(solution)/shard_map/cond/branch_1_fun/relay/pallas_call | solution.py:547
  57.6 2.1 %collective-permute-start.11 = (f32[144,1536]{1,0:T(8,128)}, f32[144,1536]{1,0:T(8,128)}, u32[]{:S(2)}, u32[]{:S(2)}) collective-permute-start(f32[144,1536]{1,0:T(8,128)} %get-tuple-element.56), channel_id=1, source_target_pairs={{0,16},{8,24},{16,0},{24,8},{1,17},{9,25},{17,1},{25,9},{2,18},{10... | collective-permute-start | bytes 2654216 | tf_op jit(solution)/shard_map/cond/branch_1_fun/ppermute | solution.py:784
  59.7 2.0 %collective-permute-start.12 = (f32[144,1536]{1,0:T(8,128)}, f32[144,1536]{1,0:T(8,128)}, u32[]{:S(2)}, u32[]{:S(2)}) collective-permute-start(f32[144,1536]{1,0:T(8,128)} %get-tuple-element.57), channel_id=1, source_target_pairs={{0,8},{8,0},{16,24},{24,16},{1,9},{9,1},{17,25},{25,17},{2,10},{10... | collective-permute-start | bytes 2654216 | tf_op jit(solution)/shard_map/cond/branch_1_fun/ppermute | solution.py:784
  61.8 1.3 %collective-permute-start.10 = (f32[352,256]{1,0:T(8,128)S(1)}, f32[352,256]{1,0:T(8,128)S(1)}, u32[]{:S(2)}, u32[]{:S(2)}) collective-permute-start(f32[352,256]{1,0:T(8,128)S(1)} %broadcast_select_fusion.5.s_ref.square_ref), channel_id=1, source_target_pairs={{0,1},{2,3},{4,5},{6,7},{8,9},{10,11},{12,13},{14,15},{16,17},{18,... | collective-permute-start | bytes 1081352 | tf_op jit(solution)/shard_map/cond/branch_1_fun/ppermute | solution.py:806
  64.4 0.7 copy-done.6
  65.1 14.6 %factor.3 = (f32[256,256]{1,0:T(8,128)}, f32[256,256]{1,0:T(8,128)}, f32[256,256]{1,0:T(8,128)}) custom-call(f32[352,256]{1,0:T(8,128)} %copy-done.5, f32[352,256]{1,0:T(8,128)} %copy-done.6), custom_call_target="tpu_custom_call" | custom-call | flops 67108864 | bytes 50000000 | tf_op jit(solution)/shard_map/cond/branch_1_fun/factor/pallas_call | solution.py:145
  79.8 1.0 %copy-done.8 = f32[1024,256]{1,0:T(8,128)} copy-done((f32[1024,256]{1,0:T(8,128)}, f32[1024,256]{1,0:T(8,128)S(1)}, u32[]{:S(2)}) %copy-start.8) | copy-done | bytes 1048600 | tf_op jit(solution)/shard_map/cond
  80.7 12.3 %finish.1 = f32[1024,1,1536]{2,1,0:T(1,128)} custom-call(s32[96]{0:T(128)} %select_reduce_fusion.mine_ref, s32[4]{0:T(128)} %convert_reduce_fusion.1.counts_ref, s32[256,128]{1,0:T(8,128)S(1)} %get-tuple-element.34.wide_ref, f32[1024,1,1536]{2,1,0:T(1,128)} %bitcast.27, f32[1024,256]{1,0:T(8,128)} %copy-done.2, f32[1024,256]{1,0:T(8,128)} %copy-done.8, ...), custom_call_target="tpu_custom_call" | custom-call | flops 2415919104 | bytes 12582912 | tf_op jit(solution)/shard_map/cond/branch_1_fun/finish/pallas_call | solution.py:724
  (38 shorter events, 5.1 us)
Async XLA Ops:
  0.0 4.9 %copy-start.12 = (s32[256]{0:T(256)S(1)}, s32[256]{0:T(256)}, u32[]{:S(2)}) copy-start(s32[256]{0:T(256)} %param.5) | copy-start | bytes 3076
  5.1 27.0 %collective-permute-start.3 = (f32[1024,256]{1,0:T(8,128)}, f32[1024,256]{1,0:T(8,128)}, u32[]{:S(2)}, u32[]{:S(2)}) collective-permute-start(f32[1024,256]{1,0:T(8,128)} %get-tuple-element.40), channel_id=1, source_target_pairs={{0,4},{8,12},{16,20},{24,28}} | collective-permute-start | bytes 3145736 | tf_op jit(solution)/shard_map/cond/branch_1_fun/ppermute | solution.py:786
  12.0 18.0 %collective-permute-start = (f32[192,256]{1,0:T(8,128)}, f32[192,256]{1,0:T(8,128)S(1)}, u32[]{:S(2)}, u32[]{:S(2)}) collective-permute-start(f32[192,256]{1,0:T(8,128)} %get-tuple-element.37), channel_id=1, source_target_pairs={{0,8},{8,0},{16,24},{24,16}} | collective-permute-start | bytes 589832 | tf_op jit(solution)/shard_map/cond/branch_1_fun/ppermute | solution.py:777
  15.0 15.7 %collective-permute-start.1 = (f32[192,256]{1,0:T(8,128)}, f32[192,256]{1,0:T(8,128)S(1)}, u32[]{:S(2)}, u32[]{:S(2)}) collective-permute-start(f32[192,256]{1,0:T(8,128)} %get-tuple-element.38), channel_id=1, source_target_pairs={{0,16},{8,24},{16,0},{24,8}} | collective-permute-start | bytes 589832 | tf_op jit(solution)/shard_map/cond/branch_1_fun/ppermute | solution.py:777
  18.5 12.3 %collective-permute-start.2 = (f32[192,256]{1,0:T(8,128)}, f32[192,256]{1,0:T(8,128)S(1)}, u32[]{:S(2)}, u32[]{:S(2)}) collective-permute-start(f32[192,256]{1,0:T(8,128)} %get-tuple-element.39), channel_id=1, source_target_pairs={{0,24},{8,16},{16,8},{24,0}} | collective-permute-start | bytes 589832 | tf_op jit(solution)/shard_map/cond/branch_1_fun/ppermute | solution.py:777
  30.0 13.3 %collective-permute-start.4 = (f32[144,1536]{1,0:T(8,128)}, f32[144,1536]{1,0:T(8,128)S(1)}, u32[]{:S(2)}, u32[]{:S(2)}) collective-permute-start(f32[144,1536]{1,0:T(8,128)} %get-tuple-element.44), channel_id=1, source_target_pairs={{0,8},{8,0},{16,24},{24,16},{1,9},{9,1},{17,25},{25,17},{2,10},{10... | collective-permute-start | bytes 2654216 | tf_op jit(solution)/shard_map/cond/branch_1_fun/ppermute | solution.py:784
  30.1 0.7 copy-start.9
  30.7 13.3 %collective-permute-start.5 = (f32[144,1536]{1,0:T(8,128)}, f32[144,1536]{1,0:T(8,128)S(1)}, u32[]{:S(2)}, u32[]{:S(2)}) collective-permute-start(f32[144,1536]{1,0:T(8,128)} %get-tuple-element.45), channel_id=1, source_target_pairs={{0,16},{8,24},{16,0},{24,8},{1,17},{9,25},{17,1},{25,9},{2,18},{10... | collective-permute-start | bytes 2654216 | tf_op jit(solution)/shard_map/cond/branch_1_fun/ppermute | solution.py:784
  30.7 0.7 copy-start.10
  31.4 0.7 copy-start.11
  33.5 18.6 %collective-permute-start.7 = (f32[1024,256]{1,0:T(8,128)S(1)}, f32[1024,256]{1,0:T(8,128)}, u32[]{:S(2)}, u32[]{:S(2)}) collective-permute-start(f32[1024,256]{1,0:T(8,128)S(1)} %broadcast_select_fusion.3), channel_id=1, source_target_pairs={{0,2},{4,6},{8,10},{12,14},{16,18},{20,22},{24,26},{28,30}} | collective-permute-start | bytes 3145736 | tf_op jit(solution)/shard_map/cond/branch_1_fun/ppermute | solution.py:802
  43.3 9.0 %copy-start.3 = (f32[144,1536]{1,0:T(8,128)}, f32[144,1536]{1,0:T(8,128)S(1)}, u32[]{:S(2)}) copy-start(f32[144,1536]{1,0:T(8,128)S(1)} %collective-permute-done.4.first_ref.refs_1_) | copy-start | bytes 2654212 | tf_op jit(solution)/shard_map/cond
  44.0 8.1 %copy-start.4 = (f32[144,1536]{1,0:T(8,128)}, f32[144,1536]{1,0:T(8,128)S(1)}, u32[]{:S(2)}) copy-start(f32[144,1536]{1,0:T(8,128)S(1)} %collective-permute-done.5.second_ref.refs_2_) | copy-start | bytes 2654212 | tf_op jit(solution)/shard_map/cond
  44.0 7.1 %collective-permute-start.6 = (f32[352,256]{1,0:T(8,128)}, f32[352,256]{1,0:T(8,128)}, u32[]{:S(2)}, u32[]{:S(2)}) collective-permute-start(f32[352,256]{1,0:T(8,128)} %pack.1), channel_id=1, source_target_pairs={{0,4},{8,12},{16,20},{24,28}} | collective-permute-start | bytes 1081352 | tf_op jit(solution)/shard_map/cond/branch_1_fun/ppermute | solution.py:803
  52.3 5.4 %copy-start.2 = (f32[1024,256]{1,0:T(8,128)}, f32[1024,256]{1,0:T(8,128)S(1)}, u32[]{:S(2)}) copy-start(f32[1024,256]{1,0:T(8,128)S(1)} %broadcast_select_fusion.4.panel_ref) | copy-start | bytes 3145732 | tf_op jit(solution)/shard_map/cond
  52.3 27.5 %collective-permute-start.8 = (f32[1024,256]{1,0:T(8,128)S(1)}, f32[1024,256]{1,0:T(8,128)S(1)}, u32[]{:S(2)}, u32[]{:S(2)}) collective-permute-start(f32[1024,256]{1,0:T(8,128)S(1)} %broadcast_select_fusion.4.panel_ref), channel_id=1, source_target_pairs={{0,1},{2,3},{4,5},{6,7},{8,9},{10,11},{12,13},{14,15},{16,17},{18,... | collective-permute-start | bytes 3145736 | tf_op jit(solution)/shard_map/cond/branch_1_fun/ppermute | solution.py:802
  53.6 8.1 %collective-permute-start.9 = (f32[352,256]{1,0:T(8,128)S(1)}, f32[352,256]{1,0:T(8,128)S(1)}, u32[]{:S(2)}, u32[]{:S(2)}) collective-permute-start(f32[352,256]{1,0:T(8,128)S(1)} %broadcast_select_fusion.6), channel_id=1, source_target_pairs={{0,2},{4,6},{8,10},{12,14},{16,18},{20,22},{24,26},{28,30}} | collective-permute-start | bytes 1081352 | tf_op jit(solution)/shard_map/cond/branch_1_fun/ppermute | solution.py:803
  57.6 22.1 %collective-permute-start.11 = (f32[144,1536]{1,0:T(8,128)}, f32[144,1536]{1,0:T(8,128)}, u32[]{:S(2)}, u32[]{:S(2)}) collective-permute-start(f32[144,1536]{1,0:T(8,128)} %get-tuple-element.56), channel_id=1, source_target_pairs={{0,16},{8,24},{16,0},{24,8},{1,17},{9,25},{17,1},{25,9},{2,18},{10... | collective-permute-start | bytes 2654216 | tf_op jit(solution)/shard_map/cond/branch_1_fun/ppermute | solution.py:784
  59.7 20.0 %collective-permute-start.12 = (f32[144,1536]{1,0:T(8,128)}, f32[144,1536]{1,0:T(8,128)}, u32[]{:S(2)}, u32[]{:S(2)}) collective-permute-start(f32[144,1536]{1,0:T(8,128)} %get-tuple-element.57), channel_id=1, source_target_pairs={{0,8},{8,0},{16,24},{24,16},{1,9},{9,1},{17,25},{25,17},{2,10},{10... | collective-permute-start | bytes 2654216 | tf_op jit(solution)/shard_map/cond/branch_1_fun/ppermute | solution.py:784
  61.8 2.6 %copy-start.5 = (f32[352,256]{1,0:T(8,128)}, f32[352,256]{1,0:T(8,128)S(1)}, u32[]{:S(2)}) copy-start(f32[352,256]{1,0:T(8,128)S(1)} %broadcast_select_fusion.5.s_ref.square_ref) | copy-start | bytes 1081348 | tf_op jit(solution)/shard_map/cond
  61.8 2.6 %collective-permute-start.10 = (f32[352,256]{1,0:T(8,128)S(1)}, f32[352,256]{1,0:T(8,128)S(1)}, u32[]{:S(2)}, u32[]{:S(2)}) collective-permute-start(f32[352,256]{1,0:T(8,128)S(1)} %broadcast_select_fusion.5.s_ref.square_ref), channel_id=1, source_target_pairs={{0,1},{2,3},{4,5},{6,7},{8,9},{10,11},{12,13},{14,15},{16,17},{18,... | collective-permute-start | bytes 1081352 | tf_op jit(solution)/shard_map/cond/branch_1_fun/ppermute | solution.py:806
  64.4 0.8 copy-start.6
  79.8 1.0 %copy-start.8 = (f32[1024,256]{1,0:T(8,128)}, f32[1024,256]{1,0:T(8,128)S(1)}, u32[]{:S(2)}) copy-start(f32[1024,256]{1,0:T(8,128)S(1)} %collective-permute-done.8.panel_new_ref) | copy-start | bytes 3145732 | tf_op jit(solution)/shard_map/cond

commit v7 on v6

--- a/solution.py
+++ b/solution.py
@@ -20,22 +20,32 @@
     return jnp.broadcast_to(tile[j:j + 1, :], (SUB, LANES))
 
 
-def factor_kernel(width, s_ref, extra_ref, packed_ref, linv_ref, uinv_ref, a_ref, m_ref, v_ref):
+def factor_kernel(width, first_ref, second_ref, packed_ref, linv_ref, uinv_ref, a_ref, m_ref, v_ref, s_ref, sem):
     groups = a_ref.shape[0]
     tiles = groups * SUB // LANES
     per_tile = LANES // SUB
     per_block = width // SUB
+    copies = [
+        pltpu.make_async_copy(ref.at[pl.ds(0, groups * SUB), :], s_ref.at[n], sem.at[n])
+        for n, ref in enumerate((first_ref, second_ref))
+    ]
+    for copy in copies:
+        copy.start()
     sub = lax.broadcasted_iota(jnp.int32, (SUB, LANES), 0)
     lane = lax.broadcasted_iota(jnp.int32, (SUB, LANES), 1)
 
     for i in range(groups):
-        a_ref[i] = s_ref[i * SUB:(i + 1) * SUB, :] + extra_ref[i * SUB:(i + 1) * SUB, :]
         diag = lane - (i % per_tile) * SUB == sub
         for t in range(tiles):
             block = jnp.where(diag, 1.0, 0.0) if i // per_tile == t else jnp.zeros((SUB, LANES), jnp.float32)
             m_ref[i, :, t * LANES:(t + 1) * LANES] = block
             if t > i // per_tile:
                 linv_ref[i * SUB:(i + 1) * SUB, t * LANES:(t + 1) * LANES] = block
+
+    for copy in copies:
+        copy.wait()
+    for i in range(groups):
+        a_ref[i] = s_ref[0, i * SUB:(i + 1) * SUB, :] + s_ref[1, i * SUB:(i + 1) * SUB, :]
 
     def span(t):
         return slice(t * LANES, (t + 1) * LANES)
@@ -145,14 +155,17 @@
     return pl.pallas_call(
         functools.partial(factor_kernel, width),
         out_shape=(out, out, out),
-        in_specs=[vmem(), vmem()],
+        in_specs=[raw(), raw()],
         out_specs=(vmem(),) * 3,
         scratch_shapes=[
             pltpu.VMEM((size // SUB, SUB, size), jnp.float32),
             pltpu.VMEM((size // SUB, SUB, size), jnp.float32),
             pltpu.VMEM((1 + size // LANES, SUB, LANES), jnp.float32),
+            pltpu.VMEM((2, size, size), jnp.float32),
+            pltpu.SemaphoreType.DMA((2,)),
         ],
         cost_estimate=pl.CostEstimate(flops=4 * size**3, bytes_accessed=50_000_000, transcendentals=0),
+        compiler_params=pltpu.CompilerParams(vmem_limit_bytes=6 << 20),
         name="factor",
     )(square, extra)
 
@@ -222,6 +235,20 @@
     high = x.astype(jnp.bfloat16)
     low = (x - high.astype(jnp.float32)).astype(jnp.bfloat16)
     return high, low
+
+
+def wide_left(x):
+    high, low = halves(x)
+    return jnp.concatenate([high, low, high], axis=1)
+
+
+def wide_right(x):
+    high, low = halves(x)
+    return jnp.concatenate([low, high, high], axis=0)
+
+
+def wide_dot(left, right):
+    return jnp.dot(left, right, preferred_element_type=jnp.float32)
 
 
 def split_dot(left, right):
@@ -364,6 +391,12 @@
 def select_dot(choice, parts):
     choice = choice.astype(jnp.bfloat16)
     high, middle, low = [jnp.dot(choice, x, preferred_element_type=jnp.float32) for x in parts]
+    return high + (middle + low)
+
+
+def pick_dot(parts, choice):
+    choice = choice.astype(jnp.bfloat16)
+    high, middle, low = [jnp.dot(x, choice, preferred_element_type=jnp.float32) for x in parts]
     return high + (middle + low)
 
 
@@ -416,6 +449,7 @@
         out_specs=(vmem(), vmem(), smem()) + (vmem(),) * n_row,
         scratch_shapes=[pltpu.SemaphoreType.DMA],
         cost_estimate=pl.CostEstimate(flops=0, bytes_accessed=10_000_000, transcendentals=0),
+        compiler_params=pltpu.CompilerParams(vmem_limit_bytes=12 << 20),
         name="begin",
     )(pivots[None, :], mat)
 
@@ -506,6 +540,7 @@
             pltpu.SemaphoreType.DMA((2,)),
         ],
         cost_estimate=pl.CostEstimate(flops=0, bytes_accessed=16_000_000, transcendentals=0),
+        compiler_params=pltpu.CompilerParams(vmem_limit_bytes=16 << 20),
         name="parcel",
     )(mine, pivots[None, :], mat)
 
@@ -551,32 +586,44 @@
         out_specs=(vmem(), vmem()),
         scratch_shapes=[pltpu.SemaphoreType.DMA((6,))],
         cost_estimate=pl.CostEstimate(flops=0, bytes_accessed=4_000_000, transcendentals=0),
+        compiler_params=pltpu.CompilerParams(vmem_limit_bytes=4 << 20),
         name="relay",
     )(kept, first, second)
 
 
 def pack_kernel(n_row, wide_ref, *refs):
-    parts, out_ref = refs[:n_row], refs[n_row]
+    parts, out_ref, stack, sem = refs[:n_row], refs[n_row], refs[n_row + 1], refs[n_row + 2]
     width = wide_ref.shape[0]
     count = out_ref.shape[0] - width
     row, col = lax.axis_index("prow"), lax.axis_index("pcol")
-    total = -(-n_row * count // LANES) * LANES
+    total = stack.shape[0]
 
     @pl.when(col == 0)
     def _():
-        pieces = [parts[k][:count, :] for k in range(n_row)]
+        copies = [
+            pltpu.make_async_copy(parts[k].at[pl.ds(0, count), :], stack.at[pl.ds(k * count, count), :], sem.at[k])
+            for k in range(n_row)
+        ]
+        for copy in copies:
+            copy.start()
+        for k in range(n_row):
+            @pl.when(row == k)
+            def _(k=k):
+                pltpu.make_async_copy(
+                    parts[k].at[pl.ds(count, count), :], out_ref.at[pl.ds(width, count), :], sem.at[n_row]
+                ).start()
         if total > n_row * count:
-            pieces.append(jnp.zeros((total - n_row * count, width), jnp.float32))
-        stack = jnp.concatenate(pieces, axis=0)
+            stack[n_row * count:, :] = jnp.zeros((total - n_row * count, width), jnp.float32)
         lanes = lax.broadcasted_iota(jnp.int32, (width, LANES), 1)
         choice = jnp.concatenate(
             [jnp.where(lanes + t * LANES == wide_ref[...], 1.0, 0.0) for t in range(total // LANES)], axis=1
         )
-        out_ref[:width, :] = select_dot(choice, thirds(stack))
-        for k in range(n_row):
-            @pl.when(row == k)
-            def _(k=k):
-                out_ref[width:, :] = parts[k][count:, :]
+        for copy in copies:
+            copy.wait()
+        out_ref[:width, :] = select_dot(choice, thirds(stack[...]))
+        pltpu.make_async_copy(
+            parts[0].at[pl.ds(count, count), :], out_ref.at[pl.ds(width, count), :], sem.at[n_row]
+        ).wait()
 
     @pl.when(col != 0)
     def _():
@@ -589,9 +636,14 @@
     return pl.pallas_call(
         functools.partial(pack_kernel, n_row),
         out_shape=jax.ShapeDtypeStruct((width + count, width), jnp.float32),
-        in_specs=[vmem()] * (n_row + 1),
+        in_specs=[vmem()] + [raw()] * n_row,
         out_specs=vmem(),
+        scratch_shapes=[
+            pltpu.VMEM((-(-n_row * count // LANES) * LANES, width), jnp.float32),
+            pltpu.SemaphoreType.DMA((n_row + 1,)),
+        ],
         cost_estimate=pl.CostEstimate(flops=0, bytes_accessed=4_000_000, transcendentals=0),
+        compiler_params=pltpu.CompilerParams(vmem_limit_bytes=6 << 20),
         name="pack",
     )(wide, *parts)
 
@@ -624,7 +676,7 @@
             target_ref[pl.ds(slot, 1), :] = rows_ref[pl.ds(i, 1), :]
         return c
 
-    lax.fori_loop(0, rows_ref.shape[0] // SUB, group, 0)
+    lax.fori_loop(0, (held + SUB - 1) // SUB, group, 0)
 
 
 def finish_kernel(
@@ -633,11 +685,12 @@
 ):
     n_parcels = 5 if n_row == 4 else n_row
     parcels, refs = refs[:n_parcels], refs[n_parcels:]
-    out_ref, block, pivot, panel, old, high, low, top, sem, in_sem, out_sem = refs
+    out_ref, block, pivot, panel, old, left, lower, top, sem, in_sem, out_sem = refs
     rows, _, cols = mat_ref.shape
     width = linv_ref.shape[0]
     count = mine_ref.shape[0]
     half = count // 2
+    stacked = n_row * count
     parts, tops = unpack_parcels(n_row, count, parcels)
     tiles = cols // width
     row, col = lax.axis_index("prow"), lax.axis_index("pcol")
@@ -653,58 +706,60 @@
     def _():
         pltpu.make_async_copy(panel_new_ref, panel.at[pl.ds(0, rows)], sem.at[0]).start()
 
-    for p in range(n_row):
-        @pl.when(row == p)
-        def _(p=p):
-            for part in range(2):
-                ref, base = tops[p][part]
-                dest = old.at[pl.ds(part * half, half), :]
-                pltpu.make_async_copy(ref.at[pl.ds(base, half), :], dest, sem.at[1]).start()
-
-    blocks = [
-        pltpu.make_async_copy(mat_ref.at[:, 0, tile(t)], block.at[pl.ds(0, rows), tile(t)], in_sem.at[t])
-        for t in range(tiles)
+    top_copies = [
+        pltpu.make_async_copy(ref.at[pl.ds(width, count), :], top.at[n], sem.at[1 + n])
+        for n, ref in enumerate((square_ref, square_new_ref))
     ]
-    pieces = [
-        pltpu.make_async_copy(
-            ref.at[pl.ds(base, half), :], pivot.at[pl.ds(n * half, half), :], sem.at[2 + n]
-        )
-        for n, (ref, base) in enumerate(parts)
-    ]
-    if pivot.shape[0] > n_row * count:
-        pivot[n_row * count:, :] = jnp.zeros((pivot.shape[0] - n_row * count, cols), jnp.float32)
-    for copy in blocks[:1] + pieces + blocks[1:]:
+    for copy in top_copies:
         copy.start()
+
+    def fetch(t, c):
+        pltpu.make_async_copy(mat_ref.at[:, 0, tile(t)], block.at[pl.ds(0, rows), tile(t)], in_sem.at[0, t]).start()
+        for n, (ref, base) in enumerate(parts):
+            dest = pivot.at[pl.ds(n * half, half), tile(t)]
+            pltpu.make_async_copy(ref.at[pl.ds(base, half), tile(t)], dest, in_sem.at[1, t]).start()
+        for p in range(n_row):
+            @pl.when(row == p)
+            def _(p=p):
+                for part, (ref, base) in enumerate(tops[p]):
+                    dest = old.at[pl.ds(part * half, half), tile(t)]
+                    pltpu.make_async_copy(ref.at[pl.ds(base, half), tile(t)], dest, in_sem.at[2, t]).start()
+        return c
+
+    lax.fori_loop(0, tiles, fetch, 0)
+    if pivot.shape[0] > stacked:
+        pivot[stacked:, :] = jnp.zeros((pivot.shape[0] - stacked, cols), jnp.float32)
 
     lanes = lax.broadcasted_iota(jnp.int32, (width, LANES), 1)
     places = jnp.concatenate(
         [jnp.where(lanes + t * LANES == wide_ref[...], 1.0, 0.0) for t in range(pivot.shape[0] // LANES)], axis=1
     )
-    spread_inv = halves(jnp.dot(linv_ref[...], places, precision=HI, preferred_element_type=jnp.float32))
-    top[...] = square_ref[width:, :] + square_new_ref[width:, :]
+    spread_inv = wide_left(pick_dot(thirds(linv_ref[...]), places))
+    for copy in top_copies:
+        copy.wait()
+    top[0] = top[0] + top[1]
     pltpu.make_async_copy(panel_ref, panel.at[pl.ds(0, rows)], sem.at[0]).wait()
-    put_rows(mine_ref, counts_ref[row], top, panel)
-    lower = split_dot(halves(panel[:rows, :]), halves(uinv_ref[...]))
-    high[...], low[...] = halves(lower)
-    pltpu.make_async_copy(mat_ref.at[pl.ds(0, count), 0, :], old, sem.at[1]).wait()
-    for copy in blocks:
-        copy.wait()
-    put_rows(mine_ref, counts_ref[row], old, block)
-
-    @pl.when(col == 0)
-    def _():
-        block[:rows, :width] = lower
-
-    for copy in pieces:
-        copy.wait()
+    put_rows(mine_ref, counts_ref[row], top.at[0], panel)
+    lower[...] = wide_dot(wide_left(panel[:rows, :]), wide_right(uinv_ref[...]))
+    left[...] = wide_left(lower[...])
 
     def step(t, c):
-        upper = split_dot(spread_inv, halves(pivot[:, tile(t)]))
         first_col = (col == 0) & (t == 0)
+        pltpu.make_async_copy(
+            mat_ref.at[pl.ds(0, stacked), 0, tile(t)], pivot.at[pl.ds(0, stacked), tile(t)], in_sem.at[1, t]
+        ).wait()
+        upper = wide_dot(spread_inv, wide_right(pivot[:, tile(t)]))
+        pltpu.make_async_copy(mat_ref.at[pl.ds(0, count), 0, tile(t)], old.at[:, tile(t)], in_sem.at[2, t]).wait()
+        pltpu.make_async_copy(mat_ref.at[:, 0, tile(t)], block.at[pl.ds(0, rows), tile(t)], in_sem.at[0, t]).wait()
 
         @pl.when(jnp.logical_not(first_col))
         def _():
-            block[:rows, tile(t)] = block[:rows, tile(t)] - split_dot((high[...], low[...]), halves(upper))
+            put_rows(mine_ref, counts_ref[row], old.at[:, tile(t)], block.at[:, tile(t)])
+            block[:rows, tile(t)] = block[:rows, tile(t)] - wide_dot(left[...], wide_right(upper))
+
+        @pl.when(first_col)
+        def _():
+            block[:rows, tile(t)] = lower[...]
 
         @pl.when(row == 0)
         def _():
@@ -714,8 +769,12 @@
         return c
 
     lax.fori_loop(0, tiles, step, 0)
-    for t in range(tiles):
+
+    def drain(t, c):
         pltpu.make_async_copy(block.at[pl.ds(0, rows), tile(t)], out_ref.at[:, 0, tile(t)], out_sem.at[t]).wait()
+        return c
+
+    lax.fori_loop(0, tiles, drain, 0)
 
 
 def finish(mine, counts, wide, mat, panels, squares, factors, parcels):
@@ -724,23 +783,24 @@
     return pl.pallas_call(
         functools.partial(finish_kernel, n_row),
         out_shape=jax.ShapeDtypeStruct(mat.shape, jnp.float32),
-        in_specs=[smem(), smem(), vmem(), raw(), raw(), raw()] + [vmem()] * 5 + [raw()] * len(parcels),
+        in_specs=[smem(), smem(), vmem()] + [raw()] * 5 + [vmem()] * 3 + [raw()] * len(parcels),
         out_specs=raw(),
         scratch_shapes=[
             pltpu.VMEM((rows + SUB, cols), jnp.float32),
             pltpu.VMEM((-(-n_row * count // LANES) * LANES, cols), jnp.float32),
             pltpu.VMEM((rows + SUB, width), jnp.float32),
             pltpu.VMEM((count, cols), jnp.float32),
-            pltpu.VMEM((rows, width), jnp.bfloat16),
-            pltpu.VMEM((rows, width), jnp.bfloat16),
-            pltpu.VMEM((count, width), jnp.float32),
-            pltpu.SemaphoreType.DMA((2 + 2 * n_row,)),
-            pltpu.SemaphoreType.DMA((cols // width,)),
+            pltpu.VMEM((rows, 3 * width), jnp.bfloat16),
+            pltpu.VMEM((rows, width), jnp.float32),
+            pltpu.VMEM((2, count, width), jnp.float32),
+            pltpu.SemaphoreType.DMA((3,)),
+            pltpu.SemaphoreType.DMA((3, cols // width)),
             pltpu.SemaphoreType.DMA((cols // width,)),
         ],
         cost_estimate=pl.CostEstimate(
             flops=6 * rows * cols * width, bytes_accessed=8 * rows * cols, transcendentals=0
         ),
+        compiler_params=pltpu.CompilerParams(vmem_limit_bytes=26 << 20),
         name="finish",
     )(mine, counts, wide, mat, *panels, *squares, *factors, *parcels)
 

time: 94.3 us -> 90.4 us (0.959)
  the two profiles are of different devices: /device:TPU:0 before, /device:TPU:27 now
where the time goes in v7:
time: 90.4 us; the launch traced here: 89.4 us
  Pallas kernels  33.6 us (37%)
  waiting for transfers between devices  32.8 us (36%)
  starting transfers between devices  15.7 us (17%)
  other arithmetic  5.3 us (6%)
    ppermute x1, waiting for transfers between devices, capped_step(): message_new = lax.ppermute(message, 'pcol', pairs[-1])  17.2 us
    ppermute x4, waiting for transfers between devices, send(): return lax.ppermute(x, 'prow', [(i, i ^ k) for i in range(n_row)])  15.6 us
    pallas_call x1, Pallas kernels, factor(): pl.pallas_call(functools.partial(factor_kernel, width), out_shape=(out, o...  12.9 us
    pallas_call x1, Pallas kernels, finish(): pl.pallas_call(functools.partial(finish_kernel, n_row), out_shape=jax.Sha...  11.6 us
    ppermute x4, starting transfers between devices, send(): return lax.ppermute(x, 'prow', [(i, i ^ k) for i in range(n_row)])  4.33 us
    pallas_call x1, Pallas kernels, parcel(): pl.pallas_call(functools.partial(parcel_kernel, n_row), out_shape=tuple((...  4.03 us
    pallas_call x1, Pallas kernels, begin(): pl.pallas_call(functools.partial(begin_kernel, n_row), out_shape=(jax.Sha...  3.84 us
    select_n x2, other arithmetic, capped_step(): panel = jnp.where(newer[n], panel_moved, panel)  3.78 us
  transfers between devices with their start and end apart: 13, of which 3 were waited for; matrix products, arithmetic and copies ran while one was open for 4% of the time, Pallas kernels for 20%

profile of v7, /device:TPU:27, one launch (start us, length us, event | category | flops | bytes accessed | tf_op | source)
XLA Modules:
  0.0 89.4 jit_solution(1558202135066051129)
XLA Ops:
  0.0 3.8 %begin.1 = (f32[1024,256]{1,0:T(8,128)}, s32[256,128]{1,0:T(8,128)}, s32[1]{0:T(128)}, f32[192,256]{1,0:T(8,128)}, f32[192,256]{1,0:T(8,128)S(1)}, /*index=5*/f32[192,256]{1,0:T(8,128)}, f32[192,256]{1,0:T(8,128)}) custom-call(s32[1,256]{1,0:T(1,128)} %bitcast.29, f32[1024,1,1536]{2,1,0:T(1,128)} %bitcast.25), custom_call_target="tpu_custom_call" | custom-call | bytes 10000000 | tf_op jit(solution)/shard_map/begin/pallas_call | solution.py:441
  4.5 84.7 %conditional.1 = (f32[1,1024,1,1536]{3,2,1,0:T(1,128)}) conditional(s32[]{:T(128)} %bitcast.12, (s32[256]{0:T(256)S(1)}, f32[1,1024,1,1536]{3,2,1,0:T(1,128)}) %tuple.33, (s32[256]{0:T(256)S(1)}, f32[1,1024,1,1536]{3,2,1,0:T(1,128)}, f32[192,256]{1,0:T(8,128)S(1)}, f32[192,256]{1,0:T(8,128)}, f32[192,256]{1,0:T(8,128)}, ...), branch_computations={%region_0.1_spmd, %region_1.5_spmd} | conditional | flops 2488416000 | bytes 214372192 | solution.py:877
  4.8 1.7 %collective-permute-start.3 = (f32[1024,256]{1,0:T(8,128)}, f32[1024,256]{1,0:T(8,128)}, u32[]{:S(2)}, u32[]{:S(2)}) collective-permute-start(f32[1024,256]{1,0:T(8,128)} %get-tuple-element.40), channel_id=1, source_target_pairs={{0,4},{8,12},{16,20},{24,28}} | collective-permute-start | bytes 3145736 | tf_op jit(solution)/shard_map/cond/branch_1_fun/ppermute | solution.py:846
  6.4 0.7 collective-permute-start
  7.1 1.4 %collective-permute-start.1 = (f32[192,256]{1,0:T(8,128)}, f32[192,256]{1,0:T(8,128)}, u32[]{:S(2)}, u32[]{:S(2)}) collective-permute-start(f32[192,256]{1,0:T(8,128)} %get-tuple-element.38), channel_id=1, source_target_pairs={{0,16},{8,24},{16,0},{24,8}} | collective-permute-start | bytes 589832 | tf_op jit(solution)/shard_map/cond/branch_1_fun/ppermute | solution.py:837
  8.4 1.3 %collective-permute-start.2 = (f32[192,256]{1,0:T(8,128)}, f32[192,256]{1,0:T(8,128)}, u32[]{:S(2)}, u32[]{:S(2)}) collective-permute-start(f32[192,256]{1,0:T(8,128)} %get-tuple-element.39), channel_id=1, source_target_pairs={{0,24},{8,16},{16,8},{24,0}} | collective-permute-start | bytes 589832 | tf_op jit(solution)/shard_map/cond/branch_1_fun/ppermute | solution.py:837
  10.1 4.0 %parcel.1 = (f32[144,1536]{1,0:T(8,128)}, f32[144,1536]{1,0:T(8,128)}, f32[288,1536]{1,0:T(8,128)S(1)}) custom-call(s32[96]{0:T(128)S(1)} %select_reduce_fusion.mine_ref, s32[1,256]{1,0:T(1,128)S(1)} %bitcast.30, f32[1024,1,1536]{2,1,0:T(1,128)} %bitcast.26), custom_call_target="tpu_custom_call" | custom-call | bytes 16000000 | tf_op jit(solution)/shard_map/cond/branch_1_fun/parcel/pallas_call | solution.py:532
  14.1 3.6 %collective-permute-start.4 = (f32[144,1536]{1,0:T(8,128)}, f32[144,1536]{1,0:T(8,128)S(1)}, u32[]{:S(2)}, u32[]{:S(2)}) collective-permute-start(f32[144,1536]{1,0:T(8,128)} %get-tuple-element.44), channel_id=1, source_target_pairs={{0,8},{8,0},{16,24},{24,16},{1,9},{9,1},{17,25},{25,17},{2,10},{10... | collective-permute-start | bytes 2654216 | tf_op jit(solution)/shard_map/cond/branch_1_fun/ppermute | solution.py:844
  17.7 0.7 copy-done.3
  18.5 2.4 %broadcast_select_fusion.3 = f32[1024,256]{1,0:T(8,128)} fusion(f32[1024,256]{1,0:T(8,128)} %collective-permute-done.3, f32[1024,256]{1,0:T(8,128)} %get-tuple-element.40, pred[]{:T(512)S(6)} %ne.60), kind=kLoop, calls=%fused_computation.31 | loop fusion | flops 262144 | bytes 3145729 | tf_op jit(solution)/shard_map/cond/branch_1_fun/jit(_where)/select_n | solution.py:861
  20.9 1.7 %collective-permute-start.7 = (f32[1024,256]{1,0:T(8,128)}, f32[1024,256]{1,0:T(8,128)}, u32[]{:S(2)}, u32[]{:S(2)}) collective-permute-start(f32[1024,256]{1,0:T(8,128)} %broadcast_select_fusion.3), channel_id=1, source_target_pairs={{0,2},{4,6},{8,10},{12,14},{16,18},{20,22},{24,26},{28,30}} | collective-permute-start | bytes 3145736 | tf_op jit(solution)/shard_map/cond/branch_1_fun/ppermute | solution.py:862
  22.5 0.8 pack.1
  23.4 14.1 %collective-permute-done.4.first_ref.refs_1_ = f32[144,1536]{1,0:T(8,128)S(1)} collective-permute-done((f32[144,1536]{1,0:T(8,128)}, f32[144,1536]{1,0:T(8,128)S(1)}, u32[]{:S(2)}, u32[]{:S(2)}) %collective-permute-start.4) | collective-permute-done | bytes 884768 | tf_op jit(solution)/shard_map/cond/branch_1_fun/ppermute | solution.py:844
  37.4 1.5 %collective-permute-done.5.second_ref.refs_2_ = f32[144,1536]{1,0:T(8,128)S(1)} collective-permute-done((f32[144,1536]{1,0:T(8,128)}, f32[144,1536]{1,0:T(8,128)S(1)}, u32[]{:S(2)}, u32[]{:S(2)}) %collective-permute-start.5) | collective-permute-done | bytes 884768 | tf_op jit(solution)/shard_map/cond/branch_1_fun/ppermute | solution.py:844
  38.9 1.4 %collective-permute-start.6 = (f32[352,256]{1,0:T(8,128)}, f32[352,256]{1,0:T(8,128)}, u32[]{:S(2)}, u32[]{:S(2)}) collective-permute-start(f32[352,256]{1,0:T(8,128)} %pack.1), channel_id=1, source_target_pairs={{0,4},{8,12},{16,20},{24,28}} | collective-permute-start | bytes 1081352 | tf_op jit(solution)/shard_map/cond/branch_1_fun/ppermute | solution.py:863
  40.3 1.0 %broadcast_select_fusion.6 = f32[352,256]{1,0:T(8,128)S(1)} fusion(f32[352,256]{1,0:T(8,128)} %collective-permute-done.6, f32[352,256]{1,0:T(8,128)} %pack.1, pred[]{:T(512)S(6)} %ne.60), kind=kLoop, calls=%fused_computation.37 | loop fusion | flops 90112 | bytes 1081345 | tf_op jit(solution)/shard_map/cond/branch_1_fun/jit(_where)/select_n | solution.py:863
  41.4 1.4 %broadcast_select_fusion.4.panel_ref = f32[1024,256]{1,0:T(8,128)S(1)} fusion(f32[1024,256]{1,0:T(8,128)} %collective-permute-done.7, f32[1024,256]{1,0:T(8,128)} %broadcast_select_fusion.3, pred[]{:T(512)S(6)} %ne.59), kind=kLoop, calls=%fused_computation.32 | loop fusion | flops 262144 | bytes 3145729 | tf_op jit(solution)/shard_map/cond/branch_1_fun/jit(_where)/select_n | solution.py:861
  42.8 1.3 %collective-permute-start.8 = (f32[1024,256]{1,0:T(8,128)S(1)}, f32[1024,256]{1,0:T(8,128)S(1)}, u32[]{:S(2)}, u32[]{:S(2)}) collective-permute-start(f32[1024,256]{1,0:T(8,128)S(1)} %broadcast_select_fusion.4.panel_ref), channel_id=1, source_target_pairs={{0,1},{2,3},{4,5},{6,7},{8,9},{10,11},{12,13},{14,15},{16,17},{18,... | collective-permute-start | bytes 3145736 | tf_op jit(solution)/shard_map/cond/branch_1_fun/ppermute | solution.py:862
  44.1 0.7 collective-permute-start.9
  44.7 0.4 relay.1
  46.0 1.3 %collective-permute-start.10 = (f32[352,256]{1,0:T(8,128)S(1)}, f32[352,256]{1,0:T(8,128)S(1)}, u32[]{:S(2)}, u32[]{:S(2)}) collective-permute-start(f32[352,256]{1,0:T(8,128)S(1)} %broadcast_select_fusion.5.first_ref.square_ref), channel_id=1, source_target_pairs={{0,1},{2,3},{4,5},{6,7},{8,9},{10,11},{12,13},{14,15},{16,17},{18,... | collective-permute-start | bytes 1081352 | tf_op jit(solution)/shard_map/cond/branch_1_fun/ppermute | solution.py:866
  47.4 17.2 %collective-permute-done.10.second_ref.square_new_ref = f32[352,256]{1,0:T(8,128)S(1)} collective-permute-done((f32[352,256]{1,0:T(8,128)S(1)}, f32[352,256]{1,0:T(8,128)S(1)}, u32[]{:S(2)}, u32[]{:S(2)}) %collective-permute-start.10) | collective-permute-done | bytes 360480 | tf_op jit(solution)/shard_map/cond/branch_1_fun/ppermute | solution.py:866
  64.6 12.9 %factor.3 = (f32[256,256]{1,0:T(8,128)S(1)}, f32[256,256]{1,0:T(8,128)S(1)}, f32[256,256]{1,0:T(8,128)S(1)}) custom-call(f32[352,256]{1,0:T(8,128)S(1)} %broadcast_select_fusion.5.first_ref.square_ref, f32[352,256]{1,0:T(8,128)S(1)} %collective-permute-done.10.second_ref.square_new_ref), custom_call_target="tpu_custom_call" | custom-call | flops 67108864 | bytes 50000000 | tf_op jit(solution)/shard_map/cond/branch_1_fun/factor/pallas_call | solution.py:155
  77.6 11.6 %finish.1 = f32[1024,1,1536]{2,1,0:T(1,128)} custom-call(s32[96]{0:T(128)S(1)} %select_reduce_fusion.mine_ref, s32[4]{0:T(128)S(1)} %convert_reduce_fusion.1.counts_ref, s32[256,128]{1,0:T(8,128)S(1)} %copy-done.9, f32[1024,1,1536]{2,1,0:T(1,128)} %bitcast.27, f32[1024,256]{1,0:T(8,128)S(1)} %broadcast_select_fusion.4.panel_ref, ...), custom_call_target="tpu_custom_call" | custom-call | flops 2415919104 | bytes 12582912 | tf_op jit(solution)/shard_map/cond/branch_1_fun/finish/pallas_call | solution.py:783
  (30 shorter events, 1.3 us)
Async XLA Ops:
  0.0 4.5 %copy-start.11 = (s32[256]{0:T(256)S(1)}, s32[256]{0:T(256)}, u32[]{:S(2)}) copy-start(s32[256]{0:T(256)} %param.5) | copy-start | bytes 3076
  4.8 13.7 %collective-permute-start.3 = (f32[1024,256]{1,0:T(8,128)}, f32[1024,256]{1,0:T(8,128)}, u32[]{:S(2)}, u32[]{:S(2)}) collective-permute-start(f32[1024,256]{1,0:T(8,128)} %get-tuple-element.40), channel_id=1, source_target_pairs={{0,4},{8,12},{16,20},{24,28}} | collective-permute-start | bytes 3145736 | tf_op jit(solution)/shard_map/cond/branch_1_fun/ppermute | solution.py:846
  6.4 11.3 %collective-permute-start = (f32[192,256]{1,0:T(8,128)S(1)}, f32[192,256]{1,0:T(8,128)S(1)}, u32[]{:S(2)}, u32[]{:S(2)}) collective-permute-start(f32[192,256]{1,0:T(8,128)S(1)} %get-tuple-element.37), channel_id=1, source_target_pairs={{0,8},{8,0},{16,24},{24,16}} | collective-permute-start | bytes 589832 | tf_op jit(solution)/shard_map/cond/branch_1_fun/ppermute | solution.py:837
  7.1 11.3 %collective-permute-start.1 = (f32[192,256]{1,0:T(8,128)}, f32[192,256]{1,0:T(8,128)}, u32[]{:S(2)}, u32[]{:S(2)}) collective-permute-start(f32[192,256]{1,0:T(8,128)} %get-tuple-element.38), channel_id=1, source_target_pairs={{0,16},{8,24},{16,0},{24,8}} | collective-permute-start | bytes 589832 | tf_op jit(solution)/shard_map/cond/branch_1_fun/ppermute | solution.py:837
  8.4 10.0 %collective-permute-start.2 = (f32[192,256]{1,0:T(8,128)}, f32[192,256]{1,0:T(8,128)}, u32[]{:S(2)}, u32[]{:S(2)}) collective-permute-start(f32[192,256]{1,0:T(8,128)} %get-tuple-element.39), channel_id=1, source_target_pairs={{0,24},{8,16},{16,8},{24,0}} | collective-permute-start | bytes 589832 | tf_op jit(solution)/shard_map/cond/branch_1_fun/ppermute | solution.py:837
  14.1 23.3 %collective-permute-start.4 = (f32[144,1536]{1,0:T(8,128)}, f32[144,1536]{1,0:T(8,128)S(1)}, u32[]{:S(2)}, u32[]{:S(2)}) collective-permute-start(f32[144,1536]{1,0:T(8,128)} %get-tuple-element.44), channel_id=1, source_target_pairs={{0,8},{8,0},{16,24},{24,16},{1,9},{9,1},{17,25},{25,17},{2,10},{10... | collective-permute-start | bytes 2654216 | tf_op jit(solution)/shard_map/cond/branch_1_fun/ppermute | solution.py:844
  17.7 0.7 copy-start.3
  18.4 20.5 %collective-permute-start.5 = (f32[144,1536]{1,0:T(8,128)}, f32[144,1536]{1,0:T(8,128)S(1)}, u32[]{:S(2)}, u32[]{:S(2)}) collective-permute-start(f32[144,1536]{1,0:T(8,128)} %get-tuple-element.45), channel_id=1, source_target_pairs={{0,16},{8,24},{16,0},{24,8},{1,17},{9,25},{17,1},{25,9},{2,18},{10... | collective-permute-start | bytes 2654216 | tf_op jit(solution)/shard_map/cond/branch_1_fun/ppermute | solution.py:844
  18.4 4.1 %copy-start.4 = (f32[192,256]{1,0:T(8,128)S(1)}, f32[192,256]{1,0:T(8,128)}, u32[]{:S(2)}) copy-start(f32[192,256]{1,0:T(8,128)} %copy-done.3) | copy-start | bytes 589828 | tf_op jit(solution)/shard_map/cond
  18.4 4.1 %copy-start.8 = (s32[256,128]{1,0:T(8,128)S(1)}, s32[256,128]{1,0:T(8,128)}, u32[]{:S(2)}) copy-start(s32[256,128]{1,0:T(8,128)} %get-tuple-element.34.wide_ref) | copy-start | bytes 393220 | tf_op jit(solution)/shard_map/cond
  18.4 4.1 %copy-start.10 = (f32[192,256]{1,0:T(8,128)S(1)}, f32[192,256]{1,0:T(8,128)}, u32[]{:S(2)}) copy-start(f32[192,256]{1,0:T(8,128)} %get-tuple-element.36.refs_0_) | copy-start | bytes 589828 | tf_op jit(solution)/shard_map/cond
  20.9 20.5 %collective-permute-start.7 = (f32[1024,256]{1,0:T(8,128)}, f32[1024,256]{1,0:T(8,128)}, u32[]{:S(2)}, u32[]{:S(2)}) collective-permute-start(f32[1024,256]{1,0:T(8,128)} %broadcast_select_fusion.3), channel_id=1, source_target_pairs={{0,2},{4,6},{8,10},{12,14},{16,18},{20,22},{24,26},{28,30}} | collective-permute-start | bytes 3145736 | tf_op jit(solution)/shard_map/cond/branch_1_fun/ppermute | solution.py:862
  38.9 1.4 %collective-permute-start.6 = (f32[352,256]{1,0:T(8,128)}, f32[352,256]{1,0:T(8,128)}, u32[]{:S(2)}, u32[]{:S(2)}) collective-permute-start(f32[352,256]{1,0:T(8,128)} %pack.1), channel_id=1, source_target_pairs={{0,4},{8,12},{16,20},{24,28}} | collective-permute-start | bytes 1081352 | tf_op jit(solution)/shard_map/cond/branch_1_fun/ppermute | solution.py:863
  42.8 34.8 %collective-permute-start.8 = (f32[1024,256]{1,0:T(8,128)S(1)}, f32[1024,256]{1,0:T(8,128)S(1)}, u32[]{:S(2)}, u32[]{:S(2)}) collective-permute-start(f32[1024,256]{1,0:T(8,128)S(1)} %broadcast_select_fusion.4.panel_ref), channel_id=1, source_target_pairs={{0,1},{2,3},{4,5},{6,7},{8,9},{10,11},{12,13},{14,15},{16,17},{18,... | collective-permute-start | bytes 3145736 | tf_op jit(solution)/shard_map/cond/branch_1_fun/ppermute | solution.py:862
  44.1 1.9 %collective-permute-start.9 = (f32[352,256]{1,0:T(8,128)S(1)}, f32[352,256]{1,0:T(8,128)S(1)}, u32[]{:S(2)}, u32[]{:S(2)}) collective-permute-start(f32[352,256]{1,0:T(8,128)S(1)} %broadcast_select_fusion.6), channel_id=1, source_target_pairs={{0,2},{4,6},{8,10},{12,14},{16,18},{20,22},{24,26},{28,30}} | collective-permute-start | bytes 1081352 | tf_op jit(solution)/shard_map/cond/branch_1_fun/ppermute | solution.py:863
  45.2 32.4 %copy-start.9 = (s32[256,128]{1,0:T(8,128)S(1)}, s32[256,128]{1,0:T(8,128)}, u32[]{:S(2)}) copy-start(s32[256,128]{1,0:T(8,128)} %get-tuple-element.34.wide_ref) | copy-start | bytes 393220 | tf_op jit(solution)/shard_map/cond
  45.2 32.3 %collective-permute-start.11 = (f32[144,1536]{1,0:T(8,128)S(1)}, f32[144,1536]{1,0:T(8,128)S(1)}, u32[]{:S(2)}, u32[]{:S(2)}) collective-permute-start(f32[144,1536]{1,0:T(8,128)S(1)} %get-tuple-element.56), channel_id=1, source_target_pairs={{0,16},{8,24},{16,0},{24,8},{1,17},{9,25},{17,1},{25,9},{2,18},{10... | collective-permute-start | bytes 2654216 | tf_op jit(solution)/shard_map/cond/branch_1_fun/ppermute | solution.py:844
  45.6 32.0 %collective-permute-start.12 = (f32[144,1536]{1,0:T(8,128)S(1)}, f32[144,1536]{1,0:T(8,128)S(1)}, u32[]{:S(2)}, u32[]{:S(2)}) collective-permute-start(f32[144,1536]{1,0:T(8,128)S(1)} %get-tuple-element.57), channel_id=1, source_target_pairs={{0,8},{8,0},{16,24},{24,16},{1,9},{9,1},{17,25},{25,17},{2,10},{10... | collective-permute-start | bytes 2654216 | tf_op jit(solution)/shard_map/cond/branch_1_fun/ppermute | solution.py:844
  46.0 18.6 %collective-permute-start.10 = (f32[352,256]{1,0:T(8,128)S(1)}, f32[352,256]{1,0:T(8,128)S(1)}, u32[]{:S(2)}, u32[]{:S(2)}) collective-permute-start(f32[352,256]{1,0:T(8,128)S(1)} %broadcast_select_fusion.5.first_ref.square_ref), channel_id=1, source_target_pairs={{0,1},{2,3},{4,5},{6,7},{8,9},{10,11},{12,13},{14,15},{16,17},{18,... | collective-permute-start | bytes 1081352 | tf_op jit(solution)/shard_map/cond/branch_1_fun/ppermute | solution.py:866

commit v8 on v7

--- a/solution.py
+++ b/solution.py
@@ -843,15 +843,16 @@
     def send(x, k):
         return lax.ppermute(x, "prow", [(i, i ^ k) for i in range(n_row)])
 
+    *moved, kept = lax.optimization_barrier((*moved, parcels[-1]))
+    parcels = parcels[:-1] + (kept,)
+    message = pack(wide, messages[:1] + moved)
     panel_moved = lax.ppermute(panel, "pcol", [(i, i + turns[0]) for i in range(0, n_col, 2 * turns[0])])
-    *moved, panel_moved = lax.optimization_barrier((*moved, panel_moved))
-    message = pack(wide, messages[:1] + moved)
+    message, panel_moved = lax.optimization_barrier((message, panel_moved))
     if n_row == 4:
         first, second = send(parcels[0], 1), send(parcels[1], 2)
-        message, first, second = lax.optimization_barrier((message, first, second))
         kept = parcels[2]
         to_y, to_x = relay(kept, first, second)
-        arrived = [kept, first, second, send(to_y, 2), send(to_x, 1)]
+        arrived = [kept, first, second]
     else:
         arrived = [parcels[0]] + [send(parcels[k], k) for k in range(1, n_row)]
 
@@ -863,6 +864,9 @@
         message = jnp.where(newer[n], lax.ppermute(message, "pcol", pairs[n]), message)
         if n + 1 < len(turns):
             message, panel_moved = lax.optimization_barrier((message, panel_moved))
+    if n_row == 4:
+        message, to_y, to_x = lax.optimization_barrier((message, to_y, to_x))
+        arrived += [send(to_y, 2), send(to_x, 1)]
     message_new = lax.ppermute(message, "pcol", pairs[-1])
     factors = factor(message, message_new)
     out = finish(

time: 90.4 us -> 86.8 us (0.960)
  other arithmetic: 5.3 us -> 2.55 us
  starting transfers between devices: 15.7 us -> 13.6 us
  local copies, waits for them, and re-layouts: 0.69 us -> 2.06 us
  waiting for transfers between devices: 32.8 us -> 33.9 us
    select_n x2, other arithmetic: 3.78 us -> 0.27 us  [capped_step(): panel = jnp.where(newer[n], panel_moved, panel)]
    cond x10 -> x16, local copies, waits for them, and re-layouts: 0.69 us -> 2.06 us
    ppermute x3, starting transfers between devices: 3.33 us -> 2.02 us  [exchange(): lax.ppermute(x, both, [(i * n_col, (i ^ k) * n_col) for i in range(n_row)])]
    ppermute x4, starting transfers between devices: 4.33 us -> 5.42 us  [send(): return lax.ppermute(x, 'prow', [(i, i ^ k) for i in range(n_row)])]
    ppermute x1, starting transfers between devices: 1.67 us -> 0.73 us  [capped_step(): lax.ppermute(panel, 'pcol', [(i, i + turns[0]) for i in range(0, n_col, 2...]
  transfers between devices with their start and end apart: 13 -> 13, of which waited for: 3 -> 3; matrix products, arithmetic and copies ran while one was open for 4% -> 3% of each run, Pallas kernels for 20% -> 19%
where the time goes in v8:
time: 86.8 us; the launch traced here: 86.5 us
  waiting for transfers between devices  33.9 us (39%)
  Pallas kernels  33 us (38%)
  starting transfers between devices  13.6 us (16%)
  other arithmetic  2.55 us (3%)
  local copies, waits for them, and re-layouts  2.06 us (2%)
    ppermute x1, waiting for transfers between devices, capped_step(): message_new = lax.ppermute(message, 'pcol', pairs[-1])  17.9 us
    ppermute x4, waiting for transfers between devices, send(): return lax.ppermute(x, 'prow', [(i, i ^ k) for i in range(n_row)])  16 us
    pallas_call x1, Pallas kernels, factor(): pl.pallas_call(functools.partial(factor_kernel, width), out_shape=(out, o...  12.9 us
    pallas_call x1, Pallas kernels, finish(): pl.pallas_call(functools.partial(finish_kernel, n_row), out_shape=jax.Sha...  12.3 us
    ppermute x4, starting transfers between devices, send(): return lax.ppermute(x, 'prow', [(i, i ^ k) for i in range(n_row)])  5.42 us
    pallas_call x1, Pallas kernels, begin(): pl.pallas_call(functools.partial(begin_kernel, n_row), out_shape=(jax.Sha...  3.87 us
    pallas_call x1, Pallas kernels, parcel(): pl.pallas_call(functools.partial(parcel_kernel, n_row), out_shape=tuple((...  3.4 us
    ppermute x2, starting transfers between devices, capped_step(): panel_moved = lax.ppermute(panel, 'pcol', pairs[n + 1])  2.15 us
  transfers between devices with their start and end apart: 13, of which 3 were waited for; matrix products, arithmetic and copies ran while one was open for 3% of the time, Pallas kernels for 19%

profile of v8, /device:TPU:27, one launch (start us, length us, event | category | flops | bytes accessed | tf_op | source)
XLA Modules:
  0.0 86.5 jit_solution(939574038014213351)
XLA Ops:
  0.0 3.9 %begin.1 = (f32[1024,256]{1,0:T(8,128)}, s32[256,128]{1,0:T(8,128)S(1)}, s32[1]{0:T(128)}, f32[192,256]{1,0:T(8,128)}, f32[192,256]{1,0:T(8,128)}, /*index=5*/f32[192,256]{1,0:T(8,128)}, f32[192,256]{1,0:T(8,128)}) custom-call(s32[1,256]{1,0:T(1,128)} %bitcast.29, f32[1024,1,1536]{2,1,0:T(1,128)} %bitcast.25), custom_call_target="tpu_custom_call" | custom-call | bytes 10000000 | tf_op jit(solution)/shard_map/begin/pallas_call | solution.py:441
  4.5 81.8 %conditional.1 = (f32[1,1024,1,1536]{3,2,1,0:T(1,128)}) conditional(s32[]{:T(128)} %bitcast.12, (s32[256]{0:T(256)S(1)}, f32[1,1024,1,1536]{3,2,1,0:T(1,128)}) %tuple.34, (s32[256]{0:T(256)S(1)}, f32[1,1024,1,1536]{3,2,1,0:T(1,128)}, f32[192,256]{1,0:T(8,128)}, f32[192,256]{1,0:T(8,128)}, f32[192,256]{1,0:T(8,128)}, ...), branch_computations={%region_0.1_spmd, %region_1.5_spmd} | conditional | flops 2488416000 | bytes 214372192 | solution.py:881
  4.8 0.7 collective-permute-start.3
  5.5 0.7 collective-permute-start
  6.2 0.7 collective-permute-start.1
  6.9 0.7 collective-permute-start.2
  7.9 3.4 %parcel.1 = (f32[144,1536]{1,0:T(8,128)}, f32[144,1536]{1,0:T(8,128)}, f32[288,1536]{1,0:T(8,128)S(1)}) custom-call(s32[96]{0:T(128)S(1)} %select_reduce_fusion.mine_ref, s32[1,256]{1,0:T(1,128)S(1)} %bitcast.30, f32[1024,1,1536]{2,1,0:T(1,128)} %bitcast.26), custom_call_target="tpu_custom_call" | custom-call | bytes 16000000 | tf_op jit(solution)/shard_map/cond/branch_1_fun/parcel/pallas_call | solution.py:532
  11.5 1.1 %copy-done.8 = f32[1024,256]{1,0:T(8,128)S(1)} copy-done((f32[1024,256]{1,0:T(8,128)S(1)}, f32[1024,256]{1,0:T(8,128)}, u32[]{:S(2)}) %copy-start.8) | copy-done | bytes 1048600 | tf_op jit(solution)/shard_map/cond
  12.7 0.7 collective-permute-start.5
  13.4 4.7 %collective-permute-start.8 = (f32[144,1536]{1,0:T(8,128)}, f32[144,1536]{1,0:T(8,128)S(1)}, u32[]{:S(2)}, u32[]{:S(2)}) collective-permute-start(f32[144,1536]{1,0:T(8,128)} %get-tuple-element.50), channel_id=1, source_target_pairs={{0,8},{8,0},{16,24},{24,16},{1,9},{9,1},{17,25},{25,17},{2,10},{10... | collective-permute-start | bytes 2654216 | tf_op jit(solution)/shard_map/cond/branch_1_fun/ppermute | solution.py:844
  18.1 0.7 collective-permute-start.4
  18.8 0.8 broadcast_select_fusion.6
  19.6 1.0 %copy-done.9 = f32[1024,256]{1,0:T(8,128)} copy-done((f32[1024,256]{1,0:T(8,128)}, f32[1024,256]{1,0:T(8,128)S(1)}, u32[]{:S(2)}) %copy-start.9) | copy-done | bytes 1048600 | tf_op jit(solution)/shard_map/cond
  20.6 1.4 %collective-permute-start.7 = (f32[352,256]{1,0:T(8,128)}, f32[352,256]{1,0:T(8,128)}, u32[]{:S(2)}, u32[]{:S(2)}) collective-permute-start(f32[352,256]{1,0:T(8,128)} %broadcast_select_fusion.6), channel_id=1, source_target_pairs={{0,2},{4,6},{8,10},{12,14},{16,18},{20,22},{24,26},{28,30}} | collective-permute-start | bytes 1081352 | tf_op jit(solution)/shard_map/cond/branch_1_fun/ppermute | solution.py:864
  22.0 15.1 %collective-permute-done.8.first_ref.refs_1_ = f32[144,1536]{1,0:T(8,128)S(1)} collective-permute-done((f32[144,1536]{1,0:T(8,128)}, f32[144,1536]{1,0:T(8,128)S(1)}, u32[]{:S(2)}, u32[]{:S(2)}) %collective-permute-start.8) | collective-permute-done | bytes 884768 | tf_op jit(solution)/shard_map/cond/branch_1_fun/ppermute | solution.py:844
  37.1 0.9 %collective-permute-done.9.second_ref.refs_2_ = f32[144,1536]{1,0:T(8,128)S(1)} collective-permute-done((f32[144,1536]{1,0:T(8,128)}, f32[144,1536]{1,0:T(8,128)S(1)}, u32[]{:S(2)}, u32[]{:S(2)}) %collective-permute-start.9) | collective-permute-done | bytes 884768 | tf_op jit(solution)/shard_map/cond/branch_1_fun/ppermute | solution.py:844
  38.0 0.4 relay.1
  38.6 1.4 %collective-permute-start.6 = (f32[1024,256]{1,0:T(8,128)S(1)}, f32[1024,256]{1,0:T(8,128)S(1)}, u32[]{:S(2)}, u32[]{:S(2)}) collective-permute-start(f32[1024,256]{1,0:T(8,128)S(1)} %broadcast_select_fusion.4.panel_ref), channel_id=1, source_target_pairs={{0,1},{2,3},{4,5},{6,7},{8,9},{10,11},{12,13},{14,15},{16,17},{18,... | collective-permute-start | bytes 3145736 | tf_op jit(solution)/shard_map/cond/branch_1_fun/ppermute | solution.py:863
  40.0 1.0 %broadcast_select_fusion.5.first_ref.square_ref = f32[352,256]{1,0:T(8,128)S(1)} fusion(f32[352,256]{1,0:T(8,128)} %collective-permute-done.7, f32[352,256]{1,0:T(8,128)} %broadcast_select_fusion.6, pred[]{:T(512)S(6)} %ne.59), kind=kLoop, calls=%fused_computation.36 | loop fusion | flops 90112 | bytes 1081345 | tf_op jit(solution)/shard_map/cond/branch_1_fun/jit(_where)/select_n | solution.py:864
  41.4 0.4 collective-permute-start.12
  41.8 1.3 %collective-permute-start.10 = (f32[352,256]{1,0:T(8,128)S(1)}, f32[352,256]{1,0:T(8,128)S(1)}, u32[]{:S(2)}, u32[]{:S(2)}) collective-permute-start(f32[352,256]{1,0:T(8,128)S(1)} %broadcast_select_fusion.5.first_ref.square_ref), channel_id=1, source_target_pairs={{0,1},{2,3},{4,5},{6,7},{8,9},{10,11},{12,13},{14,15},{16,17},{18,... | collective-permute-start | bytes 1081352 | tf_op jit(solution)/shard_map/cond/branch_1_fun/ppermute | solution.py:870
  43.2 17.9 %collective-permute-done.10.second_ref.square_new_ref = f32[352,256]{1,0:T(8,128)S(1)} collective-permute-done((f32[352,256]{1,0:T(8,128)S(1)}, f32[352,256]{1,0:T(8,128)S(1)}, u32[]{:S(2)}, u32[]{:S(2)}) %collective-permute-start.10) | collective-permute-done | bytes 360480 | tf_op jit(solution)/shard_map/cond/branch_1_fun/ppermute | solution.py:870
  61.1 12.9 %factor.3 = (f32[256,256]{1,0:T(8,128)S(1)}, f32[256,256]{1,0:T(8,128)S(1)}, f32[256,256]{1,0:T(8,128)S(1)}) custom-call(f32[352,256]{1,0:T(8,128)S(1)} %broadcast_select_fusion.5.first_ref.square_ref, f32[352,256]{1,0:T(8,128)S(1)} %collective-permute-done.10.second_ref.square_new_ref), custom_call_target="tpu_custom_call" | custom-call | flops 67108864 | bytes 50000000 | tf_op jit(solution)/shard_map/cond/branch_1_fun/factor/pallas_call | solution.py:155
  74.0 12.3 %finish.1 = f32[1024,1,1536]{2,1,0:T(1,128)} custom-call(s32[96]{0:T(128)S(1)} %select_reduce_fusion.mine_ref, s32[4]{0:T(128)S(1)} %convert_reduce_fusion.1.counts_ref, s32[256,128]{1,0:T(8,128)S(1)} %copy-done.12, f32[1024,1,1536]{2,1,0:T(1,128)} %bitcast.27, f32[1024,256]{1,0:T(8,128)S(1)} %broadcast_select_fusion.4.panel_ref, ...), custom_call_target="tpu_custom_call" | custom-call | flops 2415919104 | bytes 12582912 | tf_op jit(solution)/shard_map/cond/branch_1_fun/finish/pallas_call | solution.py:783
  (36 shorter events, 1.2 us)
Async XLA Ops:
  0.0 4.5 %copy-start.14 = (s32[256]{0:T(256)S(1)}, s32[256]{0:T(256)}, u32[]{:S(2)}) copy-start(s32[256]{0:T(256)} %param.5) | copy-start | bytes 3076
  4.8 6.6 %copy-start.11 = (s32[256,128]{1,0:T(8,128)}, s32[256,128]{1,0:T(8,128)S(1)}, u32[]{:S(2)}) copy-start(s32[256,128]{1,0:T(8,128)S(1)} %get-tuple-element.34.wide_ref) | copy-start | bytes 393220 | tf_op jit(solution)/shard_map/cond
  4.8 6.7 %collective-permute-start.3 = (f32[1024,256]{1,0:T(8,128)}, f32[1024,256]{1,0:T(8,128)S(1)}, u32[]{:S(2)}, u32[]{:S(2)}) collective-permute-start(f32[1024,256]{1,0:T(8,128)} %get-tuple-element.44), channel_id=1, source_target_pairs={{0,4},{8,12},{16,20},{24,28}} | collective-permute-start | bytes 3145736 | tf_op jit(solution)/shard_map/cond/branch_1_fun/ppermute | solution.py:849
  5.5 5.8 %collective-permute-start = (f32[192,256]{1,0:T(8,128)}, f32[192,256]{1,0:T(8,128)S(1)}, u32[]{:S(2)}, u32[]{:S(2)}) collective-permute-start(f32[192,256]{1,0:T(8,128)} %get-tuple-element.37), channel_id=1, source_target_pairs={{0,8},{8,0},{16,24},{24,16}} | collective-permute-start | bytes 589832 | tf_op jit(solution)/shard_map/cond/branch_1_fun/ppermute | solution.py:837
  6.2 5.2 %collective-permute-start.1 = (f32[192,256]{1,0:T(8,128)}, f32[192,256]{1,0:T(8,128)S(1)}, u32[]{:S(2)}, u32[]{:S(2)}) collective-permute-start(f32[192,256]{1,0:T(8,128)} %get-tuple-element.38), channel_id=1, source_target_pairs={{0,16},{8,24},{16,0},{24,8}} | collective-permute-start | bytes 589832 | tf_op jit(solution)/shard_map/cond/branch_1_fun/ppermute | solution.py:837
  6.9 4.5 %collective-permute-start.2 = (f32[192,256]{1,0:T(8,128)}, f32[192,256]{1,0:T(8,128)S(1)}, u32[]{:S(2)}, u32[]{:S(2)}) collective-permute-start(f32[192,256]{1,0:T(8,128)} %get-tuple-element.39), channel_id=1, source_target_pairs={{0,24},{8,16},{16,8},{24,0}} | collective-permute-start | bytes 589832 | tf_op jit(solution)/shard_map/cond/branch_1_fun/ppermute | solution.py:837
  7.9 3.5 %copy-start.13 = (f32[192,256]{1,0:T(8,128)S(1)}, f32[192,256]{1,0:T(8,128)}, u32[]{:S(2)}) copy-start(f32[192,256]{1,0:T(8,128)} %get-tuple-element.36.refs_0_) | copy-start | bytes 589828 | tf_op jit(solution)/shard_map/cond
  11.3 1.2 %copy-start.8 = (f32[1024,256]{1,0:T(8,128)S(1)}, f32[1024,256]{1,0:T(8,128)}, u32[]{:S(2)}) copy-start(f32[1024,256]{1,0:T(8,128)} %get-tuple-element.44) | copy-start | bytes 3145732 | tf_op jit(solution)/shard_map/cond
  12.7 6.9 %copy-start.5 = (f32[1024,256]{1,0:T(8,128)}, f32[1024,256]{1,0:T(8,128)S(1)}, u32[]{:S(2)}) copy-start(f32[1024,256]{1,0:T(8,128)S(1)} %broadcast_select_fusion.3) | copy-start | bytes 3145732 | tf_op jit(solution)/shard_map/cond
  12.7 6.9 %collective-permute-start.5 = (f32[1024,256]{1,0:T(8,128)S(1)}, f32[1024,256]{1,0:T(8,128)S(1)}, u32[]{:S(2)}, u32[]{:S(2)}) collective-permute-start(f32[1024,256]{1,0:T(8,128)S(1)} %broadcast_select_fusion.3), channel_id=1, source_target_pairs={{0,2},{4,6},{8,10},{12,14},{16,18},{20,22},{24,26},{28,30}} | collective-permute-start | bytes 3145736 | tf_op jit(solution)/shard_map/cond/branch_1_fun/ppermute | solution.py:863
  13.4 23.6 %collective-permute-start.8 = (f32[144,1536]{1,0:T(8,128)}, f32[144,1536]{1,0:T(8,128)S(1)}, u32[]{:S(2)}, u32[]{:S(2)}) collective-permute-start(f32[144,1536]{1,0:T(8,128)} %get-tuple-element.50), channel_id=1, source_target_pairs={{0,8},{8,0},{16,24},{24,16},{1,9},{9,1},{17,25},{25,17},{2,10},{10... | collective-permute-start | bytes 2654216 | tf_op jit(solution)/shard_map/cond/branch_1_fun/ppermute | solution.py:844
  18.1 19.8 %collective-permute-start.9 = (f32[144,1536]{1,0:T(8,128)}, f32[144,1536]{1,0:T(8,128)S(1)}, u32[]{:S(2)}, u32[]{:S(2)}) collective-permute-start(f32[144,1536]{1,0:T(8,128)} %get-tuple-element.51), channel_id=1, source_target_pairs={{0,16},{8,24},{16,0},{24,8},{1,17},{9,25},{17,1},{25,9},{2,18},{10... | collective-permute-start | bytes 2654216 | tf_op jit(solution)/shard_map/cond/branch_1_fun/ppermute | solution.py:844
  18.1 0.7 collective-permute-start.4
  19.6 1.0 %copy-start.9 = (f32[1024,256]{1,0:T(8,128)}, f32[1024,256]{1,0:T(8,128)S(1)}, u32[]{:S(2)}) copy-start(f32[1024,256]{1,0:T(8,128)S(1)} %collective-permute-done.5) | copy-start | bytes 3145732 | tf_op jit(solution)/shard_map/cond
  20.6 19.4 %collective-permute-start.7 = (f32[352,256]{1,0:T(8,128)}, f32[352,256]{1,0:T(8,128)}, u32[]{:S(2)}, u32[]{:S(2)}) collective-permute-start(f32[352,256]{1,0:T(8,128)} %broadcast_select_fusion.6), channel_id=1, source_target_pairs={{0,2},{4,6},{8,10},{12,14},{16,18},{20,22},{24,26},{28,30}} | collective-permute-start | bytes 1081352 | tf_op jit(solution)/shard_map/cond/branch_1_fun/ppermute | solution.py:864
  22.0 16.4 %copy-start.6 = (f32[1024,256]{1,0:T(8,128)S(1)}, f32[1024,256]{1,0:T(8,128)}, u32[]{:S(2)}) copy-start(f32[1024,256]{1,0:T(8,128)} %copy-done.5) | copy-start | bytes 3145732 | tf_op jit(solution)/shard_map/cond
  22.0 16.4 %copy-start.10 = (f32[1024,256]{1,0:T(8,128)S(1)}, f32[1024,256]{1,0:T(8,128)}, u32[]{:S(2)}) copy-start(f32[1024,256]{1,0:T(8,128)} %copy-done.9) | copy-start | bytes 3145732 | tf_op jit(solution)/shard_map/cond
  38.6 35.4 %copy-start.12 = (s32[256,128]{1,0:T(8,128)S(1)}, s32[256,128]{1,0:T(8,128)}, u32[]{:S(2)}) copy-start(s32[256,128]{1,0:T(8,128)} %copy-done.11) | copy-start | bytes 393220 | tf_op jit(solution)/shard_map/cond
  38.6 35.4 %collective-permute-start.6 = (f32[1024,256]{1,0:T(8,128)S(1)}, f32[1024,256]{1,0:T(8,128)S(1)}, u32[]{:S(2)}, u32[]{:S(2)}) collective-permute-start(f32[1024,256]{1,0:T(8,128)S(1)} %broadcast_select_fusion.4.panel_ref), channel_id=1, source_target_pairs={{0,1},{2,3},{4,5},{6,7},{8,9},{10,11},{12,13},{14,15},{16,17},{18,... | collective-permute-start | bytes 3145736 | tf_op jit(solution)/shard_map/cond/branch_1_fun/ppermute | solution.py:863
  41.1 32.9 %collective-permute-start.11 = (f32[144,1536]{1,0:T(8,128)S(1)}, f32[144,1536]{1,0:T(8,128)S(1)}, u32[]{:S(2)}, u32[]{:S(2)}) collective-permute-start(f32[144,1536]{1,0:T(8,128)S(1)} %get-tuple-element.58), channel_id=1, source_target_pairs={{0,16},{8,24},{16,0},{24,8},{1,17},{9,25},{17,1},{25,9},{2,18},{10... | collective-permute-start | bytes 2654216 | tf_op jit(solution)/shard_map/cond/branch_1_fun/ppermute | solution.py:844
  41.4 32.6 %collective-permute-start.12 = (f32[144,1536]{1,0:T(8,128)S(1)}, f32[144,1536]{1,0:T(8,128)S(1)}, u32[]{:S(2)}, u32[]{:S(2)}) collective-permute-start(f32[144,1536]{1,0:T(8,128)S(1)} %get-tuple-element.59), channel_id=1, source_target_pairs={{0,8},{8,0},{16,24},{24,16},{1,9},{9,1},{17,25},{25,17},{2,10},{10... | collective-permute-start | bytes 2654216 | tf_op jit(solution)/shard_map/cond/branch_1_fun/ppermute | solution.py:844
  41.8 19.3 %collective-permute-start.10 = (f32[352,256]{1,0:T(8,128)S(1)}, f32[352,256]{1,0:T(8,128)S(1)}, u32[]{:S(2)}, u32[]{:S(2)}) collective-permute-start(f32[352,256]{1,0:T(8,128)S(1)} %broadcast_select_fusion.5.first_ref.square_ref), channel_id=1, source_target_pairs={{0,1},{2,3},{4,5},{6,7},{8,9},{10,11},{12,13},{14,15},{16,17},{18,... | collective-permute-start | bytes 1081352 | tf_op jit(solution)/shard_map/cond/branch_1_fun/ppermute | solution.py:870

commit v9 on v8

--- a/solution.py
+++ b/solution.py
@@ -846,8 +846,8 @@
     *moved, kept = lax.optimization_barrier((*moved, parcels[-1]))
     parcels = parcels[:-1] + (kept,)
     message = pack(wide, messages[:1] + moved)
-    panel_moved = lax.ppermute(panel, "pcol", [(i, i + turns[0]) for i in range(0, n_col, 2 * turns[0])])
-    message, panel_moved = lax.optimization_barrier((message, panel_moved))
+    roots = [lax.ppermute(panel, "pcol", [(0, bit)]) for bit in turns]
+    message, *roots = lax.optimization_barrier((message, *roots))
     if n_row == 4:
         first, second = send(parcels[0], 1), send(parcels[1], 2)
         kept = parcels[2]
@@ -858,12 +858,16 @@
 
     pairs = [[(i, i + bit) for i in range(0, n_col, 2 * bit)] for bit in turns + [1]]
     newer = [(col & bit) != 0 for bit in turns]
-    for n in range(len(turns)):
-        panel = jnp.where(newer[n], panel_moved, panel)
-        panel_moved = lax.ppermute(panel, "pcol", pairs[n + 1])
+    panel = jnp.where(col == turns[0], roots[0], panel)
+    for n, bit in enumerate(turns):
+        if n + 1 < len(turns):
+            relayed = lax.ppermute(roots[0] if n == 0 else panel, "pcol", pairs[n + 1][1:])
         message = jnp.where(newer[n], lax.ppermute(message, "pcol", pairs[n]), message)
         if n + 1 < len(turns):
-            message, panel_moved = lax.optimization_barrier((message, panel_moved))
+            message, relayed = lax.optimization_barrier((message, relayed))
+            newest = jnp.where(col == turns[n + 1], roots[n + 1], relayed)
+            panel = jnp.where(newer[n + 1], newest, panel)
+    panel_moved = lax.ppermute(panel, "pcol", pairs[-1])
     if n_row == 4:
         message, to_y, to_x = lax.optimization_barrier((message, to_y, to_x))
         arrived += [send(to_y, 2), send(to_x, 1)]

time: 86.8 us -> 98.6 us (1.14)
  the two profiles are of different devices: /device:TPU:27 before, /device:TPU:21 now
where the time goes in v9:
time: 98.6 us; the launch traced here: 97.8 us
  Pallas kernels  38 us (39%)
  waiting for transfers between devices  35.3 us (36%)
  starting transfers between devices  18 us (18%)
  other arithmetic  5.05 us (5%)
    ppermute x1, waiting for transfers between devices, capped_step(): message_new = lax.ppermute(message, 'pcol', pairs[-1])  28.9 us
    pallas_call x1, Pallas kernels, finish(): pl.pallas_call(functools.partial(finish_kernel, n_row), out_shape=jax.Sha...  15.7 us
    pallas_call x1, Pallas kernels, factor(): pl.pallas_call(functools.partial(factor_kernel, width), out_shape=(out, o...  12.9 us
    ppermute x4, waiting for transfers between devices, send(): return lax.ppermute(x, 'prow', [(i, i ^ k) for i in range(n_row)])  6.43 us
    ppermute x4, starting transfers between devices, send(): return lax.ppermute(x, 'prow', [(i, i ^ k) for i in range(n_row)])  6.41 us
    pallas_call x1, Pallas kernels, parcel(): pl.pallas_call(functools.partial(parcel_kernel, n_row), out_shape=tuple((...  4.33 us
    pallas_call x1, Pallas kernels, begin(): pl.pallas_call(functools.partial(begin_kernel, n_row), out_shape=(jax.Sha...  3.87 us
    ppermute x2, starting transfers between devices, capped_step(): lax.ppermute(message, 'pcol', pairs[n])  2.84 us
  transfers between devices with their start and end apart: 14, of which 3 were waited for; matrix products, arithmetic and copies ran while one was open for 5% of the time, Pallas kernels for 19%

profile of v9, /device:TPU:21, one launch (start us, length us, event | category | flops | bytes accessed | tf_op | source)
XLA Modules:
  0.0 97.8 jit_solution(4941917909484413335)
XLA Ops:
  0.0 3.9 %begin.1 = (f32[1024,256]{1,0:T(8,128)}, s32[256,128]{1,0:T(8,128)S(1)}, s32[1]{0:T(128)}, f32[192,256]{1,0:T(8,128)}, f32[192,256]{1,0:T(8,128)}, /*index=5*/f32[192,256]{1,0:T(8,128)}, f32[192,256]{1,0:T(8,128)}) custom-call(s32[1,256]{1,0:T(1,128)} %bitcast.29, f32[1024,1,1536]{2,1,0:T(1,128)} %bitcast.25), custom_call_target="tpu_custom_call" | custom-call | bytes 10000000 | tf_op jit(solution)/shard_map/begin/pallas_call | solution.py:441
  4.5 93.1 %conditional.1 = (f32[1,1024,1,1536]{3,2,1,0:T(1,128)}) conditional(s32[]{:T(128)} %bitcast.12, (s32[256]{0:T(256)S(1)}, f32[1,1024,1,1536]{3,2,1,0:T(1,128)}) %tuple.34, (s32[256]{0:T(256)S(1)}, f32[1,1024,1,1536]{3,2,1,0:T(1,128)}, f32[192,256]{1,0:T(8,128)}, f32[192,256]{1,0:T(8,128)}, f32[192,256]{1,0:T(8,128)}, ...), branch_computations={%region_0.1_spmd, %region_1.5_spmd} | conditional | flops 2488416000 | bytes 214372192 | solution.py:885
  4.8 0.7 collective-permute-start.4
  5.5 1.7 %collective-permute-start.3 = (f32[1024,256]{1,0:T(8,128)}, f32[1024,256]{1,0:T(8,128)}, u32[]{:S(2)}, u32[]{:S(2)}) collective-permute-start(f32[1024,256]{1,0:T(8,128)} %get-tuple-element.44), channel_id=1, source_target_pairs={{0,4},{8,12},{16,20},{24,28}} | collective-permute-start | bytes 3145736 | tf_op jit(solution)/shard_map/cond/branch_1_fun/ppermute | solution.py:849
  7.9 0.7 collective-permute-start.1
  8.5 0.7 collective-permute-start.2
  9.6 4.3 %parcel.1 = (f32[144,1536]{1,0:T(8,128)}, f32[144,1536]{1,0:T(8,128)}, f32[288,1536]{1,0:T(8,128)S(1)}) custom-call(s32[96]{0:T(128)S(1)} %select_reduce_fusion.mine_ref, s32[1,256]{1,0:T(1,128)S(1)} %bitcast.30, f32[1024,1,1536]{2,1,0:T(1,128)} %bitcast.26), custom_call_target="tpu_custom_call" | custom-call | bytes 16000000 | tf_op jit(solution)/shard_map/cond/branch_1_fun/parcel/pallas_call | solution.py:532
  14.0 0.8 pack.1
  14.8 1.7 %collective-permute-start.6 = (f32[1024,256]{1,0:T(8,128)}, f32[1024,256]{1,0:T(8,128)}, u32[]{:S(2)}, u32[]{:S(2)}) collective-permute-start(f32[1024,256]{1,0:T(8,128)} %collective-permute-done.3), channel_id=1, source_target_pairs={{4,6},{12,14},{20,22},{28,30}} | collective-permute-start | bytes 3145736 | tf_op jit(solution)/shard_map/cond/branch_1_fun/ppermute | solution.py:864
  16.9 3.0 %collective-permute-start.10 = (f32[144,1536]{1,0:T(8,128)}, f32[144,1536]{1,0:T(8,128)S(1)}, u32[]{:S(2)}, u32[]{:S(2)}) collective-permute-start(f32[144,1536]{1,0:T(8,128)} %get-tuple-element.52), channel_id=1, source_target_pairs={{0,16},{8,24},{16,0},{24,8},{1,17},{9,25},{17,1},{25,9},{2,18},{10... | collective-permute-start | bytes 2654216 | tf_op jit(solution)/shard_map/cond/branch_1_fun/ppermute | solution.py:844
  19.9 1.4 %collective-permute-start.5 = (f32[352,256]{1,0:T(8,128)}, f32[352,256]{1,0:T(8,128)}, u32[]{:S(2)}, u32[]{:S(2)}) collective-permute-start(f32[352,256]{1,0:T(8,128)} %pack.1), channel_id=1, source_target_pairs={{0,4},{8,12},{16,20},{24,28}} | collective-permute-start | bytes 1081352 | tf_op jit(solution)/shard_map/cond/branch_1_fun/ppermute | solution.py:865
  21.3 1.8 %broadcast_select_fusion.4 = f32[352,256]{1,0:T(8,128)} fusion(f32[352,256]{1,0:T(8,128)} %collective-permute-done.5, f32[352,256]{1,0:T(8,128)} %pack.1, pred[]{:T(512)S(6)} %ne.60), kind=kLoop, calls=%fused_computation.36 | loop fusion | flops 90112 | bytes 1081345 | tf_op jit(solution)/shard_map/cond/branch_1_fun/jit(_where)/select_n | solution.py:865
  23.1 1.4 %collective-permute-start.8 = (f32[352,256]{1,0:T(8,128)}, f32[352,256]{1,0:T(8,128)}, u32[]{:S(2)}, u32[]{:S(2)}) collective-permute-start(f32[352,256]{1,0:T(8,128)} %broadcast_select_fusion.4), channel_id=1, source_target_pairs={{0,2},{4,6},{8,10},{12,14},{16,18},{20,22},{24,26},{28,30}} | collective-permute-start | bytes 1081352 | tf_op jit(solution)/shard_map/cond/branch_1_fun/ppermute | solution.py:865
  24.5 4.5 %collective-permute-done.9.first_ref.refs_1_ = f32[144,1536]{1,0:T(8,128)S(1)} collective-permute-done((f32[144,1536]{1,0:T(8,128)}, f32[144,1536]{1,0:T(8,128)S(1)}, u32[]{:S(2)}, u32[]{:S(2)}) %collective-permute-start.9) | collective-permute-done | bytes 884768 | tf_op jit(solution)/shard_map/cond/branch_1_fun/ppermute | solution.py:844
  29.0 2.0 %collective-permute-done.10.second_ref.refs_2_ = f32[144,1536]{1,0:T(8,128)S(1)} collective-permute-done((f32[144,1536]{1,0:T(8,128)}, f32[144,1536]{1,0:T(8,128)S(1)}, u32[]{:S(2)}, u32[]{:S(2)}) %collective-permute-start.10) | collective-permute-done | bytes 884768 | tf_op jit(solution)/shard_map/cond/branch_1_fun/ppermute | solution.py:844
  31.4 1.8 %select_select_fusion.panel_ref = f32[1024,256]{1,0:T(8,128)S(1)} fusion(f32[1024,256]{1,0:T(8,128)} %collective-permute-done.3, f32[1024,256]{1,0:T(8,128)S(1)} %copy-done.7, f32[1024,256]{1,0:T(8,128)S(1)} %copy-done.9, f32[1024,256]{1,0:T(8,128)} %collective-permute-done.6, pred[]{:T(512)S(6)} %eq.68, pred[]{:T(512)S(6)} %eq.67, pred[]{:T(512)S(6)} %ne.59), kind=kLoop, calls=%fused_computation.31 | loop fusion | flops 786432 | bytes 5242883 | tf_op jit(solution)/shard_map/cond/branch_1_fun/jit(_where)/select_n | solution.py:869
  33.2 1.4 %collective-permute-start.7 = (f32[1024,256]{1,0:T(8,128)S(1)}, f32[1024,256]{1,0:T(8,128)S(1)}, u32[]{:S(2)}, u32[]{:S(2)}) collective-permute-start(f32[1024,256]{1,0:T(8,128)S(1)} %select_select_fusion.panel_ref), channel_id=1, source_target_pairs={{0,1},{2,3},{4,5},{6,7},{8,9},{10,11},{12,13},{14,15},{16,17},{18,... | collective-permute-start | bytes 3145736 | tf_op jit(solution)/shard_map/cond/branch_1_fun/ppermute | solution.py:870
  34.7 1.0 %broadcast_select_fusion.3.first_ref.square_ref = f32[352,256]{1,0:T(8,128)S(1)} fusion(f32[352,256]{1,0:T(8,128)} %collective-permute-done.8, f32[352,256]{1,0:T(8,128)} %broadcast_select_fusion.4, pred[]{:T(512)S(6)} %ne.59), kind=kLoop, calls=%fused_computation.35 | loop fusion | flops 90112 | bytes 1081345 | tf_op jit(solution)/shard_map/cond/branch_1_fun/jit(_where)/select_n | solution.py:865
  35.7 1.5 %collective-permute-start.12 = (f32[144,1536]{1,0:T(8,128)S(1)}, f32[144,1536]{1,0:T(8,128)S(1)}, u32[]{:S(2)}, u32[]{:S(2)}) collective-permute-start(f32[144,1536]{1,0:T(8,128)S(1)} %get-tuple-element.59), channel_id=1, source_target_pairs={{0,16},{8,24},{16,0},{24,8},{1,17},{9,25},{17,1},{25,9},{2,18},{10... | collective-permute-start | bytes 2654216 | tf_op jit(solution)/shard_map/cond/branch_1_fun/ppermute | solution.py:844
  37.2 1.5 %collective-permute-start.13 = (f32[144,1536]{1,0:T(8,128)S(1)}, f32[144,1536]{1,0:T(8,128)S(1)}, u32[]{:S(2)}, u32[]{:S(2)}) collective-permute-start(f32[144,1536]{1,0:T(8,128)S(1)} %get-tuple-element.60), channel_id=1, source_target_pairs={{0,8},{8,0},{16,24},{24,16},{1,9},{9,1},{17,25},{25,17},{2,10},{10... | collective-permute-start | bytes 2654216 | tf_op jit(solution)/shard_map/cond/branch_1_fun/ppermute | solution.py:844
  38.7 1.3 %collective-permute-start.11 = (f32[352,256]{1,0:T(8,128)S(1)}, f32[352,256]{1,0:T(8,128)S(1)}, u32[]{:S(2)}, u32[]{:S(2)}) collective-permute-start(f32[352,256]{1,0:T(8,128)S(1)} %broadcast_select_fusion.3.first_ref.square_ref), channel_id=1, source_target_pairs={{0,1},{2,3},{4,5},{6,7},{8,9},{10,11},{12,13},{14,15},{16,17},{18,... | collective-permute-start | bytes 1081352 | tf_op jit(solution)/shard_map/cond/branch_1_fun/ppermute | solution.py:874
  40.1 28.9 %collective-permute-done.11.second_ref.square_new_ref = f32[352,256]{1,0:T(8,128)S(1)} collective-permute-done((f32[352,256]{1,0:T(8,128)S(1)}, f32[352,256]{1,0:T(8,128)S(1)}, u32[]{:S(2)}, u32[]{:S(2)}) %collective-permute-start.11) | collective-permute-done | bytes 360480 | tf_op jit(solution)/shard_map/cond/branch_1_fun/ppermute | solution.py:874
  69.0 12.9 %factor.3 = (f32[256,256]{1,0:T(8,128)S(1)}, f32[256,256]{1,0:T(8,128)S(1)}, f32[256,256]{1,0:T(8,128)S(1)}) custom-call(f32[352,256]{1,0:T(8,128)S(1)} %broadcast_select_fusion.3.first_ref.square_ref, f32[352,256]{1,0:T(8,128)S(1)} %collective-permute-done.11.second_ref.square_new_ref), custom_call_target="tpu_custom_call" | custom-call | flops 67108864 | bytes 50000000 | tf_op jit(solution)/shard_map/cond/branch_1_fun/factor/pallas_call | solution.py:155
  81.9 15.7 %finish.1 = f32[1024,1,1536]{2,1,0:T(1,128)} custom-call(s32[96]{0:T(128)S(1)} %select_reduce_fusion.mine_ref, s32[4]{0:T(128)S(1)} %convert_reduce_fusion.1.counts_ref, s32[256,128]{1,0:T(8,128)S(1)} %copy-done.11, f32[1024,1,1536]{2,1,0:T(1,128)S(1)} %bitcast.27, f32[1024,256]{1,0:T(8,128)S(1)} %select_select_fusion.panel_ref, ...), custom_call_target="tpu_custom_call" | custom-call | flops 2415919104 | bytes 12582912 | tf_op jit(solution)/shard_map/cond/branch_1_fun/finish/pallas_call | solution.py:783
  (35 shorter events, 2.0 us)
Async XLA Ops:
  0.0 4.5 %copy-start.13 = (s32[256]{0:T(256)S(1)}, s32[256]{0:T(256)}, u32[]{:S(2)}) copy-start(s32[256]{0:T(256)} %param.5) | copy-start | bytes 3076
  4.8 9.2 %copy-start.10 = (s32[256,128]{1,0:T(8,128)}, s32[256,128]{1,0:T(8,128)S(1)}, u32[]{:S(2)}) copy-start(s32[256,128]{1,0:T(8,128)S(1)} %get-tuple-element.34.wide_ref) | copy-start | bytes 393220 | tf_op jit(solution)/shard_map/cond
  4.8 10.0 %collective-permute-start.4 = (f32[1024,256]{1,0:T(8,128)}, f32[1024,256]{1,0:T(8,128)S(1)}, u32[]{:S(2)}, u32[]{:S(2)}) collective-permute-start(f32[1024,256]{1,0:T(8,128)} %get-tuple-element.44), channel_id=1, source_target_pairs={{0,2},{8,10},{16,18},{24,26}} | collective-permute-start | bytes 3145736 | tf_op jit(solution)/shard_map/cond/branch_1_fun/ppermute | solution.py:849
  5.5 9.3 %collective-permute-start.3 = (f32[1024,256]{1,0:T(8,128)}, f32[1024,256]{1,0:T(8,128)}, u32[]{:S(2)}, u32[]{:S(2)}) collective-permute-start(f32[1024,256]{1,0:T(8,128)} %get-tuple-element.44), channel_id=1, source_target_pairs={{0,4},{8,12},{16,20},{24,28}} | collective-permute-start | bytes 3145736 | tf_op jit(solution)/shard_map/cond/branch_1_fun/ppermute | solution.py:849
  7.2 6.7 %collective-permute-start = (f32[192,256]{1,0:T(8,128)}, f32[192,256]{1,0:T(8,128)S(1)}, u32[]{:S(2)}, u32[]{:S(2)}) collective-permute-start(f32[192,256]{1,0:T(8,128)} %get-tuple-element.37), channel_id=1, source_target_pairs={{0,8},{8,0},{16,24},{24,16}} | collective-permute-start | bytes 589832 | tf_op jit(solution)/shard_map/cond/branch_1_fun/ppermute | solution.py:837
  7.9 6.1 %collective-permute-start.1 = (f32[192,256]{1,0:T(8,128)}, f32[192,256]{1,0:T(8,128)S(1)}, u32[]{:S(2)}, u32[]{:S(2)}) collective-permute-start(f32[192,256]{1,0:T(8,128)} %get-tuple-element.38), channel_id=1, source_target_pairs={{0,16},{8,24},{16,0},{24,8}} | collective-permute-start | bytes 589832 | tf_op jit(solution)/shard_map/cond/branch_1_fun/ppermute | solution.py:837
  8.5 5.4 %collective-permute-start.2 = (f32[192,256]{1,0:T(8,128)}, f32[192,256]{1,0:T(8,128)S(1)}, u32[]{:S(2)}, u32[]{:S(2)}) collective-permute-start(f32[192,256]{1,0:T(8,128)} %get-tuple-element.39), channel_id=1, source_target_pairs={{0,24},{8,16},{16,8},{24,0}} | collective-permute-start | bytes 589832 | tf_op jit(solution)/shard_map/cond/branch_1_fun/ppermute | solution.py:837
  9.6 4.4 %copy-start.12 = (f32[192,256]{1,0:T(8,128)S(1)}, f32[192,256]{1,0:T(8,128)}, u32[]{:S(2)}) copy-start(f32[192,256]{1,0:T(8,128)} %get-tuple-element.36.refs_0_) | copy-start | bytes 589828 | tf_op jit(solution)/shard_map/cond
  14.8 1.7 %copy-start.8 = (f32[1024,256]{1,0:T(8,128)}, f32[1024,256]{1,0:T(8,128)S(1)}, u32[]{:S(2)}) copy-start(f32[1024,256]{1,0:T(8,128)S(1)} %collective-permute-done.4) | copy-start | bytes 3145732 | tf_op jit(solution)/shard_map/cond
  14.8 8.3 %collective-permute-start.6 = (f32[1024,256]{1,0:T(8,128)}, f32[1024,256]{1,0:T(8,128)}, u32[]{:S(2)}, u32[]{:S(2)}) collective-permute-start(f32[1024,256]{1,0:T(8,128)} %collective-permute-done.3), channel_id=1, source_target_pairs={{4,6},{12,14},{20,22},{28,30}} | collective-permute-start | bytes 3145736 | tf_op jit(solution)/shard_map/cond/branch_1_fun/ppermute | solution.py:864
  16.5 12.5 %collective-permute-start.9 = (f32[144,1536]{1,0:T(8,128)}, f32[144,1536]{1,0:T(8,128)S(1)}, u32[]{:S(2)}, u32[]{:S(2)}) collective-permute-start(f32[144,1536]{1,0:T(8,128)} %get-tuple-element.51), channel_id=1, source_target_pairs={{0,8},{8,0},{16,24},{24,16},{1,9},{9,1},{17,25},{25,17},{2,10},{10... | collective-permute-start | bytes 2654216 | tf_op jit(solution)/shard_map/cond/branch_1_fun/ppermute | solution.py:844
  16.9 14.0 %collective-permute-start.10 = (f32[144,1536]{1,0:T(8,128)}, f32[144,1536]{1,0:T(8,128)S(1)}, u32[]{:S(2)}, u32[]{:S(2)}) collective-permute-start(f32[144,1536]{1,0:T(8,128)} %get-tuple-element.52), channel_id=1, source_target_pairs={{0,16},{8,24},{16,0},{24,8},{1,17},{9,25},{17,1},{25,9},{2,18},{10... | collective-permute-start | bytes 2654216 | tf_op jit(solution)/shard_map/cond/branch_1_fun/ppermute | solution.py:844
  19.9 1.4 %collective-permute-start.5 = (f32[352,256]{1,0:T(8,128)}, f32[352,256]{1,0:T(8,128)}, u32[]{:S(2)}, u32[]{:S(2)}) collective-permute-start(f32[352,256]{1,0:T(8,128)} %pack.1), channel_id=1, source_target_pairs={{0,4},{8,12},{16,20},{24,28}} | collective-permute-start | bytes 1081352 | tf_op jit(solution)/shard_map/cond/branch_1_fun/ppermute | solution.py:865
  23.1 11.5 %collective-permute-start.8 = (f32[352,256]{1,0:T(8,128)}, f32[352,256]{1,0:T(8,128)}, u32[]{:S(2)}, u32[]{:S(2)}) collective-permute-start(f32[352,256]{1,0:T(8,128)} %broadcast_select_fusion.4), channel_id=1, source_target_pairs={{0,2},{4,6},{8,10},{12,14},{16,18},{20,22},{24,26},{28,30}} | collective-permute-start | bytes 1081352 | tf_op jit(solution)/shard_map/cond/branch_1_fun/ppermute | solution.py:865
  24.5 6.9 %copy-start.7 = (f32[1024,256]{1,0:T(8,128)S(1)}, f32[1024,256]{1,0:T(8,128)}, u32[]{:S(2)}) copy-start(f32[1024,256]{1,0:T(8,128)} %get-tuple-element.44) | copy-start | bytes 3145732 | tf_op jit(solution)/shard_map/cond
  24.5 6.9 %copy-start.9 = (f32[1024,256]{1,0:T(8,128)S(1)}, f32[1024,256]{1,0:T(8,128)}, u32[]{:S(2)}) copy-start(f32[1024,256]{1,0:T(8,128)} %copy-done.8) | copy-start | bytes 3145732 | tf_op jit(solution)/shard_map/cond
  31.4 50.5 %copy-start.3 = (f32[1,1024,1,1536]{3,2,1,0:T(1,128)S(1)}, f32[1,1024,1,1536]{3,2,1,0:T(1,128)}, u32[]{:S(2)}) copy-start(f32[1,1024,1,1536]{3,2,1,0:T(1,128)} %get-tuple-element.35) | copy-start | bytes 18874372 | tf_op jit(solution)/shard_map/cond
  33.2 48.7 %copy-start.11 = (s32[256,128]{1,0:T(8,128)S(1)}, s32[256,128]{1,0:T(8,128)}, u32[]{:S(2)}) copy-start(s32[256,128]{1,0:T(8,128)} %copy-done.10) | copy-start | bytes 393220 | tf_op jit(solution)/shard_map/cond
  33.2 48.6 %collective-permute-start.7 = (f32[1024,256]{1,0:T(8,128)S(1)}, f32[1024,256]{1,0:T(8,128)S(1)}, u32[]{:S(2)}, u32[]{:S(2)}) collective-permute-start(f32[1024,256]{1,0:T(8,128)S(1)} %select_select_fusion.panel_ref), channel_id=1, source_target_pairs={{0,1},{2,3},{4,5},{6,7},{8,9},{10,11},{12,13},{14,15},{16,17},{18,... | collective-permute-start | bytes 3145736 | tf_op jit(solution)/shard_map/cond/branch_1_fun/ppermute | solution.py:870
  35.7 46.2 %collective-permute-start.12 = (f32[144,1536]{1,0:T(8,128)S(1)}, f32[144,1536]{1,0:T(8,128)S(1)}, u32[]{:S(2)}, u32[]{:S(2)}) collective-permute-start(f32[144,1536]{1,0:T(8,128)S(1)} %get-tuple-element.59), channel_id=1, source_target_pairs={{0,16},{8,24},{16,0},{24,8},{1,17},{9,25},{17,1},{25,9},{2,18},{10... | collective-permute-start | bytes 2654216 | tf_op jit(solution)/shard_map/cond/branch_1_fun/ppermute | solution.py:844
  37.2 44.6 %collective-permute-start.13 = (f32[144,1536]{1,0:T(8,128)S(1)}, f32[144,1536]{1,0:T(8,128)S(1)}, u32[]{:S(2)}, u32[]{:S(2)}) collective-permute-start(f32[144,1536]{1,0:T(8,128)S(1)} %get-tuple-element.60), channel_id=1, source_target_pairs={{0,8},{8,0},{16,24},{24,16},{1,9},{9,1},{17,25},{25,17},{2,10},{10... | collective-permute-start | bytes 2654216 | tf_op jit(solution)/shard_map/cond/branch_1_fun/ppermute | solution.py:844
  38.7 30.3 %collective-permute-start.11 = (f32[352,256]{1,0:T(8,128)S(1)}, f32[352,256]{1,0:T(8,128)S(1)}, u32[]{:S(2)}, u32[]{:S(2)}) collective-permute-start(f32[352,256]{1,0:T(8,128)S(1)} %broadcast_select_fusion.3.first_ref.square_ref), channel_id=1, source_target_pairs={{0,1},{2,3},{4,5},{6,7},{8,9},{10,11},{12,13},{14,15},{16,17},{18,... | collective-permute-start | bytes 1081352 | tf_op jit(solution)/shard_map/cond/branch_1_fun/ppermute | solution.py:874

commit v10 on v8

--- a/solution.py
+++ b/solution.py
@@ -20,7 +20,7 @@
     return jnp.broadcast_to(tile[j:j + 1, :], (SUB, LANES))
 
 
-def factor_kernel(width, first_ref, second_ref, packed_ref, linv_ref, uinv_ref, a_ref, m_ref, v_ref, s_ref, sem):
+def factor_kernel(width, unroll, first_ref, second_ref, packed_ref, linv_ref, uinv_ref, a_ref, m_ref, v_ref, s_ref, sem):
     groups = a_ref.shape[0]
     tiles = groups * SUB // LANES
     per_tile = LANES // SUB
@@ -107,7 +107,7 @@
                     ref[r, :, span(t)] = x - acc[0]
             return c
 
-        lax.fori_loop(0, per_block, panel, 0)
+        lax.fori_loop(0, per_block, panel, 0, unroll=unroll)
 
         lo = (base % per_tile) * SUB
         pad = [jnp.zeros((n, LANES), jnp.float32) for n in (lo, LANES - lo - width)]
@@ -149,11 +149,11 @@
     return pl.BlockSpec(memory_space=pltpu.SMEM)
 
 
-def factor(square, extra, width=32):
+def factor(square, extra, unroll, width=32):
     size = square.shape[1]
     out = jax.ShapeDtypeStruct((size, size), jnp.float32)
     return pl.pallas_call(
-        functools.partial(factor_kernel, width),
+        functools.partial(factor_kernel, width, unroll),
         out_shape=(out, out, out),
         in_specs=[raw(), raw()],
         out_specs=(vmem(),) * 3,
@@ -165,7 +165,7 @@
             pltpu.SemaphoreType.DMA((2,)),
         ],
         cost_estimate=pl.CostEstimate(flops=4 * size**3, bytes_accessed=50_000_000, transcendentals=0),
-        compiler_params=pltpu.CompilerParams(vmem_limit_bytes=6 << 20),
+        compiler_params=pltpu.CompilerParams(vmem_limit_bytes=10 << 20),
         name="factor",
     )(square, extra)
 
@@ -356,7 +356,7 @@
     square = pick(block, slot, owned * at_first_col.astype(jnp.int32), 1)
     square = sum_over_rows(square, row_bits, n_row)
     square = spread_cols(square, col_bits[::-1])
-    packed, linv, uinv = factor(square, jnp.zeros_like(square))
+    packed, linv, uinv = factor(square, jnp.zeros_like(square), False)
 
     top = jnp.where(at_first_row, block[:width], 0.0)
     top_panel = spread_rows(top[:, :width], row_bits, n_row)
@@ -466,12 +466,15 @@
             pltpu.make_async_copy(mat_ref.at[mine_ref[i]], own.at[pl.ds(i, 1), :], sem.at[0]).start()
         return c
 
+    @pl.when(lax.axis_index("prow") == 0)
+    def _():
+        pltpu.make_async_copy(mat_ref.at[pl.ds(0, width), 0, :], block, sem.at[1]).start()
+
     lax.fori_loop(0, count // SUB, group, 0)
 
     @pl.when(lax.axis_index("prow") == 0)
     def _():
         copy = pltpu.make_async_copy(mat_ref.at[pl.ds(0, width), 0, :], block, sem.at[1])
-        copy.start()
         owner, rank = owners(pivot_ref[...], n_row)
         ordinal = lax.broadcasted_iota(jnp.int32, (count, width), 0)
         choices = [jnp.where((ordinal == rank) & (owner == p), 1.0, 0.0) for p in range(n_row)]
@@ -488,7 +491,7 @@
                         ref[pl.ds(base, half), at] = tops[first:first + half]
             return c
 
-        lax.fori_loop(0, cols // width, piece, 0)
+        lax.fori_loop(0, cols // width, piece, 0, unroll=True)
 
     pltpu.make_async_copy(mat_ref.at[pl.ds(0, count), 0, :], own, sem.at[0]).wait()
     if n_row == 4:
@@ -868,7 +871,7 @@
         message, to_y, to_x = lax.optimization_barrier((message, to_y, to_x))
         arrived += [send(to_y, 2), send(to_x, 1)]
     message_new = lax.ppermute(message, "pcol", pairs[-1])
-    factors = factor(message, message_new)
+    factors = factor(message, message_new, True)
     out = finish(
         mine, counts, wide, mat, (panel, panel_moved), (message, message_new), factors, arrived
     )

time: 86.8 us -> 83 us (0.956)
  the two profiles are of different devices: /device:TPU:27 before, /device:TPU:0 now
where the time goes in v10:
time: 83 us; the launch traced here: 81.4 us
  Pallas kernels  30.3 us (37%)
  starting transfers between devices  25.7 us (31%)
  waiting for transfers between devices  19.9 us (24%)
  other arithmetic  2.54 us (3%)
  local copies, waits for them, and re-layouts  1.64 us (2%)
  between operations  0.85 us (1%)
    ppermute x2, waiting for transfers between devices, capped_step(): lax.ppermute(message, 'pcol', pairs[n])  14.6 us
    pallas_call x1, Pallas kernels, finish(): pl.pallas_call(functools.partial(finish_kernel, n_row), out_shape=jax.Sha...  11 us
    ppermute x3, starting transfers between devices, exchange(): lax.ppermute(x, both, [(i * n_col, (i ^ k) * n_col) for i in range(n_row)])  9.21 us
    pallas_call x1, Pallas kernels, factor(): pl.pallas_call(functools.partial(factor_kernel, width, unroll), out_shape...  9.08 us
    ppermute x1, starting transfers between devices, capped_step(): lax.ppermute(panel, 'pcol', [(i, i + turns[0]) for i in range(0, n_col, 2...  6 us
    pallas_call x1, Pallas kernels, parcel(): pl.pallas_call(functools.partial(parcel_kernel, n_row), out_shape=tuple((...  4.39 us
    pallas_call x1, Pallas kernels, begin(): pl.pallas_call(functools.partial(begin_kernel, n_row), out_shape=(jax.Sha...  4.28 us
    ppermute x2, starting transfers between devices, capped_step(): lax.ppermute(message, 'pcol', pairs[n])  3.31 us
  transfers between devices with their start and end apart: 13, of which 6 were waited for; matrix products, arithmetic and copies ran while one was open for 3% of the time, Pallas kernels for 18%

profile of v10, /device:TPU:0, one launch (start us, length us, event | category | flops | bytes accessed | tf_op | source)
XLA Modules:
  0.0 81.4 jit_solution(13343462383085013803)
XLA Ops:
  0.0 4.3 %begin.1 = (f32[1024,256]{1,0:T(8,128)}, s32[256,128]{1,0:T(8,128)S(1)}, s32[1]{0:T(128)}, f32[192,256]{1,0:T(8,128)}, f32[192,256]{1,0:T(8,128)}, /*index=5*/f32[192,256]{1,0:T(8,128)}, f32[192,256]{1,0:T(8,128)}) custom-call(s32[1,256]{1,0:T(1,128)} %bitcast.29, f32[1024,1,1536]{2,1,0:T(1,128)} %bitcast.25), custom_call_target="tpu_custom_call" | custom-call | bytes 10000000 | tf_op jit(solution)/shard_map/begin/pallas_call | solution.py:441
  5.0 76.3 %conditional.1 = (f32[1,1024,1,1536]{3,2,1,0:T(1,128)}) conditional(s32[]{:T(128)} %bitcast.12, (s32[256]{0:T(256)S(1)}, f32[1,1024,1,1536]{3,2,1,0:T(1,128)}) %tuple.34, (s32[256]{0:T(256)S(1)}, f32[1,1024,1,1536]{3,2,1,0:T(1,128)}, f32[192,256]{1,0:T(8,128)}, f32[192,256]{1,0:T(8,128)}, f32[192,256]{1,0:T(8,128)}, ...), branch_computations={%region_0.1_spmd, %region_1.5_spmd} | conditional | flops 2488416000 | bytes 214372192 | solution.py:884
  5.2 6.0 %collective-permute-start.3 = (f32[1024,256]{1,0:T(8,128)}, f32[1024,256]{1,0:T(8,128)S(1)}, u32[]{:S(2)}, u32[]{:S(2)}) collective-permute-start(f32[1024,256]{1,0:T(8,128)} %get-tuple-element.44), channel_id=1, source_target_pairs={{0,4},{8,12},{16,20},{24,28}} | collective-permute-start | bytes 3145736 | tf_op jit(solution)/shard_map/cond/branch_1_fun/ppermute | solution.py:852
  11.2 3.0 %collective-permute-start = (f32[192,256]{1,0:T(8,128)}, f32[192,256]{1,0:T(8,128)S(1)}, u32[]{:S(2)}, u32[]{:S(2)}) collective-permute-start(f32[192,256]{1,0:T(8,128)} %get-tuple-element.37), channel_id=1, source_target_pairs={{0,8},{8,0},{16,24},{24,16}} | collective-permute-start | bytes 589832 | tf_op jit(solution)/shard_map/cond/branch_1_fun/ppermute | solution.py:840
  14.2 3.4 %collective-permute-start.1 = (f32[192,256]{1,0:T(8,128)}, f32[192,256]{1,0:T(8,128)S(1)}, u32[]{:S(2)}, u32[]{:S(2)}) collective-permute-start(f32[192,256]{1,0:T(8,128)} %get-tuple-element.38), channel_id=1, source_target_pairs={{0,16},{8,24},{16,0},{24,8}} | collective-permute-start | bytes 589832 | tf_op jit(solution)/shard_map/cond/branch_1_fun/ppermute | solution.py:840
  17.6 2.8 %collective-permute-start.2 = (f32[192,256]{1,0:T(8,128)}, f32[192,256]{1,0:T(8,128)S(1)}, u32[]{:S(2)}, u32[]{:S(2)}) collective-permute-start(f32[192,256]{1,0:T(8,128)} %get-tuple-element.39), channel_id=1, source_target_pairs={{0,24},{8,16},{16,8},{24,0}} | collective-permute-start | bytes 589832 | tf_op jit(solution)/shard_map/cond/branch_1_fun/ppermute | solution.py:840
  20.8 4.4 %parcel.1 = (f32[144,1536]{1,0:T(8,128)}, f32[144,1536]{1,0:T(8,128)}, f32[288,1536]{1,0:T(8,128)S(1)}) custom-call(s32[96]{0:T(128)S(1)} %select_reduce_fusion.mine_ref, s32[1,256]{1,0:T(1,128)S(1)} %bitcast.30, f32[1024,1,1536]{2,1,0:T(1,128)} %bitcast.26), custom_call_target="tpu_custom_call" | custom-call | bytes 16000000 | tf_op jit(solution)/shard_map/cond/branch_1_fun/parcel/pallas_call | solution.py:535
  25.2 3.2 %collective-permute-done.2.refs_3_ = f32[192,256]{1,0:T(8,128)S(1)} collective-permute-done((f32[192,256]{1,0:T(8,128)}, f32[192,256]{1,0:T(8,128)S(1)}, u32[]{:S(2)}, u32[]{:S(2)}) %collective-permute-start.2) | collective-permute-done | bytes 196640 | tf_op jit(solution)/shard_map/cond/branch_1_fun/ppermute | solution.py:840
  28.5 1.1 %pack.1 = f32[352,256]{1,0:T(8,128)S(1)} custom-call(s32[256,128]{1,0:T(8,128)S(1)} %get-tuple-element.34.wide_ref, f32[192,256]{1,0:T(8,128)S(1)} %copy-done.13, f32[192,256]{1,0:T(8,128)S(1)} %collective-permute-done.refs_1_, f32[192,256]{1,0:T(8,128)S(1)} %collective-permute-done.1.refs_2_, f32[192,256]{1,0:T(8,128)S(1)} %collective-permute-done.2.refs_3_), custom_call_target="tpu_custom_call" | custom-call | bytes 4000000 | tf_op jit(solution)/shard_map/cond/branch_1_fun/pack/pallas_call | solution.py:639
  29.8 1.4 %collective-permute-start.5 = (f32[1024,256]{1,0:T(8,128)S(1)}, f32[1024,256]{1,0:T(8,128)S(1)}, u32[]{:S(2)}, u32[]{:S(2)}) collective-permute-start(f32[1024,256]{1,0:T(8,128)S(1)} %broadcast_select_fusion.3), channel_id=1, source_target_pairs={{0,2},{4,6},{8,10},{12,14},{16,18},{20,22},{24,26},{28,30}} | collective-permute-start | bytes 3145736 | tf_op jit(solution)/shard_map/cond/branch_1_fun/ppermute | solution.py:866
  31.8 0.9 %collective-permute-start.9 = (f32[144,1536]{1,0:T(8,128)}, f32[144,1536]{1,0:T(8,128)S(1)}, u32[]{:S(2)}, u32[]{:S(2)}) collective-permute-start(f32[144,1536]{1,0:T(8,128)} %get-tuple-element.51), channel_id=1, source_target_pairs={{0,16},{8,24},{16,0},{24,8},{1,17},{9,25},{17,1},{25,9},{2,18},{10... | collective-permute-start | bytes 2654216 | tf_op jit(solution)/shard_map/cond/branch_1_fun/ppermute | solution.py:847
  32.7 1.3 %collective-permute-start.4 = (f32[352,256]{1,0:T(8,128)S(1)}, f32[352,256]{1,0:T(8,128)S(1)}, u32[]{:S(2)}, u32[]{:S(2)}) collective-permute-start(f32[352,256]{1,0:T(8,128)S(1)} %pack.1), channel_id=1, source_target_pairs={{0,4},{8,12},{16,20},{24,28}} | collective-permute-start | bytes 1081352 | tf_op jit(solution)/shard_map/cond/branch_1_fun/ppermute | solution.py:867
  34.0 13.3 %collective-permute-done.4 = f32[352,256]{1,0:T(8,128)S(1)} collective-permute-done((f32[352,256]{1,0:T(8,128)S(1)}, f32[352,256]{1,0:T(8,128)S(1)}, u32[]{:S(2)}, u32[]{:S(2)}) %collective-permute-start.4) | collective-permute-done | bytes 360480 | tf_op jit(solution)/shard_map/cond/branch_1_fun/ppermute | solution.py:867
  47.3 0.8 broadcast_select_fusion.6
  48.0 1.0 %copy-done.9 = f32[1024,256]{1,0:T(8,128)} copy-done((f32[1024,256]{1,0:T(8,128)}, f32[1024,256]{1,0:T(8,128)S(1)}, u32[]{:S(2)}) %copy-start.9) | copy-done | bytes 1048600 | tf_op jit(solution)/shard_map/cond
  49.0 2.0 %collective-permute-start.7 = (f32[352,256]{1,0:T(8,128)}, f32[352,256]{1,0:T(8,128)}, u32[]{:S(2)}, u32[]{:S(2)}) collective-permute-start(f32[352,256]{1,0:T(8,128)} %broadcast_select_fusion.6), channel_id=1, source_target_pairs={{0,2},{4,6},{8,10},{12,14},{16,18},{20,22},{24,26},{28,30}} | collective-permute-start | bytes 1081352 | tf_op jit(solution)/shard_map/cond/branch_1_fun/ppermute | solution.py:867
  52.7 1.5 %collective-permute-start.6 = (f32[1024,256]{1,0:T(8,128)S(1)}, f32[1024,256]{1,0:T(8,128)S(1)}, u32[]{:S(2)}, u32[]{:S(2)}) collective-permute-start(f32[1024,256]{1,0:T(8,128)S(1)} %broadcast_select_fusion.4.panel_ref), channel_id=1, source_target_pairs={{0,1},{2,3},{4,5},{6,7},{8,9},{10,11},{12,13},{14,15},{16,17},{18,... | collective-permute-start | bytes 3145736 | tf_op jit(solution)/shard_map/cond/branch_1_fun/ppermute | solution.py:866
  54.2 1.3 %collective-permute-done.7 = f32[352,256]{1,0:T(8,128)} collective-permute-done((f32[352,256]{1,0:T(8,128)}, f32[352,256]{1,0:T(8,128)}, u32[]{:S(2)}, u32[]{:S(2)}) %collective-permute-start.7) | collective-permute-done | bytes 360480 | tf_op jit(solution)/shard_map/cond/branch_1_fun/ppermute | solution.py:867
  55.5 1.0 %broadcast_select_fusion.5.first_ref.square_ref = f32[352,256]{1,0:T(8,128)S(1)} fusion(f32[352,256]{1,0:T(8,128)} %collective-permute-done.7, f32[352,256]{1,0:T(8,128)} %broadcast_select_fusion.6, pred[]{:T(512)S(6)} %ne.59), kind=kLoop, calls=%fused_computation.36 | loop fusion | flops 90112 | bytes 1081345 | tf_op jit(solution)/shard_map/cond/branch_1_fun/jit(_where)/select_n | solution.py:867
  57.2 0.9 %collective-permute-start.12 = (f32[144,1536]{1,0:T(8,128)S(1)}, f32[144,1536]{1,0:T(8,128)S(1)}, u32[]{:S(2)}, u32[]{:S(2)}) collective-permute-start(f32[144,1536]{1,0:T(8,128)S(1)} %get-tuple-element.59), channel_id=1, source_target_pairs={{0,8},{8,0},{16,24},{24,16},{1,9},{9,1},{17,25},{25,17},{2,10},{10... | collective-permute-start | bytes 2654216 | tf_op jit(solution)/shard_map/cond/branch_1_fun/ppermute | solution.py:847
  58.1 1.3 %collective-permute-start.10 = (f32[352,256]{1,0:T(8,128)S(1)}, f32[352,256]{1,0:T(8,128)S(1)}, u32[]{:S(2)}, u32[]{:S(2)}) collective-permute-start(f32[352,256]{1,0:T(8,128)S(1)} %broadcast_select_fusion.5.first_ref.square_ref), channel_id=1, source_target_pairs={{0,1},{2,3},{4,5},{6,7},{8,9},{10,11},{12,13},{14,15},{16,17},{18,... | collective-permute-start | bytes 1081352 | tf_op jit(solution)/shard_map/cond/branch_1_fun/ppermute | solution.py:873
  59.5 1.1 %collective-permute-done.10.second_ref.square_new_ref = f32[352,256]{1,0:T(8,128)S(1)} collective-permute-done((f32[352,256]{1,0:T(8,128)S(1)}, f32[352,256]{1,0:T(8,128)S(1)}, u32[]{:S(2)}, u32[]{:S(2)}) %collective-permute-start.10) | collective-permute-done | bytes 360480 | tf_op jit(solution)/shard_map/cond/branch_1_fun/ppermute | solution.py:873
  60.7 9.1 %factor.3 = (f32[256,256]{1,0:T(8,128)S(1)}, f32[256,256]{1,0:T(8,128)S(1)}, f32[256,256]{1,0:T(8,128)S(1)}) custom-call(f32[352,256]{1,0:T(8,128)S(1)} %broadcast_select_fusion.5.first_ref.square_ref, f32[352,256]{1,0:T(8,128)S(1)} %collective-permute-done.10.second_ref.square_new_ref), custom_call_target="tpu_custom_call" | custom-call | flops 67108864 | bytes 50000000 | tf_op jit(solution)/shard_map/cond/branch_1_fun/factor/pallas_call | solution.py:155
  70.2 11.0 %finish.1 = f32[1024,1,1536]{2,1,0:T(1,128)} custom-call(s32[96]{0:T(128)S(1)} %select_reduce_fusion.mine_ref, s32[4]{0:T(128)S(1)} %convert_reduce_fusion.1.counts_ref, s32[256,128]{1,0:T(8,128)S(1)} %copy-done.12, f32[1024,1,1536]{2,1,0:T(1,128)} %bitcast.27, f32[1024,256]{1,0:T(8,128)S(1)} %broadcast_select_fusion.4.panel_ref, ...), custom_call_target="tpu_custom_call" | custom-call | flops 2415919104 | bytes 12582912 | tf_op jit(solution)/shard_map/cond/branch_1_fun/finish/pallas_call | solution.py:786
  (36 shorter events, 3.9 us)
Async XLA Ops:
  0.0 4.9 %copy-start.14 = (s32[256]{0:T(256)S(1)}, s32[256]{0:T(256)}, u32[]{:S(2)}) copy-start(s32[256]{0:T(256)} %param.5) | copy-start | bytes 3076
  5.2 23.3 %copy-start.11 = (s32[256,128]{1,0:T(8,128)}, s32[256,128]{1,0:T(8,128)S(1)}, u32[]{:S(2)}) copy-start(s32[256,128]{1,0:T(8,128)S(1)} %get-tuple-element.34.wide_ref) | copy-start | bytes 393220 | tf_op jit(solution)/shard_map/cond
  5.2 24.4 %collective-permute-start.3 = (f32[1024,256]{1,0:T(8,128)}, f32[1024,256]{1,0:T(8,128)S(1)}, u32[]{:S(2)}, u32[]{:S(2)}) collective-permute-start(f32[1024,256]{1,0:T(8,128)} %get-tuple-element.44), channel_id=1, source_target_pairs={{0,4},{8,12},{16,20},{24,28}} | collective-permute-start | bytes 3145736 | tf_op jit(solution)/shard_map/cond/branch_1_fun/ppermute | solution.py:852
  11.2 14.0 %collective-permute-start = (f32[192,256]{1,0:T(8,128)}, f32[192,256]{1,0:T(8,128)S(1)}, u32[]{:S(2)}, u32[]{:S(2)}) collective-permute-start(f32[192,256]{1,0:T(8,128)} %get-tuple-element.37), channel_id=1, source_target_pairs={{0,8},{8,0},{16,24},{24,16}} | collective-permute-start | bytes 589832 | tf_op jit(solution)/shard_map/cond/branch_1_fun/ppermute | solution.py:840
  14.2 11.0 %collective-permute-start.1 = (f32[192,256]{1,0:T(8,128)}, f32[192,256]{1,0:T(8,128)S(1)}, u32[]{:S(2)}, u32[]{:S(2)}) collective-permute-start(f32[192,256]{1,0:T(8,128)} %get-tuple-element.38), channel_id=1, source_target_pairs={{0,16},{8,24},{16,0},{24,8}} | collective-permute-start | bytes 589832 | tf_op jit(solution)/shard_map/cond/branch_1_fun/ppermute | solution.py:840
  17.6 10.8 %collective-permute-start.2 = (f32[192,256]{1,0:T(8,128)}, f32[192,256]{1,0:T(8,128)S(1)}, u32[]{:S(2)}, u32[]{:S(2)}) collective-permute-start(f32[192,256]{1,0:T(8,128)} %get-tuple-element.39), channel_id=1, source_target_pairs={{0,24},{8,16},{16,8},{24,0}} | collective-permute-start | bytes 589832 | tf_op jit(solution)/shard_map/cond/branch_1_fun/ppermute | solution.py:840
  20.8 7.7 %copy-start.13 = (f32[192,256]{1,0:T(8,128)S(1)}, f32[192,256]{1,0:T(8,128)}, u32[]{:S(2)}) copy-start(f32[192,256]{1,0:T(8,128)} %get-tuple-element.36.refs_0_) | copy-start | bytes 589828 | tf_op jit(solution)/shard_map/cond
  25.2 4.4 %copy-start.8 = (f32[1024,256]{1,0:T(8,128)S(1)}, f32[1024,256]{1,0:T(8,128)}, u32[]{:S(2)}) copy-start(f32[1024,256]{1,0:T(8,128)} %get-tuple-element.44) | copy-start | bytes 3145732 | tf_op jit(solution)/shard_map/cond
  29.8 18.3 %copy-start.5 = (f32[1024,256]{1,0:T(8,128)}, f32[1024,256]{1,0:T(8,128)S(1)}, u32[]{:S(2)}) copy-start(f32[1024,256]{1,0:T(8,128)S(1)} %broadcast_select_fusion.3) | copy-start | bytes 3145732 | tf_op jit(solution)/shard_map/cond
  29.8 18.3 %collective-permute-start.5 = (f32[1024,256]{1,0:T(8,128)S(1)}, f32[1024,256]{1,0:T(8,128)S(1)}, u32[]{:S(2)}, u32[]{:S(2)}) collective-permute-start(f32[1024,256]{1,0:T(8,128)S(1)} %broadcast_select_fusion.3), channel_id=1, source_target_pairs={{0,2},{4,6},{8,10},{12,14},{16,18},{20,22},{24,26},{28,30}} | collective-permute-start | bytes 3145736 | tf_op jit(solution)/shard_map/cond/branch_1_fun/ppermute | solution.py:866
  31.2 19.9 %collective-permute-start.8 = (f32[144,1536]{1,0:T(8,128)}, f32[144,1536]{1,0:T(8,128)S(1)}, u32[]{:S(2)}, u32[]{:S(2)}) collective-permute-start(f32[144,1536]{1,0:T(8,128)} %get-tuple-element.50), channel_id=1, source_target_pairs={{0,8},{8,0},{16,24},{24,16},{1,9},{9,1},{17,25},{25,17},{2,10},{10... | collective-permute-start | bytes 2654216 | tf_op jit(solution)/shard_map/cond/branch_1_fun/ppermute | solution.py:847
  31.8 19.7 %collective-permute-start.9 = (f32[144,1536]{1,0:T(8,128)}, f32[144,1536]{1,0:T(8,128)S(1)}, u32[]{:S(2)}, u32[]{:S(2)}) collective-permute-start(f32[144,1536]{1,0:T(8,128)} %get-tuple-element.51), channel_id=1, source_target_pairs={{0,16},{8,24},{16,0},{24,8},{1,17},{9,25},{17,1},{25,9},{2,18},{10... | collective-permute-start | bytes 2654216 | tf_op jit(solution)/shard_map/cond/branch_1_fun/ppermute | solution.py:847
  32.7 14.6 %collective-permute-start.4 = (f32[352,256]{1,0:T(8,128)S(1)}, f32[352,256]{1,0:T(8,128)S(1)}, u32[]{:S(2)}, u32[]{:S(2)}) collective-permute-start(f32[352,256]{1,0:T(8,128)S(1)} %pack.1), channel_id=1, source_target_pairs={{0,4},{8,12},{16,20},{24,28}} | collective-permute-start | bytes 1081352 | tf_op jit(solution)/shard_map/cond/branch_1_fun/ppermute | solution.py:867
  48.0 1.0 %copy-start.9 = (f32[1024,256]{1,0:T(8,128)}, f32[1024,256]{1,0:T(8,128)S(1)}, u32[]{:S(2)}) copy-start(f32[1024,256]{1,0:T(8,128)S(1)} %collective-permute-done.5) | copy-start | bytes 3145732 | tf_op jit(solution)/shard_map/cond
  49.0 6.5 %collective-permute-start.7 = (f32[352,256]{1,0:T(8,128)}, f32[352,256]{1,0:T(8,128)}, u32[]{:S(2)}, u32[]{:S(2)}) collective-permute-start(f32[352,256]{1,0:T(8,128)} %broadcast_select_fusion.6), channel_id=1, source_target_pairs={{0,2},{4,6},{8,10},{12,14},{16,18},{20,22},{24,26},{28,30}} | collective-permute-start | bytes 1081352 | tf_op jit(solution)/shard_map/cond/branch_1_fun/ppermute | solution.py:867
  51.0 1.2 %copy-start.6 = (f32[1024,256]{1,0:T(8,128)S(1)}, f32[1024,256]{1,0:T(8,128)}, u32[]{:S(2)}) copy-start(f32[1024,256]{1,0:T(8,128)} %copy-done.5) | copy-start | bytes 3145732 | tf_op jit(solution)/shard_map/cond
  51.0 1.5 %copy-start.10 = (f32[1024,256]{1,0:T(8,128)S(1)}, f32[1024,256]{1,0:T(8,128)}, u32[]{:S(2)}) copy-start(f32[1024,256]{1,0:T(8,128)} %copy-done.9) | copy-start | bytes 3145732 | tf_op jit(solution)/shard_map/cond
  52.7 17.5 %copy-start.12 = (s32[256,128]{1,0:T(8,128)S(1)}, s32[256,128]{1,0:T(8,128)}, u32[]{:S(2)}) copy-start(s32[256,128]{1,0:T(8,128)} %copy-done.11) | copy-start | bytes 393220 | tf_op jit(solution)/shard_map/cond
  52.7 17.0 %collective-permute-start.6 = (f32[1024,256]{1,0:T(8,128)S(1)}, f32[1024,256]{1,0:T(8,128)S(1)}, u32[]{:S(2)}, u32[]{:S(2)}) collective-permute-start(f32[1024,256]{1,0:T(8,128)S(1)} %broadcast_select_fusion.4.panel_ref), channel_id=1, source_target_pairs={{0,1},{2,3},{4,5},{6,7},{8,9},{10,11},{12,13},{14,15},{16,17},{18,... | collective-permute-start | bytes 3145736 | tf_op jit(solution)/shard_map/cond/branch_1_fun/ppermute | solution.py:866
  56.6 13.2 %collective-permute-start.11 = (f32[144,1536]{1,0:T(8,128)S(1)}, f32[144,1536]{1,0:T(8,128)S(1)}, u32[]{:S(2)}, u32[]{:S(2)}) collective-permute-start(f32[144,1536]{1,0:T(8,128)S(1)} %get-tuple-element.58), channel_id=1, source_target_pairs={{0,16},{8,24},{16,0},{24,8},{1,17},{9,25},{17,1},{25,9},{2,18},{10... | collective-permute-start | bytes 2654216 | tf_op jit(solution)/shard_map/cond/branch_1_fun/ppermute | solution.py:847
  57.2 13.0 %collective-permute-start.12 = (f32[144,1536]{1,0:T(8,128)S(1)}, f32[144,1536]{1,0:T(8,128)S(1)}, u32[]{:S(2)}, u32[]{:S(2)}) collective-permute-start(f32[144,1536]{1,0:T(8,128)S(1)} %get-tuple-element.59), channel_id=1, source_target_pairs={{0,8},{8,0},{16,24},{24,16},{1,9},{9,1},{17,25},{25,17},{2,10},{10... | collective-permute-start | bytes 2654216 | tf_op jit(solution)/shard_map/cond/branch_1_fun/ppermute | solution.py:847
  58.1 2.6 %collective-permute-start.10 = (f32[352,256]{1,0:T(8,128)S(1)}, f32[352,256]{1,0:T(8,128)S(1)}, u32[]{:S(2)}, u32[]{:S(2)}) collective-permute-start(f32[352,256]{1,0:T(8,128)S(1)} %broadcast_select_fusion.5.first_ref.square_ref), channel_id=1, source_target_pairs={{0,1},{2,3},{4,5},{6,7},{8,9},{10,11},{12,13},{14,15},{16,17},{18,... | collective-permute-start | bytes 1081352 | tf_op jit(solution)/shard_map/cond/branch_1_fun/ppermute | solution.py:873

commit v11 on v10

--- a/solution.py
+++ b/solution.py
@@ -861,11 +861,23 @@
 
     pairs = [[(i, i + bit) for i in range(0, n_col, 2 * bit)] for bit in turns + [1]]
     newer = [(col & bit) != 0 for bit in turns]
+    last = len(turns) - 1
     for n in range(len(turns)):
-        panel = jnp.where(newer[n], panel_moved, panel)
-        panel_moved = lax.ppermute(panel, "pcol", pairs[n + 1])
+        arrived_now = panel_moved
+        if n == last:
+            arrived_now = jnp.where(col == turns[n], back, panel_moved)
+        source = panel_moved if last == 1 else None
+        panel = jnp.where(newer[n], arrived_now, panel)
+        if n + 1 == last:
+            source = panel if source is None else source
+            panel_moved = lax.ppermute(source, "pcol", pairs[n + 1][1:])
+            back = lax.ppermute(source, "pcol", [(turns[n], turns[n + 1])])
+        else:
+            panel_moved = lax.ppermute(panel, "pcol", pairs[n + 1])
         message = jnp.where(newer[n], lax.ppermute(message, "pcol", pairs[n]), message)
-        if n + 1 < len(turns):
+        if n + 1 == last:
+            message, panel_moved, back = lax.optimization_barrier((message, panel_moved, back))
+        elif n < last:
             message, panel_moved = lax.optimization_barrier((message, panel_moved))
     if n_row == 4:
         message, to_y, to_x = lax.optimization_barrier((message, to_y, to_x))
@@ -873,7 +885,7 @@
     message_new = lax.ppermute(message, "pcol", pairs[-1])
     factors = factor(message, message_new, True)
     out = finish(
-        mine, counts, wide, mat, (panel, panel_moved), (message, message_new), factors, arrived
+        mine, counts, wide, pltpu.with_memory_space_constraint(mat, pltpu.HBM), (panel, panel_moved), (message, message_new), factors, arrived
     )
     return out.reshape(matrix.shape)
 

time: 83 us -> 85.9 us (1.035)
  starting transfers between devices: 25.7 us -> 30 us
  other arithmetic: 2.54 us -> 4.92 us
  waiting for transfers between devices: 19.9 us -> 17.6 us
  local copies, waits for them, and re-layouts: 1.64 us -> 0.02 us
    ppermute x2, waiting for transfers between devices: 14.6 us -> 4.48 us  [capped_step(): lax.ppermute(message, 'pcol', pairs[n])]
    ppermute x4, waiting for transfers between devices: 0.89 us -> 8.74 us  [send(): return lax.ppermute(x, 'prow', [(i, i ^ k) for i in range(n_row)])]
    ppermute x0 -> x2, starting transfers between devices: none -> 3.3 us  [the longest x1 1.67 us: capped_step(): back = lax.ppermute(source, 'pcol', [(turns[n], turns[n + 1])])]
    cond x16 -> x6, local copies, waits for them, and re-layouts: 1.63 us -> 0.01 us
    select_n x2 -> x1, other arithmetic: 0.27 us -> 1.65 us  [capped_step(): panel = jnp.where(newer[n], arrived_now, panel)]
    ppermute x2 -> x1, starting transfers between devices: 2.84 us -> 1.49 us  [capped_step(): panel_moved = lax.ppermute(panel, 'pcol', pairs[n + 1])]
    select_n x2, other arithmetic: 1.82 us -> 2.83 us  [capped_step(): jnp.where(newer[n], lax.ppermute(message, 'pcol', pairs[n]), message)]
    ppermute x1, starting transfers between devices: 6 us -> 6.95 us  [capped_step(): lax.ppermute(panel, 'pcol', [(i, i + turns[0]) for i in range(0, n_col, 2...]
  transfers between devices with their start and end apart: 13 -> 14, of which waited for: 6 -> 5; matrix products, arithmetic and copies ran while one was open for 3% -> 6% of each run, Pallas kernels for 18% -> 19%
where the time goes in v11:
time: 85.9 us; the launch traced here: 84.7 us
  Pallas kernels  30.9 us (36%)
  starting transfers between devices  30 us (35%)
  waiting for transfers between devices  17.6 us (20%)
  other arithmetic  4.92 us (6%)
    pallas_call x1, Pallas kernels, finish(): pl.pallas_call(functools.partial(finish_kernel, n_row), out_shape=jax.Sha...  11 us
    ppermute x3, starting transfers between devices, exchange(): lax.ppermute(x, both, [(i * n_col, (i ^ k) * n_col) for i in range(n_row)])  9.2 us
    pallas_call x1, Pallas kernels, factor(): pl.pallas_call(functools.partial(factor_kernel, width, unroll), out_shape...  9.07 us
    ppermute x4, waiting for transfers between devices, send(): return lax.ppermute(x, 'prow', [(i, i ^ k) for i in range(n_row)])  8.74 us
    ppermute x1, starting transfers between devices, capped_step(): lax.ppermute(panel, 'pcol', [(i, i + turns[0]) for i in range(0, n_col, 2...  6.95 us
    ppermute x2, waiting for transfers between devices, capped_step(): lax.ppermute(message, 'pcol', pairs[n])  4.48 us
    pallas_call x1, Pallas kernels, parcel(): pl.pallas_call(functools.partial(parcel_kernel, n_row), out_shape=tuple((...  4.4 us
    pallas_call x1, Pallas kernels, begin(): pl.pallas_call(functools.partial(begin_kernel, n_row), out_shape=(jax.Sha...  4.12 us
  transfers between devices with their start and end apart: 14, of which 5 were waited for; matrix products, arithmetic and copies ran while one was open for 6% of the time, Pallas kernels for 19%

profile of v11, /device:TPU:0, one launch (start us, length us, event | category | flops | bytes accessed | tf_op | source)
XLA Modules:
  0.0 84.7 jit_solution(3721809421742130347)
XLA Ops:
  0.0 4.1 %begin.1 = (f32[1024,256]{1,0:T(8,128)}, s32[256,128]{1,0:T(8,128)S(1)}, s32[1]{0:T(128)}, f32[192,256]{1,0:T(8,128)S(1)}, f32[192,256]{1,0:T(8,128)S(1)}, /*index=5*/f32[192,256]{1,0:T(8,128)}, f32[192,256]{1,0:T(8,128)}) custom-call(s32[1,256]{1,0:T(1,128)} %bitcast.29, f32[1024,1,1536]{2,1,0:T(1,128)} %bitcast.25), custom_call_target="tpu_custom_call" | custom-call | bytes 10000000 | tf_op jit(solution)/shard_map/begin/pallas_call | solution.py:441
  4.8 79.8 %conditional.1 = (f32[1,1024,1,1536]{3,2,1,0:T(1,128)}) conditional(s32[]{:T(128)} %bitcast.12, (s32[256]{0:T(256)S(1)}, f32[1,1024,1,1536]{3,2,1,0:T(1,128)}) %tuple.34, (s32[256]{0:T(256)S(1)}, f32[1,1024,1,1536]{3,2,1,0:T(1,128)}, f32[192,256]{1,0:T(8,128)S(1)}, f32[192,256]{1,0:T(8,128)}, f32[192,256]{1,0:T(8,128)}, ...), branch_computations={%region_0.1_spmd, %region_1.5_spmd} | conditional | flops 2488416000 | bytes 214372192 | solution.py:896
  5.0 7.0 %collective-permute-start.3 = (f32[1024,256]{1,0:T(8,128)}, f32[1024,256]{1,0:T(8,128)}, u32[]{:S(2)}, u32[]{:S(2)}) collective-permute-start(f32[1024,256]{1,0:T(8,128)} %get-tuple-element.44), channel_id=1, source_target_pairs={{0,4},{8,12},{16,20},{24,28}} | collective-permute-start | bytes 3145736 | tf_op jit(solution)/shard_map/cond/branch_1_fun/ppermute | solution.py:852
  12.0 3.0 %collective-permute-start = (f32[192,256]{1,0:T(8,128)S(1)}, f32[192,256]{1,0:T(8,128)S(1)}, u32[]{:S(2)}, u32[]{:S(2)}) collective-permute-start(f32[192,256]{1,0:T(8,128)S(1)} %get-tuple-element.37), channel_id=1, source_target_pairs={{0,8},{8,0},{16,24},{24,16}} | collective-permute-start | bytes 589832 | tf_op jit(solution)/shard_map/cond/branch_1_fun/ppermute | solution.py:840
  15.0 3.4 %collective-permute-start.1 = (f32[192,256]{1,0:T(8,128)}, f32[192,256]{1,0:T(8,128)S(1)}, u32[]{:S(2)}, u32[]{:S(2)}) collective-permute-start(f32[192,256]{1,0:T(8,128)} %get-tuple-element.38), channel_id=1, source_target_pairs={{0,16},{8,24},{16,0},{24,8}} | collective-permute-start | bytes 589832 | tf_op jit(solution)/shard_map/cond/branch_1_fun/ppermute | solution.py:840
  18.4 2.8 %collective-permute-start.2 = (f32[192,256]{1,0:T(8,128)}, f32[192,256]{1,0:T(8,128)S(1)}, u32[]{:S(2)}, u32[]{:S(2)}) collective-permute-start(f32[192,256]{1,0:T(8,128)} %get-tuple-element.39), channel_id=1, source_target_pairs={{0,24},{8,16},{16,8},{24,0}} | collective-permute-start | bytes 589832 | tf_op jit(solution)/shard_map/cond/branch_1_fun/ppermute | solution.py:840
  21.6 4.4 %parcel.1 = (f32[144,1536]{1,0:T(8,128)}, f32[144,1536]{1,0:T(8,128)}, f32[288,1536]{1,0:T(8,128)S(1)}) custom-call(s32[96]{0:T(128)S(1)} %select_reduce_fusion.mine_ref, s32[1,256]{1,0:T(1,128)S(1)} %bitcast.30, f32[1024,1,1536]{2,1,0:T(1,128)} %bitcast.26), custom_call_target="tpu_custom_call" | custom-call | bytes 16000000 | tf_op jit(solution)/shard_map/cond/branch_1_fun/parcel/pallas_call | solution.py:535
  26.0 3.3 %collective-permute-done.2.refs_3_ = f32[192,256]{1,0:T(8,128)S(1)} collective-permute-done((f32[192,256]{1,0:T(8,128)}, f32[192,256]{1,0:T(8,128)S(1)}, u32[]{:S(2)}, u32[]{:S(2)}) %collective-permute-start.2) | collective-permute-done | bytes 196640 | tf_op jit(solution)/shard_map/cond/branch_1_fun/ppermute | solution.py:840
  29.3 1.9 %pack.1 = f32[352,256]{1,0:T(8,128)} custom-call(s32[256,128]{1,0:T(8,128)S(1)} %get-tuple-element.34.wide_ref, f32[192,256]{1,0:T(8,128)S(1)} %get-tuple-element.36.refs_0_, f32[192,256]{1,0:T(8,128)S(1)} %collective-permute-done.refs_1_, f32[192,256]{1,0:T(8,128)S(1)} %collective-permute-done.1.refs_2_, f32[192,256]{1,0:T(8,128)S(1)} %collective-permute-done.2.refs_3_), custom_call_target="tpu_custom_call" | custom-call | bytes 4000000 | tf_op jit(solution)/shard_map/cond/branch_1_fun/pack/pallas_call | solution.py:639
  31.1 1.7 %collective-permute-start.6 = (f32[1024,256]{1,0:T(8,128)}, f32[1024,256]{1,0:T(8,128)}, u32[]{:S(2)}, u32[]{:S(2)}) collective-permute-start(f32[1024,256]{1,0:T(8,128)} %collective-permute-done.3), channel_id=1, source_target_pairs={{4,2},{12,10},{20,18},{28,26}} | collective-permute-start | bytes 3145736 | tf_op jit(solution)/shard_map/cond/branch_1_fun/ppermute | solution.py:874
  32.8 1.6 %collective-permute-start.5 = (f32[1024,256]{1,0:T(8,128)}, f32[1024,256]{1,0:T(8,128)}, u32[]{:S(2)}, u32[]{:S(2)}) collective-permute-start(f32[1024,256]{1,0:T(8,128)} %collective-permute-done.3), channel_id=1, source_target_pairs={{4,6},{12,14},{20,22},{28,30}} | collective-permute-start | bytes 3145736 | tf_op jit(solution)/shard_map/cond/branch_1_fun/ppermute | solution.py:873
  35.9 2.1 %collective-permute-start.4 = (f32[352,256]{1,0:T(8,128)}, f32[352,256]{1,0:T(8,128)}, u32[]{:S(2)}, u32[]{:S(2)}) collective-permute-start(f32[352,256]{1,0:T(8,128)} %pack.1), channel_id=1, source_target_pairs={{0,4},{8,12},{16,20},{24,28}} | collective-permute-start | bytes 1081352 | tf_op jit(solution)/shard_map/cond/branch_1_fun/ppermute | solution.py:877
  37.9 4.5 %collective-permute-done.4 = f32[352,256]{1,0:T(8,128)} collective-permute-done((f32[352,256]{1,0:T(8,128)}, f32[352,256]{1,0:T(8,128)}, u32[]{:S(2)}, u32[]{:S(2)}) %collective-permute-start.4) | collective-permute-done | bytes 360480 | tf_op jit(solution)/shard_map/cond/branch_1_fun/ppermute | solution.py:877
  42.4 1.8 %broadcast_select_fusion.4 = f32[352,256]{1,0:T(8,128)} fusion(f32[352,256]{1,0:T(8,128)} %collective-permute-done.4, f32[352,256]{1,0:T(8,128)} %pack.1, pred[]{:T(512)S(6)} %ne.60), kind=kLoop, calls=%fused_computation.36 | loop fusion | flops 90112 | bytes 1081345 | tf_op jit(solution)/shard_map/cond/branch_1_fun/jit(_where)/select_n | solution.py:877
  44.2 2.1 %collective-permute-start.8 = (f32[352,256]{1,0:T(8,128)}, f32[352,256]{1,0:T(8,128)}, u32[]{:S(2)}, u32[]{:S(2)}) collective-permute-start(f32[352,256]{1,0:T(8,128)} %broadcast_select_fusion.4), channel_id=1, source_target_pairs={{0,2},{4,6},{8,10},{12,14},{16,18},{20,22},{24,26},{28,30}} | collective-permute-start | bytes 1081352 | tf_op jit(solution)/shard_map/cond/branch_1_fun/ppermute | solution.py:877
  46.3 6.4 %collective-permute-done.9.first_ref.refs_1_ = f32[144,1536]{1,0:T(8,128)S(1)} collective-permute-done((f32[144,1536]{1,0:T(8,128)}, f32[144,1536]{1,0:T(8,128)S(1)}, u32[]{:S(2)}, u32[]{:S(2)}) %collective-permute-start.9) | collective-permute-done | bytes 884768 | tf_op jit(solution)/shard_map/cond/branch_1_fun/ppermute | solution.py:847
  52.7 2.3 %collective-permute-done.10.second_ref.refs_2_ = f32[144,1536]{1,0:T(8,128)S(1)} collective-permute-done((f32[144,1536]{1,0:T(8,128)}, f32[144,1536]{1,0:T(8,128)S(1)}, u32[]{:S(2)}, u32[]{:S(2)}) %collective-permute-start.10) | collective-permute-done | bytes 884768 | tf_op jit(solution)/shard_map/cond/branch_1_fun/ppermute | solution.py:847
  55.4 1.6 %select_select_fusion.panel_ref = f32[1024,256]{1,0:T(8,128)S(1)} fusion(f32[1024,256]{1,0:T(8,128)} %collective-permute-done.3, f32[1024,256]{1,0:T(8,128)S(1)} %copy-done.6, f32[1024,256]{1,0:T(8,128)} %collective-permute-done.6, f32[1024,256]{1,0:T(8,128)} %collective-permute-done.5, pred[]{:T(512)S(6)} %ne.60, pred[]{:T(512)S(6)} %eq.65, pred[]{:T(512)S(6)} %ne.59), kind=kLoop, calls=%fused_computation.31 | loop fusion | flops 786432 | bytes 5242883 | tf_op jit(solution)/shard_map/cond/branch_1_fun/jit(_where)/select_n | solution.py:870
  57.1 1.5 %collective-permute-start.7 = (f32[1024,256]{1,0:T(8,128)S(1)}, f32[1024,256]{1,0:T(8,128)S(1)}, u32[]{:S(2)}, u32[]{:S(2)}) collective-permute-start(f32[1024,256]{1,0:T(8,128)S(1)} %select_select_fusion.panel_ref), channel_id=1, source_target_pairs={{0,1},{2,3},{4,5},{6,7},{8,9},{10,11},{12,13},{14,15},{16,17},{18,... | collective-permute-start | bytes 3145736 | tf_op jit(solution)/shard_map/cond/branch_1_fun/ppermute | solution.py:876
  60.0 1.8 %collective-permute-start.13 = (f32[144,1536]{1,0:T(8,128)S(1)}, f32[144,1536]{1,0:T(8,128)S(1)}, u32[]{:S(2)}, u32[]{:S(2)}) collective-permute-start(f32[144,1536]{1,0:T(8,128)S(1)} %get-tuple-element.60), channel_id=1, source_target_pairs={{0,8},{8,0},{16,24},{24,16},{1,9},{9,1},{17,25},{25,17},{2,10},{10... | collective-permute-start | bytes 2654216 | tf_op jit(solution)/shard_map/cond/branch_1_fun/ppermute | solution.py:847
  61.8 1.3 %collective-permute-start.11 = (f32[352,256]{1,0:T(8,128)S(1)}, f32[352,256]{1,0:T(8,128)S(1)}, u32[]{:S(2)}, u32[]{:S(2)}) collective-permute-start(f32[352,256]{1,0:T(8,128)S(1)} %broadcast_select_fusion.3.first_ref.square_ref), channel_id=1, source_target_pairs={{0,1},{2,3},{4,5},{6,7},{8,9},{10,11},{12,13},{14,15},{16,17},{18,... | collective-permute-start | bytes 1081352 | tf_op jit(solution)/shard_map/cond/branch_1_fun/ppermute | solution.py:885
  63.3 1.1 %collective-permute-done.11.second_ref.square_new_ref = f32[352,256]{1,0:T(8,128)S(1)} collective-permute-done((f32[352,256]{1,0:T(8,128)S(1)}, f32[352,256]{1,0:T(8,128)S(1)}, u32[]{:S(2)}, u32[]{:S(2)}) %collective-permute-start.11) | collective-permute-done | bytes 360480 | tf_op jit(solution)/shard_map/cond/branch_1_fun/ppermute | solution.py:885
  64.4 9.1 %factor.3 = (f32[256,256]{1,0:T(8,128)S(1)}, f32[256,256]{1,0:T(8,128)S(1)}, f32[256,256]{1,0:T(8,128)S(1)}) custom-call(f32[352,256]{1,0:T(8,128)S(1)} %broadcast_select_fusion.3.first_ref.square_ref, f32[352,256]{1,0:T(8,128)S(1)} %collective-permute-done.11.second_ref.square_new_ref), custom_call_target="tpu_custom_call" | custom-call | flops 67108864 | bytes 50000000 | tf_op jit(solution)/shard_map/cond/branch_1_fun/factor/pallas_call | solution.py:155
  73.5 11.0 %finish.1 = f32[1024,1,1536]{2,1,0:T(1,128)} custom-call(s32[96]{0:T(128)S(1)} %select_reduce_fusion.mine_ref, s32[4]{0:T(128)S(1)} %convert_reduce_fusion.1.counts_ref, s32[256,128]{1,0:T(8,128)S(1)} %copy-done.8, f32[1024,1,1536]{2,1,0:T(1,128)} %bitcast.27, f32[1024,256]{1,0:T(8,128)S(1)} %select_select_fusion.panel_ref, ...), custom_call_target="tpu_custom_call" | custom-call | flops 2415919104 | bytes 12582912 | tf_op jit(solution)/shard_map/cond/branch_1_fun/finish/pallas_call | solution.py:786
  (27 shorter events, 3.8 us)
Async XLA Ops:
  0.0 4.8 %copy-start.9 = (s32[256]{0:T(256)S(1)}, s32[256]{0:T(256)}, u32[]{:S(2)}) copy-start(s32[256]{0:T(256)} %param.5) | copy-start | bytes 3076
  5.0 24.2 %copy-start.7 = (s32[256,128]{1,0:T(8,128)}, s32[256,128]{1,0:T(8,128)S(1)}, u32[]{:S(2)}) copy-start(s32[256,128]{1,0:T(8,128)S(1)} %get-tuple-element.34.wide_ref) | copy-start | bytes 393220 | tf_op jit(solution)/shard_map/cond
  5.0 26.1 %collective-permute-start.3 = (f32[1024,256]{1,0:T(8,128)}, f32[1024,256]{1,0:T(8,128)}, u32[]{:S(2)}, u32[]{:S(2)}) collective-permute-start(f32[1024,256]{1,0:T(8,128)} %get-tuple-element.44), channel_id=1, source_target_pairs={{0,4},{8,12},{16,20},{24,28}} | collective-permute-start | bytes 3145736 | tf_op jit(solution)/shard_map/cond/branch_1_fun/ppermute | solution.py:852
  12.0 14.0 %collective-permute-start = (f32[192,256]{1,0:T(8,128)S(1)}, f32[192,256]{1,0:T(8,128)S(1)}, u32[]{:S(2)}, u32[]{:S(2)}) collective-permute-start(f32[192,256]{1,0:T(8,128)S(1)} %get-tuple-element.37), channel_id=1, source_target_pairs={{0,8},{8,0},{16,24},{24,16}} | collective-permute-start | bytes 589832 | tf_op jit(solution)/shard_map/cond/branch_1_fun/ppermute | solution.py:840
  15.0 11.0 %collective-permute-start.1 = (f32[192,256]{1,0:T(8,128)}, f32[192,256]{1,0:T(8,128)S(1)}, u32[]{:S(2)}, u32[]{:S(2)}) collective-permute-start(f32[192,256]{1,0:T(8,128)} %get-tuple-element.38), channel_id=1, source_target_pairs={{0,16},{8,24},{16,0},{24,8}} | collective-permute-start | bytes 589832 | tf_op jit(solution)/shard_map/cond/branch_1_fun/ppermute | solution.py:840
  18.4 10.8 %collective-permute-start.2 = (f32[192,256]{1,0:T(8,128)}, f32[192,256]{1,0:T(8,128)S(1)}, u32[]{:S(2)}, u32[]{:S(2)}) collective-permute-start(f32[192,256]{1,0:T(8,128)} %get-tuple-element.39), channel_id=1, source_target_pairs={{0,24},{8,16},{16,8},{24,0}} | collective-permute-start | bytes 589832 | tf_op jit(solution)/shard_map/cond/branch_1_fun/ppermute | solution.py:840
  31.1 13.1 %collective-permute-start.6 = (f32[1024,256]{1,0:T(8,128)}, f32[1024,256]{1,0:T(8,128)}, u32[]{:S(2)}, u32[]{:S(2)}) collective-permute-start(f32[1024,256]{1,0:T(8,128)} %collective-permute-done.3), channel_id=1, source_target_pairs={{4,2},{12,10},{20,18},{28,26}} | collective-permute-start | bytes 3145736 | tf_op jit(solution)/shard_map/cond/branch_1_fun/ppermute | solution.py:874
  32.8 11.4 %collective-permute-start.5 = (f32[1024,256]{1,0:T(8,128)}, f32[1024,256]{1,0:T(8,128)}, u32[]{:S(2)}, u32[]{:S(2)}) collective-permute-start(f32[1024,256]{1,0:T(8,128)} %collective-permute-done.3), channel_id=1, source_target_pairs={{4,6},{12,14},{20,22},{28,30}} | collective-permute-start | bytes 3145736 | tf_op jit(solution)/shard_map/cond/branch_1_fun/ppermute | solution.py:873
  34.4 18.2 %collective-permute-start.9 = (f32[144,1536]{1,0:T(8,128)}, f32[144,1536]{1,0:T(8,128)S(1)}, u32[]{:S(2)}, u32[]{:S(2)}) collective-permute-start(f32[144,1536]{1,0:T(8,128)} %get-tuple-element.51), channel_id=1, source_target_pairs={{0,8},{8,0},{16,24},{24,16},{1,9},{9,1},{17,25},{25,17},{2,10},{10... | collective-permute-start | bytes 2654216 | tf_op jit(solution)/shard_map/cond/branch_1_fun/ppermute | solution.py:847
  35.0 20.0 %collective-permute-start.10 = (f32[144,1536]{1,0:T(8,128)}, f32[144,1536]{1,0:T(8,128)S(1)}, u32[]{:S(2)}, u32[]{:S(2)}) collective-permute-start(f32[144,1536]{1,0:T(8,128)} %get-tuple-element.52), channel_id=1, source_target_pairs={{0,16},{8,24},{16,0},{24,8},{1,17},{9,25},{17,1},{25,9},{2,18},{10... | collective-permute-start | bytes 2654216 | tf_op jit(solution)/shard_map/cond/branch_1_fun/ppermute | solution.py:847
  35.9 6.5 %collective-permute-start.4 = (f32[352,256]{1,0:T(8,128)}, f32[352,256]{1,0:T(8,128)}, u32[]{:S(2)}, u32[]{:S(2)}) collective-permute-start(f32[352,256]{1,0:T(8,128)} %pack.1), channel_id=1, source_target_pairs={{0,4},{8,12},{16,20},{24,28}} | collective-permute-start | bytes 1081352 | tf_op jit(solution)/shard_map/cond/branch_1_fun/ppermute | solution.py:877
  44.2 14.4 %collective-permute-start.8 = (f32[352,256]{1,0:T(8,128)}, f32[352,256]{1,0:T(8,128)}, u32[]{:S(2)}, u32[]{:S(2)}) collective-permute-start(f32[352,256]{1,0:T(8,128)} %broadcast_select_fusion.4), channel_id=1, source_target_pairs={{0,2},{4,6},{8,10},{12,14},{16,18},{20,22},{24,26},{28,30}} | collective-permute-start | bytes 1081352 | tf_op jit(solution)/shard_map/cond/branch_1_fun/ppermute | solution.py:877
  46.3 9.2 %copy-start.6 = (f32[1024,256]{1,0:T(8,128)S(1)}, f32[1024,256]{1,0:T(8,128)}, u32[]{:S(2)}) copy-start(f32[1024,256]{1,0:T(8,128)} %get-tuple-element.44) | copy-start | bytes 3145732 | tf_op jit(solution)/shard_map/cond
  57.1 16.4 %copy-start.8 = (s32[256,128]{1,0:T(8,128)S(1)}, s32[256,128]{1,0:T(8,128)}, u32[]{:S(2)}) copy-start(s32[256,128]{1,0:T(8,128)} %copy-done.7) | copy-start | bytes 393220 | tf_op jit(solution)/shard_map/cond
  57.1 16.4 %collective-permute-start.7 = (f32[1024,256]{1,0:T(8,128)S(1)}, f32[1024,256]{1,0:T(8,128)S(1)}, u32[]{:S(2)}, u32[]{:S(2)}) collective-permute-start(f32[1024,256]{1,0:T(8,128)S(1)} %select_select_fusion.panel_ref), channel_id=1, source_target_pairs={{0,1},{2,3},{4,5},{6,7},{8,9},{10,11},{12,13},{14,15},{16,17},{18,... | collective-permute-start | bytes 3145736 | tf_op jit(solution)/shard_map/cond/branch_1_fun/ppermute | solution.py:876
  59.7 13.8 %collective-permute-start.12 = (f32[144,1536]{1,0:T(8,128)S(1)}, f32[144,1536]{1,0:T(8,128)S(1)}, u32[]{:S(2)}, u32[]{:S(2)}) collective-permute-start(f32[144,1536]{1,0:T(8,128)S(1)} %get-tuple-element.59), channel_id=1, source_target_pairs={{0,16},{8,24},{16,0},{24,8},{1,17},{9,25},{17,1},{25,9},{2,18},{10... | collective-permute-start | bytes 2654216 | tf_op jit(solution)/shard_map/cond/branch_1_fun/ppermute | solution.py:847
  60.0 13.5 %collective-permute-start.13 = (f32[144,1536]{1,0:T(8,128)S(1)}, f32[144,1536]{1,0:T(8,128)S(1)}, u32[]{:S(2)}, u32[]{:S(2)}) collective-permute-start(f32[144,1536]{1,0:T(8,128)S(1)} %get-tuple-element.60), channel_id=1, source_target_pairs={{0,8},{8,0},{16,24},{24,16},{1,9},{9,1},{17,25},{25,17},{2,10},{10... | collective-permute-start | bytes 2654216 | tf_op jit(solution)/shard_map/cond/branch_1_fun/ppermute | solution.py:847
  61.8 2.6 %collective-permute-start.11 = (f32[352,256]{1,0:T(8,128)S(1)}, f32[352,256]{1,0:T(8,128)S(1)}, u32[]{:S(2)}, u32[]{:S(2)}) collective-permute-start(f32[352,256]{1,0:T(8,128)S(1)} %broadcast_select_fusion.3.first_ref.square_ref), channel_id=1, source_target_pairs={{0,1},{2,3},{4,5},{6,7},{8,9},{10,11},{12,13},{14,15},{16,17},{18,... | collective-permute-start | bytes 1081352 | tf_op jit(solution)/shard_map/cond/branch_1_fun/ppermute | solution.py:885

commit v12 on v11

--- a/solution.py
+++ b/solution.py
@@ -880,7 +880,6 @@
         elif n < last:
             message, panel_moved = lax.optimization_barrier((message, panel_moved))
     if n_row == 4:
-        message, to_y, to_x = lax.optimization_barrier((message, to_y, to_x))
         arrived += [send(to_y, 2), send(to_x, 1)]
     message_new = lax.ppermute(message, "pcol", pairs[-1])
     factors = factor(message, message_new, True)

time: 85.9 us -> 84.1 us (0.979)
  other arithmetic: 4.92 us -> 3.17 us
  waiting for transfers between devices: 17.6 us -> 19.1 us
  starting transfers between devices: 30 us -> 29.1 us
    ppermute x4, waiting for transfers between devices: 8.74 us -> 11.6 us  [send(): return lax.ppermute(x, 'prow', [(i, i ^ k) for i in range(n_row)])]
    select_n x2, other arithmetic: 2.83 us -> 1.08 us  [capped_step(): jnp.where(newer[n], lax.ppermute(message, 'pcol', pairs[n]), message)]
    ppermute x2, waiting for transfers between devices: 4.48 us -> 3.06 us  [capped_step(): lax.ppermute(message, 'pcol', pairs[n])]
  transfers between devices with their start and end apart: 14 -> 14, of which waited for: 5 -> 5; matrix products, arithmetic and copies ran while one was open for 6% -> 4% of each run, Pallas kernels for 19% -> 19%
where the time goes in v12:
time: 84.1 us; the launch traced here: 83.5 us
  Pallas kernels  30.9 us (37%)
  starting transfers between devices  29.1 us (35%)
  waiting for transfers between devices  19.1 us (23%)
  other arithmetic  3.17 us (4%)
  between operations  0.85 us (1%)
    ppermute x4, waiting for transfers between devices, send(): return lax.ppermute(x, 'prow', [(i, i ^ k) for i in range(n_row)])  11.6 us
    pallas_call x1, Pallas kernels, finish(): pl.pallas_call(functools.partial(finish_kernel, n_row), out_shape=jax.Sha...  11 us
    ppermute x3, starting transfers between devices, exchange(): lax.ppermute(x, both, [(i * n_col, (i ^ k) * n_col) for i in range(n_row)])  9.2 us
    pallas_call x1, Pallas kernels, factor(): pl.pallas_call(functools.partial(factor_kernel, width, unroll), out_shape...  9.07 us
    ppermute x1, starting transfers between devices, capped_step(): lax.ppermute(panel, 'pcol', [(i, i + turns[0]) for i in range(0, n_col, 2...  6.95 us
    pallas_call x1, Pallas kernels, parcel(): pl.pallas_call(functools.partial(parcel_kernel, n_row), out_shape=tuple((...  4.4 us
    pallas_call x1, Pallas kernels, begin(): pl.pallas_call(functools.partial(begin_kernel, n_row), out_shape=(jax.Sha...  4.12 us
    ppermute x2, starting transfers between devices, capped_step(): lax.ppermute(message, 'pcol', pairs[n])  3.84 us
  transfers between devices with their start and end apart: 14, of which 5 were waited for; matrix products, arithmetic and copies ran while one was open for 4% of the time, Pallas kernels for 19%

profile of v12, /device:TPU:0, one launch (start us, length us, event | category | flops | bytes accessed | tf_op | source)
XLA Modules:
  0.0 83.5 jit_solution(5142099856058801430)
XLA Ops:
  0.0 4.1 %begin.1 = (f32[1024,256]{1,0:T(8,128)}, s32[256,128]{1,0:T(8,128)S(1)}, s32[1]{0:T(128)}, f32[192,256]{1,0:T(8,128)S(1)}, f32[192,256]{1,0:T(8,128)S(1)}, /*index=5*/f32[192,256]{1,0:T(8,128)}, f32[192,256]{1,0:T(8,128)}) custom-call(s32[1,256]{1,0:T(1,128)} %bitcast.29, f32[1024,1,1536]{2,1,0:T(1,128)} %bitcast.25), custom_call_target="tpu_custom_call" | custom-call | bytes 10000000 | tf_op jit(solution)/shard_map/begin/pallas_call | solution.py:441
  4.8 78.5 %conditional.1 = (f32[1,1024,1,1536]{3,2,1,0:T(1,128)}) conditional(s32[]{:T(128)} %bitcast.12, (s32[256]{0:T(256)S(1)}, f32[1,1024,1,1536]{3,2,1,0:T(1,128)}) %tuple.33, (s32[256]{0:T(256)S(1)}, f32[1,1024,1,1536]{3,2,1,0:T(1,128)}, f32[192,256]{1,0:T(8,128)S(1)}, f32[192,256]{1,0:T(8,128)}, f32[192,256]{1,0:T(8,128)}, ...), branch_computations={%region_0.1_spmd, %region_1.5_spmd} | conditional | flops 2488416000 | bytes 214372192 | solution.py:895
  5.0 7.0 %collective-permute-start.3 = (f32[1024,256]{1,0:T(8,128)}, f32[1024,256]{1,0:T(8,128)}, u32[]{:S(2)}, u32[]{:S(2)}) collective-permute-start(f32[1024,256]{1,0:T(8,128)} %get-tuple-element.44), channel_id=1, source_target_pairs={{0,4},{8,12},{16,20},{24,28}} | collective-permute-start | bytes 3145736 | tf_op jit(solution)/shard_map/cond/branch_1_fun/ppermute | solution.py:852
  12.0 3.0 %collective-permute-start = (f32[192,256]{1,0:T(8,128)S(1)}, f32[192,256]{1,0:T(8,128)S(1)}, u32[]{:S(2)}, u32[]{:S(2)}) collective-permute-start(f32[192,256]{1,0:T(8,128)S(1)} %get-tuple-element.37), channel_id=1, source_target_pairs={{0,8},{8,0},{16,24},{24,16}} | collective-permute-start | bytes 589832 | tf_op jit(solution)/shard_map/cond/branch_1_fun/ppermute | solution.py:840
  15.0 3.4 %collective-permute-start.1 = (f32[192,256]{1,0:T(8,128)}, f32[192,256]{1,0:T(8,128)S(1)}, u32[]{:S(2)}, u32[]{:S(2)}) collective-permute-start(f32[192,256]{1,0:T(8,128)} %get-tuple-element.38), channel_id=1, source_target_pairs={{0,16},{8,24},{16,0},{24,8}} | collective-permute-start | bytes 589832 | tf_op jit(solution)/shard_map/cond/branch_1_fun/ppermute | solution.py:840
  18.4 2.8 %collective-permute-start.2 = (f32[192,256]{1,0:T(8,128)}, f32[192,256]{1,0:T(8,128)S(1)}, u32[]{:S(2)}, u32[]{:S(2)}) collective-permute-start(f32[192,256]{1,0:T(8,128)} %get-tuple-element.39), channel_id=1, source_target_pairs={{0,24},{8,16},{16,8},{24,0}} | collective-permute-start | bytes 589832 | tf_op jit(solution)/shard_map/cond/branch_1_fun/ppermute | solution.py:840
  21.6 4.4 %parcel.1 = (f32[144,1536]{1,0:T(8,128)}, f32[144,1536]{1,0:T(8,128)}, f32[288,1536]{1,0:T(8,128)S(1)}) custom-call(s32[96]{0:T(128)S(1)} %select_reduce_fusion.mine_ref, s32[1,256]{1,0:T(1,128)S(1)} %bitcast.30, f32[1024,1,1536]{2,1,0:T(1,128)} %bitcast.26), custom_call_target="tpu_custom_call" | custom-call | bytes 16000000 | tf_op jit(solution)/shard_map/cond/branch_1_fun/parcel/pallas_call | solution.py:535
  26.0 3.2 %collective-permute-done.2.refs_3_ = f32[192,256]{1,0:T(8,128)S(1)} collective-permute-done((f32[192,256]{1,0:T(8,128)}, f32[192,256]{1,0:T(8,128)S(1)}, u32[]{:S(2)}, u32[]{:S(2)}) %collective-permute-start.2) | collective-permute-done | bytes 196640 | tf_op jit(solution)/shard_map/cond/branch_1_fun/ppermute | solution.py:840
  29.2 1.9 %pack.1 = f32[352,256]{1,0:T(8,128)} custom-call(s32[256,128]{1,0:T(8,128)S(1)} %get-tuple-element.34.wide_ref, f32[192,256]{1,0:T(8,128)S(1)} %get-tuple-element.36.refs_0_, f32[192,256]{1,0:T(8,128)S(1)} %collective-permute-done.refs_1_, f32[192,256]{1,0:T(8,128)S(1)} %collective-permute-done.1.refs_2_, f32[192,256]{1,0:T(8,128)S(1)} %collective-permute-done.2.refs_3_), custom_call_target="tpu_custom_call" | custom-call | bytes 4000000 | tf_op jit(solution)/shard_map/cond/branch_1_fun/pack/pallas_call | solution.py:639
  31.1 1.7 %collective-permute-start.6 = (f32[1024,256]{1,0:T(8,128)}, f32[1024,256]{1,0:T(8,128)}, u32[]{:S(2)}, u32[]{:S(2)}) collective-permute-start(f32[1024,256]{1,0:T(8,128)} %collective-permute-done.3), channel_id=1, source_target_pairs={{4,2},{12,10},{20,18},{28,26}} | collective-permute-start | bytes 3145736 | tf_op jit(solution)/shard_map/cond/branch_1_fun/ppermute | solution.py:874
  32.8 1.6 %collective-permute-start.5 = (f32[1024,256]{1,0:T(8,128)}, f32[1024,256]{1,0:T(8,128)}, u32[]{:S(2)}, u32[]{:S(2)}) collective-permute-start(f32[1024,256]{1,0:T(8,128)} %collective-permute-done.3), channel_id=1, source_target_pairs={{4,6},{12,14},{20,22},{28,30}} | collective-permute-start | bytes 3145736 | tf_op jit(solution)/shard_map/cond/branch_1_fun/ppermute | solution.py:873
  34.4 2.0 %collective-permute-start.4 = (f32[352,256]{1,0:T(8,128)}, f32[352,256]{1,0:T(8,128)}, u32[]{:S(2)}, u32[]{:S(2)}) collective-permute-start(f32[352,256]{1,0:T(8,128)} %pack.1), channel_id=1, source_target_pairs={{0,4},{8,12},{16,20},{24,28}} | collective-permute-start | bytes 1081352 | tf_op jit(solution)/shard_map/cond/branch_1_fun/ppermute | solution.py:877
  37.0 0.9 %collective-permute-start.11 = (f32[144,1536]{1,0:T(8,128)}, f32[144,1536]{1,0:T(8,128)S(1)}, u32[]{:S(2)}, u32[]{:S(2)}) collective-permute-start(f32[144,1536]{1,0:T(8,128)} %get-tuple-element.55), channel_id=1, source_target_pairs={{0,16},{8,24},{16,0},{24,8},{1,17},{9,25},{17,1},{25,9},{2,18},{10... | collective-permute-start | bytes 2654216 | tf_op jit(solution)/shard_map/cond/branch_1_fun/ppermute | solution.py:847
  37.9 3.1 %collective-permute-done.4 = f32[352,256]{1,0:T(8,128)} collective-permute-done((f32[352,256]{1,0:T(8,128)}, f32[352,256]{1,0:T(8,128)}, u32[]{:S(2)}, u32[]{:S(2)}) %collective-permute-start.4) | collective-permute-done | bytes 360480 | tf_op jit(solution)/shard_map/cond/branch_1_fun/ppermute | solution.py:877
  41.0 1.0 %broadcast_select_fusion.4 = f32[352,256]{1,0:T(8,128)S(1)} fusion(f32[352,256]{1,0:T(8,128)} %collective-permute-done.4, f32[352,256]{1,0:T(8,128)} %pack.1, pred[]{:T(512)S(6)} %ne.60), kind=kLoop, calls=%fused_computation.36 | loop fusion | flops 90112 | bytes 1081345 | tf_op jit(solution)/shard_map/cond/branch_1_fun/jit(_where)/select_n | solution.py:877
  42.0 1.6 %select_select_fusion.panel_ref = f32[1024,256]{1,0:T(8,128)S(1)} fusion(f32[1024,256]{1,0:T(8,128)} %collective-permute-done.3, f32[1024,256]{1,0:T(8,128)S(1)} %copy-done.6, f32[1024,256]{1,0:T(8,128)} %collective-permute-done.6, f32[1024,256]{1,0:T(8,128)} %collective-permute-done.5, pred[]{:T(512)S(6)} %ne.60, pred[]{:T(512)S(6)} %eq.65, pred[]{:T(512)S(6)} %ne.59), kind=kLoop, calls=%fused_computation.31 | loop fusion | flops 786432 | bytes 5242883 | tf_op jit(solution)/shard_map/cond/branch_1_fun/jit(_where)/select_n | solution.py:870
  43.7 1.4 %collective-permute-start.7 = (f32[1024,256]{1,0:T(8,128)S(1)}, f32[1024,256]{1,0:T(8,128)S(1)}, u32[]{:S(2)}, u32[]{:S(2)}) collective-permute-start(f32[1024,256]{1,0:T(8,128)S(1)} %select_select_fusion.panel_ref), channel_id=1, source_target_pairs={{0,1},{2,3},{4,5},{6,7},{8,9},{10,11},{12,13},{14,15},{16,17},{18,... | collective-permute-start | bytes 3145736 | tf_op jit(solution)/shard_map/cond/branch_1_fun/ppermute | solution.py:876
  45.0 1.8 %collective-permute-start.8 = (f32[352,256]{1,0:T(8,128)S(1)}, f32[352,256]{1,0:T(8,128)S(1)}, u32[]{:S(2)}, u32[]{:S(2)}) collective-permute-start(f32[352,256]{1,0:T(8,128)S(1)} %broadcast_select_fusion.4), channel_id=1, source_target_pairs={{0,2},{4,6},{8,10},{12,14},{16,18},{20,22},{24,26},{28,30}} | collective-permute-start | bytes 1081352 | tf_op jit(solution)/shard_map/cond/branch_1_fun/ppermute | solution.py:877
  46.8 11.1 %collective-permute-done.10.first_ref.refs_1_ = f32[144,1536]{1,0:T(8,128)S(1)} collective-permute-done((f32[144,1536]{1,0:T(8,128)}, f32[144,1536]{1,0:T(8,128)S(1)}, u32[]{:S(2)}, u32[]{:S(2)}) %collective-permute-start.10) | collective-permute-done | bytes 884768 | tf_op jit(solution)/shard_map/cond/branch_1_fun/ppermute | solution.py:847
  58.4 0.9 %collective-permute-start.12 = (f32[144,1536]{1,0:T(8,128)S(1)}, f32[144,1536]{1,0:T(8,128)S(1)}, u32[]{:S(2)}, u32[]{:S(2)}) collective-permute-start(f32[144,1536]{1,0:T(8,128)S(1)} %get-tuple-element.56), channel_id=1, source_target_pairs={{0,16},{8,24},{16,0},{24,8},{1,17},{9,25},{17,1},{25,9},{2,18},{10... | collective-permute-start | bytes 2654216 | tf_op jit(solution)/shard_map/cond/branch_1_fun/ppermute | solution.py:847
  60.1 1.3 %collective-permute-start.9 = (f32[352,256]{1,0:T(8,128)S(1)}, f32[352,256]{1,0:T(8,128)S(1)}, u32[]{:S(2)}, u32[]{:S(2)}) collective-permute-start(f32[352,256]{1,0:T(8,128)S(1)} %broadcast_select_fusion.3.first_ref.square_ref), channel_id=1, source_target_pairs={{0,1},{2,3},{4,5},{6,7},{8,9},{10,11},{12,13},{14,15},{16,17},{18,... | collective-permute-start | bytes 1081352 | tf_op jit(solution)/shard_map/cond/branch_1_fun/ppermute | solution.py:884
  61.5 1.1 %collective-permute-done.9.second_ref.square_new_ref = f32[352,256]{1,0:T(8,128)S(1)} collective-permute-done((f32[352,256]{1,0:T(8,128)S(1)}, f32[352,256]{1,0:T(8,128)S(1)}, u32[]{:S(2)}, u32[]{:S(2)}) %collective-permute-start.9) | collective-permute-done | bytes 360480 | tf_op jit(solution)/shard_map/cond/branch_1_fun/ppermute | solution.py:884
  62.7 9.1 %factor.3 = (f32[256,256]{1,0:T(8,128)S(1)}, f32[256,256]{1,0:T(8,128)S(1)}, f32[256,256]{1,0:T(8,128)S(1)}) custom-call(f32[352,256]{1,0:T(8,128)S(1)} %broadcast_select_fusion.3.first_ref.square_ref, f32[352,256]{1,0:T(8,128)S(1)} %collective-permute-done.9.second_ref.square_new_ref), custom_call_target="tpu_custom_call" | custom-call | flops 67108864 | bytes 50000000 | tf_op jit(solution)/shard_map/cond/branch_1_fun/factor/pallas_call | solution.py:155
  72.3 11.0 %finish.1 = f32[1024,1,1536]{2,1,0:T(1,128)} custom-call(s32[96]{0:T(128)S(1)} %select_reduce_fusion.mine_ref, s32[4]{0:T(128)S(1)} %convert_reduce_fusion.1.counts_ref, s32[256,128]{1,0:T(8,128)S(1)} %copy-done.8, f32[1024,1,1536]{2,1,0:T(1,128)} %bitcast.27, f32[1024,256]{1,0:T(8,128)S(1)} %select_select_fusion.panel_ref, ...), custom_call_target="tpu_custom_call" | custom-call | flops 2415919104 | bytes 12582912 | tf_op jit(solution)/shard_map/cond/branch_1_fun/finish/pallas_call | solution.py:786
  (27 shorter events, 2.8 us)
Async XLA Ops:
  0.0 4.8 %copy-start.9 = (s32[256]{0:T(256)S(1)}, s32[256]{0:T(256)}, u32[]{:S(2)}) copy-start(s32[256]{0:T(256)} %param.5) | copy-start | bytes 3076
  5.0 24.2 %copy-start.7 = (s32[256,128]{1,0:T(8,128)}, s32[256,128]{1,0:T(8,128)S(1)}, u32[]{:S(2)}) copy-start(s32[256,128]{1,0:T(8,128)S(1)} %get-tuple-element.34.wide_ref) | copy-start | bytes 393220 | tf_op jit(solution)/shard_map/cond
  5.0 26.1 %collective-permute-start.3 = (f32[1024,256]{1,0:T(8,128)}, f32[1024,256]{1,0:T(8,128)}, u32[]{:S(2)}, u32[]{:S(2)}) collective-permute-start(f32[1024,256]{1,0:T(8,128)} %get-tuple-element.44), channel_id=1, source_target_pairs={{0,4},{8,12},{16,20},{24,28}} | collective-permute-start | bytes 3145736 | tf_op jit(solution)/shard_map/cond/branch_1_fun/ppermute | solution.py:852
  12.0 14.0 %collective-permute-start = (f32[192,256]{1,0:T(8,128)S(1)}, f32[192,256]{1,0:T(8,128)S(1)}, u32[]{:S(2)}, u32[]{:S(2)}) collective-permute-start(f32[192,256]{1,0:T(8,128)S(1)} %get-tuple-element.37), channel_id=1, source_target_pairs={{0,8},{8,0},{16,24},{24,16}} | collective-permute-start | bytes 589832 | tf_op jit(solution)/shard_map/cond/branch_1_fun/ppermute | solution.py:840
  15.0 11.0 %collective-permute-start.1 = (f32[192,256]{1,0:T(8,128)}, f32[192,256]{1,0:T(8,128)S(1)}, u32[]{:S(2)}, u32[]{:S(2)}) collective-permute-start(f32[192,256]{1,0:T(8,128)} %get-tuple-element.38), channel_id=1, source_target_pairs={{0,16},{8,24},{16,0},{24,8}} | collective-permute-start | bytes 589832 | tf_op jit(solution)/shard_map/cond/branch_1_fun/ppermute | solution.py:840
  18.4 10.8 %collective-permute-start.2 = (f32[192,256]{1,0:T(8,128)}, f32[192,256]{1,0:T(8,128)S(1)}, u32[]{:S(2)}, u32[]{:S(2)}) collective-permute-start(f32[192,256]{1,0:T(8,128)} %get-tuple-element.39), channel_id=1, source_target_pairs={{0,24},{8,16},{16,8},{24,0}} | collective-permute-start | bytes 589832 | tf_op jit(solution)/shard_map/cond/branch_1_fun/ppermute | solution.py:840
  31.1 10.9 %collective-permute-start.6 = (f32[1024,256]{1,0:T(8,128)}, f32[1024,256]{1,0:T(8,128)}, u32[]{:S(2)}, u32[]{:S(2)}) collective-permute-start(f32[1024,256]{1,0:T(8,128)} %collective-permute-done.3), channel_id=1, source_target_pairs={{4,2},{12,10},{20,18},{28,26}} | collective-permute-start | bytes 3145736 | tf_op jit(solution)/shard_map/cond/branch_1_fun/ppermute | solution.py:874
  32.8 9.2 %collective-permute-start.5 = (f32[1024,256]{1,0:T(8,128)}, f32[1024,256]{1,0:T(8,128)}, u32[]{:S(2)}, u32[]{:S(2)}) collective-permute-start(f32[1024,256]{1,0:T(8,128)} %collective-permute-done.3), channel_id=1, source_target_pairs={{4,6},{12,14},{20,22},{28,30}} | collective-permute-start | bytes 3145736 | tf_op jit(solution)/shard_map/cond/branch_1_fun/ppermute | solution.py:873
  34.4 6.5 %collective-permute-start.4 = (f32[352,256]{1,0:T(8,128)}, f32[352,256]{1,0:T(8,128)}, u32[]{:S(2)}, u32[]{:S(2)}) collective-permute-start(f32[352,256]{1,0:T(8,128)} %pack.1), channel_id=1, source_target_pairs={{0,4},{8,12},{16,20},{24,28}} | collective-permute-start | bytes 1081352 | tf_op jit(solution)/shard_map/cond/branch_1_fun/ppermute | solution.py:877
  36.5 21.5 %collective-permute-start.10 = (f32[144,1536]{1,0:T(8,128)}, f32[144,1536]{1,0:T(8,128)S(1)}, u32[]{:S(2)}, u32[]{:S(2)}) collective-permute-start(f32[144,1536]{1,0:T(8,128)} %get-tuple-element.54), channel_id=1, source_target_pairs={{0,8},{8,0},{16,24},{24,16},{1,9},{9,1},{17,25},{25,17},{2,10},{10... | collective-permute-start | bytes 2654216 | tf_op jit(solution)/shard_map/cond/branch_1_fun/ppermute | solution.py:847
  37.0 21.0 %collective-permute-start.11 = (f32[144,1536]{1,0:T(8,128)}, f32[144,1536]{1,0:T(8,128)S(1)}, u32[]{:S(2)}, u32[]{:S(2)}) collective-permute-start(f32[144,1536]{1,0:T(8,128)} %get-tuple-element.55), channel_id=1, source_target_pairs={{0,16},{8,24},{16,0},{24,8},{1,17},{9,25},{17,1},{25,9},{2,18},{10... | collective-permute-start | bytes 2654216 | tf_op jit(solution)/shard_map/cond/branch_1_fun/ppermute | solution.py:847
  37.9 4.1 %copy-start.6 = (f32[1024,256]{1,0:T(8,128)S(1)}, f32[1024,256]{1,0:T(8,128)}, u32[]{:S(2)}) copy-start(f32[1024,256]{1,0:T(8,128)} %get-tuple-element.44) | copy-start | bytes 3145732 | tf_op jit(solution)/shard_map/cond
  43.7 28.6 %collective-permute-start.7 = (f32[1024,256]{1,0:T(8,128)S(1)}, f32[1024,256]{1,0:T(8,128)S(1)}, u32[]{:S(2)}, u32[]{:S(2)}) collective-permute-start(f32[1024,256]{1,0:T(8,128)S(1)} %select_select_fusion.panel_ref), channel_id=1, source_target_pairs={{0,1},{2,3},{4,5},{6,7},{8,9},{10,11},{12,13},{14,15},{16,17},{18,... | collective-permute-start | bytes 3145736 | tf_op jit(solution)/shard_map/cond/branch_1_fun/ppermute | solution.py:876
  45.0 15.0 %collective-permute-start.8 = (f32[352,256]{1,0:T(8,128)S(1)}, f32[352,256]{1,0:T(8,128)S(1)}, u32[]{:S(2)}, u32[]{:S(2)}) collective-permute-start(f32[352,256]{1,0:T(8,128)S(1)} %broadcast_select_fusion.4), channel_id=1, source_target_pairs={{0,2},{4,6},{8,10},{12,14},{16,18},{20,22},{24,26},{28,30}} | collective-permute-start | bytes 1081352 | tf_op jit(solution)/shard_map/cond/branch_1_fun/ppermute | solution.py:877
  58.4 13.9 %copy-start.8 = (s32[256,128]{1,0:T(8,128)S(1)}, s32[256,128]{1,0:T(8,128)}, u32[]{:S(2)}) copy-start(s32[256,128]{1,0:T(8,128)} %copy-done.7) | copy-start | bytes 393220 | tf_op jit(solution)/shard_map/cond
  58.4 13.4 %collective-permute-start.12 = (f32[144,1536]{1,0:T(8,128)S(1)}, f32[144,1536]{1,0:T(8,128)S(1)}, u32[]{:S(2)}, u32[]{:S(2)}) collective-permute-start(f32[144,1536]{1,0:T(8,128)S(1)} %get-tuple-element.56), channel_id=1, source_target_pairs={{0,16},{8,24},{16,0},{24,8},{1,17},{9,25},{17,1},{25,9},{2,18},{10... | collective-permute-start | bytes 2654216 | tf_op jit(solution)/shard_map/cond/branch_1_fun/ppermute | solution.py:847
  59.3 13.0 %collective-permute-start.13 = (f32[144,1536]{1,0:T(8,128)S(1)}, f32[144,1536]{1,0:T(8,128)S(1)}, u32[]{:S(2)}, u32[]{:S(2)}) collective-permute-start(f32[144,1536]{1,0:T(8,128)S(1)} %get-tuple-element.57), channel_id=1, source_target_pairs={{0,8},{8,0},{16,24},{24,16},{1,9},{9,1},{17,25},{25,17},{2,10},{10... | collective-permute-start | bytes 2654216 | tf_op jit(solution)/shard_map/cond/branch_1_fun/ppermute | solution.py:847
  60.1 2.6 %collective-permute-start.9 = (f32[352,256]{1,0:T(8,128)S(1)}, f32[352,256]{1,0:T(8,128)S(1)}, u32[]{:S(2)}, u32[]{:S(2)}) collective-permute-start(f32[352,256]{1,0:T(8,128)S(1)} %broadcast_select_fusion.3.first_ref.square_ref), channel_id=1, source_target_pairs={{0,1},{2,3},{4,5},{6,7},{8,9},{10,11},{12,13},{14,15},{16,17},{18,... | collective-permute-start | bytes 1081352 | tf_op jit(solution)/shard_map/cond/branch_1_fun/ppermute | solution.py:884

commit v13 on v10

--- a/solution.py
+++ b/solution.py
@@ -868,7 +868,6 @@
         if n + 1 < len(turns):
             message, panel_moved = lax.optimization_barrier((message, panel_moved))
     if n_row == 4:
-        message, to_y, to_x = lax.optimization_barrier((message, to_y, to_x))
         arrived += [send(to_y, 2), send(to_x, 1)]
     message_new = lax.ppermute(message, "pcol", pairs[-1])
     factors = factor(message, message_new, True)

time: 83 us -> 84.2 us (1.014)
  local copies, waits for them, and re-layouts: 1.64 us -> 0.02 us
  other arithmetic: 2.54 us -> 4.01 us
    ppermute x4, waiting for transfers between devices: 0.89 us -> 3.34 us  [send(): return lax.ppermute(x, 'prow', [(i, i ^ k) for i in range(n_row)])]
    ppermute x2, waiting for transfers between devices: 14.6 us -> 12.3 us  [capped_step(): lax.ppermute(message, 'pcol', pairs[n])]
    select_n x2, other arithmetic: 0.27 us -> 2.48 us  [capped_step(): panel = jnp.where(newer[n], panel_moved, panel)]
    cond x16 -> x8, local copies, waits for them, and re-layouts: 1.63 us -> 0.02 us
  transfers between devices with their start and end apart: 13 -> 13, of which waited for: 6 -> 6; matrix products, arithmetic and copies ran while one was open for 3% -> 4% of each run, Pallas kernels for 18% -> 19%
where the time goes in v13:
time: 84.2 us; the launch traced here: 82.6 us
  Pallas kernels  31 us (37%)
  starting transfers between devices  26.2 us (31%)
  waiting for transfers between devices  20.1 us (24%)
  other arithmetic  4.01 us (5%)
  between operations  0.85 us (1%)
    ppermute x2, waiting for transfers between devices, capped_step(): lax.ppermute(message, 'pcol', pairs[n])  12.3 us
    pallas_call x1, Pallas kernels, finish(): pl.pallas_call(functools.partial(finish_kernel, n_row), out_shape=jax.Sha...  11 us
    ppermute x3, starting transfers between devices, exchange(): lax.ppermute(x, both, [(i * n_col, (i ^ k) * n_col) for i in range(n_row)])  9.21 us
    pallas_call x1, Pallas kernels, factor(): pl.pallas_call(functools.partial(factor_kernel, width, unroll), out_shape...  9.07 us
    ppermute x1, starting transfers between devices, capped_step(): lax.ppermute(panel, 'pcol', [(i, i + turns[0]) for i in range(0, n_col, 2...  6 us
    pallas_call x1, Pallas kernels, parcel(): pl.pallas_call(functools.partial(parcel_kernel, n_row), out_shape=tuple((...  4.39 us
    pallas_call x1, Pallas kernels, begin(): pl.pallas_call(functools.partial(begin_kernel, n_row), out_shape=(jax.Sha...  4.26 us
    ppermute x2, starting transfers between devices, capped_step(): panel_moved = lax.ppermute(panel, 'pcol', pairs[n + 1])  3.65 us
  transfers between devices with their start and end apart: 13, of which 6 were waited for; matrix products, arithmetic and copies ran while one was open for 4% of the time, Pallas kernels for 19%

profile of v13, /device:TPU:0, one launch (start us, length us, event | category | flops | bytes accessed | tf_op | source)
XLA Modules:
  0.0 82.6 jit_solution(12545648947100214100)
XLA Ops:
  0.0 4.3 %begin.1 = (f32[1024,256]{1,0:T(8,128)}, s32[256,128]{1,0:T(8,128)S(1)}, s32[1]{0:T(128)}, f32[192,256]{1,0:T(8,128)}, f32[192,256]{1,0:T(8,128)}, /*index=5*/f32[192,256]{1,0:T(8,128)}, f32[192,256]{1,0:T(8,128)}) custom-call(s32[1,256]{1,0:T(1,128)} %bitcast.29, f32[1024,1,1536]{2,1,0:T(1,128)} %bitcast.25), custom_call_target="tpu_custom_call" | custom-call | bytes 10000000 | tf_op jit(solution)/shard_map/begin/pallas_call | solution.py:441
  4.9 77.5 %conditional.1 = (f32[1,1024,1,1536]{3,2,1,0:T(1,128)}) conditional(s32[]{:T(128)} %bitcast.12, (s32[256]{0:T(256)S(1)}, f32[1,1024,1,1536]{3,2,1,0:T(1,128)}) %tuple.33, (s32[256]{0:T(256)S(1)}, f32[1,1024,1,1536]{3,2,1,0:T(1,128)}, f32[192,256]{1,0:T(8,128)}, f32[192,256]{1,0:T(8,128)}, f32[192,256]{1,0:T(8,128)}, ...), branch_computations={%region_0.1_spmd, %region_1.5_spmd} | conditional | flops 2488416000 | bytes 214372192 | solution.py:883
  5.2 6.0 %collective-permute-start.3 = (f32[1024,256]{1,0:T(8,128)}, f32[1024,256]{1,0:T(8,128)S(1)}, u32[]{:S(2)}, u32[]{:S(2)}) collective-permute-start(f32[1024,256]{1,0:T(8,128)} %get-tuple-element.44), channel_id=1, source_target_pairs={{0,4},{8,12},{16,20},{24,28}} | collective-permute-start | bytes 3145736 | tf_op jit(solution)/shard_map/cond/branch_1_fun/ppermute | solution.py:852
  11.2 3.0 %collective-permute-start = (f32[192,256]{1,0:T(8,128)}, f32[192,256]{1,0:T(8,128)S(1)}, u32[]{:S(2)}, u32[]{:S(2)}) collective-permute-start(f32[192,256]{1,0:T(8,128)} %get-tuple-element.37), channel_id=1, source_target_pairs={{0,8},{8,0},{16,24},{24,16}} | collective-permute-start | bytes 589832 | tf_op jit(solution)/shard_map/cond/branch_1_fun/ppermute | solution.py:840
  14.2 3.4 %collective-permute-start.1 = (f32[192,256]{1,0:T(8,128)}, f32[192,256]{1,0:T(8,128)S(1)}, u32[]{:S(2)}, u32[]{:S(2)}) collective-permute-start(f32[192,256]{1,0:T(8,128)} %get-tuple-element.38), channel_id=1, source_target_pairs={{0,16},{8,24},{16,0},{24,8}} | collective-permute-start | bytes 589832 | tf_op jit(solution)/shard_map/cond/branch_1_fun/ppermute | solution.py:840
  17.6 2.8 %collective-permute-start.2 = (f32[192,256]{1,0:T(8,128)}, f32[192,256]{1,0:T(8,128)S(1)}, u32[]{:S(2)}, u32[]{:S(2)}) collective-permute-start(f32[192,256]{1,0:T(8,128)} %get-tuple-element.39), channel_id=1, source_target_pairs={{0,24},{8,16},{16,8},{24,0}} | collective-permute-start | bytes 589832 | tf_op jit(solution)/shard_map/cond/branch_1_fun/ppermute | solution.py:840
  20.8 4.4 %parcel.1 = (f32[144,1536]{1,0:T(8,128)}, f32[144,1536]{1,0:T(8,128)}, f32[288,1536]{1,0:T(8,128)S(1)}) custom-call(s32[96]{0:T(128)S(1)} %select_reduce_fusion.mine_ref, s32[1,256]{1,0:T(1,128)S(1)} %bitcast.30, f32[1024,1,1536]{2,1,0:T(1,128)} %bitcast.26), custom_call_target="tpu_custom_call" | custom-call | bytes 16000000 | tf_op jit(solution)/shard_map/cond/branch_1_fun/parcel/pallas_call | solution.py:535
  25.2 3.3 %collective-permute-done.2.refs_3_ = f32[192,256]{1,0:T(8,128)S(1)} collective-permute-done((f32[192,256]{1,0:T(8,128)}, f32[192,256]{1,0:T(8,128)S(1)}, u32[]{:S(2)}, u32[]{:S(2)}) %collective-permute-start.2) | collective-permute-done | bytes 196640 | tf_op jit(solution)/shard_map/cond/branch_1_fun/ppermute | solution.py:840
  28.5 1.9 %pack.1 = f32[352,256]{1,0:T(8,128)} custom-call(s32[256,128]{1,0:T(8,128)S(1)} %get-tuple-element.34.wide_ref, f32[192,256]{1,0:T(8,128)S(1)} %copy-done.9, f32[192,256]{1,0:T(8,128)S(1)} %collective-permute-done.refs_1_, f32[192,256]{1,0:T(8,128)S(1)} %collective-permute-done.1.refs_2_, f32[192,256]{1,0:T(8,128)S(1)} %collective-permute-done.2.refs_3_), custom_call_target="tpu_custom_call" | custom-call | bytes 4000000 | tf_op jit(solution)/shard_map/cond/branch_1_fun/pack/pallas_call | solution.py:639
  30.4 1.1 %broadcast_select_fusion.3 = f32[1024,256]{1,0:T(8,128)} fusion(f32[1024,256]{1,0:T(8,128)S(1)} %collective-permute-done.3, f32[1024,256]{1,0:T(8,128)S(1)} %copy-done.6, pred[]{:T(512)S(6)} %ne.60), kind=kLoop, calls=%fused_computation.31 | loop fusion | flops 262144 | bytes 3145729 | tf_op jit(solution)/shard_map/cond/branch_1_fun/jit(_where)/select_n | solution.py:865
  31.5 2.3 %collective-permute-start.5 = (f32[1024,256]{1,0:T(8,128)}, f32[1024,256]{1,0:T(8,128)}, u32[]{:S(2)}, u32[]{:S(2)}) collective-permute-start(f32[1024,256]{1,0:T(8,128)} %broadcast_select_fusion.3), channel_id=1, source_target_pairs={{0,2},{4,6},{8,10},{12,14},{16,18},{20,22},{24,26},{28,30}} | collective-permute-start | bytes 3145736 | tf_op jit(solution)/shard_map/cond/branch_1_fun/ppermute | solution.py:866
  33.8 2.0 %collective-permute-start.4 = (f32[352,256]{1,0:T(8,128)}, f32[352,256]{1,0:T(8,128)}, u32[]{:S(2)}, u32[]{:S(2)}) collective-permute-start(f32[352,256]{1,0:T(8,128)} %pack.1), channel_id=1, source_target_pairs={{0,4},{8,12},{16,20},{24,28}} | collective-permute-start | bytes 1081352 | tf_op jit(solution)/shard_map/cond/branch_1_fun/ppermute | solution.py:867
  36.2 1.0 %collective-permute-start.10 = (f32[144,1536]{1,0:T(8,128)}, f32[144,1536]{1,0:T(8,128)S(1)}, u32[]{:S(2)}, u32[]{:S(2)}) collective-permute-start(f32[144,1536]{1,0:T(8,128)} %get-tuple-element.54), channel_id=1, source_target_pairs={{0,16},{8,24},{16,0},{24,8},{1,17},{9,25},{17,1},{25,9},{2,18},{10... | collective-permute-start | bytes 2654216 | tf_op jit(solution)/shard_map/cond/branch_1_fun/ppermute | solution.py:847
  37.2 12.0 %collective-permute-done.4 = f32[352,256]{1,0:T(8,128)} collective-permute-done((f32[352,256]{1,0:T(8,128)}, f32[352,256]{1,0:T(8,128)}, u32[]{:S(2)}, u32[]{:S(2)}) %collective-permute-start.4) | collective-permute-done | bytes 360480 | tf_op jit(solution)/shard_map/cond/branch_1_fun/ppermute | solution.py:867
  49.2 1.0 %broadcast_select_fusion.6 = f32[352,256]{1,0:T(8,128)S(1)} fusion(f32[352,256]{1,0:T(8,128)} %collective-permute-done.4, f32[352,256]{1,0:T(8,128)} %pack.1, pred[]{:T(512)S(6)} %ne.60), kind=kLoop, calls=%fused_computation.37 | loop fusion | flops 90112 | bytes 1081345 | tf_op jit(solution)/shard_map/cond/branch_1_fun/jit(_where)/select_n | solution.py:867
  50.3 1.4 %broadcast_select_fusion.4.panel_ref = f32[1024,256]{1,0:T(8,128)S(1)} fusion(f32[1024,256]{1,0:T(8,128)} %collective-permute-done.5, f32[1024,256]{1,0:T(8,128)} %broadcast_select_fusion.3, pred[]{:T(512)S(6)} %ne.59), kind=kLoop, calls=%fused_computation.32 | loop fusion | flops 262144 | bytes 3145729 | tf_op jit(solution)/shard_map/cond/branch_1_fun/jit(_where)/select_n | solution.py:865
  51.7 1.4 %collective-permute-start.6 = (f32[1024,256]{1,0:T(8,128)S(1)}, f32[1024,256]{1,0:T(8,128)S(1)}, u32[]{:S(2)}, u32[]{:S(2)}) collective-permute-start(f32[1024,256]{1,0:T(8,128)S(1)} %broadcast_select_fusion.4.panel_ref), channel_id=1, source_target_pairs={{0,1},{2,3},{4,5},{6,7},{8,9},{10,11},{12,13},{14,15},{16,17},{18,... | collective-permute-start | bytes 3145736 | tf_op jit(solution)/shard_map/cond/branch_1_fun/ppermute | solution.py:866
  53.0 1.3 %collective-permute-start.7 = (f32[352,256]{1,0:T(8,128)S(1)}, f32[352,256]{1,0:T(8,128)S(1)}, u32[]{:S(2)}, u32[]{:S(2)}) collective-permute-start(f32[352,256]{1,0:T(8,128)S(1)} %broadcast_select_fusion.6), channel_id=1, source_target_pairs={{0,2},{4,6},{8,10},{12,14},{16,18},{20,22},{24,26},{28,30}} | collective-permute-start | bytes 1081352 | tf_op jit(solution)/shard_map/cond/branch_1_fun/ppermute | solution.py:867
  54.3 2.9 %collective-permute-done.9.first_ref.refs_1_ = f32[144,1536]{1,0:T(8,128)S(1)} collective-permute-done((f32[144,1536]{1,0:T(8,128)}, f32[144,1536]{1,0:T(8,128)S(1)}, u32[]{:S(2)}, u32[]{:S(2)}) %collective-permute-start.9) | collective-permute-done | bytes 884768 | tf_op jit(solution)/shard_map/cond/branch_1_fun/ppermute | solution.py:847
  57.7 0.6 collective-permute-start.11
  59.3 1.3 %collective-permute-start.8 = (f32[352,256]{1,0:T(8,128)S(1)}, f32[352,256]{1,0:T(8,128)S(1)}, u32[]{:S(2)}, u32[]{:S(2)}) collective-permute-start(f32[352,256]{1,0:T(8,128)S(1)} %broadcast_select_fusion.5.first_ref.square_ref), channel_id=1, source_target_pairs={{0,1},{2,3},{4,5},{6,7},{8,9},{10,11},{12,13},{14,15},{16,17},{18,... | collective-permute-start | bytes 1081352 | tf_op jit(solution)/shard_map/cond/branch_1_fun/ppermute | solution.py:872
  60.7 1.1 %collective-permute-done.8.second_ref.square_new_ref = f32[352,256]{1,0:T(8,128)S(1)} collective-permute-done((f32[352,256]{1,0:T(8,128)S(1)}, f32[352,256]{1,0:T(8,128)S(1)}, u32[]{:S(2)}, u32[]{:S(2)}) %collective-permute-start.8) | collective-permute-done | bytes 360480 | tf_op jit(solution)/shard_map/cond/branch_1_fun/ppermute | solution.py:872
  61.9 9.1 %factor.3 = (f32[256,256]{1,0:T(8,128)S(1)}, f32[256,256]{1,0:T(8,128)S(1)}, f32[256,256]{1,0:T(8,128)S(1)}) custom-call(f32[352,256]{1,0:T(8,128)S(1)} %broadcast_select_fusion.5.first_ref.square_ref, f32[352,256]{1,0:T(8,128)S(1)} %collective-permute-done.8.second_ref.square_new_ref), custom_call_target="tpu_custom_call" | custom-call | flops 67108864 | bytes 50000000 | tf_op jit(solution)/shard_map/cond/branch_1_fun/factor/pallas_call | solution.py:155
  71.4 11.0 %finish.1 = f32[1024,1,1536]{2,1,0:T(1,128)} custom-call(s32[96]{0:T(128)S(1)} %select_reduce_fusion.mine_ref, s32[4]{0:T(128)S(1)} %convert_reduce_fusion.1.counts_ref, s32[256,128]{1,0:T(8,128)S(1)} %copy-done.8, f32[1024,1,1536]{2,1,0:T(1,128)} %bitcast.27, f32[1024,256]{1,0:T(8,128)S(1)} %broadcast_select_fusion.4.panel_ref, ...), custom_call_target="tpu_custom_call" | custom-call | flops 2415919104 | bytes 12582912 | tf_op jit(solution)/shard_map/cond/branch_1_fun/finish/pallas_call | solution.py:786
  (28 shorter events, 2.7 us)
Async XLA Ops:
  0.0 4.9 %copy-start.10 = (s32[256]{0:T(256)S(1)}, s32[256]{0:T(256)}, u32[]{:S(2)}) copy-start(s32[256]{0:T(256)} %param.5) | copy-start | bytes 3076
  5.2 23.3 %copy-start.7 = (s32[256,128]{1,0:T(8,128)}, s32[256,128]{1,0:T(8,128)S(1)}, u32[]{:S(2)}) copy-start(s32[256,128]{1,0:T(8,128)S(1)} %get-tuple-element.34.wide_ref) | copy-start | bytes 393220 | tf_op jit(solution)/shard_map/cond
  5.2 25.2 %collective-permute-start.3 = (f32[1024,256]{1,0:T(8,128)}, f32[1024,256]{1,0:T(8,128)S(1)}, u32[]{:S(2)}, u32[]{:S(2)}) collective-permute-start(f32[1024,256]{1,0:T(8,128)} %get-tuple-element.44), channel_id=1, source_target_pairs={{0,4},{8,12},{16,20},{24,28}} | collective-permute-start | bytes 3145736 | tf_op jit(solution)/shard_map/cond/branch_1_fun/ppermute | solution.py:852
  11.2 14.0 %collective-permute-start = (f32[192,256]{1,0:T(8,128)}, f32[192,256]{1,0:T(8,128)S(1)}, u32[]{:S(2)}, u32[]{:S(2)}) collective-permute-start(f32[192,256]{1,0:T(8,128)} %get-tuple-element.37), channel_id=1, source_target_pairs={{0,8},{8,0},{16,24},{24,16}} | collective-permute-start | bytes 589832 | tf_op jit(solution)/shard_map/cond/branch_1_fun/ppermute | solution.py:840
  14.2 11.0 %collective-permute-start.1 = (f32[192,256]{1,0:T(8,128)}, f32[192,256]{1,0:T(8,128)S(1)}, u32[]{:S(2)}, u32[]{:S(2)}) collective-permute-start(f32[192,256]{1,0:T(8,128)} %get-tuple-element.38), channel_id=1, source_target_pairs={{0,16},{8,24},{16,0},{24,8}} | collective-permute-start | bytes 589832 | tf_op jit(solution)/shard_map/cond/branch_1_fun/ppermute | solution.py:840
  17.6 10.8 %collective-permute-start.2 = (f32[192,256]{1,0:T(8,128)}, f32[192,256]{1,0:T(8,128)S(1)}, u32[]{:S(2)}, u32[]{:S(2)}) collective-permute-start(f32[192,256]{1,0:T(8,128)} %get-tuple-element.39), channel_id=1, source_target_pairs={{0,24},{8,16},{16,8},{24,0}} | collective-permute-start | bytes 589832 | tf_op jit(solution)/shard_map/cond/branch_1_fun/ppermute | solution.py:840
  20.8 7.7 %copy-start.9 = (f32[192,256]{1,0:T(8,128)S(1)}, f32[192,256]{1,0:T(8,128)}, u32[]{:S(2)}) copy-start(f32[192,256]{1,0:T(8,128)} %get-tuple-element.36.refs_0_) | copy-start | bytes 589828 | tf_op jit(solution)/shard_map/cond
  25.2 5.2 %copy-start.6 = (f32[1024,256]{1,0:T(8,128)S(1)}, f32[1024,256]{1,0:T(8,128)}, u32[]{:S(2)}) copy-start(f32[1024,256]{1,0:T(8,128)} %get-tuple-element.44) | copy-start | bytes 3145732 | tf_op jit(solution)/shard_map/cond
  31.5 18.8 %collective-permute-start.5 = (f32[1024,256]{1,0:T(8,128)}, f32[1024,256]{1,0:T(8,128)}, u32[]{:S(2)}, u32[]{:S(2)}) collective-permute-start(f32[1024,256]{1,0:T(8,128)} %broadcast_select_fusion.3), channel_id=1, source_target_pairs={{0,2},{4,6},{8,10},{12,14},{16,18},{20,22},{24,26},{28,30}} | collective-permute-start | bytes 3145736 | tf_op jit(solution)/shard_map/cond/branch_1_fun/ppermute | solution.py:866
  33.8 15.5 %collective-permute-start.4 = (f32[352,256]{1,0:T(8,128)}, f32[352,256]{1,0:T(8,128)}, u32[]{:S(2)}, u32[]{:S(2)}) collective-permute-start(f32[352,256]{1,0:T(8,128)} %pack.1), channel_id=1, source_target_pairs={{0,4},{8,12},{16,20},{24,28}} | collective-permute-start | bytes 1081352 | tf_op jit(solution)/shard_map/cond/branch_1_fun/ppermute | solution.py:867
  35.8 21.5 %collective-permute-start.9 = (f32[144,1536]{1,0:T(8,128)}, f32[144,1536]{1,0:T(8,128)S(1)}, u32[]{:S(2)}, u32[]{:S(2)}) collective-permute-start(f32[144,1536]{1,0:T(8,128)} %get-tuple-element.53), channel_id=1, source_target_pairs={{0,8},{8,0},{16,24},{24,16},{1,9},{9,1},{17,25},{25,17},{2,10},{10... | collective-permute-start | bytes 2654216 | tf_op jit(solution)/shard_map/cond/branch_1_fun/ppermute | solution.py:847
  36.2 21.0 %collective-permute-start.10 = (f32[144,1536]{1,0:T(8,128)}, f32[144,1536]{1,0:T(8,128)S(1)}, u32[]{:S(2)}, u32[]{:S(2)}) collective-permute-start(f32[144,1536]{1,0:T(8,128)} %get-tuple-element.54), channel_id=1, source_target_pairs={{0,16},{8,24},{16,0},{24,8},{1,17},{9,25},{17,1},{25,9},{2,18},{10... | collective-permute-start | bytes 2654216 | tf_op jit(solution)/shard_map/cond/branch_1_fun/ppermute | solution.py:847
  51.7 19.7 %collective-permute-start.6 = (f32[1024,256]{1,0:T(8,128)S(1)}, f32[1024,256]{1,0:T(8,128)S(1)}, u32[]{:S(2)}, u32[]{:S(2)}) collective-permute-start(f32[1024,256]{1,0:T(8,128)S(1)} %broadcast_select_fusion.4.panel_ref), channel_id=1, source_target_pairs={{0,1},{2,3},{4,5},{6,7},{8,9},{10,11},{12,13},{14,15},{16,17},{18,... | collective-permute-start | bytes 3145736 | tf_op jit(solution)/shard_map/cond/branch_1_fun/ppermute | solution.py:866
  53.0 6.2 %collective-permute-start.7 = (f32[352,256]{1,0:T(8,128)S(1)}, f32[352,256]{1,0:T(8,128)S(1)}, u32[]{:S(2)}, u32[]{:S(2)}) collective-permute-start(f32[352,256]{1,0:T(8,128)S(1)} %broadcast_select_fusion.6), channel_id=1, source_target_pairs={{0,2},{4,6},{8,10},{12,14},{16,18},{20,22},{24,26},{28,30}} | collective-permute-start | bytes 1081352 | tf_op jit(solution)/shard_map/cond/branch_1_fun/ppermute | solution.py:867
  57.7 13.7 %copy-start.8 = (s32[256,128]{1,0:T(8,128)S(1)}, s32[256,128]{1,0:T(8,128)}, u32[]{:S(2)}) copy-start(s32[256,128]{1,0:T(8,128)} %copy-done.7) | copy-start | bytes 393220 | tf_op jit(solution)/shard_map/cond
  57.7 13.3 %collective-permute-start.11 = (f32[144,1536]{1,0:T(8,128)S(1)}, f32[144,1536]{1,0:T(8,128)S(1)}, u32[]{:S(2)}, u32[]{:S(2)}) collective-permute-start(f32[144,1536]{1,0:T(8,128)S(1)} %get-tuple-element.55), channel_id=1, source_target_pairs={{0,16},{8,24},{16,0},{24,8},{1,17},{9,25},{17,1},{25,9},{2,18},{10... | collective-permute-start | bytes 2654216 | tf_op jit(solution)/shard_map/cond/branch_1_fun/ppermute | solution.py:847
  58.4 13.0 %collective-permute-start.12 = (f32[144,1536]{1,0:T(8,128)S(1)}, f32[144,1536]{1,0:T(8,128)S(1)}, u32[]{:S(2)}, u32[]{:S(2)}) collective-permute-start(f32[144,1536]{1,0:T(8,128)S(1)} %get-tuple-element.56), channel_id=1, source_target_pairs={{0,8},{8,0},{16,24},{24,16},{1,9},{9,1},{17,25},{25,17},{2,10},{10... | collective-permute-start | bytes 2654216 | tf_op jit(solution)/shard_map/cond/branch_1_fun/ppermute | solution.py:847
  59.3 2.6 %collective-permute-start.8 = (f32[352,256]{1,0:T(8,128)S(1)}, f32[352,256]{1,0:T(8,128)S(1)}, u32[]{:S(2)}, u32[]{:S(2)}) collective-permute-start(f32[352,256]{1,0:T(8,128)S(1)} %broadcast_select_fusion.5.first_ref.square_ref), channel_id=1, source_target_pairs={{0,1},{2,3},{4,5},{6,7},{8,9},{10,11},{12,13},{14,15},{16,17},{18,... | collective-permute-start | bytes 1081352 | tf_op jit(solution)/shard_map/cond/branch_1_fun/ppermute | solution.py:872
